TPU v7x, 32 devices: a whole 2x2x4 slice. The times are simulated.
32 devices in a mesh: sp: 4 (over y, x), fsdp: 8 (over z, core).
Axes of the slice: x: 2, y: 2, z: 4, core: 2. Of those that a mesh axis runs over, the one named last changes fastest.
Arguments:
- tokens: bfloat16 [24576, 768], P(('fsdp', 'sp')), may hold values from -6 to 6
- segments: int32 [8, 3072], P('fsdp'), may hold values from 0 to 31, never falling along the last dimension, each value on 1 to 1536 neighbouring positions
- cotangent: bfloat16 [24576, 768], P(('fsdp', 'sp')), may hold values from -6 to 6
- w_qkv: bfloat16 [768, 2304], P(('sp', 'fsdp')), may hold values from -0.3125 to 0.3125
- b_query: bfloat16 [768], P(('sp', 'fsdp')), may hold values from -3 to 3
- b_value: bfloat16 [768], P(('sp', 'fsdp')), may hold values from -3 to 3
- w_out: bfloat16 [768, 768], P(('sp', 'fsdp')), may hold values from -0.625 to 0.625
- b_out: bfloat16 [768], P(('sp', 'fsdp')), may hold values from -2 to 2
- ln1_gain: bfloat16 [768], P(('sp', 'fsdp')), may hold values from 0.5 to 1.5
- ln1_bias: bfloat16 [768], P(('sp', 'fsdp')), may hold values from -2 to 2
- w_up: bfloat16 [768, 3072], P(('sp', 'fsdp')), may hold values from -0.21875 to 0.21875
- b_up: bfloat16 [3072], P(('sp', 'fsdp')), may hold values from -3 to 3
- w_down: bfloat16 [3072, 768], P(('sp', 'fsdp')), may hold values from -0.15625 to 0.15625
- b_down: bfloat16 [768], P(('sp', 'fsdp')), may hold values from -2 to 2
- ln2_gain: bfloat16 [768], P(('sp', 'fsdp')), may hold values from 0.5 to 1.5
- ln2_bias: bfloat16 [768], P(('sp', 'fsdp')), may hold values from -2 to 2
Outputs:
- output: bfloat16 [24576, 768], P(('fsdp', 'sp'))
- grad_input: float32 [24576, 768], P(('fsdp', 'sp'))
- grad_w_qkv: float32 [768, 2304], P(('sp', 'fsdp'))
- grad_b_query: float32 [768], P(('sp', 'fsdp'))
- grad_b_value: float32 [768], P(('sp', 'fsdp'))
- grad_w_out: float32 [768, 768], P(('sp', 'fsdp'))
- grad_b_out: float32 [768], P(('sp', 'fsdp'))
- grad_ln1_gain: float32 [768], P(('sp', 'fsdp'))
- grad_ln1_bias: float32 [768], P(('sp', 'fsdp'))
- grad_w_up: float32 [768, 3072], P(('sp', 'fsdp'))
- grad_b_up: float32 [3072], P(('sp', 'fsdp'))
- grad_w_down: float32 [3072, 768], P(('sp', 'fsdp'))
- grad_b_down: float32 [768], P(('sp', 'fsdp'))
- grad_ln2_gain: float32 [768], P(('sp', 'fsdp'))
- grad_ln2_bias: float32 [768], P(('sp', 'fsdp'))
Inputs may be any that keep to these rules, and one draw needn't show every extreme that they name: `segments`: within a sequence the ids never fall; every document has at most 1536 tokens and one document of each sequence has exactly that many.
All inputs are finite; a program needn't handle non-finite values.
Results may differ from a plain program's by a relative error of at most 0.014.
The roundings to bfloat16 on the way count: a program that leaves them out, or rounds other values in their place, can miss the bound.
Values may be sent and summed in bfloat16 or wider, within the bound.
No kernel may reach another device: no remote copies, remote signals or barrier semaphores. Data moves between devices by JAX's collectives and lax.ppermute only.
A program may use at most 192 MiB of HBM per device.

v0:
```python
from functools import partial

import jax
import jax.numpy as jnp
from jax import lax
from jax.sharding import PartitionSpec as P

HEADS = 12
HEAD = 64


norm_eps = 1e-06
masked = -1e30


def layer_normalizer(values, norm_gain, norm_shift):
    center = jnp.mean(values, -1, keepdims=True)
    mean_removed = values - center
    spread = jnp.mean(mean_removed * mean_removed, -1, keepdims=True)
    inverse_deviation = lax.rsqrt(spread + norm_eps)
    normalized_rows = mean_removed * inverse_deviation
    return (normalized_rows * norm_gain + norm_shift, normalized_rows, inverse_deviation)


def norm_reverse_pass(upstream_gradient, normalized_rows, inverse_deviation, norm_gain):
    norm_gain_gradient = jnp.sum(upstream_gradient * normalized_rows, 0)
    grad_shift = jnp.sum(upstream_gradient, 0)
    scaled_rows = upstream_gradient * norm_gain
    inner_activation = jnp.mean(scaled_rows * normalized_rows, -1, keepdims=True)
    incoming_gradient = inverse_deviation * (
        scaled_rows - jnp.mean(scaled_rows, -1, keepdims=True) - normalized_rows * inner_activation
    )
    return (incoming_gradient, norm_gain_gradient, grad_shift)


def body(
    tokens,
    segments,
    cotangent,
    w_qkv,
    b_query,
    b_value,
    w_out,
    b_out,
    ln1_gain,
    ln1_bias,
    w_up,
    b_up,
    w_down,
    b_down,
    ln2_gain,
    ln2_bias,
):
    whole = (
        lax.all_gather(w_qkv, ("sp", "fsdp"), axis=0, tiled=True),
        lax.all_gather(b_query, ("sp", "fsdp"), axis=0, tiled=True),
        lax.all_gather(b_value, ("sp", "fsdp"), axis=0, tiled=True),
        lax.all_gather(w_out, ("sp", "fsdp"), axis=0, tiled=True),
        lax.all_gather(b_out, ("sp", "fsdp"), axis=0, tiled=True),
        lax.all_gather(ln1_gain, ("sp", "fsdp"), axis=0, tiled=True),
        lax.all_gather(ln1_bias, ("sp", "fsdp"), axis=0, tiled=True),
        lax.all_gather(w_up, ("sp", "fsdp"), axis=0, tiled=True),
        lax.all_gather(b_up, ("sp", "fsdp"), axis=0, tiled=True),
        lax.all_gather(w_down, ("sp", "fsdp"), axis=0, tiled=True),
        lax.all_gather(b_down, ("sp", "fsdp"), axis=0, tiled=True),
        lax.all_gather(ln2_gain, ("sp", "fsdp"), axis=0, tiled=True),
        lax.all_gather(ln2_bias, ("sp", "fsdp"), axis=0, tiled=True),
    )
    (
        full_qkv,
        bias_query,
        bias_value,
        full_out,
        bias_out,
        attention_norm_gain,
        attention_norm_shift,
        full_up,
        bias_up,
        full_down,
        bias_down,
        feedforward_norm_gain,
        feedforward_norm_shift,
    ) = whole
    bias_query = bias_query.astype(jnp.float32)
    bias_value = bias_value.astype(jnp.float32)
    bias_out = bias_out.astype(jnp.float32)
    attention_norm_gain = attention_norm_gain.astype(jnp.float32)
    attention_norm_shift = attention_norm_shift.astype(jnp.float32)
    bias_up = bias_up.astype(jnp.float32)
    bias_down = bias_down.astype(jnp.float32)
    feedforward_norm_gain = feedforward_norm_gain.astype(jnp.float32)
    feedforward_norm_shift = feedforward_norm_shift.astype(jnp.float32)
    groups = lax.axis_size("sp")
    rows = tokens.shape[0]
    width_all = tokens.shape[1]
    heads_local = HEADS // groups
    width = heads_local * HEAD
    seq_len = rows * groups
    block = min(512, seq_len)
    nblocks = seq_len // block
    input_tokens = tokens.astype(jnp.float32)
    bias_qkv = jnp.concatenate([bias_query, jnp.zeros_like(bias_query), bias_value])
    packed = (jnp.dot(tokens, full_qkv, preferred_element_type=jnp.float32) + bias_qkv).astype(
        jnp.bfloat16
    )
    heads_in = lax.all_to_all(
        packed.reshape(rows, 3, groups, width), "sp", split_axis=2, concat_axis=0, tiled=True
    )
    queries = heads_in[:, 0, 0].reshape(seq_len, heads_local, HEAD)
    keys = heads_in[:, 1, 0].reshape(seq_len, heads_local, HEAD)
    values = heads_in[:, 2, 0].reshape(seq_len, heads_local, HEAD)
    seg_row = segments[0]
    blocked_q = queries.reshape(nblocks, block, heads_local, HEAD)
    blocked_s = seg_row.reshape(nblocks, block)

    def block_scores(query_block, seg_block):
        scores = (
            jnp.einsum("qhe,khe->hqk", query_block, keys, preferred_element_type=jnp.float32)
            * 0.125
        )
        same = seg_block[:, None] == seg_row[None, :]
        return jnp.where(same[None], scores, masked)

    def forward_block(pair):
        query_block, seg_block = pair
        scores = block_scores(query_block, seg_block)
        peak = jnp.max(scores, -1, keepdims=True)
        expo = jnp.exp(scores - peak)
        total = jnp.sum(expo, -1, keepdims=True)
        weights = (expo / total).astype(jnp.bfloat16)
        attended = jnp.einsum("hqk,khe->qhe", weights, values, preferred_element_type=jnp.float32)
        return (attended.astype(jnp.bfloat16), (peak + jnp.log(total))[..., 0])

    attended, logsum = lax.map(forward_block, (blocked_q, blocked_s))
    back_tokens = lax.all_to_all(
        attended.reshape(seq_len, 1, width), "sp", split_axis=0, concat_axis=1, tiled=True
    )
    mixed = back_tokens.reshape(rows, width_all)
    residual_branch = jnp.dot(mixed, full_out, preferred_element_type=jnp.float32) + bias_out
    attention_output, attention_normalized, attention_inverse_deviation = layer_normalizer(
        input_tokens + residual_branch, attention_norm_gain, attention_norm_shift
    )
    first_low = attention_output.astype(jnp.bfloat16)
    pre = jnp.dot(first_low, full_up, preferred_element_type=jnp.float32) + bias_up
    activ = jax.nn.gelu(pre, approximate=False).astype(jnp.bfloat16)
    feedforward_net = jnp.dot(activ, full_down, preferred_element_type=jnp.float32) + bias_down
    layer_output, feedforward_normalized, feedforward_inverse_deviation = layer_normalizer(
        attention_output + feedforward_net, feedforward_norm_gain, feedforward_norm_shift
    )
    output = layer_output.astype(jnp.bfloat16)
    again = (
        lax.all_gather(w_qkv, ("sp", "fsdp"), axis=0, tiled=True),
        lax.all_gather(w_out, ("sp", "fsdp"), axis=0, tiled=True),
        lax.all_gather(ln1_gain, ("sp", "fsdp"), axis=0, tiled=True),
        lax.all_gather(w_up, ("sp", "fsdp"), axis=0, tiled=True),
        lax.all_gather(w_down, ("sp", "fsdp"), axis=0, tiled=True),
        lax.all_gather(ln2_gain, ("sp", "fsdp"), axis=0, tiled=True),
    )
    back_qkv, back_out, reverse_attention_gain, back_up, back_down, reverse_feedforward_gain = again
    reverse_attention_gain = reverse_attention_gain.astype(jnp.float32)
    reverse_feedforward_gain = reverse_feedforward_gain.astype(jnp.float32)
    outgoing_gradient = cotangent.astype(jnp.float32)
    hidden_two_gradient, feedforward_gain_gradient, feedforward_shift_gradient = norm_reverse_pass(
        outgoing_gradient,
        feedforward_normalized,
        feedforward_inverse_deviation,
        reverse_feedforward_gain,
    )
    grad_ffn = hidden_two_gradient.astype(jnp.bfloat16)
    grad_bias_down = jnp.sum(grad_ffn.astype(jnp.float32), 0)
    grad_full_down = jnp.einsum("tf,td->fd", activ, grad_ffn, preferred_element_type=jnp.float32)
    grad_activ = jnp.einsum("td,fd->tf", grad_ffn, back_down, preferred_element_type=jnp.float32)
    gelu_value, gelu_pull = jax.vjp(partial(jax.nn.gelu, approximate=False), pre)
    grad_pre = gelu_pull(grad_activ)[0].astype(jnp.bfloat16)
    grad_bias_up = jnp.sum(grad_pre.astype(jnp.float32), 0)
    grad_full_up = jnp.einsum("td,tf->df", first_low, grad_pre, preferred_element_type=jnp.float32)
    attention_output_gradient = hidden_two_gradient + jnp.einsum(
        "tf,df->td", grad_pre, back_up, preferred_element_type=jnp.float32
    )
    grad_h1, grad_gain_one, grad_shift_one = norm_reverse_pass(
        attention_output_gradient,
        attention_normalized,
        attention_inverse_deviation,
        reverse_attention_gain,
    )
    grad_branch = grad_h1.astype(jnp.bfloat16)
    grad_bias_out = jnp.sum(grad_branch.astype(jnp.float32), 0)
    grad_full_out = jnp.einsum("td,te->de", mixed, grad_branch, preferred_element_type=jnp.float32)
    grad_mixed = jnp.einsum(
        "te,de->td", grad_branch, back_out, preferred_element_type=jnp.float32
    ).astype(jnp.bfloat16)
    grad_heads = lax.all_to_all(
        grad_mixed.reshape(rows, groups, width), "sp", split_axis=1, concat_axis=0, tiled=True
    )
    grad_blocks = grad_heads.reshape(nblocks, block, heads_local, HEAD)

    def back_block(carry, item):
        grad_keys, grad_values = carry
        query_block, seg_block, lse_block, grad_block = item
        scores = block_scores(query_block, seg_block)
        probs = jnp.exp(scores - lse_block[..., None])
        weights = probs.astype(jnp.bfloat16)
        grad_probs = jnp.einsum(
            "qhe,khe->hqk", grad_block, values, preferred_element_type=jnp.float32
        )
        inner_activation = jnp.sum(grad_probs * probs, -1, keepdims=True)
        grad_scores = (probs * (grad_probs - inner_activation)).astype(jnp.bfloat16)
        grad_query = (
            jnp.einsum("hqk,khe->qhe", grad_scores, keys, preferred_element_type=jnp.float32)
            * 0.125
        )
        grad_keys = (
            grad_keys
            + jnp.einsum(
                "hqk,qhe->khe", grad_scores, query_block, preferred_element_type=jnp.float32
            )
            * 0.125
        )
        grad_values = grad_values + jnp.einsum(
            "hqk,qhe->khe", weights, grad_block, preferred_element_type=jnp.float32
        )
        return ((grad_keys, grad_values), grad_query)

    empty = jnp.zeros((seq_len, heads_local, HEAD), jnp.float32)
    (grad_keys, grad_values), grad_query = lax.scan(
        back_block, (empty, empty), (blocked_q, blocked_s, logsum, grad_blocks)
    )
    stacked = jnp.stack(
        [
            grad_query.reshape(seq_len, width),
            grad_keys.reshape(seq_len, width),
            grad_values.reshape(seq_len, width),
        ],
        1,
    )
    stacked = stacked.astype(jnp.bfloat16)[:, :, None, :]
    grad_back = lax.all_to_all(stacked, "sp", split_axis=0, concat_axis=2, tiled=True)
    grad_packed = grad_back.reshape(rows, 3 * width_all)
    grad_wide = grad_packed.astype(jnp.float32)
    grad_bias_query = jnp.sum(grad_wide[:, :width_all], 0)
    grad_bias_value = jnp.sum(grad_wide[:, 2 * width_all :], 0)
    grad_full_qkv = jnp.einsum("td,tc->dc", tokens, grad_packed, preferred_element_type=jnp.float32)
    grad_input = grad_h1 + jnp.einsum(
        "tc,dc->td", grad_packed, back_qkv, preferred_element_type=jnp.float32
    )
    grads = (
        grad_full_qkv,
        grad_bias_query,
        grad_bias_value,
        grad_full_out,
        grad_bias_out,
        grad_gain_one,
        grad_shift_one,
        grad_full_up,
        grad_bias_up,
        grad_full_down,
        grad_bias_down,
        feedforward_gain_gradient,
        feedforward_shift_gradient,
    )
    owned = (
        lax.psum_scatter(grads[0], ("sp", "fsdp"), scatter_dimension=0, tiled=True),
        lax.psum_scatter(grads[1], ("sp", "fsdp"), scatter_dimension=0, tiled=True),
        lax.psum_scatter(grads[2], ("sp", "fsdp"), scatter_dimension=0, tiled=True),
        lax.psum_scatter(grads[3], ("sp", "fsdp"), scatter_dimension=0, tiled=True),
        lax.psum_scatter(grads[4], ("sp", "fsdp"), scatter_dimension=0, tiled=True),
        lax.psum_scatter(grads[5], ("sp", "fsdp"), scatter_dimension=0, tiled=True),
        lax.psum_scatter(grads[6], ("sp", "fsdp"), scatter_dimension=0, tiled=True),
        lax.psum_scatter(grads[7], ("sp", "fsdp"), scatter_dimension=0, tiled=True),
        lax.psum_scatter(grads[8], ("sp", "fsdp"), scatter_dimension=0, tiled=True),
        lax.psum_scatter(grads[9], ("sp", "fsdp"), scatter_dimension=0, tiled=True),
        lax.psum_scatter(grads[10], ("sp", "fsdp"), scatter_dimension=0, tiled=True),
        lax.psum_scatter(grads[11], ("sp", "fsdp"), scatter_dimension=0, tiled=True),
        lax.psum_scatter(grads[12], ("sp", "fsdp"), scatter_dimension=0, tiled=True),
    )
    return (
        output,
        grad_input,
        owned[0],
        owned[1],
        owned[2],
        owned[3],
        owned[4],
        owned[5],
        owned[6],
        owned[7],
        owned[8],
        owned[9],
        owned[10],
        owned[11],
        owned[12],
    )


def solution(mesh):
    in_specs = (
        P(("fsdp", "sp"), None),
        P("fsdp", None),
        P(("fsdp", "sp"), None),
        P(("sp", "fsdp"), None),
        P(("sp", "fsdp")),
        P(("sp", "fsdp")),
        P(("sp", "fsdp"), None),
        P(("sp", "fsdp")),
        P(("sp", "fsdp")),
        P(("sp", "fsdp")),
        P(("sp", "fsdp"), None),
        P(("sp", "fsdp")),
        P(("sp", "fsdp"), None),
        P(("sp", "fsdp")),
        P(("sp", "fsdp")),
        P(("sp", "fsdp")),
    )
    out_specs = (
        P(("fsdp", "sp"), None),
        P(("fsdp", "sp"), None),
        P(("sp", "fsdp"), None),
        P(("sp", "fsdp")),
        P(("sp", "fsdp")),
        P(("sp", "fsdp"), None),
        P(("sp", "fsdp")),
        P(("sp", "fsdp")),
        P(("sp", "fsdp")),
        P(("sp", "fsdp"), None),
        P(("sp", "fsdp")),
        P(("sp", "fsdp"), None),
        P(("sp", "fsdp")),
        P(("sp", "fsdp")),
        P(("sp", "fsdp")),
    )
    return jax.shard_map(body, mesh=mesh, in_specs=in_specs, out_specs=out_specs, check_vma=False)
```

profile of v0, /device:TPU:0, one launch (start us, length us, event | category | flops | bytes accessed | tf_op | source)
XLA Modules:
  0.0 1089.3 jit_solution(329805828917027170)
XLA Ops:
  17.0 42.8 %all-reduce.19 = (bf16[768]{0:T(1024)(128)(2,1)S(1)}, bf16[768]{0:T(1024)(128)(2,1)S(1)}, bf16[768]{0:T(1024)(128)(2,1)}, bf16[768]{0:T(1024)(128)(2,1)}, bf16[7...) all-reduce(bf16[768]{0:T(1024)(128)(2,1)S(1)} %dynamic-update-slice, ...), channel_id=1, replica_groups=mesh['sp'=4,'fsdp'=8] {'sp','fsdp'}, use_global_device_ids=true, to_apply=%add.1 | all-reduce | flops 9216 | bytes 36864
  59.7 14.3 %all-gather.5.cloned.1.call-done = bf16[768,2304]{1,0:T(8,128)(2,1)} async-done(((bf16[24,2304]{1,0:T(8,128)(2,1)}), bf16[768,2304]{1,0:T(8,128)(2,1)}) %all-gather.5.cloned.1.call-update) | async-done | bytes 3538960 | tf_op jit(solution)/shard_map/all_gather | solution.py:55
  74.1 7.0 add_convert_fusion.1
  95.2 40.5 %all-to-all-done = bf16[768,3,4,192]{0,3,1,2:T(8,128)(2,1)S(1)} async-done(((bf16[768,3,4,192]{0,3,1,2:T(8,128)(2,1)}), bf16[768,3,4,192]{0,3,1,2:T(8,128)(2,1)S(1)}, u32[]{:S(2)}, u32[]{:S(2)}) %all-to-all-start) | async-done | bytes 3538976 | tf_op jit(solution)/shard_map/all_to_all | solution.py:106
  140.8 123.8 %while.27 = (s32[]{:T(128)}, bf16[6,512,3,64]{1,3,2,0:T(8,128)(2,1)}, f32[6,3,512]{2,1,0:T(4,128)}, s32[6,512]{1,0:T(8,128)}, s32[1,3072]{1,0:T(1,128)S(1)}, /*i...) while((s32[]{:T(128)}, ...), condition=%wide.region_3.4_spmd, body=%wide.region_0.3_spmd.sunk | while | flops 1266252288 | bytes 65738336 | solution.py:134
  153.7 7.8 fusion.119
  174.3 7.8 fusion.119
  183.7 5.3 fusion.117
  194.9 7.8 fusion.119
  204.4 5.3 fusion.117
  215.6 7.8 fusion.119
  225.0 5.3 fusion.117
  236.2 7.8 fusion.119
  256.9 7.8 fusion.119
  264.6 5.4 copy.127
  270.0 11.5 %reshape.259 = bf16[3072,1,192]{2,1,0:T(2,128)(2,1)S(1)} reshape(bf16[6,512,3,64]{3,2,1,0:T(4,128)(2,1)} %copy.127) | data formatting | bytes 2359296 | tf_op jit(solution)/shard_map/reshape | solution.py:136
  282.1 18.3 %reduce.4 = bf16[3072,192]{1,0:T(8,128)(2,1)} reduce(bf16[3072,1,192]{2,1,0:T(2,128)(2,1)S(1)} %reshape.259, bf16[]{:T(256)} %broadcast.372), dimensions={1}, to_apply=%reshape.259.reduce_sub_computation | reduce | bytes 2359298 | tf_op jit(solution)/shard_map/reshape | solution.py:136
  316.2 8.1 all-to-all-done.1
  327.8 6.0 copy.108
  340.5 28.8 %multiply_convert_fusion.1 = (bf16[768,3072]{1,0:T(8,128)(2,1)}, f32[768,3072]{1,0:T(8,128)}, f32[768,3072]{1,0:T(8,128)}) fusion(f32[3072]{0:T(1024)} %convert_element_type.102, bf16[768,3072]{1,0:T(8,128)(2,1)} %all-gather.9.cloned.1.call-done, f32[768,768]{0,1:T(8,128)S(1)} %get-tuple-element.392, f32[768]{0:T(1024)} %convert_element_type.100, ...), kind=kOutput, calls=%fused_computation.55 | convolution fusion | flops 3782541312 | bytes 30695424 | tf_op jit(solution)/shard_map/dot_general | solution.py:144
  369.2 7.8 fusion.68
  382.7 14.6 %convert_reduce_fusion = (f32[3072]{0:T(1024)}, bf16[768,3072]{1,0:T(8,128)(2,1)}) fusion(f32[768,3072]{1,0:T(8,128)} %get-tuple-element.382, f32[768,3072]{1,0:T(8,128)} %get-tuple-element.393, f32[3072]{0:T(1024)S(1)} %copy-done.24, bf16[768,768]{0,1:T(8,128)(2,1)S(1)} %get-tuple-element.376, bf16[3072,768]{1,0:T(8,128)(2,1)} %all-gather.11.cloned.1.call-done), kind=kOutput, calls=%fused_computation.53 | convolution fusion | flops 3663983616 | bytes 29515776 | tf_op jit(solution)/shard_map/td,fd->tf/dot_general | solution.py:172
  397.3 8.0 multiply_reduce_fusion.1
  411.5 8.8 fusion.60
  428.3 8.7 fusion.69
  437.1 5.6 all-to-all-done.2
  448.9 397.9 %while.28 = (s32[]{:T(128)}, f32[3072,3,64]{0,2,1:T(8,128)}, f32[3072,3,64]{0,2,1:T(8,128)}, bf16[6,512,3,64]{1,3,2,0:T(8,128)(2,1)}, bf16[6,512,3,64]{1,3,2,0:T...) while((s32[]{:T(128)}, f32[3072,3,64]{0,2,1:T(8,128)}, ...), condition=%wide.region_14.15_spmd.clone, body=%wide.region_12.14_spmd.clone.sunk | while | flops 3095296512 | bytes 204536528 | solution.py:225
  449.3 9.1 fusion.129
  460.9 13.8 %multiply_reduce_fusion.7 = (f32[3,512]{1,0:T(4,128)S(1)}, f32[3,512,3072]{2,1,0:T(8,128)}) fusion(f32[3,512,3072]{2,1,0:T(8,128)} %fusion.129, f32[3,512]{1,0:T(4,128)S(1)} %dynamic-slice_bitcast_fusion.2, pred[512,3072]{1,0:T(8,128)(4,1)S(1)} %broadcast_compare_fusion.5, bf16[3072,3,64]{0,2,1:T(8,128)(2,1)S(1)} %copy-done.3, ...), kind=kOutput, calls=%fused_computation.19.clone.1 | convolution fusion | flops 627571200 | bytes 40710656 | tf_op jit(solution)/shard_map/while/body/eval_jaxpr/qhe,khe->hqk/dot_general | solution.py:203
  474.8 17.8 %multiply_convert_fusion.3 = bf16[3,512,3072]{2,1,0:T(8,128)(2,1)} fusion(f32[3,512,3072]{2,1,0:T(8,128)} %get-tuple-element.521, f32[3,512,3072]{2,1,0:T(8,128)} %fusion.129, f32[3,512]{1,0:T(4,128)S(1)} %get-tuple-element.522, f32[3,512]{1,0:T(4,128)S(1)} %dynamic-slice_bitcast_fusion.2, pred[512,3072]{1,0:T(8,128)(4,1)S(1)} %broadcast_compare_fusion.5), kind=kLoop, calls=%fused_computation.18.clone.1 | loop fusion | flops 28311552 | bytes 48771072 | tf_op jit(solution)/shard_map/while/body/eval_jaxpr/convert_element_type | solution.py:207
  492.6 7.2 fusion.130
  503.4 10.4 fusion.131
  513.8 9.1 fusion.129
  525.4 14.3 %multiply_reduce_fusion.7 = (f32[3,512]{1,0:T(4,128)S(1)}, f32[3,512,3072]{2,1,0:T(8,128)}) fusion(f32[3,512,3072]{2,1,0:T(8,128)} %fusion.129, f32[3,512]{1,0:T(4,128)S(1)} %dynamic-slice_bitcast_fusion.2, pred[512,3072]{1,0:T(8,128)(4,1)S(1)} %broadcast_compare_fusion.5, bf16[3072,3,64]{0,2,1:T(8,128)(2,1)S(1)} %copy-done.3, ...), kind=kOutput, calls=%fused_computation.19.clone.1 | convolution fusion | flops 627571200 | bytes 40710656 | tf_op jit(solution)/shard_map/while/body/eval_jaxpr/qhe,khe->hqk/dot_general | solution.py:203
  539.6 18.9 %multiply_convert_fusion.3 = bf16[3,512,3072]{2,1,0:T(8,128)(2,1)} fusion(f32[3,512,3072]{2,1,0:T(8,128)} %get-tuple-element.521, f32[3,512,3072]{2,1,0:T(8,128)} %fusion.129, f32[3,512]{1,0:T(4,128)S(1)} %get-tuple-element.522, f32[3,512]{1,0:T(4,128)S(1)} %dynamic-slice_bitcast_fusion.2, pred[512,3072]{1,0:T(8,128)(4,1)S(1)} %broadcast_compare_fusion.5), kind=kLoop, calls=%fused_computation.18.clone.1 | loop fusion | flops 28311552 | bytes 48771072 | tf_op jit(solution)/shard_map/while/body/eval_jaxpr/convert_element_type | solution.py:207
  558.5 7.8 fusion.130
  570.0 10.9 %fusion.131 = f32[3072,3,64]{0,2,1:T(8,128)} fusion(f32[3,512,3072]{2,1,0:T(8,128)} %fusion.129, f32[3,512]{1,0:T(4,128)S(1)} %dynamic-slice_bitcast_fusion.2, pred[512,3072]{1,0:T(8,128)(4,1)S(1)} %broadcast_compare_fusion.5, f32[3072,3,64]{0,2,1:T(8,128)} %get-tuple-element.565, pred[]{:T(512)S(6)} %compare.3, ...), kind=kOutput, calls=%fused_computation.28.clone.1 | convolution fusion | flops 624033792 | bytes 25369088 | tf_op jit(solution)/shard_map/while/body/eval_jaxpr/hqk,qhe->khe/dot_general | solution.py:219
  580.9 9.0 fusion.129
  592.4 14.1 %multiply_reduce_fusion.7 = (f32[3,512]{1,0:T(4,128)S(1)}, f32[3,512,3072]{2,1,0:T(8,128)}) fusion(f32[3,512,3072]{2,1,0:T(8,128)} %fusion.129, f32[3,512]{1,0:T(4,128)S(1)} %dynamic-slice_bitcast_fusion.2, pred[512,3072]{1,0:T(8,128)(4,1)S(1)} %broadcast_compare_fusion.5, bf16[3072,3,64]{0,2,1:T(8,128)(2,1)S(1)} %copy-done.3, ...), kind=kOutput, calls=%fused_computation.19.clone.1 | convolution fusion | flops 627571200 | bytes 40710656 | tf_op jit(solution)/shard_map/while/body/eval_jaxpr/qhe,khe->hqk/dot_general | solution.py:203
  606.5 17.8 %multiply_convert_fusion.3 = bf16[3,512,3072]{2,1,0:T(8,128)(2,1)} fusion(f32[3,512,3072]{2,1,0:T(8,128)} %get-tuple-element.521, f32[3,512,3072]{2,1,0:T(8,128)} %fusion.129, f32[3,512]{1,0:T(4,128)S(1)} %get-tuple-element.522, f32[3,512]{1,0:T(4,128)S(1)} %dynamic-slice_bitcast_fusion.2, pred[512,3072]{1,0:T(8,128)(4,1)S(1)} %broadcast_compare_fusion.5), kind=kLoop, calls=%fused_computation.18.clone.1 | loop fusion | flops 28311552 | bytes 48771072 | tf_op jit(solution)/shard_map/while/body/eval_jaxpr/convert_element_type | solution.py:207
  624.4 7.9 fusion.130
  636.0 11.0 %fusion.131 = f32[3072,3,64]{0,2,1:T(8,128)} fusion(f32[3,512,3072]{2,1,0:T(8,128)} %fusion.129, f32[3,512]{1,0:T(4,128)S(1)} %dynamic-slice_bitcast_fusion.2, pred[512,3072]{1,0:T(8,128)(4,1)S(1)} %broadcast_compare_fusion.5, f32[3072,3,64]{0,2,1:T(8,128)} %get-tuple-element.565, pred[]{:T(512)S(6)} %compare.3, ...), kind=kOutput, calls=%fused_computation.28.clone.1 | convolution fusion | flops 624033792 | bytes 25369088 | tf_op jit(solution)/shard_map/while/body/eval_jaxpr/hqk,qhe->khe/dot_general | solution.py:219
  647.0 8.8 fusion.129
  658.3 14.0 %multiply_reduce_fusion.7 = (f32[3,512]{1,0:T(4,128)S(1)}, f32[3,512,3072]{2,1,0:T(8,128)}) fusion(f32[3,512,3072]{2,1,0:T(8,128)} %fusion.129, f32[3,512]{1,0:T(4,128)S(1)} %dynamic-slice_bitcast_fusion.2, pred[512,3072]{1,0:T(8,128)(4,1)S(1)} %broadcast_compare_fusion.5, bf16[3072,3,64]{0,2,1:T(8,128)(2,1)S(1)} %copy-done.3, ...), kind=kOutput, calls=%fused_computation.19.clone.1 | convolution fusion | flops 627571200 | bytes 40710656 | tf_op jit(solution)/shard_map/while/body/eval_jaxpr/qhe,khe->hqk/dot_general | solution.py:203
  672.3 18.9 %multiply_convert_fusion.3 = bf16[3,512,3072]{2,1,0:T(8,128)(2,1)} fusion(f32[3,512,3072]{2,1,0:T(8,128)} %get-tuple-element.521, f32[3,512,3072]{2,1,0:T(8,128)} %fusion.129, f32[3,512]{1,0:T(4,128)S(1)} %get-tuple-element.522, f32[3,512]{1,0:T(4,128)S(1)} %dynamic-slice_bitcast_fusion.2, pred[512,3072]{1,0:T(8,128)(4,1)S(1)} %broadcast_compare_fusion.5), kind=kLoop, calls=%fused_computation.18.clone.1 | loop fusion | flops 28311552 | bytes 48771072 | tf_op jit(solution)/shard_map/while/body/eval_jaxpr/convert_element_type | solution.py:207
  691.2 8.3 fusion.130
  703.2 12.1 %fusion.131 = f32[3072,3,64]{0,2,1:T(8,128)} fusion(f32[3,512,3072]{2,1,0:T(8,128)} %fusion.129, f32[3,512]{1,0:T(4,128)S(1)} %dynamic-slice_bitcast_fusion.2, pred[512,3072]{1,0:T(8,128)(4,1)S(1)} %broadcast_compare_fusion.5, f32[3072,3,64]{0,2,1:T(8,128)} %get-tuple-element.565, pred[]{:T(512)S(6)} %compare.3, ...), kind=kOutput, calls=%fused_computation.28.clone.1 | convolution fusion | flops 624033792 | bytes 25369088 | tf_op jit(solution)/shard_map/while/body/eval_jaxpr/hqk,qhe->khe/dot_general | solution.py:219
  715.3 9.0 fusion.129
  726.8 14.0 %multiply_reduce_fusion.7 = (f32[3,512]{1,0:T(4,128)S(1)}, f32[3,512,3072]{2,1,0:T(8,128)}) fusion(f32[3,512,3072]{2,1,0:T(8,128)} %fusion.129, f32[3,512]{1,0:T(4,128)S(1)} %dynamic-slice_bitcast_fusion.2, pred[512,3072]{1,0:T(8,128)(4,1)S(1)} %broadcast_compare_fusion.5, bf16[3072,3,64]{0,2,1:T(8,128)(2,1)S(1)} %copy-done.3, ...), kind=kOutput, calls=%fused_computation.19.clone.1 | convolution fusion | flops 627571200 | bytes 40710656 | tf_op jit(solution)/shard_map/while/body/eval_jaxpr/qhe,khe->hqk/dot_general | solution.py:203
  740.8 18.1 %multiply_convert_fusion.3 = bf16[3,512,3072]{2,1,0:T(8,128)(2,1)} fusion(f32[3,512,3072]{2,1,0:T(8,128)} %get-tuple-element.521, f32[3,512,3072]{2,1,0:T(8,128)} %fusion.129, f32[3,512]{1,0:T(4,128)S(1)} %get-tuple-element.522, f32[3,512]{1,0:T(4,128)S(1)} %dynamic-slice_bitcast_fusion.2, pred[512,3072]{1,0:T(8,128)(4,1)S(1)} %broadcast_compare_fusion.5), kind=kLoop, calls=%fused_computation.18.clone.1 | loop fusion | flops 28311552 | bytes 48771072 | tf_op jit(solution)/shard_map/while/body/eval_jaxpr/convert_element_type | solution.py:207
  758.9 7.8 fusion.130
  770.4 11.0 %fusion.131 = f32[3072,3,64]{0,2,1:T(8,128)} fusion(f32[3,512,3072]{2,1,0:T(8,128)} %fusion.129, f32[3,512]{1,0:T(4,128)S(1)} %dynamic-slice_bitcast_fusion.2, pred[512,3072]{1,0:T(8,128)(4,1)S(1)} %broadcast_compare_fusion.5, f32[3072,3,64]{0,2,1:T(8,128)} %get-tuple-element.565, pred[]{:T(512)S(6)} %compare.3, ...), kind=kOutput, calls=%fused_computation.28.clone.1 | convolution fusion | flops 624033792 | bytes 25369088 | tf_op jit(solution)/shard_map/while/body/eval_jaxpr/hqk,qhe->khe/dot_general | solution.py:219
  781.4 9.0 fusion.129
  792.8 13.8 %multiply_reduce_fusion.7 = (f32[3,512]{1,0:T(4,128)S(1)}, f32[3,512,3072]{2,1,0:T(8,128)}) fusion(f32[3,512,3072]{2,1,0:T(8,128)} %fusion.129, f32[3,512]{1,0:T(4,128)S(1)} %dynamic-slice_bitcast_fusion.2, pred[512,3072]{1,0:T(8,128)(4,1)S(1)} %broadcast_compare_fusion.5, bf16[3072,3,64]{0,2,1:T(8,128)(2,1)S(1)} %copy-done.3, ...), kind=kOutput, calls=%fused_computation.19.clone.1 | convolution fusion | flops 627571200 | bytes 40710656 | tf_op jit(solution)/shard_map/while/body/eval_jaxpr/qhe,khe->hqk/dot_general | solution.py:203
  806.6 17.7 %multiply_convert_fusion.3 = bf16[3,512,3072]{2,1,0:T(8,128)(2,1)} fusion(f32[3,512,3072]{2,1,0:T(8,128)} %get-tuple-element.521, f32[3,512,3072]{2,1,0:T(8,128)} %fusion.129, f32[3,512]{1,0:T(4,128)S(1)} %get-tuple-element.522, f32[3,512]{1,0:T(4,128)S(1)} %dynamic-slice_bitcast_fusion.2, pred[512,3072]{1,0:T(8,128)(4,1)S(1)} %broadcast_compare_fusion.5), kind=kLoop, calls=%fused_computation.18.clone.1 | loop fusion | flops 28311552 | bytes 48771072 | tf_op jit(solution)/shard_map/while/body/eval_jaxpr/convert_element_type | solution.py:207
  824.3 7.8 fusion.130
  835.8 10.9 fusion.131
  856.4 6.9 copy.117
  863.3 75.8 %all_to_all.63 = bf16[3072,3,1,192]{3,1,2,0:T(4,128)(2,1)} all-to-all(bf16[3072,3,1,192]{3,1,2,0:T(4,128)(2,1)} %copy.117), channel_id=1, replica_groups=mesh['sp'=4,'fsdp'=8] {'sp'}, dimensions={0} | all-to-all | bytes 7077888 | tf_op jit(solution)/shard_map/all_to_all | solution.py:237
  939.2 10.5 copy.128
  957.0 8.1 copy.129
  968.9 39.2 %all-reduce.18 = (f32[768]{0:T(1024)}, f32[768]{0:T(1024)}, f32[768]{0:T(1024)}, f32[768]{0:T(1024)}, f32[768]{0:T(1024)}, /*index=5*/f32[3072]{0:T(1024)}, f32[768]{0:T(1024)}, f32[768]{0:T(1024)}, f32[768]{0:T(1024)}) all-reduce(f32[768]{0:T(1024)S(1)} %get-tuple-element.310, ...), channel_id=3, replica_groups=mesh['sp'=4,'fsdp'=8] {'sp','fsdp'}, use_global_device_ids=true, to_apply=%region_17.18.clone | all-reduce | flops 9216 | bytes 73728
  1018.1 7.1 convolution_add_fusion
  1029.5 52.7 %reduce-scatter.13.cloned.1.call-done = f32[24,2304]{1,0:T(8,128)} async-done(((f32[768,2304]{1,0:T(8,128)}), f32[24,2304]{1,0:T(8,128)}) %reduce-scatter.13.cloned.1.call-update) | async-done | bytes 221200
  (257 shorter events, 214.0 us)
Async XLA Ops:
  7.2 66.9 %all-gather.5.cloned.1.call-start = ((), (), s32[]{:S(2)}) async-start(), calls=%async_computation.8 | async-start | bytes 3649536 | tf_op jit(solution)/shard_map/all_gather | solution.py:55
  7.9 328.8 %all-gather.7.cloned.1.call-start = ((), (), s32[]{:S(2)}) async-start(), calls=%async_computation.9 | async-start | bytes 1216512 | tf_op jit(solution)/shard_map/all_gather | solution.py:58
  8.7 331.8 %all-gather.9.cloned.1.call-start = ((), (), s32[]{:S(2)}) async-start(), calls=%async_computation.10 | async-start | bytes 4866048 | tf_op jit(solution)/shard_map/all_gather | solution.py:62
  87.6 5.0 copy-start.10
  87.6 48.0 %all-to-all-start = ((bf16[768,3,4,192]{0,3,1,2:T(8,128)(2,1)}), bf16[768,3,4,192]{0,3,1,2:T(8,128)(2,1)S(1)}, u32[]{:S(2)}, u32[]{:S(2)}) async-start(bf16[768,3,4,192]{0,3,1,2:T(8,128)(2,1)} %copy.103), calls=%async_computation | async-start | bytes 7077888 | tf_op jit(solution)/shard_map/all_to_all | solution.py:106
  91.5 277.8 %all-gather.11.cloned.1.call-start = ((), (), s32[]{:S(2)}) async-start(), calls=%async_computation.11 | async-start | bytes 4866048 | tf_op jit(solution)/shard_map/all_gather | solution.py:64
  300.3 9.0 copy-start.14
  304.8 6.4 copy-start.32
  304.8 6.4 copy-start.31
  304.8 7.0 copy-start.30
  304.8 7.6 copy-start.25
  304.8 8.2 copy-start.29
  304.8 8.8 copy-start.28
  304.8 9.4 copy-start.13
  304.9 19.5 %all-to-all-start.1 = ((bf16[4,2,73728]{2,1,0:T(2,128)(2,1)}), bf16[4,2,73728]{2,1,0:T(2,128)(2,1)}, u32[]{:S(2)}, u32[]{:S(2)}) async-start(bf16[4,2,73728]{2,1,0:T(2,128)(2,1)} %reshape.271), calls=%async_computation.1 | async-start | bytes 2359296 | tf_op jit(solution)/shard_map/all_to_all | solution.py:135
  309.3 6.4 copy-start.27
  309.3 720.2 %reduce-scatter.7.cloned.1.call-start = ((), (), s32[]{:S(2)}) async-start(), calls=%async_computation.12 | async-start | bytes 2433024 | tf_op jit(solution)/shard_map/reduce_scatter | solution.py:265
  377.0 1.3 copy-start.6
  377.0 1.3 copy-start.16
  377.3 2.6 copy-start.21
  379.9 2.7 copy-start.24
  379.9 17.4 %slice-start = ((s8[4718592]{0:T(1024)(128)(4,1)}), s8[4194304]{0:T(1024)(128)(4,1)S(1)}, s32[]{:S(2)}) async-start(s8[4718592]{0:T(1024)(128)(4,1)} %bitcast.168), calls=%async_computation.16 | async-start | bytes 8388608
  382.7 14.6 %copy-start.11 = (bf16[768,768]{0,1:T(8,128)(2,1)}, bf16[768,768]{0,1:T(8,128)(2,1)S(1)}, u32[]{:S(2)}) copy-start(bf16[768,768]{0,1:T(8,128)(2,1)S(1)} %get-tuple-element.376) | copy-start | bytes 3538948
  382.7 14.6 %copy-start.17 = (f32[768]{0:T(1024)S(1)}, f32[768]{0:T(1024)}, u32[]{:S(2)}) copy-start(f32[768]{0:T(1024)} %convert_element_type.99) | copy-start | bytes 9220
  382.7 14.6 %copy-start.19 = (f32[768]{0:T(1024)S(1)}, f32[768]{0:T(1024)}, u32[]{:S(2)}) copy-start(f32[768]{0:T(1024)} %add_rsqrt_fusion.1) | copy-start | bytes 9220
  382.7 14.6 %slice-start.1 = ((s8[4718592]{0:T(1024)(128)(4,1)}), s8[524288]{0:T(1024)(128)(4,1)S(1)}, s32[]{:S(2)}) async-start(s8[4718592]{0:T(1024)(128)(4,1)} %bitcast.168), calls=%async_computation.17 | async-start | bytes 1048576
  406.9 1.4 copy-start.7
  410.8 0.7 copy-start.18
  410.8 0.7 copy-start.20
  410.8 0.7 copy-start.26
  410.9 618.6 %reduce-scatter.9.cloned.1.call-start = ((), (), s32[]{:S(2)}) async-start(), calls=%async_computation.13 | async-start | bytes 9732096 | tf_op jit(solution)/shard_map/reduce_scatter | solution.py:269
  420.4 1.7 copy-start.8
  420.4 2.0 copy-start.33
  424.6 3.8 copy-start.12
  424.6 18.1 %all-to-all-start.2 = ((bf16[768,4,192]{0,2,1:T(8,128)(2,1)}), bf16[768,4,192]{0,2,1:T(8,128)(2,1)S(1)}, u32[]{:S(2)}, u32[]{:S(2)}) async-start(bf16[768,4,192]{0,2,1:T(8,128)(2,1)} %bitcast.13), calls=%async_computation.2 | async-start | bytes 2359296 | tf_op jit(solution)/shard_map/all_to_all | solution.py:192
  428.2 601.3 %reduce-scatter.11.cloned.1.call-start = ((), (), s32[]{:S(2)}) async-start(), calls=%async_computation.14 | async-start | bytes 9732096 | tf_op jit(solution)/shard_map/reduce_scatter | solution.py:271
  437.0 645.2 %reduce-scatter.13.cloned.1.call-start = ((), (), s32[]{:S(2)}) async-start(), calls=%async_computation.15 | async-start | bytes 7299072
  444.7 4.3 copy-start.2
  458.5 2.5 copy-start.3
  492.6 7.2 copy-start
  522.9 2.5 copy-start.3
  558.5 7.8 copy-start
  589.9 2.5 copy-start.3
  624.4 8.0 copy-start
  655.8 2.5 copy-start.3
  691.2 8.3 copy-start
  724.4 2.5 copy-start.3
  758.9 7.8 copy-start
  790.3 2.5 copy-start.3
  824.3 7.8 copy-start
  846.8 7.0 copy-start.1
  854.0 2.0 copy-start.9
  949.7 2.3 copy-start.15
  950.2 1.8 copy-start.4
  965.1 2.6 copy-start.5
  968.2 0.7 copy-start.22
  968.2 0.7 copy-start.23
Sparse Core Ops, SparseCore 0:
  11.0 62.9 all-gather.4
  77.1 63.5 all-gather.6
  143.6 62.7 all-gather.8
  209.3 62.5 all-gather.10
  411.0 97.8 reduce-scatter.6
  516.2 134.3 reduce-scatter.8
  657.1 134.7 reduce-scatter.10
  965.2 116.9 reduce-scatter.12
where the time goes:
time: 1100 us; the launch traced here: 1090 us
  matrix products  455 us (41%)
  other arithmetic  189 us (17%)
  blocking collectives  158 us (14%)
  local copies, waits for them, and re-layouts  136 us (12%)
  waiting for transfers between devices  124 us (11%)
  between operations  14.8 us (1%)
  starting transfers between devices  12.3 us (1%)
    convert_element_type x6, other arithmetic, back_block(): grad_scores = (probs * (grad_probs - inner_activation)).astype(jnp.bfloat16)  109 us
    dot_general x12, matrix products, block_scores(): jnp.einsum('qhe,khe->hqk', query_block, keys, preferred_element_type=jnp....  86 us
    dot_general x6, matrix products, back_block(): jnp.einsum('qhe,khe->hqk', grad_block, values, preferred_element_type=jnp...  84 us
    unnamed x2, blocking collectives  81.9 us
    all_to_all x1, blocking collectives, body(): lax.all_to_all(stacked, 'sp', split_axis=0, concat_axis=2, tiled=True)  75.8 us
    dot_general x6, matrix products, back_block(): jnp.einsum('hqk,qhe->khe', weights, grad_block, preferred_element_type=jn...  66.3 us
    unnamed x9, waiting for transfers between devices  55.4 us
    unnamed x104, local copies, waits for them, and re-layouts  53 us
  transfers between devices with their start and end apart: 11, of which 5 were waited for; matrix products, arithmetic and copies ran while one was open for 67% of the time, Pallas kernels for 0%

commit v1 on v0

--- a/solution.py
+++ b/solution.py
@@ -3,14 +3,269 @@
 import jax
 import jax.numpy as jnp
 from jax import lax
+from jax.experimental import pallas as pl
+from jax.experimental.pallas import tpu as pltpu
 from jax.sharding import PartitionSpec as P
 
 HEADS = 12
 HEAD = 64
-
-
+IDS = 32
+far = 1e30
+QB = 256
+KB = 256
+f32 = jnp.float32
+bf16 = jnp.bfloat16
 norm_eps = 1e-06
-masked = -1e30
+
+
+def padded_width(width):
+    return -(-(width + IDS) // 128) * 128
+
+
+def spans(seg_row, block):
+    seq = seg_row.shape[0]
+    count = seq // block
+    first = seg_row[::block]
+    last = seg_row[block - 1 :: block]
+    lo = jnp.sum((seg_row[None, :] < first[:, None]).astype(jnp.int32), 1)
+    hi = jnp.sum((seg_row[None, :] <= last[:, None]).astype(jnp.int32), 1)
+    return lo, hi
+
+
+def windows(seg_row, block, step, grain):
+    lo, hi = spans(seg_row, block)
+    seq = seg_row.shape[0]
+    start = lo // grain * grain
+    number = -(-(hi - start) // step)
+    start = jnp.minimum(start, seq - number * step)
+    return start.astype(jnp.int32), number.astype(jnp.int32)
+
+
+def lanes_of(head, shape):
+    lane = lax.broadcasted_iota(jnp.int32, shape, len(shape) - 1)
+    return (lane >= head * HEAD) & (lane < (head + 1) * HEAD)
+
+
+def forward_kernel(heads, start_ref, number_ref, q_ref, k_ref, v_ref, o_ref, lse_ref, kh, vt, acc):
+    step = pl.program_id(0)
+    seq, wide = k_ref.shape
+    width = heads * HEAD
+
+    @pl.when(step == 0)
+    def _():
+        def part(i, carry):
+            rows = pl.ds(i * KB, KB)
+            k = k_ref[rows, :]
+            lane = lax.broadcasted_iota(jnp.int32, k.shape, 1)
+            for h in range(heads):
+                keep = lanes_of(h, k.shape) | (lane >= width)
+                kh[h, rows, :] = jnp.where(keep, k, jnp.zeros_like(k))
+            vt[:, rows] = v_ref[rows, :].T
+            return carry
+
+        lax.fori_loop(0, seq // KB, part, 0)
+
+    q = q_ref[...]
+    start = start_ref[step]
+    acc[...] = jnp.zeros_like(acc)
+
+    def one(j, carry):
+        at = pl.multiple_of(start + j * KB, 128)
+        rows = pl.ds(at, KB)
+        out = []
+        for h in range(heads):
+            top, total = carry[2 * h], carry[2 * h + 1]
+            s = lax.dot_general(
+                kh[h, rows, :], q, (((1,), (1,)), ((), ())), preferred_element_type=f32
+            )
+            new = jnp.maximum(top, jnp.max(s, 0, keepdims=True))
+            p = jnp.exp(s - new)
+            fade = jnp.exp(top - new)
+            total = total * fade + jnp.sum(p, 0, keepdims=True)
+            part = jnp.dot(
+                vt[h * HEAD : (h + 1) * HEAD, rows], p.astype(bf16), preferred_element_type=f32
+            )
+            mine = slice(h * HEAD, (h + 1) * HEAD)
+            acc[mine, :] = acc[mine, :] * fade + part
+            out += [new, total]
+        return tuple(out)
+
+    first = (jnp.full((1, QB), -jnp.inf, f32), jnp.zeros((1, QB), f32)) * heads
+    done = lax.fori_loop(0, number_ref[step], one, first)
+    for h in range(heads):
+        mine = slice(h * HEAD, (h + 1) * HEAD)
+        acc[mine, :] = acc[mine, :] / done[2 * h + 1]
+        lse_ref[h : h + 1, :] = done[2 * h] + jnp.log(done[2 * h + 1])
+    o_ref[...] = acc[...].T.astype(bf16)
+
+
+def attend_forward(q, k, v, starts, numbers, heads):
+    seq, wide = q.shape
+    width = heads * HEAD
+    steps = seq // QB
+    cost = pl.CostEstimate(
+        flops=2 * heads * seq * seq * HEAD, bytes_accessed=8 * seq * wide, transcendentals=heads * seq * seq // 3
+    )
+    return pl.pallas_call(
+        lambda *refs: forward_kernel(heads, *refs),
+        grid_spec=pltpu.PrefetchScalarGridSpec(
+            num_scalar_prefetch=2,
+            grid=(steps,),
+            in_specs=[
+                pl.BlockSpec((QB, wide), lambda i, a, b: (i, 0)),
+                pl.BlockSpec((seq, wide), lambda i, a, b: (0, 0)),
+                pl.BlockSpec((seq, width), lambda i, a, b: (0, 0)),
+            ],
+            out_specs=[
+                pl.BlockSpec((QB, width), lambda i, a, b: (i, 0)),
+                pl.BlockSpec((8, QB), lambda i, a, b: (0, i)),
+            ],
+            scratch_shapes=[
+                pltpu.VMEM((heads, seq, wide), bf16),
+                pltpu.VMEM((width, seq), bf16),
+                pltpu.VMEM((width, QB), f32),
+            ],
+        ),
+        out_shape=[
+            jax.ShapeDtypeStruct((seq, width), bf16),
+            jax.ShapeDtypeStruct((8, seq), f32),
+        ],
+        cost_estimate=cost,
+        compiler_params=pltpu.CompilerParams(vmem_limit_bytes=48 << 20),
+        name="attend_forward",
+    )(starts, numbers, q, k, v)
+
+
+def backward_kernel(
+    heads, start_ref, number_ref, q_ref, k_ref, v_ref, g_ref, o_ref, lse_ref,
+    dq_ref, dk_ref, dv_ref, qh, gh, gq, dqt, delta, dk, dv,
+):
+    step = pl.program_id(0)
+    seq, wide = q_ref.shape
+    width = heads * HEAD
+
+    @pl.when(step == 0)
+    def _():
+        def part(i, carry):
+            rows = pl.ds(i * QB, QB)
+            q = q_ref[rows, :]
+            g = g_ref[rows, :]
+            base = i * (heads * QB)
+            gz = jnp.concatenate([g, jnp.zeros((QB, wide - width), bf16)], 1)
+            gq[rows, :] = gz
+            for h in range(heads):
+                keep = lanes_of(h, q.shape)
+                qh[pl.ds(base + h * QB, QB), :] = jnp.where(keep, q, jnp.zeros_like(q))
+                gh[pl.ds(base + h * QB, QB), :] = jnp.where(keep, gz, jnp.zeros_like(gz))
+            product = g.astype(f32) * o_ref[rows, :].astype(f32)
+            lane = lax.broadcasted_iota(jnp.int32, (8, width), 1)
+            row = lax.broadcasted_iota(jnp.int32, (8, width), 0)
+            pick = ((lane >= row * HEAD) & (lane < (row + 1) * HEAD)).astype(f32)
+            delta[:, rows] = lax.dot_general(
+                pick, product, (((1,), (1,)), ((), ())),
+                preferred_element_type=f32, precision=lax.Precision.HIGHEST,
+            )
+            dqt[:, rows] = jnp.zeros((width, QB), f32)
+            return carry
+
+        lax.fori_loop(0, seq // QB, part, 0)
+
+    start = start_ref[step]
+    k = k_ref[...]
+    v = v_ref[...]
+    lane = lax.broadcasted_iota(jnp.int32, k.shape, 1)
+    vz = jnp.concatenate([v, jnp.zeros((KB, wide - width), bf16)], 1)
+    kh = [jnp.where(lanes_of(h, k.shape) | (lane >= width), k, jnp.zeros_like(k)) for h in range(heads)]
+    vh = [jnp.where(lanes_of(h, k.shape), vz, jnp.zeros_like(vz)) for h in range(heads)]
+    kt = k[:, :].T
+    dk[...] = jnp.zeros_like(dk)
+    dv[...] = jnp.zeros_like(dv)
+
+    def one(i, carry):
+        block = start + i
+        rows = pl.ds(pl.multiple_of(block * QB, QB), QB)
+        tall = pl.ds(pl.multiple_of(block * (heads * QB), heads * QB), heads * QB)
+        q = q_ref[rows, :]
+        g = gq[rows, :]
+        ps, dss = [], []
+        for h in range(heads):
+            s = lax.dot_general(kh[h], q, (((1,), (1,)), ((), ())), preferred_element_type=f32)
+            p = jnp.exp(s - lse_ref[h : h + 1, rows])
+            dp = lax.dot_general(vh[h], g, (((1,), (1,)), ((), ())), preferred_element_type=f32)
+            ds = (p * (dp - delta[h : h + 1, rows])).astype(bf16)
+            ps.append(p.astype(bf16))
+            dss.append(ds)
+            mine = slice(h * HEAD, (h + 1) * HEAD)
+            dqt[mine, rows] += jnp.dot(kt[mine, :], ds, preferred_element_type=f32)
+        dv[...] += jnp.dot(jnp.concatenate(ps, 1), gh[tall, :], preferred_element_type=f32)
+        dk[...] += jnp.dot(jnp.concatenate(dss, 1), qh[tall, :], preferred_element_type=f32)
+        return carry
+
+    lax.fori_loop(0, number_ref[step], one, 0)
+    dk_ref[...] = dk[:, :width].astype(bf16)
+    dv_ref[...] = dv[:, :width].astype(bf16)
+
+    @pl.when(step == pl.num_programs(0) - 1)
+    def _():
+        def part(i, carry):
+            rows = pl.ds(i * QB, QB)
+            dq_ref[rows, :] = (dqt[:, rows] * 0.125).T.astype(bf16)
+            return carry
+
+        lax.fori_loop(0, seq // QB, part, 0)
+
+
+def attend_backward(q, k, v, g, o, lse, starts, numbers, heads):
+    seq, wide = q.shape
+    width = heads * HEAD
+    steps = seq // KB
+    whole = lambda shape: pl.BlockSpec(shape, lambda i, a, b: (0, 0))
+    cost = pl.CostEstimate(
+        flops=5 * heads * seq * seq * HEAD, bytes_accessed=16 * seq * wide, transcendentals=heads * seq * seq // 3
+    )
+    return pl.pallas_call(
+        lambda *refs: backward_kernel(heads, *refs),
+        grid_spec=pltpu.PrefetchScalarGridSpec(
+            num_scalar_prefetch=2,
+            grid=(steps,),
+            in_specs=[
+                whole((seq, wide)),
+                pl.BlockSpec((KB, wide), lambda i, a, b: (i, 0)),
+                pl.BlockSpec((KB, width), lambda i, a, b: (i, 0)),
+                whole((seq, width)),
+                whole((seq, width)),
+                whole((8, seq)),
+            ],
+            out_specs=[
+                whole((seq, width)),
+                pl.BlockSpec((KB, width), lambda i, a, b: (i, 0)),
+                pl.BlockSpec((KB, width), lambda i, a, b: (i, 0)),
+            ],
+            scratch_shapes=[
+                pltpu.VMEM((heads * seq, wide), bf16),
+                pltpu.VMEM((heads * seq, wide), bf16),
+                pltpu.VMEM((seq, wide), bf16),
+                pltpu.VMEM((width, seq), f32),
+                pltpu.VMEM((8, seq), f32),
+                pltpu.VMEM((KB, wide), f32),
+                pltpu.VMEM((KB, wide), f32),
+            ],
+        ),
+        out_shape=[jax.ShapeDtypeStruct((seq, width), bf16)] * 3,
+        cost_estimate=cost,
+        compiler_params=pltpu.CompilerParams(vmem_limit_bytes=56 << 20),
+        name="attend_backward",
+    )(starts, numbers, q, k, v, g, o, lse)
+
+
+def augment(q, k, seg_row):
+    seq, width = q.shape
+    wide = padded_width(width)
+    hot = (seg_row[:, None] == jnp.arange(IDS)[None, :])
+    rest = jnp.zeros((seq, wide - width - IDS), bf16)
+    qa = jnp.concatenate([q * jnp.asarray(0.125, bf16), hot.astype(bf16), rest], 1)
+    ka = jnp.concatenate([k, jnp.where(hot, 0.0, -far).astype(bf16), rest], 1)
+    return qa, ka
 
 
 def layer_normalizer(values, norm_gain, norm_shift):
@@ -96,8 +351,6 @@
     heads_local = HEADS // groups
     width = heads_local * HEAD
     seq_len = rows * groups
-    block = min(512, seq_len)
-    nblocks = seq_len // block
     input_tokens = tokens.astype(jnp.float32)
     bias_qkv = jnp.concatenate([bias_query, jnp.zeros_like(bias_query), bias_value])
     packed = (jnp.dot(tokens, full_qkv, preferred_element_type=jnp.float32) + bias_qkv).astype(
@@ -106,32 +359,14 @@
     heads_in = lax.all_to_all(
         packed.reshape(rows, 3, groups, width), "sp", split_axis=2, concat_axis=0, tiled=True
     )
-    queries = heads_in[:, 0, 0].reshape(seq_len, heads_local, HEAD)
-    keys = heads_in[:, 1, 0].reshape(seq_len, heads_local, HEAD)
-    values = heads_in[:, 2, 0].reshape(seq_len, heads_local, HEAD)
     seg_row = segments[0]
-    blocked_q = queries.reshape(nblocks, block, heads_local, HEAD)
-    blocked_s = seg_row.reshape(nblocks, block)
-
-    def block_scores(query_block, seg_block):
-        scores = (
-            jnp.einsum("qhe,khe->hqk", query_block, keys, preferred_element_type=jnp.float32)
-            * 0.125
-        )
-        same = seg_block[:, None] == seg_row[None, :]
-        return jnp.where(same[None], scores, masked)
-
-    def forward_block(pair):
-        query_block, seg_block = pair
-        scores = block_scores(query_block, seg_block)
-        peak = jnp.max(scores, -1, keepdims=True)
-        expo = jnp.exp(scores - peak)
-        total = jnp.sum(expo, -1, keepdims=True)
-        weights = (expo / total).astype(jnp.bfloat16)
-        attended = jnp.einsum("hqk,khe->qhe", weights, values, preferred_element_type=jnp.float32)
-        return (attended.astype(jnp.bfloat16), (peak + jnp.log(total))[..., 0])
-
-    attended, logsum = lax.map(forward_block, (blocked_q, blocked_s))
+    queries, keys = augment(heads_in[:, 0, 0], heads_in[:, 1, 0], seg_row)
+    values = heads_in[:, 2, 0]
+    forward_start, forward_number = windows(seg_row, QB, KB, 128)
+    backward_start, backward_number = windows(seg_row, KB, QB, QB)
+    attended, logsum = attend_forward(
+        queries, keys, values, forward_start, forward_number, heads_local
+    )
     back_tokens = lax.all_to_all(
         attended.reshape(seq_len, 1, width), "sp", split_axis=0, concat_axis=1, tiled=True
     )
@@ -192,38 +427,16 @@
     grad_heads = lax.all_to_all(
         grad_mixed.reshape(rows, groups, width), "sp", split_axis=1, concat_axis=0, tiled=True
     )
-    grad_blocks = grad_heads.reshape(nblocks, block, heads_local, HEAD)
-
-    def back_block(carry, item):
-        grad_keys, grad_values = carry
-        query_block, seg_block, lse_block, grad_block = item
-        scores = block_scores(query_block, seg_block)
-        probs = jnp.exp(scores - lse_block[..., None])
-        weights = probs.astype(jnp.bfloat16)
-        grad_probs = jnp.einsum(
-            "qhe,khe->hqk", grad_block, values, preferred_element_type=jnp.float32
-        )
-        inner_activation = jnp.sum(grad_probs * probs, -1, keepdims=True)
-        grad_scores = (probs * (grad_probs - inner_activation)).astype(jnp.bfloat16)
-        grad_query = (
-            jnp.einsum("hqk,khe->qhe", grad_scores, keys, preferred_element_type=jnp.float32)
-            * 0.125
-        )
-        grad_keys = (
-            grad_keys
-            + jnp.einsum(
-                "hqk,qhe->khe", grad_scores, query_block, preferred_element_type=jnp.float32
-            )
-            * 0.125
-        )
-        grad_values = grad_values + jnp.einsum(
-            "hqk,qhe->khe", weights, grad_block, preferred_element_type=jnp.float32
-        )
-        return ((grad_keys, grad_values), grad_query)
-
-    empty = jnp.zeros((seq_len, heads_local, HEAD), jnp.float32)
-    (grad_keys, grad_values), grad_query = lax.scan(
-        back_block, (empty, empty), (blocked_q, blocked_s, logsum, grad_blocks)
+    grad_query, grad_keys, grad_values = attend_backward(
+        queries,
+        keys,
+        values,
+        grad_heads.reshape(seq_len, width),
+        attended,
+        logsum,
+        backward_start // QB,
+        backward_number,
+        heads_local,
     )
     stacked = jnp.stack(
         [
@@ -233,7 +446,7 @@
         ],
         1,
     )
-    stacked = stacked.astype(jnp.bfloat16)[:, :, None, :]
+    stacked = stacked[:, :, None, :]
     grad_back = lax.all_to_all(stacked, "sp", split_axis=0, concat_axis=2, tiled=True)
     grad_packed = grad_back.reshape(rows, 3 * width_all)
     grad_wide = grad_packed.astype(jnp.float32)

time: 1100 us -> 895 us (0.81)
  matrix products: 455 us -> 111 us
  waiting for transfers between devices: 124 us -> 293 us
  other arithmetic: 189 us -> 26.2 us
  Pallas kernels: 0 us -> 130 us
  blocking collectives: 158 us -> 191 us
  local copies, waits for them, and re-layouts: 136 us -> 110 us
    dot_general x42 -> x0, matrix products: 352 us -> none  [the longest x12 86 us: block_scores(): jnp.einsum('qhe,khe->hqk', query_block, keys, preferred_element_type=jnp....]
    pallas_call x0 -> x2, Pallas kernels: none -> 130 us  [the longest x1 88.5 us: attend_backward(): pl.pallas_call(lambda *refs: backward_kernel(heads, *refs), grid_spec=plt...]
    convert_element_type x6 -> x2, other arithmetic: 109 us -> 5.25 us  [the longest x1 2.62 us: augment(): hot.astype(bf16)]
    reduce_scatter x1, waiting for transfers between devices: 0.01 us -> 81.5 us  [body(): lax.psum_scatter(grads[9], ('sp', 'fsdp'), scatter_dimension=0, tiled=True)]
    unnamed x9, waiting for transfers between devices: 55.4 us -> 128 us
    reduce_sum x6 -> x1, other arithmetic: 31.7 us -> 0.89 us  [spans(): hi = jnp.sum((seg_row[None, :] <= last[:, None]).astype(jnp.int32), 1)]
    all_gather x1, waiting for transfers between devices: 0.01 us -> 26.5 us  [body(): lax.all_gather(w_down, ('sp', 'fsdp'), axis=0, tiled=True)]
    broadcast_in_dim x0 -> x2, local copies, waits for them, and re-layouts: none -> 23.9 us  [the longest x1 23.9 us: body(): stacked = stacked[:, :, None, :]]
  transfers between devices with their start and end apart: 11 -> 10, of which waited for: 5 -> 6; matrix products, arithmetic and copies ran while one was open for 67% -> 21% of each run, Pallas kernels for 0% -> 15%
where the time goes in v1:
time: 895 us; the launch traced here: 885 us
  waiting for transfers between devices  293 us (33%)
  blocking collectives  191 us (21%)
  Pallas kernels  130 us (15%)
  matrix products  111 us (12%)
  local copies, waits for them, and re-layouts  110 us (12%)
  other arithmetic  26.2 us (3%)
  between operations  15 us (2%)
    unnamed x9, waiting for transfers between devices  128 us
    all_to_all x1, blocking collectives, body(): lax.all_to_all(stacked, 'sp', split_axis=0, concat_axis=2, tiled=True)  88.9 us
    pallas_call x1, Pallas kernels, attend_backward(): pl.pallas_call(lambda *refs: backward_kernel(heads, *refs), grid_spec=plt...  88.5 us
    unnamed x2, blocking collectives  83.3 us
    reduce_scatter x1, waiting for transfers between devices, body(): lax.psum_scatter(grads[9], ('sp', 'fsdp'), scatter_dimension=0, tiled=True)  81.5 us
    unnamed x96, local copies, waits for them, and re-layouts  51.8 us
    pallas_call x1, Pallas kernels, attend_forward(): pl.pallas_call(lambda *refs: forward_kernel(heads, *refs), grid_spec=pltp...  41.5 us
    all_to_all x1, waiting for transfers between devices, body(): lax.all_to_all(packed.reshape(rows, 3, groups, width), 'sp', split_axis=2...  35.1 us
  transfers between devices with their start and end apart: 10, of which 6 were waited for; matrix products, arithmetic and copies ran while one was open for 21% of the time, Pallas kernels for 15%

profile of v1, /device:TPU:0, one launch (start us, length us, event | category | flops | bytes accessed | tf_op | source)
XLA Modules:
  0.0 884.9 jit_solution(15836196790488813736)
XLA Ops:
  17.0 42.8 %all-reduce.19 = (bf16[768]{0:T(1024)(128)(2,1)S(1)}, bf16[768]{0:T(1024)(128)(2,1)S(1)}, bf16[768]{0:T(1024)(128)(2,1)}, bf16[768]{0:T(1024)(128)(2,1)}, bf16[7...) all-reduce(bf16[768]{0:T(1024)(128)(2,1)S(1)} %dynamic-update-slice, ...), channel_id=1, replica_groups=mesh['sp'=4,'fsdp'=8] {'sp','fsdp'}, use_global_device_ids=true, to_apply=%add.1 | all-reduce | flops 9216 | bytes 36864
  59.7 14.3 %all-gather.5.cloned.1.call-done = bf16[768,2304]{1,0:T(8,128)(2,1)} async-done(((bf16[24,2304]{1,0:T(8,128)(2,1)}), bf16[768,2304]{1,0:T(8,128)(2,1)}) %all-gather.5.cloned.1.call-update) | async-done | bytes 3538960 | tf_op jit(solution)/shard_map/all_gather | solution.py:310
  74.0 7.1 add_convert_fusion.1
  81.1 4.5 copy.87
  85.7 2.1 copy.88
  87.8 3.9 all-to-all-start
  95.5 2.6 fusion.15
  98.1 2.6 select_convert_fusion
  100.7 35.1 %all-to-all-done = bf16[768,3,4,192]{0,3,1,2:T(8,128)(2,1)S(1)} async-done(((bf16[768,3,4,192]{0,3,1,2:T(8,128)(2,1)}), bf16[768,3,4,192]{0,3,1,2:T(8,128)(2,1)S(1)}, u32[]{:S(2)}, u32[]{:S(2)}) %all-to-all-start) | async-done | bytes 3538976 | tf_op jit(solution)/shard_map/all_to_all | solution.py:359
  135.8 4.0 copy.89
  139.8 3.9 slice_bitcast_fusion
  143.7 1.2 maximum_maximum_fusion.1
  144.9 41.5 %attend_forward.1 = (bf16[3072,192]{1,0:T(8,128)(2,1)S(1)}, f32[8,3072]{1,0:T(8,128)S(1)}) custom-call(s32[12]{0:T(128)S(1)} %get-tuple-element.146.refs_0_, s32[12]{0:T(128)S(1)} %get-tuple-element.147.refs_1_, bf16[3072,256]{1,0:T(8,128)(2,1)S(1)} %get-tuple-element.151.refs_2_, bf16[3072,256]{1,0:T(8,128)(2,1)S(1)} %get-tuple-element.150.refs_3_, ...), custom_call_target="tpu_custom_call" | custom-call | flops 3623878656 | bytes 6291456 | tf_op jit(solution)/shard_map/attend_forward/pallas_call | solution.py:109
  187.7 1.7 reduce
  189.3 2.9 reshape.130
  192.2 4.4 all-to-all-start.1
  197.0 2.4 copy.86
  201.2 1.4 copy.94
  203.2 7.3 all-to-all-done.1
  210.5 3.5 reshape.131
  214.0 6.0 copy.91
  220.1 2.7 all_to_all.51
  222.9 2.8 fusion.32
  226.1 28.9 %multiply_convert_fusion = (bf16[768,3072]{1,0:T(8,128)(2,1)}, f32[768,3072]{1,0:T(8,128)}, f32[768,3072]{1,0:T(8,128)}) fusion(f32[3072]{0:T(1024)} %convert_element_type.97, bf16[768,3072]{1,0:T(8,128)(2,1)} %all-gather.9.cloned.1.call-done, f32[768,768]{0,1:T(8,128)S(1)} %get-tuple-element.153, f32[768]{0:T(1024)} %convert_element_type.95, ...), kind=kOutput, calls=%fused_computation.4 | convolution fusion | flops 3782541312 | bytes 30695424 | tf_op jit(solution)/shard_map/dot_general | solution.py:379
  255.0 26.5 %all-gather.11.cloned.1.call-done = bf16[3072,768]{1,0:T(8,128)(2,1)} async-done(((bf16[96,768]{1,0:T(8,128)(2,1)}), bf16[3072,768]{1,0:T(8,128)(2,1)}) %all-gather.11.cloned.1.call-update) | async-done | bytes 4718608 | tf_op jit(solution)/shard_map/all_gather | solution.py:319
  281.4 16.2 %fusion.33 = (f32[768]{0:T(1024)S(1)}, f32[768,768]{0,1:T(8,128)S(1)}) fusion(f32[768]{0:T(1024)} %convert_element_type.99, bf16[768,3072]{1,0:T(8,128)(2,1)} %get-tuple-element.138, bf16[3072,768]{1,0:T(8,128)(2,1)} %all-gather.11.cloned.1.call-done, f32[768]{0:T(1024)} %convert_element_type.95, f32[768]{0:T(1024)S(1)} %convert_element_type.94, ...), kind=kOutput, calls=%fused_computation.104 | convolution fusion | flops 3628006656 | bytes 14174208 | tf_op jit(solution)/shard_map/dot_general | solution.py:381
  298.0 0.9 copy-done.6
  298.9 1.7 fusion.12
  300.6 2.7 convert_reduce_fusion.2
  303.3 14.6 %convert_reduce_fusion = (f32[3072]{0:T(1024)}, bf16[768,3072]{1,0:T(8,128)(2,1)}) fusion(f32[768,3072]{1,0:T(8,128)} %get-tuple-element.139, f32[768,3072]{1,0:T(8,128)} %get-tuple-element.154, f32[3072]{0:T(1024)S(1)} %copy-done.19, bf16[768,768]{0,1:T(8,128)(2,1)S(1)} %get-tuple-element.131, bf16[3072,768]{1,0:T(8,128)(2,1)} %all-gather.11.cloned.1.call-done), kind=kOutput, calls=%fused_computation.2 | convolution fusion | flops 3663983616 | bytes 29515776 | tf_op jit(solution)/shard_map/td,fd->tf/dot_general | solution.py:407
  317.9 8.1 multiply_reduce_fusion
  326.0 1.5 convert_reduce_fusion.3
  327.5 1.4 copy-done.7
  328.9 2.5 fusion.21
  332.1 9.0 %fusion.24 = f32[768,3072]{1,0:T(8,128)} fusion(bf16[768,3072]{1,0:T(8,128)(2,1)} %get-tuple-element.133, f32[768,768]{0,1:T(8,128)S(1)} %get-tuple-element.153, f32[768]{0:T(1024)S(1)} %copy-done.21, f32[768]{0:T(1024)S(1)} %convert_element_type.94, f32[768]{0:T(1024)S(1)} %add_rsqrt_fusion.1, f32[768]{0:T(1024)S(1)} %broadcast_multiply_fusion.5), kind=kOutput, calls=%fused_computation.101 | convolution fusion | flops 3626827776 | bytes 16527360 | tf_op jit(solution)/shard_map/td,tf->df/dot_general | solution.py:411
  341.2 1.2 copy-done.12
  342.4 8.8 fusion.34
  351.2 1.6 copy-done.8
  353.2 1.1 convolution_convert_fusion
  354.3 18.7 %all_to_all.63 = bf16[768,4,192]{0,2,1:T(8,128)(2,1)S(1)} all-to-all(bf16[768,4,192]{0,2,1:T(8,128)(2,1)S(1)} %bitcast.70), channel_id=1, replica_groups=mesh['sp'=4,'fsdp'=8] {'sp'}, dimensions={1} | all-to-all | bytes 2359296 | tf_op jit(solution)/shard_map/all_to_all | solution.py:427
  373.0 1.5 copy.96
  374.5 88.5 %attend_backward.1 = (bf16[3072,192]{1,0:T(8,128)(2,1)}, bf16[3072,192]{1,0:T(8,128)(2,1)}, bf16[3072,192]{1,0:T(8,128)(2,1)}) custom-call(s32[12]{0:T(128)} %get-tuple-element.136.refs_0_, s32[12]{0:T(128)} %get-tuple-element.137.refs_1_, bf16[3072,256]{1,0:T(8,128)(2,1)} %copy-done.2, bf16[3072,256]{1,0:T(8,128)(2,1)} %copy-done.1, ...), custom_call_target="tpu_custom_call" | custom-call | flops 9059696640 | bytes 12582912 | tf_op jit(solution)/shard_map/attend_backward/pallas_call | solution.py:226
  463.0 3.1 maximum_bitcast_fusion
  466.1 23.9 %copy.97 = bf16[3072,3,1,192]{3,1,2,0:T(4,128)(2,1)S(1)} copy(bf16[3072,3,1,192]{3,0,1,2:T(8,128)(2,1)S(1)} %maximum_bitcast_fusion) | data formatting | bytes 7077888 | tf_op jit(solution)/shard_map/broadcast_in_dim | solution.py:449
  490.1 88.9 %all_to_all.64 = bf16[3072,3,1,192]{3,1,2,0:T(4,128)(2,1)} all-to-all(bf16[3072,3,1,192]{3,1,2,0:T(4,128)(2,1)S(1)} %copy.97), channel_id=1, replica_groups=mesh['sp'=4,'fsdp'=8] {'sp'}, dimensions={0} | all-to-all | bytes 7077888 | tf_op jit(solution)/shard_map/all_to_all | solution.py:450
  579.0 10.5 %copy.107 = bf16[4,768,3,1,192]{1,0,4,2,3:T(4,128)(2,1)S(1)} copy(bf16[4,768,3,1,192]{4,2,1,0,3:T(4,128)(2,1)} %bitcast.54) | data formatting | bytes 7077888 | tf_op jit(solution)/shard_map/all_to_all | solution.py:450
  590.1 1.7 copy-done.4
  591.8 4.9 convolution_bitcast_fusion
  596.7 8.0 copy.108
  604.8 2.5 copy.101
  608.5 40.5 %all-reduce.18 = (f32[768]{0:T(1024)}, f32[768]{0:T(1024)}, f32[768]{0:T(1024)}, f32[768]{0:T(1024)}, f32[768]{0:T(1024)}, /*index=5*/f32[3072]{0:T(1024)}, f32[768]{0:T(1024)}, f32[768]{0:T(1024)}, f32[768]{0:T(1024)}) all-reduce(f32[768]{0:T(1024)S(1)} %get-tuple-element.101, ...), channel_id=3, replica_groups=mesh['sp'=4,'fsdp'=8] {'sp','fsdp'}, use_global_device_ids=true, to_apply=%region_12.13.clone | all-reduce | flops 9216 | bytes 73728
  649.1 1.3 dynamic-slice
  650.3 1.3 dynamic-slice.1
  651.6 1.3 dynamic-slice.2
  652.9 1.3 dynamic-slice.3
  654.1 1.3 dynamic-slice.4
  655.4 1.3 dynamic-slice.6
  656.6 1.3 dynamic-slice.7
  657.9 1.2 dynamic-slice.8
  659.1 7.1 convolution_add_fusion
  666.2 3.1 copy.102
  669.4 1.3 dynamic-slice.5
  670.6 81.5 %reduce-scatter.11.cloned.1.call-done = f32[96,768]{1,0:T(8,128)} async-done(((f32[3072,768]{1,0:T(8,128)}), f32[96,768]{1,0:T(8,128)}) %reduce-scatter.11.cloned.1.call-update) | async-done | bytes 294928 | tf_op jit(solution)/shard_map/reduce_scatter | solution.py:484
  752.2 125.5 %reduce-scatter.13.cloned.1.call-done = f32[24,2304]{1,0:T(8,128)} async-done(((f32[768,2304]{1,0:T(8,128)}), f32[24,2304]{1,0:T(8,128)}) %reduce-scatter.13.cloned.1.call-update) | async-done | bytes 221200
  (128 shorter events, 21.1 us)
Async XLA Ops:
  7.2 66.9 %all-gather.5.cloned.1.call-start = ((), (), s32[]{:S(2)}) async-start(), calls=%async_computation.8 | async-start | bytes 3649536 | tf_op jit(solution)/shard_map/all_gather | solution.py:310
  7.9 215.0 %all-gather.7.cloned.1.call-start = ((), (), s32[]{:S(2)}) async-start(), calls=%async_computation.9 | async-start | bytes 1216512 | tf_op jit(solution)/shard_map/all_gather | solution.py:313
  8.7 217.4 %all-gather.9.cloned.1.call-start = ((), (), s32[]{:S(2)}) async-start(), calls=%async_computation.10 | async-start | bytes 4866048 | tf_op jit(solution)/shard_map/all_gather | solution.py:317
  87.8 4.5 copy-start.15
  87.8 48.0 %all-to-all-start = ((bf16[768,3,4,192]{0,3,1,2:T(8,128)(2,1)}), bf16[768,3,4,192]{0,3,1,2:T(8,128)(2,1)S(1)}, u32[]{:S(2)}, u32[]{:S(2)}) async-start(bf16[768,3,4,192]{0,3,1,2:T(8,128)(2,1)} %copy.88), calls=%async_computation | async-start | bytes 7077888 | tf_op jit(solution)/shard_map/all_to_all | solution.py:359
  91.7 189.8 %all-gather.11.cloned.1.call-start = ((), (), s32[]{:S(2)}) async-start(), calls=%async_computation.11 | async-start | bytes 4866048 | tf_op jit(solution)/shard_map/all_gather | solution.py:319
  139.8 3.9 copy-start.9
  139.8 3.9 copy-start.10
  139.8 3.9 copy-start.27
  144.9 41.6 %copy-start.1 = (bf16[3072,256]{1,0:T(8,128)(2,1)}, bf16[3072,256]{1,0:T(8,128)(2,1)S(1)}, u32[]{:S(2)}) copy-start(bf16[3072,256]{1,0:T(8,128)(2,1)S(1)} %get-tuple-element.150.refs_3_) | copy-start | bytes 4718596
  144.9 41.6 %copy-start.2 = (bf16[3072,256]{1,0:T(8,128)(2,1)}, bf16[3072,256]{1,0:T(8,128)(2,1)S(1)}, u32[]{:S(2)}) copy-start(bf16[3072,256]{1,0:T(8,128)(2,1)S(1)} %get-tuple-element.151.refs_2_) | copy-start | bytes 4718596
  186.5 0.6 copy-start.3
  187.1 5.1 copy-start
  192.2 7.2 copy-start.26
  192.2 7.2 copy-start.25
  192.2 7.2 copy-start.24
  192.2 7.8 copy-start.20
  192.2 8.4 copy-start.23
  192.2 9.0 %copy-start.22 = (bf16[768]{0:T(1024)(128)(2,1)S(1)}, bf16[768]{0:T(1024)(128)(2,1)}, u32[]{:S(2)}) copy-start(bf16[768]{0:T(1024)(128)(2,1)} %get-tuple-element.129) | copy-start | bytes 4612
  192.2 9.0 %copy-start.13 = (bf16[768,768]{1,0:T(8,128)(2,1)S(1)}, bf16[768,768]{1,0:T(8,128)(2,1)}, u32[]{:S(2)}) copy-start(bf16[768,768]{1,0:T(8,128)(2,1)} %param.18) | copy-start | bytes 3538948
  192.2 18.3 %all-to-all-start.1 = ((bf16[4,2,73728]{2,1,0:T(2,128)(2,1)}), bf16[4,2,73728]{2,1,0:T(2,128)(2,1)}, u32[]{:S(2)}, u32[]{:S(2)}) async-start(bf16[4,2,73728]{2,1,0:T(2,128)(2,1)} %reshape.130), calls=%async_computation.1 | async-start | bytes 2359296 | tf_op jit(solution)/shard_map/all_to_all | solution.py:370
  196.7 474.0 %reduce-scatter.7.cloned.1.call-start = ((), (), s32[]{:S(2)}) async-start(), calls=%async_computation.12 | async-start | bytes 2433024 | tf_op jit(solution)/shard_map/reduce_scatter | solution.py:478
  297.7 1.3 copy-start.6
  298.0 2.6 copy-start.16
  300.6 2.7 copy-start.19
  300.6 17.3 %slice-start = ((s8[4718592]{0:T(1024)(128)(4,1)}), s8[4194304]{0:T(1024)(128)(4,1)S(1)}, s32[]{:S(2)}) async-start(s8[4718592]{0:T(1024)(128)(4,1)} %bitcast.76), calls=%async_computation.16 | async-start | bytes 8388608
  303.3 14.6 %copy-start.11 = (bf16[768,768]{0,1:T(8,128)(2,1)}, bf16[768,768]{0,1:T(8,128)(2,1)S(1)}, u32[]{:S(2)}) copy-start(bf16[768,768]{0,1:T(8,128)(2,1)S(1)} %get-tuple-element.131) | copy-start | bytes 3538948
  303.3 14.6 %slice-start.1 = ((s8[4718592]{0:T(1024)(128)(4,1)}), s8[524288]{0:T(1024)(128)(4,1)S(1)}, s32[]{:S(2)}) async-start(s8[4718592]{0:T(1024)(128)(4,1)} %bitcast.76), calls=%async_computation.17 | async-start | bytes 1048576
  327.5 1.4 copy-start.7
  331.4 0.7 copy-start.21
  331.5 339.2 %reduce-scatter.9.cloned.1.call-start = ((), (), s32[]{:S(2)}) async-start(), calls=%async_computation.13 | async-start | bytes 9732096 | tf_op jit(solution)/shard_map/reduce_scatter | solution.py:482
  341.1 1.3 copy-start.12
  341.1 411.0 %reduce-scatter.11.cloned.1.call-start = ((), (), s32[]{:S(2)}) async-start(), calls=%async_computation.14 | async-start | bytes 9732096 | tf_op jit(solution)/shard_map/reduce_scatter | solution.py:484
  351.2 1.7 copy-start.8
  351.2 2.0 copy-start.28
  351.2 526.5 %reduce-scatter.13.cloned.1.call-start = ((), (), s32[]{:S(2)}) async-start(), calls=%async_computation.15 | async-start | bytes 7299072
  589.5 2.3 copy-start.14
  590.1 1.8 copy-start.4
  604.7 2.6 copy-start.5
  607.9 0.7 copy-start.17
  607.9 0.7 copy-start.18
Sparse Core Ops, SparseCore 0:
  11.0 62.9 all-gather.4
  77.1 63.6 all-gather.6
  143.8 72.8 all-gather.8
  219.6 61.8 all-gather.10
  331.6 97.8 reduce-scatter.6
  436.8 174.1 reduce-scatter.8
  617.5 134.6 reduce-scatter.10
  759.4 118.2 reduce-scatter.12

commit v2 on v1

--- a/solution.py
+++ b/solution.py
@@ -288,6 +288,46 @@
     return (incoming_gradient, norm_gain_gradient, grad_shift)
 
 
+def by_sp(value, flip):
+    groups = lax.axis_size("sp")
+    return lax.ppermute(value, "sp", [(i, i ^ flip) for i in range(groups)])
+
+
+def gather_tokens(tokens):
+    rows = tokens.shape[0]
+    half = rows // 2
+    along_x = by_sp(tokens, 1)
+    along_y = by_sp(tokens, 2)
+    upper = by_sp(along_y[:half], 1)
+    lower = by_sp(along_x[half:], 2)
+    me = lax.axis_index("sp")
+    out = jnp.zeros((4 * rows, tokens.shape[1]), tokens.dtype)
+    for flip, part in ((0, tokens), (1, along_x), (2, along_y)):
+        out = lax.dynamic_update_slice(out, part, ((me ^ flip) * rows, 0))
+    out = lax.dynamic_update_slice(out, upper, ((me ^ 3) * rows, 0))
+    return lax.dynamic_update_slice(out, lower, ((me ^ 3) * rows + half, 0))
+
+
+def scatter_rows(partial):
+    rows = partial.shape[0] // 4
+    half = rows // 2
+    me = lax.axis_index("sp")
+
+    def piece(flip, lower):
+        at = (me ^ flip) * rows + (half if lower else 0)
+        return lax.dynamic_slice(partial, (at, 0), (half, partial.shape[1]))
+
+    sent_x = jnp.concatenate([piece(1, False), piece(3, False)], 0).astype(bf16)
+    sent_y = jnp.concatenate([piece(2, True), piece(3, True)], 0).astype(bf16)
+    got_x = by_sp(sent_x, 1).astype(f32)
+    got_y = by_sp(sent_y, 2).astype(f32)
+    next_y = by_sp((piece(2, False) + got_x[half:]).astype(bf16), 2).astype(f32)
+    next_x = by_sp((piece(1, True) + got_y[half:]).astype(bf16), 1).astype(f32)
+    upper = piece(0, False) + got_x[:half] + next_y
+    lower = piece(0, True) + got_y[:half] + next_x
+    return jnp.concatenate([upper, lower], 0)
+
+
 def body(
     tokens,
     segments,
@@ -306,126 +346,146 @@
     ln2_gain,
     ln2_bias,
 ):
-    whole = (
-        lax.all_gather(w_qkv, ("sp", "fsdp"), axis=0, tiled=True),
-        lax.all_gather(b_query, ("sp", "fsdp"), axis=0, tiled=True),
-        lax.all_gather(b_value, ("sp", "fsdp"), axis=0, tiled=True),
-        lax.all_gather(w_out, ("sp", "fsdp"), axis=0, tiled=True),
-        lax.all_gather(b_out, ("sp", "fsdp"), axis=0, tiled=True),
-        lax.all_gather(ln1_gain, ("sp", "fsdp"), axis=0, tiled=True),
-        lax.all_gather(ln1_bias, ("sp", "fsdp"), axis=0, tiled=True),
-        lax.all_gather(w_up, ("sp", "fsdp"), axis=0, tiled=True),
-        lax.all_gather(b_up, ("sp", "fsdp"), axis=0, tiled=True),
-        lax.all_gather(w_down, ("sp", "fsdp"), axis=0, tiled=True),
-        lax.all_gather(b_down, ("sp", "fsdp"), axis=0, tiled=True),
-        lax.all_gather(ln2_gain, ("sp", "fsdp"), axis=0, tiled=True),
-        lax.all_gather(ln2_bias, ("sp", "fsdp"), axis=0, tiled=True),
-    )
-    (
-        full_qkv,
-        bias_query,
-        bias_value,
-        full_out,
-        bias_out,
-        attention_norm_gain,
-        attention_norm_shift,
-        full_up,
-        bias_up,
-        full_down,
-        bias_down,
-        feedforward_norm_gain,
-        feedforward_norm_shift,
-    ) = whole
-    bias_query = bias_query.astype(jnp.float32)
-    bias_value = bias_value.astype(jnp.float32)
-    bias_out = bias_out.astype(jnp.float32)
-    attention_norm_gain = attention_norm_gain.astype(jnp.float32)
-    attention_norm_shift = attention_norm_shift.astype(jnp.float32)
-    bias_up = bias_up.astype(jnp.float32)
-    bias_down = bias_down.astype(jnp.float32)
-    feedforward_norm_gain = feedforward_norm_gain.astype(jnp.float32)
-    feedforward_norm_shift = feedforward_norm_shift.astype(jnp.float32)
+    both = ("sp", "fsdp")
     groups = lax.axis_size("sp")
-    rows = tokens.shape[0]
-    width_all = tokens.shape[1]
+    shards = lax.axis_size("fsdp")
+    devices = groups * shards
+    rows, model = tokens.shape
+    hidden = w_up.shape[1]
+    ratio = hidden // model
+    own = w_qkv.shape[0]
     heads_local = HEADS // groups
     width = heads_local * HEAD
     seq_len = rows * groups
-    input_tokens = tokens.astype(jnp.float32)
+    seg_row = segments[0]
+
+    vectors = [b_out, ln1_gain, ln1_bias, b_down, ln2_gain, ln2_bias, b_up]
+    sizes = [item.shape[0] for item in vectors]
+    flat = jnp.concatenate(vectors)
+    flat = jnp.concatenate([flat, jnp.zeros((8 * model - flat.shape[0],), bf16)]).reshape(8, model)
+    up_blocks = [w_up[:, c * model : (c + 1) * model] for c in range(ratio)]
+    pack = jnp.concatenate([w_down] + up_blocks + [w_out, flat], 0)
+    packed_weights = lax.all_gather(pack, both, axis=0, tiled=False)
+    at = ratio * own
+    full_down = packed_weights[:, :at].reshape(hidden, model)
+    full_up = (
+        packed_weights[:, at : 2 * at]
+        .reshape(devices, ratio, own, model)
+        .transpose(0, 2, 1, 3)
+        .reshape(model, hidden)
+    )
+    full_out = packed_weights[:, 2 * at : 2 * at + own].reshape(model, model)
+    flat_all = packed_weights[:, 2 * at + own :].reshape(devices, 8 * model)
+    full_vectors = []
+    spot = 0
+    for size in sizes:
+        full_vectors.append(flat_all[:, spot : spot + size].reshape(-1).astype(f32))
+        spot += size
+    bias_out, gain_one, shift_one, bias_down, gain_two, shift_two, bias_up = full_vectors
+
+    by_group = w_qkv.reshape(own, 3, groups, width).transpose(2, 0, 1, 3).reshape(groups, own, 3 * width)
+    mine = lax.all_to_all(by_group, "sp", split_axis=0, concat_axis=0, tiled=True)
+    biases = jnp.concatenate([b_query, b_value]).reshape(1, 2 * own)
+    biases = jnp.pad(biases, ((0, 0), (0, 3 * width - 2 * own)))
+    sent = jnp.concatenate([mine.reshape(groups * own, 3 * width), jnp.pad(biases, ((0, 7), (0, 0)))], 0)
+    all_f = lax.all_gather(sent, "fsdp", axis=0, tiled=False)
+    weights_qkv = (
+        all_f[:, : groups * own]
+        .reshape(shards, groups, own, 3 * width)
+        .transpose(1, 0, 2, 3)
+        .reshape(model, 3 * width)
+    )
+    bias_row = all_f[:, groups * own]
+    bias_query = bias_row[:, :own].reshape(-1).astype(f32)
+    bias_value = bias_row[:, own : 2 * own].reshape(-1).astype(f32)
     bias_qkv = jnp.concatenate([bias_query, jnp.zeros_like(bias_query), bias_value])
-    packed = (jnp.dot(tokens, full_qkv, preferred_element_type=jnp.float32) + bias_qkv).astype(
-        jnp.bfloat16
-    )
-    heads_in = lax.all_to_all(
-        packed.reshape(rows, 3, groups, width), "sp", split_axis=2, concat_axis=0, tiled=True
-    )
-    seg_row = segments[0]
-    queries, keys = augment(heads_in[:, 0, 0], heads_in[:, 1, 0], seg_row)
-    values = heads_in[:, 2, 0]
+
+    tokens_all = gather_tokens(tokens)
+    packed = (jnp.dot(tokens_all, weights_qkv, preferred_element_type=f32) + bias_qkv).astype(bf16)
+    queries, keys = augment(packed[:, :width], packed[:, width : 2 * width], seg_row)
+    values = packed[:, 2 * width :]
     forward_start, forward_number = windows(seg_row, QB, KB, 128)
     backward_start, backward_number = windows(seg_row, KB, QB, QB)
     attended, logsum = attend_forward(
         queries, keys, values, forward_start, forward_number, heads_local
     )
     back_tokens = lax.all_to_all(
-        attended.reshape(seq_len, 1, width), "sp", split_axis=0, concat_axis=1, tiled=True
-    )
-    mixed = back_tokens.reshape(rows, width_all)
-    residual_branch = jnp.dot(mixed, full_out, preferred_element_type=jnp.float32) + bias_out
-    attention_output, attention_normalized, attention_inverse_deviation = layer_normalizer(
-        input_tokens + residual_branch, attention_norm_gain, attention_norm_shift
-    )
-    first_low = attention_output.astype(jnp.bfloat16)
-    pre = jnp.dot(first_low, full_up, preferred_element_type=jnp.float32) + bias_up
-    activ = jax.nn.gelu(pre, approximate=False).astype(jnp.bfloat16)
-    feedforward_net = jnp.dot(activ, full_down, preferred_element_type=jnp.float32) + bias_down
-    layer_output, feedforward_normalized, feedforward_inverse_deviation = layer_normalizer(
-        attention_output + feedforward_net, feedforward_norm_gain, feedforward_norm_shift
-    )
-    output = layer_output.astype(jnp.bfloat16)
-    again = (
-        lax.all_gather(w_qkv, ("sp", "fsdp"), axis=0, tiled=True),
-        lax.all_gather(w_out, ("sp", "fsdp"), axis=0, tiled=True),
-        lax.all_gather(ln1_gain, ("sp", "fsdp"), axis=0, tiled=True),
-        lax.all_gather(w_up, ("sp", "fsdp"), axis=0, tiled=True),
-        lax.all_gather(w_down, ("sp", "fsdp"), axis=0, tiled=True),
-        lax.all_gather(ln2_gain, ("sp", "fsdp"), axis=0, tiled=True),
-    )
-    back_qkv, back_out, reverse_attention_gain, back_up, back_down, reverse_feedforward_gain = again
-    reverse_attention_gain = reverse_attention_gain.astype(jnp.float32)
-    reverse_feedforward_gain = reverse_feedforward_gain.astype(jnp.float32)
-    outgoing_gradient = cotangent.astype(jnp.float32)
-    hidden_two_gradient, feedforward_gain_gradient, feedforward_shift_gradient = norm_reverse_pass(
-        outgoing_gradient,
-        feedforward_normalized,
-        feedforward_inverse_deviation,
-        reverse_feedforward_gain,
-    )
-    grad_ffn = hidden_two_gradient.astype(jnp.bfloat16)
-    grad_bias_down = jnp.sum(grad_ffn.astype(jnp.float32), 0)
-    grad_full_down = jnp.einsum("tf,td->fd", activ, grad_ffn, preferred_element_type=jnp.float32)
-    grad_activ = jnp.einsum("td,fd->tf", grad_ffn, back_down, preferred_element_type=jnp.float32)
+        attended.reshape(groups, rows, width), "sp", split_axis=0, concat_axis=0, tiled=True
+    )
+    mixed = back_tokens.transpose(1, 0, 2).reshape(rows, model)
+
+    input_tokens = tokens.astype(f32)
+    residual_branch = jnp.dot(mixed, full_out, preferred_element_type=f32) + bias_out
+    first, first_hat, first_rstd = layer_normalizer(
+        input_tokens + residual_branch, gain_one, shift_one
+    )
+    first_low = first.astype(bf16)
+    pre = jnp.dot(first_low, full_up, preferred_element_type=f32) + bias_up
+    activ = jax.nn.gelu(pre, approximate=False).astype(bf16)
+    feedforward_net = jnp.dot(activ, full_down, preferred_element_type=f32) + bias_down
+    layer_output, second_hat, second_rstd = layer_normalizer(
+        first + feedforward_net, gain_two, shift_two
+    )
+    output = layer_output.astype(bf16)
+    outgoing_gradient = cotangent.astype(f32)
+    hidden_two_gradient, grad_gain_two, grad_shift_two = norm_reverse_pass(
+        outgoing_gradient, second_hat, second_rstd, gain_two
+    )
+    grad_ffn = hidden_two_gradient.astype(bf16)
+    grad_bias_down = jnp.sum(grad_ffn.astype(f32), 0)
+    grad_full_down = jnp.einsum("tf,td->fd", activ, grad_ffn, preferred_element_type=f32)
+    grad_activ = jnp.einsum("td,fd->tf", grad_ffn, full_down, preferred_element_type=f32)
     gelu_value, gelu_pull = jax.vjp(partial(jax.nn.gelu, approximate=False), pre)
-    grad_pre = gelu_pull(grad_activ)[0].astype(jnp.bfloat16)
-    grad_bias_up = jnp.sum(grad_pre.astype(jnp.float32), 0)
-    grad_full_up = jnp.einsum("td,tf->df", first_low, grad_pre, preferred_element_type=jnp.float32)
+    grad_pre = gelu_pull(grad_activ)[0].astype(bf16)
+    grad_bias_up = jnp.sum(grad_pre.astype(f32), 0)
+    grad_full_up = jnp.einsum("td,tf->df", first_low, grad_pre, preferred_element_type=f32)
     attention_output_gradient = hidden_two_gradient + jnp.einsum(
-        "tf,df->td", grad_pre, back_up, preferred_element_type=jnp.float32
+        "tf,df->td", grad_pre, full_up, preferred_element_type=f32
     )
     grad_h1, grad_gain_one, grad_shift_one = norm_reverse_pass(
-        attention_output_gradient,
-        attention_normalized,
-        attention_inverse_deviation,
-        reverse_attention_gain,
-    )
-    grad_branch = grad_h1.astype(jnp.bfloat16)
-    grad_bias_out = jnp.sum(grad_branch.astype(jnp.float32), 0)
-    grad_full_out = jnp.einsum("td,te->de", mixed, grad_branch, preferred_element_type=jnp.float32)
-    grad_mixed = jnp.einsum(
-        "te,de->td", grad_branch, back_out, preferred_element_type=jnp.float32
-    ).astype(jnp.bfloat16)
+        attention_output_gradient, first_hat, first_rstd, gain_one
+    )
+    grad_branch = grad_h1.astype(bf16)
+    grad_bias_out = jnp.sum(grad_branch.astype(f32), 0)
+    grad_full_out = jnp.einsum("td,te->de", mixed, grad_branch, preferred_element_type=f32)
+    grad_mixed = jnp.einsum("te,de->td", grad_branch, full_out, preferred_element_type=f32).astype(
+        bf16
+    )
+
+    grad_vectors = [
+        grad_bias_out,
+        grad_gain_one,
+        grad_shift_one,
+        grad_bias_down,
+        grad_gain_two,
+        grad_shift_two,
+        grad_bias_up,
+    ]
+    flat = jnp.concatenate([item.reshape(devices, -1) for item in grad_vectors], 1)
+    flat = jnp.pad(flat, ((0, 0), (0, 8 * model - flat.shape[1]))).reshape(devices, 8, model)
+    grad_up_blocks = (
+        grad_full_up.reshape(devices, own, ratio, model)
+        .transpose(0, 2, 1, 3)
+        .reshape(devices, ratio * own, model)
+    )
+    grad_pack = jnp.concatenate(
+        [
+            grad_full_down.reshape(devices, ratio * own, model).astype(bf16),
+            grad_up_blocks.astype(bf16),
+            grad_full_out.reshape(devices, own, model).astype(bf16),
+            flat.astype(bf16),
+        ],
+        1,
+    )
+    grad_pack = grad_pack.reshape(-1, model)
+    reduced = lax.psum_scatter(grad_pack, both, scatter_dimension=0, tiled=True).astype(f32)
+
     grad_heads = lax.all_to_all(
-        grad_mixed.reshape(rows, groups, width), "sp", split_axis=1, concat_axis=0, tiled=True
+        grad_mixed.reshape(rows, groups, width).transpose(1, 0, 2),
+        "sp",
+        split_axis=0,
+        concat_axis=0,
+        tiled=True,
     )
     grad_query, grad_keys, grad_values = attend_backward(
         queries,
@@ -438,70 +498,58 @@
         backward_number,
         heads_local,
     )
-    stacked = jnp.stack(
-        [
-            grad_query.reshape(seq_len, width),
-            grad_keys.reshape(seq_len, width),
-            grad_values.reshape(seq_len, width),
-        ],
-        1,
-    )
-    stacked = stacked[:, :, None, :]
-    grad_back = lax.all_to_all(stacked, "sp", split_axis=0, concat_axis=2, tiled=True)
-    grad_packed = grad_back.reshape(rows, 3 * width_all)
-    grad_wide = grad_packed.astype(jnp.float32)
-    grad_bias_query = jnp.sum(grad_wide[:, :width_all], 0)
-    grad_bias_value = jnp.sum(grad_wide[:, 2 * width_all :], 0)
-    grad_full_qkv = jnp.einsum("td,tc->dc", tokens, grad_packed, preferred_element_type=jnp.float32)
-    grad_input = grad_h1 + jnp.einsum(
-        "tc,dc->td", grad_packed, back_qkv, preferred_element_type=jnp.float32
-    )
-    grads = (
-        grad_full_qkv,
-        grad_bias_query,
-        grad_bias_value,
-        grad_full_out,
-        grad_bias_out,
-        grad_gain_one,
-        grad_shift_one,
-        grad_full_up,
-        grad_bias_up,
-        grad_full_down,
-        grad_bias_down,
-        feedforward_gain_gradient,
-        feedforward_shift_gradient,
-    )
-    owned = (
-        lax.psum_scatter(grads[0], ("sp", "fsdp"), scatter_dimension=0, tiled=True),
-        lax.psum_scatter(grads[1], ("sp", "fsdp"), scatter_dimension=0, tiled=True),
-        lax.psum_scatter(grads[2], ("sp", "fsdp"), scatter_dimension=0, tiled=True),
-        lax.psum_scatter(grads[3], ("sp", "fsdp"), scatter_dimension=0, tiled=True),
-        lax.psum_scatter(grads[4], ("sp", "fsdp"), scatter_dimension=0, tiled=True),
-        lax.psum_scatter(grads[5], ("sp", "fsdp"), scatter_dimension=0, tiled=True),
-        lax.psum_scatter(grads[6], ("sp", "fsdp"), scatter_dimension=0, tiled=True),
-        lax.psum_scatter(grads[7], ("sp", "fsdp"), scatter_dimension=0, tiled=True),
-        lax.psum_scatter(grads[8], ("sp", "fsdp"), scatter_dimension=0, tiled=True),
-        lax.psum_scatter(grads[9], ("sp", "fsdp"), scatter_dimension=0, tiled=True),
-        lax.psum_scatter(grads[10], ("sp", "fsdp"), scatter_dimension=0, tiled=True),
-        lax.psum_scatter(grads[11], ("sp", "fsdp"), scatter_dimension=0, tiled=True),
-        lax.psum_scatter(grads[12], ("sp", "fsdp"), scatter_dimension=0, tiled=True),
-    )
+    grad_packed = jnp.concatenate([grad_query, grad_keys, grad_values], 1)
+    grad_qkv = jnp.einsum("td,tc->dc", tokens_all, grad_packed, preferred_element_type=f32)
+    by_shard = (
+        grad_qkv.reshape(groups, shards, own, 3 * width)
+        .transpose(1, 0, 2, 3)
+        .reshape(shards, groups * own, 3 * width)
+        .astype(bf16)
+    )
+    by_shard = lax.all_to_all(by_shard, "fsdp", split_axis=0, concat_axis=0, tiled=True)
+    small = jnp.sum(by_shard.astype(f32), 0)
+    owned_qkv = lax.all_to_all(
+        small.reshape(groups, own, 3 * width), "sp", split_axis=0, concat_axis=0, tiled=True
+    )
+    owned_qkv = (
+        owned_qkv.reshape(groups, own, 3, width).transpose(1, 2, 0, 3).reshape(own, 3 * model)
+    )
+    ones = jnp.ones((8, seq_len), bf16)
+    bias_sums = jnp.dot(ones, grad_packed, preferred_element_type=f32)[0].reshape(3, shards, own)
+    bias_sums = jnp.concatenate([bias_sums[0], bias_sums[2]], 1)
+    bias_sums = lax.all_to_all(bias_sums, "fsdp", split_axis=0, concat_axis=0, tiled=True)
+    bias_sums = jnp.sum(bias_sums, 0)
+    grad_query_bias = bias_sums[:own]
+    grad_value_bias = bias_sums[own:]
+    partial_in = jnp.einsum("tc,dc->td", grad_packed, weights_qkv, preferred_element_type=f32)
+    grad_input = grad_h1 + scatter_rows(partial_in)
+
+    owned_down = reduced[:at]
+    owned_up = reduced[at : 2 * at].reshape(ratio, own, model).transpose(1, 0, 2).reshape(own, hidden)
+    owned_out = reduced[2 * at : 2 * at + own]
+    flat = reduced[2 * at + own :].reshape(-1)
+    pieces = []
+    spot = 0
+    for size in sizes:
+        pieces.append(flat[spot : spot + size])
+        spot += size
+    grad_b_out, grad_g1, grad_s1, grad_b_down, grad_g2, grad_s2, grad_b_up = pieces
     return (
         output,
         grad_input,
-        owned[0],
-        owned[1],
-        owned[2],
-        owned[3],
-        owned[4],
-        owned[5],
-        owned[6],
-        owned[7],
-        owned[8],
-        owned[9],
-        owned[10],
-        owned[11],
-        owned[12],
+        owned_qkv,
+        grad_query_bias,
+        grad_value_bias,
+        owned_out,
+        grad_b_out,
+        grad_g1,
+        grad_s1,
+        owned_up,
+        grad_b_up,
+        owned_down,
+        grad_b_down,
+        grad_g2,
+        grad_s2,
     )
 
 

time: 895 us -> 525 us (0.59)
  waiting for transfers between devices: 293 us -> 65.3 us
  blocking collectives: 191 us -> 23.1 us
  starting transfers between devices: 8.86 us -> 63.9 us
  Pallas kernels: 130 us -> 104 us
  other arithmetic: 26.2 us -> 42.9 us
    unnamed x9 -> x2, waiting for transfers between devices: 128 us -> 0.03 us
    all_to_all x2 -> x0, blocking collectives: 108 us -> none  [the longest x1 88.9 us: body(): lax.all_to_all(stacked, 'sp', split_axis=0, concat_axis=2, tiled=True)]
    unnamed x2 -> x0, blocking collectives: 83.3 us -> none
    reduce_scatter x3 -> x1, waiting for transfers between devices: 81.5 us -> 0.01 us  [body(): lax.psum_scatter(grad_pack, both, scatter_dimension=0, tiled=True)]
    all_to_all x2 -> x6, starting transfers between devices: 8.29 us -> 53.4 us  [the longest x1 32.6 us: body(): lax.all_to_all(bias_sums, 'fsdp', split_axis=0, concat_axis=0, tiled=True)]
    all_gather x4 -> x1, waiting for transfers between devices: 40.8 us -> 0.02 us  [body(): packed_weights = lax.all_gather(pack, both, axis=0, tiled=False)]
    ppermute x0 -> x8, waiting for transfers between devices: none -> 32.1 us  [by_sp(): return lax.ppermute(value, 'sp', [(i, i ^ flip) for i in range(groups)])]
    unnamed x96 -> x128, local copies, waits for them, and re-layouts: 51.8 us -> 24.7 us
  transfers between devices with their start and end apart: 10 -> 16, of which waited for: 6 -> 8; matrix products, arithmetic and copies ran while one was open for 21% -> 19% of each run, Pallas kernels for 15% -> 20%
where the time goes in v2:
time: 525 us; the launch traced here: 520 us
  matrix products  104 us (20%)
  Pallas kernels  104 us (20%)
  local copies, waits for them, and re-layouts  102 us (19%)
  waiting for transfers between devices  65.3 us (12%)
  starting transfers between devices  63.9 us (12%)
  other arithmetic  42.9 us (8%)
  blocking collectives  23.1 us (4%)
  between operations  15.2 us (3%)
    pallas_call x1, Pallas kernels, attend_backward(): pl.pallas_call(lambda *refs: backward_kernel(heads, *refs), grid_spec=plt...  70.3 us
    pallas_call x1, Pallas kernels, attend_forward(): pl.pallas_call(lambda *refs: forward_kernel(heads, *refs), grid_spec=pltp...  33.5 us
    all_to_all x1, starting transfers between devices, body(): lax.all_to_all(bias_sums, 'fsdp', split_axis=0, concat_axis=0, tiled=True)  32.6 us
    ppermute x8, waiting for transfers between devices, by_sp(): return lax.ppermute(value, 'sp', [(i, i ^ flip) for i in range(groups)])  32.1 us
    dot_general x1, matrix products, body(): pre = jnp.dot(first_low, full_up, preferred_element_type=f32) + bias_up  30.4 us
    unnamed x128, local copies, waits for them, and re-layouts  24.7 us
    all_gather x1, blocking collectives, body(): all_f = lax.all_gather(sent, 'fsdp', axis=0, tiled=False)  23.1 us
    convert_element_type x2, local copies, waits for them, and re-layouts, body(): grad_up_blocks.astype(bf16)  15.5 us
  transfers between devices with their start and end apart: 16, of which 8 were waited for; matrix products, arithmetic and copies ran while one was open for 19% of the time, Pallas kernels for 20%

profile of v2, /device:TPU:0, one launch (start us, length us, event | category | flops | bytes accessed | tf_op | source)
XLA Modules:
  0.0 520.0 jit_solution(18288387781056968737)
XLA Ops:
  11.4 4.8 concatenate.50
  17.8 3.0 collective-permute-start
  20.8 1.5 collective-permute-start.1
  24.3 3.9 all-to-all-start
  29.8 1.5 copy.126
  34.9 2.2 copy-done.12
  39.0 2.1 select_convert_fusion
  41.2 12.6 %all-to-all-done = bf16[4,24,576]{2,1,0:T(8,128)(2,1)} async-done(((bf16[4,24,576]{2,1,0:T(8,128)(2,1)}), bf16[4,24,576]{2,1,0:T(8,128)(2,1)}, u32[]{:S(2)}, u32[]{:S(2)}) %all-to-all-start) | async-done | bytes 110624 | tf_op jit(solution)/shard_map/all_to_all | solution.py:387
  54.7 23.1 %all-gather = bf16[832,576]{1,0:T(8,128)(2,1)S(1)} all-gather(bf16[104,576]{1,0:T(8,128)(2,1)S(1)} %fusion.22), channel_id=2, replica_groups=mesh['sp'=4,'fsdp'=8] {'fsdp'}, dimensions={0}, use_global_device_ids=true | all-gather | bytes 1078272 | tf_op jit(solution)/shard_map/all_gather | solution.py:391
  77.9 1.9 slice.187
  80.7 2.1 slice.188
  85.4 2.4 constant_dynamic-update-slice_fusion.6
  87.7 2.4 constant_dynamic-update-slice_fusion.5
  90.1 18.2 %collective-permute-done.2 = bf16[384,768]{1,0:T(8,128)(2,1)S(1)} collective-permute-done((bf16[384,768]{1,0:T(8,128)(2,1)}, bf16[384,768]{1,0:T(8,128)(2,1)S(1)}, u32[]{:S(2)}, u32[]{:S(2)}) %collective-permute-start.2) | collective-permute-done | bytes 589856 | tf_op jit(solution)/shard_map/ppermute | solution.py:293
  109.1 2.4 collective-permute-done.3
  111.6 1.9 constant_dynamic-update-slice_fusion.3
  113.5 6.2 %add_convert_fusion.1 = bf16[3072,576]{1,0:T(8,128)(2,1)S(1)} fusion(bf16[3072,768]{1,0:T(8,128)(2,1)} %constant_dynamic-update-slice_fusion.3, bf16[768,576]{1,0:T(8,128)(2,1)S(1)} %bitcast.109, f32[576]{0:T(1024)S(1)} %pad_maximum_fusion.4), kind=kOutput, calls=%fused_computation.18 | convolution fusion | flops 2721447936 | bytes 9144576 | tf_op jit(solution)/shard_map/dot_general | solution.py:404
  119.7 1.8 fusion.43
  122.7 33.5 %attend_forward.1 = (bf16[3072,192]{1,0:T(8,128)(2,1)S(1)}, f32[8,3072]{1,0:T(8,128)S(1)}) custom-call(s32[12]{0:T(128)S(1)} %get-tuple-element.155.refs_0_, s32[12]{0:T(128)S(1)} %get-tuple-element.156.refs_1_, bf16[3072,256]{1,0:T(8,128)(2,1)S(1)} %get-tuple-element.160.refs_2_, bf16[3072,256]{1,0:T(8,128)(2,1)S(1)} %get-tuple-element.159.refs_3_, ...), custom_call_target="tpu_custom_call" | custom-call | flops 3623878656 | bytes 6291456 | tf_op jit(solution)/shard_map/attend_forward/pallas_call | solution.py:109
  156.9 1.5 copy.130
  158.4 4.3 all-to-all-start.1
  164.8 2.4 slice.196
  168.6 8.0 %fusion.42 = (bf16[32,96,768]{2,1,0:T(8,128)(2,1)}, bf16[32,96,768]{2,1,0:T(8,128)(2,1)}) fusion(bf16[32,224,768]{2,1,0:T(8,128)(2,1)} %bitcast.85), kind=kLoop, calls=%fused_computation.149 | loop fusion | bytes 18874368 | tf_op jit(solution)/shard_map/slice | solution.py:370
  176.6 3.2 fusion.47
  184.1 4.7 copy.131
  188.8 3.2 copy.161
  194.7 30.4 %multiply_convert_fusion = (bf16[768,3072]{1,0:T(8,128)(2,1)S(1)}, f32[768,3072]{1,0:T(8,128)}, f32[768,3072]{1,0:T(8,128)}) fusion(f32[3072]{0:T(1024)} %reshape.288, bf16[768,3072]{1,0:T(8,128)(2,1)} %bitcast.86, f32[768,768]{0,1:T(8,128)S(1)} %get-tuple-element.162, f32[768]{0:T(1024)} %reshape.287, f32[768]{0:T(1024)} %reshape.286, ...), kind=kOutput, calls=%fused_computation.4 | convolution fusion | flops 3782541312 | bytes 30695424 | tf_op jit(solution)/shard_map/dot_general | solution.py:423
  225.2 9.2 %fusion.48 = (f32[768]{0:T(1024)S(1)}, f32[768,768]{0,1:T(8,128)S(1)}) fusion(f32[768]{0:T(1024)S(1)} %copy-done.39, bf16[768,3072]{1,0:T(8,128)(2,1)S(1)} %get-tuple-element.119, bf16[3072,768]{1,0:T(8,128)(2,1)} %bitcast.91, f32[768]{0:T(1024)S(1)} %copy-done.37, f32[768]{0:T(1024)S(1)} %copy-done.30, f32[768]{0:T(1024)S(1)} %copy-done.32, ...), kind=kOutput, calls=%fused_computation.155 | convolution fusion | flops 3628006656 | bytes 14174208 | tf_op jit(solution)/shard_map/dot_general | solution.py:425
  238.0 3.5 fusion.12
  242.6 5.7 %convolution_convert_fusion.1 = bf16[3072,768]{1,0:T(8,128)(2,1)} fusion(bf16[768,3072]{1,0:T(8,128)(2,1)S(1)} %copy-done.52, bf16[768,768]{0,1:T(8,128)(2,1)S(1)} %get-tuple-element.114), kind=kOutput, calls=%fused_computation.20 | convolution fusion | flops 3626237952 | bytes 10616832 | tf_op jit(solution)/shard_map/tf,td->fd/dot_general | solution.py:436
  248.4 13.2 %fusion.36 = (bf16[3072]{0:T(1024)(128)(2,1)}, bf16[768,3072]{1,0:T(8,128)(2,1)}) fusion(f32[768,3072]{1,0:T(8,128)} %get-tuple-element.120, f32[768,3072]{1,0:T(8,128)} %get-tuple-element.163, f32[3072]{0:T(1024)S(1)} %copy-done.34, bf16[768,768]{0,1:T(8,128)(2,1)S(1)} %get-tuple-element.114, bf16[3072,768]{1,0:T(8,128)(2,1)S(1)} %bitcast.94), kind=kOutput, calls=%fused_computation.147 | convolution fusion | flops 3661624320 | bytes 29509632 | tf_op jit(solution)/shard_map/td,fd->tf/dot_general | solution.py:437
  261.6 8.3 %convolution_convert_fusion = bf16[768,3072]{1,0:T(8,128)(2,1)} fusion(bf16[768,3072]{1,0:T(8,128)(2,1)} %get-tuple-element.112, f32[768,768]{0,1:T(8,128)S(1)} %copy-done.6, f32[768]{0:T(1024)S(1)} %copy-done.38, f32[768]{0:T(1024)S(1)} %copy-done.31, f32[768]{0:T(1024)S(1)} %copy-done.33, f32[768]{0:T(1024)S(1)} %copy-done.26), kind=kOutput, calls=%fused_computation.19 | convolution fusion | flops 3629187072 | bytes 11808768 | tf_op jit(solution)/shard_map/td,tf->df/dot_general | solution.py:441
  269.9 6.9 %multiply_reduce_fusion = (bf16[768]{0:T(1024)(128)(2,1)}, f32[768]{0:T(1024)}, f32[768]{0:T(1024)}, bf16[768]{0:T(1024)(128)(2,1)}, f32[768,768]{0,1:T(8,128)}) fusion(f32[768,768]{0,1:T(8,128)S(1)} %copy-done.6, f32[768]{0:T(1024)S(1)} %copy-done.33, f32[768]{0:T(1024)S(1)} %copy-done.26, f32[768]{0:T(1024)S(1)} %copy-done.31, ...), kind=kOutput, calls=%fused_computation.32 | convolution fusion | flops 3634492416 | bytes 17728512 | tf_op jit(solution)/shard_map/tf,df->td/dot_general | solution.py:442
  276.9 10.0 %convert_element_type.250 = bf16[32,24,4,768]{3,2,1,0:T(4,128)(2,1)} reshape(bf16[768,3072]{1,0:T(8,128)(2,1)} %convolution_convert_fusion) | data formatting | bytes 9437184 | tf_op jit(solution)/shard_map/convert_element_type | solution.py:474
  286.9 5.5 %copy.147 = bf16[32,4,24,768]{3,2,1,0:T(8,128)(2,1)} copy(bf16[32,4,24,768]{3,1,2,0:T(4,128)(2,1)} %bitcast.80) | data formatting | bytes 9437184 | tf_op jit(solution)/shard_map/convert_element_type | solution.py:474
  294.3 2.5 convolution_convert_fusion.3
  297.0 7.7 %pad_maximum_fusion = bf16[32,224,768]{2,1,0:T(8,128)(2,1)} fusion(bf16[32,8,768]{2,1,0:T(8,128)(2,1)S(1)} %bitcast.104, bf16[32,24,768]{2,1,0:T(8,128)(2,1)S(1)} %convolution_convert_fusion.3, bf16[32,96,768]{2,1,0:T(8,128)(2,1)S(1)} %bitcast.81, bf16[32,96,768]{2,1,0:T(8,128)(2,1)} %bitcast.90), kind=kLoop, calls=%fused_computation.1 | loop fusion | flops 44040192 | bytes 22020096 | tf_op jit(solution)/shard_map/concatenate | solution.py:471
  306.0 2.1 convolution_convert_fusion.2
  308.1 4.1 all-to-all-start.2
  312.2 11.0 %all-to-all-done.2 = bf16[4,768,192]{1,2,0:T(8,128)(2,1)S(1)} async-done(((bf16[4,768,192]{1,2,0:T(8,128)(2,1)}), bf16[4,768,192]{1,2,0:T(8,128)(2,1)S(1)}, u32[]{:S(2)}, u32[]{:S(2)}) %all-to-all-start.2) | async-done | bytes 1179680 | tf_op jit(solution)/shard_map/all_to_all | solution.py:483
  323.2 1.5 copy.135
  324.7 70.3 %attend_backward.1 = (bf16[3072,192]{1,0:T(8,128)(2,1)}, bf16[3072,192]{1,0:T(8,128)(2,1)}, bf16[3072,192]{1,0:T(8,128)(2,1)}) custom-call(s32[12]{0:T(128)} %get-tuple-element.117.refs_0_, s32[12]{0:T(128)} %get-tuple-element.118.refs_1_, bf16[3072,256]{1,0:T(8,128)(2,1)} %copy-done.2, bf16[3072,256]{1,0:T(8,128)(2,1)} %copy-done.1, ...), custom_call_target="tpu_custom_call" | custom-call | flops 9059696640 | bytes 12582912 | tf_op jit(solution)/shard_map/attend_backward/pallas_call | solution.py:226
  395.1 3.4 fusion.23
  399.3 32.6 %all-to-all-start.5 = ((f32[8,1,48]{2,1,0:T(1,128)}), f32[8,1,48]{2,1,0:T(1,128)S(1)}, u32[]{:S(2)}, u32[]{:S(2)}) async-start(f32[8,1,48]{2,1,0:T(1,128)} %bitcast.25), calls=%async_computation.5 | async-start | bytes 8192 | tf_op jit(solution)/shard_map/all_to_all | solution.py:520
  431.9 5.9 %fusion.35 = f32[3072,768]{0,1:T(8,128)S(1)} fusion(bf16[768,576]{1,0:T(8,128)(2,1)S(1)} %bitcast.110, bf16[3072,192]{1,0:T(8,128)(2,1)} %get-tuple-element.24, bf16[3072,192]{1,0:T(8,128)(2,1)} %get-tuple-element.23, bf16[3072,192]{1,0:T(8,128)(2,1)} %get-tuple-element.22), kind=kOutput, calls=%fused_computation.146 | convolution fusion | flops 2728525824 | bytes 13860864 | tf_op jit(solution)/shard_map/tc,dc->td/dot_general | solution.py:524
  437.9 3.5 copy-done.10
  442.9 1.4 collective-permute-start.6
  446.0 7.2 %convolution_convert_fusion.4 = bf16[768,576]{0,1:T(8,128)(2,1)} fusion(bf16[3072,768]{1,0:T(8,128)(2,1)} %constant_dynamic-update-slice_fusion.3, bf16[3072,192]{1,0:T(8,128)(2,1)S(1)} %copy-done.49, bf16[3072,192]{1,0:T(8,128)(2,1)S(1)} %copy-done.48, bf16[3072,192]{1,0:T(8,128)(2,1)S(1)} %copy-done.47), kind=kOutput, calls=%fused_computation.55 | convolution fusion | flops 2728968192 | bytes 9142272 | tf_op jit(solution)/shard_map/td,tc->dc/dot_general | solution.py:502
  453.2 1.5 copy.144
  455.8 5.1 all-to-all-start.3
  460.9 10.7 %collective-permute-done.6 = bf16[768,768]{0,1:T(8,128)(2,1)} collective-permute-done((bf16[768,768]{0,1:T(8,128)(2,1)}, bf16[768,768]{0,1:T(8,128)(2,1)}, u32[]{:S(2)}, u32[]{:S(2)}) %collective-permute-start.6) | collective-permute-done | bytes 1179680 | tf_op jit(solution)/shard_map/ppermute | solution.py:293
  471.6 1.4 convert_element_type.239
  473.9 1.4 convert_element_type.236
  475.3 3.9 fusion.17
  479.2 1.5 collective-permute-start.5
  481.2 1.4 copy.150
  482.7 3.5 all-to-all-done.3
  486.2 2.1 convert_reduce_fusion
  488.3 3.4 all-to-all-start.4
  492.3 6.0 %all-to-all-done.4 = f32[4,24,576]{2,1,0:T(8,128)S(1)} async-done(((f32[4,24,576]{2,1,0:T(8,128)}), f32[4,24,576]{2,1,0:T(8,128)S(1)}, u32[]{:S(2)}, u32[]{:S(2)}) %all-to-all-start.4) | async-done | bytes 221216 | tf_op jit(solution)/shard_map/all_to_all | solution.py:511
  499.5 3.0 fusion.18
  502.5 1.7 maximum_add_fusion
  504.2 3.0 copy.151
  509.2 1.7 fusion.44
  (219 shorter events, 52.6 us)
Async XLA Ops:
  7.2 22.6 %copy-start.11 = (bf16[768,768]{1,0:T(8,128)(2,1)S(1)}, bf16[768,768]{1,0:T(8,128)(2,1)}, u32[]{:S(2)}) copy-start(bf16[768,768]{1,0:T(8,128)(2,1)} %param.16) | copy-start | bytes 3538948
  7.2 24.1 %copy-start.13 = (bf16[768,768]{1,0:T(8,128)(2,1)S(1)}, bf16[768,768]{1,0:T(8,128)(2,1)}, u32[]{:S(2)}) copy-start(bf16[768,768]{1,0:T(8,128)(2,1)} %param.18) | copy-start | bytes 3538948
  7.2 155.8 %all-gather.4.cloned.1.call-start = ((), (), s32[]{:S(2)}) async-start(), calls=%async_computation.8 | async-start | bytes 11354112 | tf_op jit(solution)/shard_map/all_gather | solution.py:368
  17.8 62.9 %collective-permute-start = (bf16[768,768]{1,0:T(8,128)(2,1)}, bf16[768,768]{1,0:T(8,128)(2,1)}, u32[]{:S(2)}, u32[]{:S(2)}) collective-permute-start(bf16[768,768]{1,0:T(8,128)(2,1)} %param.16), channel_id=1, source_target_pairs={{0,8},{8,0},{16,24},{24,16},{1,9},{9,1},{17,25},{25,17},{2,10},{10... | collective-permute-start | bytes 3538952 | tf_op jit(solution)/shard_map/ppermute | solution.py:293
  20.8 57.1 %collective-permute-start.1 = (bf16[768,768]{1,0:T(8,128)(2,1)}, bf16[768,768]{1,0:T(8,128)(2,1)}, u32[]{:S(2)}, u32[]{:S(2)}) collective-permute-start(bf16[768,768]{1,0:T(8,128)(2,1)} %param.16), channel_id=1, source_target_pairs={{0,16},{8,24},{16,0},{24,8},{1,17},{9,25},{17,1},{25,9},{2,18},{10... | collective-permute-start | bytes 3538952 | tf_op jit(solution)/shard_map/ppermute | solution.py:293
  24.3 29.6 %all-to-all-start = ((bf16[4,24,576]{2,1,0:T(8,128)(2,1)}), bf16[4,24,576]{2,1,0:T(8,128)(2,1)}, u32[]{:S(2)}, u32[]{:S(2)}) async-start(bf16[4,24,576]{2,1,0:T(8,128)(2,1)} %reshape.254), calls=%async_computation | async-start | bytes 245760 | tf_op jit(solution)/shard_map/all_to_all | solution.py:387
  34.7 2.9 copy-start.21
  34.7 6.4 %copy-start.45 = (bf16[24]{0:T(256)(128)(2,1)S(1)}, bf16[24]{0:T(256)(128)(2,1)}, u32[]{:S(2)}) copy-start(bf16[24]{0:T(256)(128)(2,1)} %param.21) | copy-start | bytes 148
  34.7 6.4 %copy-start.46 = (bf16[24]{0:T(256)(128)(2,1)S(1)}, bf16[24]{0:T(256)(128)(2,1)}, u32[]{:S(2)}) copy-start(bf16[24]{0:T(256)(128)(2,1)} %param.20) | copy-start | bytes 148
  34.8 2.2 copy-start.12
  79.8 28.4 %collective-permute-start.2 = (bf16[384,768]{1,0:T(8,128)(2,1)}, bf16[384,768]{1,0:T(8,128)(2,1)S(1)}, u32[]{:S(2)}, u32[]{:S(2)}) collective-permute-start(bf16[384,768]{1,0:T(8,128)(2,1)} %slice.187), channel_id=1, source_target_pairs={{0,8},{8,0},{16,24},{24,16},{1,9},{9,1},{17,25},{25,17},{2,10},{10... | collective-permute-start | bytes 1769480 | tf_op jit(solution)/shard_map/ppermute | solution.py:293
  82.7 28.8 %collective-permute-start.3 = (bf16[384,768]{1,0:T(8,128)(2,1)}, bf16[384,768]{1,0:T(8,128)(2,1)}, u32[]{:S(2)}, u32[]{:S(2)}) collective-permute-start(bf16[384,768]{1,0:T(8,128)(2,1)} %slice.188), channel_id=1, source_target_pairs={{0,16},{8,24},{16,0},{24,8},{1,17},{9,25},{17,1},{25,9},{2,18},{10... | collective-permute-start | bytes 1769480 | tf_op jit(solution)/shard_map/ppermute | solution.py:293
  84.5 28.9 %copy-start.18 = (bf16[8,4,24,576]{3,2,0,1:T(8,128)(2,1)}, bf16[8,4,24,576]{3,2,0,1:T(8,128)(2,1)S(1)}, u32[]{:S(2)}) copy-start(bf16[8,4,24,576]{3,2,0,1:T(8,128)(2,1)S(1)} %copy.128) | copy-start | bytes 2654212
  119.7 1.8 copy-start.15
  119.7 1.8 copy-start.44
  122.7 33.5 %copy-start.1 = (bf16[3072,256]{1,0:T(8,128)(2,1)}, bf16[3072,256]{1,0:T(8,128)(2,1)S(1)}, u32[]{:S(2)}) copy-start(bf16[3072,256]{1,0:T(8,128)(2,1)S(1)} %get-tuple-element.159.refs_3_) | copy-start | bytes 4718596
  122.7 33.5 %copy-start.2 = (bf16[3072,256]{1,0:T(8,128)(2,1)}, bf16[3072,256]{1,0:T(8,128)(2,1)S(1)}, u32[]{:S(2)}) copy-start(bf16[3072,256]{1,0:T(8,128)(2,1)S(1)} %get-tuple-element.160.refs_2_) | copy-start | bytes 4718596
  156.9 1.5 copy-start
  158.4 18.2 %all-to-all-start.1 = ((bf16[4,768,192]{1,2,0:T(8,128)(2,1)}), bf16[4,768,192]{1,2,0:T(8,128)(2,1)}, u32[]{:S(2)}, u32[]{:S(2)}) async-start(bf16[4,768,192]{1,2,0:T(8,128)(2,1)} %copy.130), calls=%async_computation.1 | async-start | bytes 2359296 | tf_op jit(solution)/shard_map/all_to_all | solution.py:412
  162.7 344.6 %reduce-scatter.2.cloned.1.call-start = ((), (), s32[]{:S(2)}) async-start(), calls=%async_computation.7 | async-start | bytes 11354112 | tf_op jit(solution)/shard_map/reduce_scatter | solution.py:481
  179.8 14.9 %copy-start.5 = (f32[768,768]{0,1:T(8,128)}, f32[768,768]{0,1:T(8,128)S(1)}, u32[]{:S(2)}) copy-start(f32[768,768]{0,1:T(8,128)S(1)} %get-tuple-element.162) | copy-start | bytes 7077892
  194.7 30.5 %copy-start.25 = (f32[768]{0:T(1024)S(1)}, f32[768]{0:T(1024)}, u32[]{:S(2)}) copy-start(f32[768]{0:T(1024)} %copy-done.24) | copy-start | bytes 9220
  194.7 30.5 %copy-start.30 = (f32[768]{0:T(1024)S(1)}, f32[768]{0:T(1024)}, u32[]{:S(2)}) copy-start(f32[768]{0:T(1024)} %reshape.286) | copy-start | bytes 9220
  194.7 30.5 %copy-start.32 = (f32[768]{0:T(1024)S(1)}, f32[768]{0:T(1024)}, u32[]{:S(2)}) copy-start(f32[768]{0:T(1024)} %add_rsqrt_fusion.1) | copy-start | bytes 9220
  194.7 30.5 %copy-start.37 = (f32[768]{0:T(1024)S(1)}, f32[768]{0:T(1024)}, u32[]{:S(2)}) copy-start(f32[768]{0:T(1024)} %reshape.287) | copy-start | bytes 9220
  194.7 30.5 %copy-start.39 = (f32[768]{0:T(1024)S(1)}, f32[768]{0:T(1024)}, u32[]{:S(2)}) copy-start(f32[768]{0:T(1024)} %reshape.289) | copy-start | bytes 9220
  225.2 9.2 %copy-start.51 = (bf16[768,3072]{1,0:T(8,128)(2,1)}, bf16[768,3072]{1,0:T(8,128)(2,1)S(1)}, u32[]{:S(2)}) copy-start(bf16[768,3072]{1,0:T(8,128)(2,1)S(1)} %get-tuple-element.119) | copy-start | bytes 14155780
  238.0 3.6 copy-start.23
  238.0 3.6 copy-start.27
  238.0 3.6 copy-start.28
  238.0 4.6 copy-start.52
  241.6 6.7 %slice-start.2 = ((s8[4718592]{0:T(1024)(128)(4,1)}), s8[4194304]{0:T(1024)(128)(4,1)S(1)}, s32[]{:S(2)}) async-start(s8[4718592]{0:T(1024)(128)(4,1)} %bitcast.92), calls=%async_computation.11 | async-start | bytes 8388608
  242.6 5.7 %slice-start.3 = ((s8[4718592]{0:T(1024)(128)(4,1)}), s8[524288]{0:T(1024)(128)(4,1)S(1)}, s32[]{:S(2)}) async-start(s8[4718592]{0:T(1024)(128)(4,1)} %bitcast.92), calls=%async_computation.12 | async-start | bytes 1048576
  242.6 5.7 %copy-start.34 = (f32[3072]{0:T(1024)S(1)}, f32[3072]{0:T(1024)}, u32[]{:S(2)}) copy-start(f32[3072]{0:T(1024)} %reshape.288) | copy-start | bytes 36868
  242.6 27.3 %slice-start = ((s8[4718592]{0:T(1024)(128)(4,1)}), s8[4194304]{0:T(1024)(128)(4,1)S(1)}, s32[]{:S(2)}) async-start(s8[4718592]{0:T(1024)(128)(4,1)} %bitcast.87), calls=%async_computation.9 | async-start | bytes 8388608
  248.3 13.3 %copy-start.6 = (f32[768,768]{0,1:T(8,128)S(1)}, f32[768,768]{0,1:T(8,128)}, u32[]{:S(2)}) copy-start(f32[768,768]{0,1:T(8,128)} %copy-done.5) | copy-start | bytes 7077892
  248.3 13.3 %copy-start.26 = (f32[768]{0:T(1024)S(1)}, f32[768]{0:T(1024)}, u32[]{:S(2)}) copy-start(f32[768]{0:T(1024)} %copy-done.24) | copy-start | bytes 9220
  248.3 13.3 %copy-start.31 = (f32[768]{0:T(1024)S(1)}, f32[768]{0:T(1024)}, u32[]{:S(2)}) copy-start(f32[768]{0:T(1024)} %reshape.286) | copy-start | bytes 9220
  248.3 13.3 %copy-start.33 = (f32[768]{0:T(1024)S(1)}, f32[768]{0:T(1024)}, u32[]{:S(2)}) copy-start(f32[768]{0:T(1024)} %add_rsqrt_fusion.1) | copy-start | bytes 9220
  248.3 13.3 %copy-start.38 = (f32[768]{0:T(1024)S(1)}, f32[768]{0:T(1024)}, u32[]{:S(2)}) copy-start(f32[768]{0:T(1024)} %reshape.287) | copy-start | bytes 9220
  248.3 21.6 %slice-start.1 = ((s8[4718592]{0:T(1024)(128)(4,1)}), s8[524288]{0:T(1024)(128)(4,1)S(1)}, s32[]{:S(2)}) async-start(s8[4718592]{0:T(1024)(128)(4,1)} %bitcast.87), calls=%async_computation.10 | async-start | bytes 1048576
  261.6 8.3 %copy-start.50 = (bf16[768,3072]{1,0:T(8,128)(2,1)S(1)}, bf16[768,3072]{1,0:T(8,128)(2,1)}, u32[]{:S(2)}) copy-start(bf16[768,3072]{1,0:T(8,128)(2,1)} %get-tuple-element.112) | copy-start | bytes 14155780
  286.9 5.6 %copy-start.41 = (f32[768]{0:T(1024)S(1)}, f32[768]{0:T(1024)}, u32[]{:S(2)}) copy-start(f32[768]{0:T(1024)} %get-tuple-element.101) | copy-start | bytes 9220
  286.9 5.6 %copy-start.40 = (f32[768]{0:T(1024)S(1)}, f32[768]{0:T(1024)}, u32[]{:S(2)}) copy-start(f32[768]{0:T(1024)} %get-tuple-element.104) | copy-start | bytes 9220
  286.9 5.6 %copy-start.7 = (f32[768,768]{0,1:T(8,128)S(1)}, f32[768,768]{0,1:T(8,128)}, u32[]{:S(2)}) copy-start(f32[768,768]{0,1:T(8,128)} %copy-done.5) | copy-start | bytes 7077892
  286.9 5.6 %copy-start.16 = (f32[768,768]{0,1:T(8,128)S(1)}, f32[768,768]{0,1:T(8,128)}, u32[]{:S(2)}) copy-start(f32[768,768]{0,1:T(8,128)} %get-tuple-element.166) | copy-start | bytes 7077892
  292.5 1.5 copy-start.29
  294.3 2.7 copy-start.4
  308.1 15.1 %all-to-all-start.2 = ((bf16[4,768,192]{1,2,0:T(8,128)(2,1)}), bf16[4,768,192]{1,2,0:T(8,128)(2,1)S(1)}, u32[]{:S(2)}, u32[]{:S(2)}) async-start(bf16[4,768,192]{1,2,0:T(8,128)(2,1)} %bitcast.107), calls=%async_computation.2 | async-start | bytes 2359296 | tf_op jit(solution)/shard_map/all_to_all | solution.py:483
  395.1 36.9 %copy-start.19 = (bf16[8,4,24,576]{3,2,0,1:T(8,128)(2,1)S(1)}, bf16[8,4,24,576]{3,2,0,1:T(8,128)(2,1)}, u32[]{:S(2)}) copy-start(bf16[8,4,24,576]{3,2,0,1:T(8,128)(2,1)} %copy-done.18) | copy-start | bytes 2654212
  399.3 56.5 %all-to-all-start.5 = ((f32[8,1,48]{2,1,0:T(1,128)}), f32[8,1,48]{2,1,0:T(1,128)S(1)}, u32[]{:S(2)}, u32[]{:S(2)}) async-start(f32[8,1,48]{2,1,0:T(1,128)} %bitcast.25), calls=%async_computation.5 | async-start | bytes 8192 | tf_op jit(solution)/shard_map/all_to_all | solution.py:520
  437.9 3.5 copy-start.10
  441.8 4.2 copy-start.47
  441.8 4.2 copy-start.48
  441.8 4.2 copy-start.49
  442.9 28.7 %collective-permute-start.6 = (bf16[768,768]{0,1:T(8,128)(2,1)}, bf16[768,768]{0,1:T(8,128)(2,1)}, u32[]{:S(2)}, u32[]{:S(2)}) collective-permute-start(bf16[768,768]{0,1:T(8,128)(2,1)} %pad_maximum_fusion.3), channel_id=1, source_target_pairs={{0,16},{8,24},{16,0},{24,8},{1,17},{9,25},{17,1},{25,9},{2,18},{10... | collective-permute-start | bytes 3538952 | tf_op jit(solution)/shard_map/ppermute | solution.py:293
  445.5 28.4 %collective-permute-start.4 = (bf16[768,768]{0,1:T(8,128)(2,1)}, bf16[768,768]{0,1:T(8,128)(2,1)}, u32[]{:S(2)}, u32[]{:S(2)}) collective-permute-start(bf16[768,768]{0,1:T(8,128)(2,1)} %pad_maximum_fusion.2), channel_id=1, source_target_pairs={{0,8},{8,0},{16,24},{24,16},{1,9},{9,1},{17,25},{25,17},{2,10},{10... | collective-permute-start | bytes 3538952 | tf_op jit(solution)/shard_map/ppermute | solution.py:293
  455.8 30.4 %all-to-all-start.3 = ((bf16[8,96,576]{2,1,0:T(8,128)(2,1)}), bf16[8,96,576]{2,1,0:T(8,128)(2,1)}, u32[]{:S(2)}, u32[]{:S(2)}) async-start(bf16[8,96,576]{2,1,0:T(8,128)(2,1)} %bitcast.98), calls=%async_computation.3 | async-start | bytes 1966080 | tf_op jit(solution)/shard_map/all_to_all | solution.py:509
  473.0 6.2 %copy-start.8 = (f32[768,768]{0,1:T(8,128)}, f32[768,768]{0,1:T(8,128)S(1)}, u32[]{:S(2)}) copy-start(f32[768,768]{0,1:T(8,128)S(1)} %convert_element_type.239) | copy-start | bytes 7077892
  475.3 3.9 copy-start.9
  475.3 5.9 %copy-start.14 = (bf16[768,768]{0,1:T(8,128)(2,1)S(1)}, bf16[768,768]{0,1:T(8,128)(2,1)}, u32[]{:S(2)}) copy-start(bf16[768,768]{0,1:T(8,128)(2,1)} %get-tuple-element.136) | copy-start | bytes 3538948
  479.2 20.3 %collective-permute-start.5 = (bf16[384,768]{0,1:T(8,128)(2,1)}, bf16[384,768]{0,1:T(8,128)(2,1)}, u32[]{:S(2)}, u32[]{:S(2)}) collective-permute-start(bf16[384,768]{0,1:T(8,128)(2,1)} %get-tuple-element.127), channel_id=1, source_target_pairs={{0,16},{8,24},{16,0},{24,8},{1,17},{9,25},{17,1},{25,9},{2,18},{10... | collective-permute-start | bytes 1769480 | tf_op jit(solution)/shard_map/ppermute | solution.py:293
  480.7 18.8 %collective-permute-start.7 = (bf16[384,768]{0,1:T(8,128)(2,1)}, bf16[384,768]{0,1:T(8,128)(2,1)}, u32[]{:S(2)}, u32[]{:S(2)}) collective-permute-start(bf16[384,768]{0,1:T(8,128)(2,1)} %get-tuple-element.128), channel_id=1, source_target_pairs={{0,8},{8,0},{16,24},{24,16},{1,9},{9,1},{17,25},{25,17},{2,10},{10... | collective-permute-start | bytes 1769480 | tf_op jit(solution)/shard_map/ppermute | solution.py:293
  488.3 10.0 %all-to-all-start.4 = ((f32[4,24,576]{2,1,0:T(8,128)}), f32[4,24,576]{2,1,0:T(8,128)S(1)}, u32[]{:S(2)}, u32[]{:S(2)}) async-start(f32[4,24,576]{2,1,0:T(8,128)} %bitcast.23), calls=%async_computation.4 | async-start | bytes 491520 | tf_op jit(solution)/shard_map/all_to_all | solution.py:511
  (9 other events, 8.9 us)
Sparse Core Ops, SparseCore 0:
  17.9 113.2 all-gather.3
  304.9 150.7 reduce-scatter.1

commit v3 on v2

v3 whole, which is shorter than its diff:
```python
import jax
import jax.numpy as jnp
from jax import lax
from jax.experimental import pallas as pl
from jax.experimental.pallas import tpu as pltpu
from jax.sharding import PartitionSpec as P

HEADS = 12
HEAD = 64
IDS = 32
far = 1e30
FQ, FK = 512, 512
BQ, BK = 512, 256
ROWS = 256
f32 = jnp.float32
bf16 = jnp.bfloat16
norm_eps = 1e-06


def padded_width(width):
    return -(-(width + IDS) // 128) * 128


def spans(seg_row, block):
    seq = seg_row.shape[0]
    count = seq // block
    first = seg_row[::block]
    last = seg_row[block - 1 :: block]
    lo = jnp.sum((seg_row[None, :] < first[:, None]).astype(jnp.int32), 1)
    hi = jnp.sum((seg_row[None, :] <= last[:, None]).astype(jnp.int32), 1)
    return lo, hi


def windows(seg_row, block, step, grain):
    lo, hi = spans(seg_row, block)
    seq = seg_row.shape[0]
    start = lo // grain * grain
    number = -(-(hi - start) // step)
    start = jnp.minimum(start, seq - number * step)
    return start.astype(jnp.int32), number.astype(jnp.int32)


def lanes_of(head, shape):
    lane = lax.broadcasted_iota(jnp.int32, shape, len(shape) - 1)
    return (lane >= head * HEAD) & (lane < (head + 1) * HEAD)


def mm(a, b):
    return jnp.dot(a, b, preferred_element_type=f32)


def mm_nt(a, b):
    return lax.dot_general(a, b, (((1,), (1,)), ((), ())), preferred_element_type=f32)


def forward_kernel(heads, start_ref, number_ref, q_ref, k_ref, v_ref, o_ref, lse_ref, kh, vt, scores, acc):
    step = pl.program_id(0)
    seq, wide = k_ref.shape
    width = heads * HEAD
    tall = HEAD + 16

    @pl.when(step == 0)
    def _():
        row = lax.broadcasted_iota(jnp.int32, (16, FK), 0)
        ones = jnp.where(row == 0, 1.0, 0.0).astype(bf16)

        def part(i, carry):
            rows = pl.ds(pl.multiple_of(i * FK, FK), FK)
            k = k_ref[rows, :]
            lane = lax.broadcasted_iota(jnp.int32, k.shape, 1)
            turned = v_ref[rows, :].T
            for h in range(heads):
                keep = lanes_of(h, k.shape) | (lane >= width)
                kept = jnp.where(keep, k, jnp.zeros_like(k))
                for c in range(FK // 128):
                    at = pl.multiple_of(i * (FK * heads) + (c * heads + h) * 128, 128)
                    kh[pl.ds(at, 128), :] = kept[c * 128 : (c + 1) * 128]
                vt[h * tall : h * tall + HEAD, rows] = turned[h * HEAD : (h + 1) * HEAD]
                vt[h * tall + HEAD : (h + 1) * tall, rows] = ones
            return carry

        lax.fori_loop(0, seq // FK, part, 0)

    q = q_ref[...]
    start = start_ref[step]
    number = number_ref[step]

    def score(j, tops):
        at = pl.multiple_of((start + j * FK) * heads, 128)
        every = mm_nt(kh[pl.ds(at, FK * heads), :], q)
        news = list(tops)
        for c in range(FK // 128):
            for h in range(heads):
                s = every[(c * heads + h) * 128 : (c * heads + h + 1) * 128]
                scores[h, pl.ds(pl.multiple_of(j * FK + c * 128, 128), 128), :] = s
                news[h] = jnp.maximum(news[h], jnp.max(s.reshape(16, 8, FQ), 0))
        return tuple(news)

    tops = lax.fori_loop(0, number, score, (jnp.full((8, FQ), -jnp.inf, f32),) * heads)
    tops = [jnp.max(top, 0, keepdims=True) for top in tops]
    acc[...] = jnp.zeros_like(acc)

    def mix(j, carry):
        rows = pl.ds(pl.multiple_of(start + j * FK, 128), FK)
        out = pl.ds(pl.multiple_of(j * FK, FK), FK)
        for h in range(heads):
            p = jnp.exp(scores[h, out, :] - tops[h]).astype(bf16)
            acc[h] += mm(vt[h * tall : (h + 1) * tall, rows], p)
        return carry

    lax.fori_loop(0, number, mix, 0)
    outs = []
    for h in range(heads):
        total = acc[h, HEAD : HEAD + 1, :]
        outs.append(acc[h, :HEAD, :] / total)
        lse_ref[h : h + 1, :] = tops[h] + jnp.log(total)
    o_ref[...] = jnp.concatenate(outs, 0).T.astype(bf16)


def attend_forward(q, k, v, starts, numbers, heads):
    seq, wide = q.shape
    width = heads * HEAD
    steps = seq // FQ
    cost = pl.CostEstimate(
        flops=2 * heads * seq * seq * HEAD, bytes_accessed=8 * seq * wide, transcendentals=heads * seq * seq // 3
    )
    return pl.pallas_call(
        lambda *refs: forward_kernel(heads, *refs),
        grid_spec=pltpu.PrefetchScalarGridSpec(
            num_scalar_prefetch=2,
            grid=(steps,),
            in_specs=[
                pl.BlockSpec((FQ, wide), lambda i, a, b: (i, 0)),
                pl.BlockSpec((seq, wide), lambda i, a, b: (0, 0)),
                pl.BlockSpec((seq, width), lambda i, a, b: (0, 0)),
            ],
            out_specs=[
                pl.BlockSpec((FQ, width), lambda i, a, b: (i, 0)),
                pl.BlockSpec((8, FQ), lambda i, a, b: (0, i)),
            ],
            scratch_shapes=[
                pltpu.VMEM((heads * seq, wide), bf16),
                pltpu.VMEM((heads * (HEAD + 16), seq), bf16),
                pltpu.VMEM((heads, seq, FQ), f32),
                pltpu.VMEM((heads, HEAD + 16, FQ), f32),
            ],
        ),
        out_shape=[
            jax.ShapeDtypeStruct((seq, width), bf16),
            jax.ShapeDtypeStruct((8, seq), f32),
        ],
        cost_estimate=cost,
        compiler_params=pltpu.CompilerParams(vmem_limit_bytes=48 << 20),
        name="attend_forward",
    )(starts, numbers, q, k, v)


def backward_kernel(
    heads, start_ref, number_ref, q_ref, k_ref, v_ref, g_ref, o_ref, lse_ref,
    dq_ref, dk_ref, dv_ref, gq, qt, gt, dqt, delta, dkt, dvt, kh, vh,
):
    step = pl.program_id(0)
    seq, wide = q_ref.shape
    width = heads * HEAD

    @pl.when(step == 0)
    def _():
        def part(i, carry):
            rows = pl.ds(pl.multiple_of(i * 256, 256), 256)
            g = g_ref[rows, :]
            gq[rows, :] = jnp.concatenate([g, jnp.zeros((256, wide - width), bf16)], 1)
            qt[:, rows] = q_ref[rows, :].T[:width]
            gt[:, rows] = g.T
            product = g.astype(f32) * o_ref[rows, :].astype(f32)
            lane = lax.broadcasted_iota(jnp.int32, (8, width), 1)
            row = lax.broadcasted_iota(jnp.int32, (8, width), 0)
            pick = ((lane >= row * HEAD) & (lane < (row + 1) * HEAD)).astype(f32)
            delta[:, rows] = lax.dot_general(
                pick, product, (((1,), (1,)), ((), ())),
                preferred_element_type=f32, precision=lax.Precision.HIGHEST,
            )
            dqt[:, rows] = jnp.zeros((width, 256), f32)
            return carry

        lax.fori_loop(0, seq // 256, part, 0)

    start = start_ref[step]
    k = k_ref[...]
    v = v_ref[...]
    lane = lax.broadcasted_iota(jnp.int32, k.shape, 1)
    vz = jnp.concatenate([v, jnp.zeros((BK, wide - width), bf16)], 1)
    for h in range(heads):
        part = slice(h * BK, (h + 1) * BK)
        keep = lanes_of(h, k.shape)
        kh[part, :] = jnp.where(keep | (lane >= width), k, jnp.zeros_like(k))
        vh[part, :] = jnp.where(keep, vz, jnp.zeros_like(vz))
    kt = k.T
    dkt[...] = jnp.zeros_like(dkt)
    dvt[...] = jnp.zeros_like(dvt)

    def one(i, carry):
        rows = pl.ds(pl.multiple_of(start + i * BQ, 128), BQ)
        q = q_ref[rows, :]
        g = gq[rows, :]
        ss = mm_nt(kh[...], q)
        dps = mm_nt(vh[...], g)
        for h in range(heads):
            mine = slice(h * HEAD, (h + 1) * HEAD)
            part = slice(h * BK, (h + 1) * BK)
            p = jnp.exp(ss[part] - lse_ref[h : h + 1, rows])
            dp = dps[part]
            ds = (p * (dp - delta[h : h + 1, rows])).astype(bf16)
            dvt[mine, :] += mm_nt(gt[mine, rows], p.astype(bf16))
            dkt[mine, :] += mm_nt(qt[mine, rows], ds)
            dqt[mine, rows] += mm(kt[mine, :], ds)
        return carry

    lax.fori_loop(0, number_ref[step], one, 0)
    dk_ref[...] = dkt[...].T.astype(bf16)
    dv_ref[...] = dvt[...].T.astype(bf16)

    @pl.when(step == pl.num_programs(0) - 1)
    def _():
        def part(i, carry):
            rows = pl.ds(pl.multiple_of(i * 256, 256), 256)
            dq_ref[rows, :] = (dqt[:, rows] * 0.125).T.astype(bf16)
            return carry

        lax.fori_loop(0, seq // 256, part, 0)


def attend_backward(q, k, v, g, o, lse, starts, numbers, heads):
    seq, wide = q.shape
    width = heads * HEAD
    steps = seq // BK
    whole = lambda shape: pl.BlockSpec(shape, lambda i, a, b: (0, 0))
    cost = pl.CostEstimate(
        flops=5 * heads * seq * seq * HEAD, bytes_accessed=16 * seq * wide, transcendentals=heads * seq * seq // 3
    )
    return pl.pallas_call(
        lambda *refs: backward_kernel(heads, *refs),
        grid_spec=pltpu.PrefetchScalarGridSpec(
            num_scalar_prefetch=2,
            grid=(steps,),
            in_specs=[
                whole((seq, wide)),
                pl.BlockSpec((BK, wide), lambda i, a, b: (i, 0)),
                pl.BlockSpec((BK, width), lambda i, a, b: (i, 0)),
                whole((seq, width)),
                whole((seq, width)),
                whole((8, seq)),
            ],
            out_specs=[
                whole((seq, width)),
                pl.BlockSpec((BK, width), lambda i, a, b: (i, 0)),
                pl.BlockSpec((BK, width), lambda i, a, b: (i, 0)),
            ],
            scratch_shapes=[
                pltpu.VMEM((seq, wide), bf16),
                pltpu.VMEM((width, seq), bf16),
                pltpu.VMEM((width, seq), bf16),
                pltpu.VMEM((width, seq), f32),
                pltpu.VMEM((8, seq), f32),
                pltpu.VMEM((width, BK), f32),
                pltpu.VMEM((width, BK), f32),
                pltpu.VMEM((heads * BK, wide), bf16),
                pltpu.VMEM((heads * BK, wide), bf16),
            ],
        ),
        out_shape=[jax.ShapeDtypeStruct((seq, width), bf16)] * 3,
        cost_estimate=cost,
        compiler_params=pltpu.CompilerParams(vmem_limit_bytes=56 << 20),
        name="attend_backward",
    )(starts, numbers, q, k, v, g, o, lse)


def pack_kernel(ratio, down_ref, up_ref, out_ref, *refs):
    vectors, (packed_ref, rows_ref) = refs[:-2], refs[-2:]
    own, model = out_ref.shape
    at = ratio * own
    packed_ref[:at] = down_ref[...]
    for c in range(ratio):
        packed_ref[at + c * own : at + (c + 1) * own] = up_ref[:, c * model : (c + 1) * model]
    packed_ref[2 * at : 2 * at + own] = out_ref[...]
    rows_ref[...] = jnp.zeros_like(rows_ref)
    for j, vector in enumerate(vectors):
        rows_ref[j : j + 1, : vector.shape[1]] = vector[...].astype(f32)
    packed_ref[2 * at + own :] = rows_ref[...].astype(bf16)


def pack_weights(w_down, w_up, w_out, vectors):
    own, model = w_out.shape
    ratio = w_down.shape[0] // own
    if own % 8 == 0:
        return pl.pallas_call(
            lambda *refs: pack_kernel(ratio, *refs),
            out_shape=jax.ShapeDtypeStruct((own * (2 * ratio + 1) + 8, model), bf16),
            scratch_shapes=[pltpu.VMEM((8, model), f32)],
            name="pack_weights",
        )(w_down, w_up, w_out, *[item[None] for item in vectors])
    up_blocks = [w_up[:, c * model : (c + 1) * model] for c in range(ratio)]
    rows = [jnp.pad(item, (0, model - item.shape[0]))[None] for item in vectors]
    rows.append(jnp.zeros((8 - len(rows), model), bf16))
    return jnp.concatenate([w_down] + up_blocks + [w_out] + rows, 0)


def spread_kernel(groups, width, w_ref, q_ref, v_ref, out_ref, rows_ref):
    own = w_ref.shape[0]
    model = groups * width
    rows_ref[...] = jnp.zeros_like(rows_ref)
    rows_ref[0:1, :own] = q_ref[...].astype(f32)
    rows_ref[1:2, :own] = v_ref[...].astype(f32)
    biases = rows_ref[...].astype(bf16)
    for g in range(groups):
        parts = [w_ref[:, c * model + g * width : c * model + (g + 1) * width] for c in range(3)]
        block = jnp.concatenate(parts, 1)
        for i in range(out_ref.shape[1]):
            out_ref[g, i, :own, :] = block
            out_ref[g, i, own:, :] = biases


def spread_qkv(w_qkv, b_query, b_value, groups, shards):
    own = w_qkv.shape[0]
    width = w_qkv.shape[1] // (3 * groups)
    shape = (groups, shards, own + 8, 3 * width)
    if own % 8 == 0:
        return pl.pallas_call(
            lambda *refs: spread_kernel(groups, width, *refs),
            out_shape=jax.ShapeDtypeStruct(shape, bf16),
            scratch_shapes=[pltpu.VMEM((8, 3 * width), f32)],
            name="spread_qkv",
        )(w_qkv, b_query[None], b_value[None])
    block = w_qkv.reshape(own, 3, groups, width).transpose(2, 0, 1, 3).reshape(groups, own, 3 * width)
    rows = jnp.pad(jnp.stack([b_query, b_value]), ((0, 6), (0, 3 * width - own)))
    block = jnp.concatenate([block, jnp.broadcast_to(rows, (groups, 8, 3 * width))], 1)
    return jnp.broadcast_to(block[:, None], shape)


def project_kernel(
    heads, me_ref, x0_ref, x1_ref, x2_ref, upper_ref, lower_ref, seg_ref, w_ref, bias_ref,
    q_ref, k_ref, v_ref, all_ref, wide_w,
):
    step = pl.program_id(0)
    rows = x0_ref.shape[0]
    half = rows // 2
    width = heads * HEAD
    wide = q_ref.shape[1]
    slot = lax.bitwise_xor(step, me_ref[0])

    @pl.when(step == 0)
    def _():
        whole = w_ref[...].reshape(x0_ref.shape[1], 3 * width)
        for c in range(3):
            wide_w[c] = whole[:, c * width : (c + 1) * width]

    for k, part in ((0, x0_ref), (1, x1_ref), (2, x2_ref)):

        @pl.when(slot == k)
        def _():
            all_ref[...] = part[...]

    @pl.when(slot == 3)
    def _():
        all_ref[:half] = upper_ref[...]
        all_ref[half:] = lower_ref[...]

    size = 256

    def part(i, carry):
        at = pl.ds(pl.multiple_of(i * size, size), size)
        x = all_ref[at, :]
        lane = lax.broadcasted_iota(jnp.int32, (size, wide - width), 1)
        same = lane == seg_ref[at, :]
        q = (mm(x, wide_w[0]) + bias_ref[0:1, :width]).astype(bf16)
        q_ref[at, :width] = q * jnp.asarray(0.125, bf16)
        q_ref[at, width:] = jnp.where(same, 1.0, 0.0).astype(bf16)
        k_ref[at, :width] = mm(x, wide_w[1]).astype(bf16)
        k_ref[at, width:] = jnp.where(same, 0.0, -far).astype(bf16)
        v_ref[at, :] = (mm(x, wide_w[2]) + bias_ref[1:2, :width]).astype(bf16)
        return carry

    lax.fori_loop(0, rows // size, part, 0)


def project(blocks, seg_row, weights, biases, heads):
    own_rows, model = blocks[0].shape
    width = heads * HEAD
    wide = padded_width(width)
    seq = 4 * own_rows
    pieces = weights.shape[0]
    once = dict(pipeline_mode=pl.Buffered(1))
    fixed = lambda a: pl.BlockSpec(a, lambda s, m: (0,) * len(a), **once)
    cost = pl.CostEstimate(
        flops=6 * seq * model * width, bytes_accessed=4 * seq * (model + wide), transcendentals=0
    )
    return pl.pallas_call(
        lambda *refs: project_kernel(heads, *refs),
        grid_spec=pltpu.PrefetchScalarGridSpec(
            num_scalar_prefetch=1,
            grid=(4,),
            in_specs=[
                fixed((own_rows, model)),
                fixed((own_rows, model)),
                fixed((own_rows, model)),
                fixed((own_rows // 2, model)),
                fixed((own_rows // 2, model)),
                pl.BlockSpec((own_rows, 1), lambda s, m: (s, 0)),
                fixed((pieces, model // pieces, 3 * width)),
                fixed((8, width)),
            ],
            out_specs=[
                pl.BlockSpec((own_rows, wide), lambda s, m: (s, 0)),
                pl.BlockSpec((own_rows, wide), lambda s, m: (s, 0)),
                pl.BlockSpec((own_rows, width), lambda s, m: (s, 0)),
                pl.BlockSpec((own_rows, model), lambda s, m: (s, 0)),
            ],
            scratch_shapes=[pltpu.VMEM((3, model, width), bf16)],
        ),
        out_shape=[
            jax.ShapeDtypeStruct((seq, wide), bf16),
            jax.ShapeDtypeStruct((seq, wide), bf16),
            jax.ShapeDtypeStruct((seq, width), bf16),
            jax.ShapeDtypeStruct((seq, model), bf16),
        ],
        cost_estimate=cost,
        compiler_params=pltpu.CompilerParams(vmem_limit_bytes=40 << 20),
        name="project",
    )(lax.axis_index("sp").reshape(1).astype(jnp.int32), *blocks, seg_row[:, None], weights, biases)


def normal_rows(z):
    center = jnp.mean(z, -1, keepdims=True)
    moved = z - center
    rstd = lax.rsqrt(jnp.mean(moved * moved, -1, keepdims=True) + norm_eps)
    return moved * rstd, rstd


def norm_pull(s, hat, rstd):
    inner = jnp.mean(s * hat, -1, keepdims=True)
    return rstd * (s - jnp.mean(s, -1, keepdims=True) - hat * inner)


def gelu_both(x):
    z = jnp.abs(x) * 0.7071067811865476
    t = 1.0 / (1.0 + 0.3275911 * z)
    e = jnp.exp(-(z * z))
    poly = t * (
        0.127414796 + t * (-0.142248368 + t * (0.7107068705 + t * (-0.7265760135 + t * 0.5307027145)))
    )
    tail = poly * e
    cdf = jnp.where(x >= 0.0, 1.0 - tail, tail)
    return x * cdf, cdf + x * (e * 0.3989422804014327)


def spread_vectors(chunks, small_ref, vec_ref):
    pieces, _, model = small_ref.shape

    def spread(block, size):
        count = block.shape[0]
        lane = lax.broadcasted_iota(jnp.int32, (128, model), 1)
        row = lax.broadcasted_iota(jnp.int32, (128, model), 0)
        tile = jnp.where(lax.rem(lane, size) == row, 1.0, 0.0).astype(bf16)
        wide = mm(block, tile)
        lane = lax.broadcasted_iota(jnp.int32, (count, model), 1)
        row = lax.broadcasted_iota(jnp.int32, (count, model), 0)
        keep = lane // size == row
        return jnp.sum(jnp.where(keep, wide, 0.0), 0, keepdims=True)

    vec_ref[...] = jnp.zeros_like(vec_ref)
    for j in range(6):
        vec_ref[j : j + 1, :] = spread(small_ref[:, j, :128], model // pieces)
    share = pieces // chunks
    for c in range(chunks):
        block = small_ref[c * share : (c + 1) * share, 6, :128]
        vec_ref[8 + c : 9 + c, :] = spread(block, model // share)


def gather_vectors(chunks, vec_ref, wide_ref, small_ref):
    pieces, _, model = small_ref.shape
    wide_ref[...] = jnp.zeros_like(wide_ref)

    def gather(vector, size, count):
        lane = lax.broadcasted_iota(jnp.int32, (128, model), 1)
        row = lax.broadcasted_iota(jnp.int32, (128, model), 0)
        tile = jnp.where(lax.rem(lane, size) == row, 1.0, 0.0).astype(bf16)
        lane = lax.broadcasted_iota(jnp.int32, (count, model), 1)
        row = lax.broadcasted_iota(jnp.int32, (count, model), 0)
        kept = jnp.where(lane // size == row, vector, 0.0).astype(bf16)
        return mm_nt(kept, tile)

    for j in range(6):
        wide_ref[:, j, :128] = gather(vec_ref[j : j + 1, :], model // pieces, pieces)
    share = pieces // chunks
    for c in range(chunks):
        block = gather(vec_ref[8 + c : 9 + c, :], model // share, share)
        wide_ref[c * share : (c + 1) * share, 6, :128] = block
    small_ref[...] = wide_ref[...].astype(bf16)


def middle_kernel(
    groups, chunks, x_ref, cot_ref, mixed_ref, out_w_ref, up_ref, down_ref, small_ref,
    y_ref, gh1_ref, gmix_ref, sent_ref,
    first_low, first_t, hat1, rstd1, activ_t, slope, total, gffn, gpre, vec_ref,
    gvec_ref, gdown, gup, gout, gwide, gsmall, down_sem, up_sem, out_sem, small_sem,
):
    step = pl.program_id(0)
    rows, model = x_ref.shape
    parts = rows // ROWS
    width = mixed_ref.shape[2]

    def out_w(g):
        share = out_w_ref.shape[0] // groups
        return out_w_ref[g * share : (g + 1) * share].reshape(width, model)

    def up_w():
        return up_ref[...].reshape(model, model)

    def down_w():
        return down_ref[...].reshape(model, model)

    pieces, own = out_w_ref.shape[:2]
    share = pieces // groups

    def down_copy(slot, chunk):
        return pltpu.make_async_copy(
            gdown.at[slot], sent_ref.at[:, chunk, : chunks * own, :], down_sem.at[slot]
        )

    def up_copies(slot, chunk):
        at = pl.multiple_of((chunks + chunk) * own, 8)
        return [
            pltpu.make_async_copy(
                gup.at[slot, g * share : (g + 1) * share],
                sent_ref.at[:, g, pl.ds(at, own), :],
                up_sem.at[slot, g],
            )
            for g in range(groups)
        ]

    def out_copies():
        at = 2 * chunks * own
        return [
            pltpu.make_async_copy(
                gout.at[g * share : (g + 1) * share], sent_ref.at[:, g, at : at + own, :], out_sem.at[g]
            )
            for g in range(groups)
        ]

    def small_copies():
        at = 2 * chunks * own + own
        return [
            pltpu.make_async_copy(
                gsmall.at[g * share : (g + 1) * share], sent_ref.at[:, g, at : at + 8, :], small_sem.at[g]
            )
            for g in range(groups)
        ]

    def vec(i):
        return vec_ref[i : i + 1, :]

    def sums(value):
        return jnp.sum(value, 0, keepdims=True)

    @pl.when(step == 0)
    def _():
        gvec_ref[...] = jnp.zeros_like(gvec_ref)
        spread_vectors(chunks, small_ref, vec_ref)

        def part(i, carry):
            at = pl.ds(pl.multiple_of(i * ROWS, ROWS), ROWS)
            branch = vec(0)
            for g in range(groups):
                branch = branch + mm(mixed_ref[g, at, :], out_w(g))
            hat, rstd = normal_rows(x_ref[at, :].astype(f32) + branch)
            value = hat * vec(1) + vec(2)
            hat1[at, :] = hat
            rstd1[at, :] = jnp.broadcast_to(rstd, (ROWS, 128))
            low = value.astype(bf16)
            first_low[at, :] = low
            first_t[:, at] = low.T
            total[at, :] = value + vec(3)
            return carry

        lax.fori_loop(0, parts, part, 0)

    @pl.when(step < chunks)
    def _():
        def part(i, carry):
            at = pl.ds(pl.multiple_of(i * ROWS, ROWS), ROWS)
            pre = mm(first_low[at, :], up_w()) + vec_ref[pl.ds(8 + step, 1), :]
            value, pull = gelu_both(pre)
            low = value.astype(bf16)
            slope[step, at, :] = pull
            activ_t[step, :, at] = low.T
            total[at, :] += mm(low, down_w())
            return carry

        lax.fori_loop(0, parts, part, 0)

    @pl.when(step == chunks - 1)
    def _():
        def part(i, carry):
            at = pl.ds(pl.multiple_of(i * ROWS, ROWS), ROWS)
            hat, rstd = normal_rows(total[at, :])
            y_ref[at, :] = (hat * vec(4) + vec(5)).astype(bf16)
            g = cot_ref[at, :].astype(f32)
            gh2 = norm_pull(g * vec(4), hat, rstd)
            total[at, :] = gh2
            low = gh2.astype(bf16)
            gffn[at, :] = low
            gvec_ref[3:4, :] += sums(low.astype(f32))
            gvec_ref[4:5, :] += sums(g * hat)
            gvec_ref[5:6, :] += sums(g)
            return carry

        lax.fori_loop(0, parts, part, 0)

    @pl.when(step >= chunks)
    def _():
        chunk = 2 * chunks - 1 - step
        slot = lax.rem(step, 2)

        @pl.when(step >= chunks + 2)
        def _():
            down_copy(slot, chunk).wait()
            for copy in up_copies(slot, chunk):
                copy.wait()

        def part(i, carry):
            at = pl.ds(pl.multiple_of(i * ROWS, ROWS), ROWS)
            low = (mm_nt(gffn[at, :], down_w()) * slope[chunk, at, :]).astype(bf16)
            gpre[at, :] = low
            gvec_ref[pl.ds(8 + chunk, 1), :] += sums(low.astype(f32))
            total[at, :] += mm_nt(low, up_w())
            return carry

        lax.fori_loop(0, parts, part, 0)
        tall = 4 * chunks * own

        def weights_down(i, carry):
            at = pl.ds(pl.multiple_of(i * tall, tall), tall)
            value = mm(activ_t[chunk, at, :], gffn[...]).astype(bf16)
            gdown[slot, pl.ds(i * 4, 4)] = value.reshape(4, chunks * own, model)
            return carry

        lax.fori_loop(0, model // tall, weights_down, 0)
        down_copy(slot, chunk).start()
        high = 16 * own

        def weights_up(i, carry):
            at = pl.ds(pl.multiple_of(i * high, high), high)
            value = mm(first_t[at, :], gpre[...]).astype(bf16)
            gup[slot, pl.ds(i * 16, 16)] = value.reshape(16, own, model)
            return carry

        lax.fori_loop(0, model // high, weights_up, 0)
        for copy in up_copies(slot, chunk):
            copy.start()

    @pl.when(step == 2 * chunks - 1)
    def _():
        def part(i, carry):
            at = pl.ds(pl.multiple_of(i * ROWS, ROWS), ROWS)
            g = total[at, :]
            hat = hat1[at, :]
            gh1 = norm_pull(g * vec(1), hat, rstd1[at, :1])
            gh1_ref[at, :] = gh1
            low = gh1.astype(bf16)
            gpre[at, :] = low
            gvec_ref[0:1, :] += sums(low.astype(f32))
            gvec_ref[1:2, :] += sums(g * hat)
            gvec_ref[2:3, :] += sums(g)
            for k in range(groups):
                gmix_ref[k, at, :] = mm_nt(low, out_w(k)).astype(bf16)
            return carry

        lax.fori_loop(0, parts, part, 0)
        for k in range(groups):
            value = lax.dot_general(
                mixed_ref[k], gpre[...], (((0,), (0,)), ((), ())), preferred_element_type=f32
            ).astype(bf16)
            gout[k * share : (k + 1) * share] = value.reshape(share, own, model)
        for copy in out_copies():
            copy.start()
        gather_vectors(chunks, gvec_ref, gwide, gsmall)
        for copy in small_copies():
            copy.start()
        for back in range(2):
            down_copy(back, 0).wait()
            for copy in up_copies(back, 0):
                copy.wait()
        for copy in out_copies() + small_copies():
            copy.wait()


def middle(x, cot, mixed, packed):
    rows, model = x.shape
    groups, _, width = mixed.shape
    pieces = packed.shape[0]
    own = model // pieces
    chunks = (packed.shape[1] - 8 - own) // (2 * own)
    last = 2 * chunks - 1
    back = lambda s: jnp.minimum(s, last - s)
    assert chunks == groups and pieces % (8 * groups) == 0
    once = dict(pipeline_mode=pl.Buffered(1))
    fixed2 = lambda a: pl.BlockSpec(a, lambda s: (0, 0), **once)
    fixed3 = lambda a: pl.BlockSpec(a, lambda s: (0, 0, 0), **once)
    vectors_at = own * (2 * chunks + 1) // 8
    cost = pl.CostEstimate(
        flops=2 * rows * model * model * (3 + 6 * chunks),
        bytes_accessed=2 * model * model * (4 * chunks + 8),
        transcendentals=rows * model * chunks,
    )
    return pl.pallas_call(
        lambda *refs: middle_kernel(groups, chunks, *refs),
        grid=(2 * chunks,),
        in_specs=[
            fixed2((rows, model)),
            fixed2((rows, model)),
            fixed3((groups, rows, width)),
            pl.BlockSpec((pieces, own, model), lambda s: (0, 2 * chunks, 0), **once),
            pl.BlockSpec((pieces, own, model), lambda s: (0, chunks + back(s), 0)),
            pl.BlockSpec((pieces // chunks, chunks * own, model), lambda s: (back(s), 0, 0)),
            pl.BlockSpec((pieces, 8, model), lambda s: (0, vectors_at, 0), **once),
        ],
        out_specs=[
            fixed2((rows, model)),
            fixed2((rows, model)),
            fixed3((groups, rows, width)),
            pl.BlockSpec(memory_space=pl.ANY),
        ],
        out_shape=[
            jax.ShapeDtypeStruct((rows, model), bf16),
            jax.ShapeDtypeStruct((rows, model), f32),
            jax.ShapeDtypeStruct((groups, rows, width), bf16),
            jax.ShapeDtypeStruct((pieces // groups, groups, packed.shape[1], model), bf16),
        ],
        scratch_shapes=[
            pltpu.VMEM((rows, model), bf16),
            pltpu.VMEM((model, rows), bf16),
            pltpu.VMEM((rows, model), f32),
            pltpu.VMEM((rows, 128), f32),
            pltpu.VMEM((chunks, model, rows), bf16),
            pltpu.VMEM((chunks, rows, model), f32),
            pltpu.VMEM((rows, model), f32),
            pltpu.VMEM((rows, model), bf16),
            pltpu.VMEM((rows, model), bf16),
            pltpu.VMEM((16, model), f32),
            pltpu.VMEM((16, model), f32),
            pltpu.VMEM((2, pieces // chunks, chunks * own, model), bf16),
            pltpu.VMEM((2, pieces, own, model), bf16),
            pltpu.VMEM((pieces, own, model), bf16),
            pltpu.VMEM((pieces, 8, model), f32),
            pltpu.VMEM((pieces, 8, model), bf16),
            pltpu.SemaphoreType.DMA((2,)),
            pltpu.SemaphoreType.DMA((2, groups)),
            pltpu.SemaphoreType.DMA((groups,)),
            pltpu.SemaphoreType.DMA((groups,)),
        ],
        cost_estimate=cost,
        compiler_params=pltpu.CompilerParams(vmem_limit_bytes=60 << 20),
        name="middle",
    )(x, cot, mixed, packed, packed, packed, packed)


def by_sp(value, flip):
    groups = lax.axis_size("sp")
    return lax.ppermute(value, "sp", [(i, i ^ flip) for i in range(groups)])


def gather_tokens(tokens):
    half = tokens.shape[0] // 2
    along_x = by_sp(tokens, 1)
    along_y = by_sp(tokens, 2)
    upper = by_sp(along_y[:half], 1)
    lower = by_sp(along_x[half:], 2)
    return tokens, along_x, along_y, upper, lower


def scatter_rows(partial):
    rows = partial.shape[0] // 4
    half = rows // 2
    me = lax.axis_index("sp")

    def piece(flip, lower):
        at = (me ^ flip) * rows + (half if lower else 0)
        return lax.dynamic_slice(partial, (at, 0), (half, partial.shape[1]))

    sent_x = jnp.concatenate([piece(1, False), piece(3, False)], 0).astype(bf16)
    sent_y = jnp.concatenate([piece(2, True), piece(3, True)], 0).astype(bf16)
    got_x = by_sp(sent_x, 1).astype(f32)
    got_y = by_sp(sent_y, 2).astype(f32)
    next_y = by_sp((piece(2, False) + got_x[half:]).astype(bf16), 2).astype(f32)
    next_x = by_sp((piece(1, True) + got_y[half:]).astype(bf16), 1).astype(f32)
    upper = piece(0, False) + got_x[:half] + next_y
    lower = piece(0, True) + got_y[:half] + next_x
    return jnp.concatenate([upper, lower], 0)


def unpack(packed, ratio):
    pieces, _, model = packed.shape
    own = model // pieces
    at = ratio * own
    down = packed[:, :at].reshape(ratio * model, model)
    up = packed[:, at : 2 * at].reshape(pieces, ratio, own, model).transpose(1, 0, 2, 3)
    out = packed[:, 2 * at : 2 * at + own].reshape(model, model)
    vectors = [packed[:, 2 * at + own + j, :own].reshape(-1) for j in range(6)]
    vectors.append(packed[:, 2 * at + own + 6, :at].reshape(-1))
    return down, up.reshape(ratio, model, model), out, vectors


def repack(packed, ratio, pieces):
    if packed.shape[0] == pieces:
        return packed
    down, up, out, vectors = unpack(packed, ratio)
    model = out.shape[0]
    own = model // pieces
    up = up.reshape(ratio, pieces, own, model).transpose(1, 0, 2, 3)
    rows = [jnp.pad(v.reshape(pieces, -1), ((0, 0), (0, model - v.shape[0] // pieces))) for v in vectors]
    rows.append(jnp.zeros_like(rows[0]))
    return jnp.concatenate(
        [
            down.reshape(pieces, ratio * own, model),
            up.reshape(pieces, ratio * own, model),
            out.reshape(pieces, own, model),
            jnp.stack(rows, 1),
        ],
        1,
    )


def body(
    tokens,
    segments,
    cotangent,
    w_qkv,
    b_query,
    b_value,
    w_out,
    b_out,
    ln1_gain,
    ln1_bias,
    w_up,
    b_up,
    w_down,
    b_down,
    ln2_gain,
    ln2_bias,
):
    both = ("sp", "fsdp")
    groups = lax.axis_size("sp")
    shards = lax.axis_size("fsdp")
    devices = groups * shards
    rows, model = tokens.shape
    hidden = w_up.shape[1]
    ratio = hidden // model
    own = w_qkv.shape[0]
    pieces = devices if own % 8 == 0 else 8 * groups
    heads_local = HEADS // groups
    width = heads_local * HEAD
    seq_len = rows * groups
    seg_row = segments[0]

    blocks = gather_tokens(tokens)
    pack = pack_weights(
        w_down, w_up, w_out, [b_out, ln1_gain, ln1_bias, b_down, ln2_gain, ln2_bias, b_up]
    )
    packed_weights = repack(lax.all_gather(pack, both, axis=0, tiled=False), ratio, pieces)

    by_device = spread_qkv(w_qkv, b_query, b_value, groups, shards)
    arrived = lax.all_to_all(
        by_device.reshape(devices, own + 8, 3 * width), both, split_axis=0, concat_axis=0, tiled=True
    )
    bias_rows = lax.dynamic_slice(
        arrived, (lax.axis_index("sp") * shards, own, 0), (shards, 2, own)
    )
    bias_rows = bias_rows.transpose(1, 0, 2).reshape(2, width).astype(f32)
    bias_rows = jnp.pad(bias_rows, ((0, 6), (0, 0)))
    weights = arrived if own % 8 == 0 else arrived[:, :own].reshape(pieces, model // pieces, 3 * width)
    queries, keys, values, tokens_all = project(blocks, seg_row, weights, bias_rows, heads_local)
    forward_start, forward_number = windows(seg_row, FQ, FK, 128)
    backward_start, backward_number = windows(seg_row, BK, BQ, 128)
    attended, logsum = attend_forward(
        queries, keys, values, forward_start, forward_number, heads_local
    )
    mixed = lax.all_to_all(
        attended.reshape(groups, rows, width), "sp", split_axis=0, concat_axis=0, tiled=True
    )
    output, grad_h1, grad_mixed, sent = middle(tokens, cotangent, mixed, packed_weights)

    lines = sent.shape[2]
    if pieces != devices:
        sent = sent.transpose(1, 0, 2, 3).reshape(pieces, lines, model)
        sent = repack(sent, ratio, devices)
        lines = sent.shape[1]
        sent = sent.reshape(groups, shards, lines, model).transpose(1, 0, 2, 3)
    reduced = lax.psum_scatter(
        sent.reshape(devices * lines, model), "fsdp", scatter_dimension=0, tiled=True
    )
    reduced = lax.all_to_all(
        reduced.reshape(groups, lines, model), "sp", split_axis=0, concat_axis=0, tiled=True
    )
    reduced = jnp.sum(reduced.astype(f32), 0)

    grad_heads = lax.all_to_all(grad_mixed, "sp", split_axis=0, concat_axis=0, tiled=True)
    grad_query, grad_keys, grad_values = attend_backward(
        queries,
        keys,
        values,
        grad_heads.reshape(seq_len, width),
        attended,
        logsum,
        backward_start,
        backward_number,
        heads_local,
    )
    grad_packed = jnp.concatenate([grad_query, grad_keys, grad_values], 1)
    weights_qkv = arrived[:, :own].reshape(model, 3 * width)
    extra = 8
    partial_in = jnp.einsum("tc,dc->td", grad_packed, weights_qkv, preferred_element_type=f32)
    grad_input = grad_h1 + scatter_rows(partial_in)

    grad_qkv = jnp.einsum("td,tc->dc", tokens_all, grad_packed, preferred_element_type=f32)
    ones = jnp.ones((8, seq_len), bf16)
    bias_sums = jnp.dot(ones, grad_packed, preferred_element_type=f32)[0].reshape(3, shards, own)
    bias_sums = jnp.concatenate([bias_sums[0], bias_sums[2]], 1).astype(bf16)
    bias_sums = jnp.pad(bias_sums[:, None], ((0, 0), (0, extra - 1), (0, 3 * width - 2 * own)))
    bias_sums = jnp.broadcast_to(bias_sums[None], (groups, shards, extra, 3 * width))
    by_owner = jnp.concatenate(
        [
            grad_qkv.astype(bf16).reshape(devices, own, 3 * width),
            bias_sums.reshape(devices, extra, 3 * width),
        ],
        1,
    )
    by_owner = lax.all_to_all(by_owner, both, split_axis=0, concat_axis=0, tiled=True)
    by_owner = by_owner.reshape(groups, shards, own + extra, 3 * width).astype(f32)
    by_owner = jnp.sum(by_owner, 1)
    owned_qkv = by_owner[:, :own].reshape(groups, own, 3, width).transpose(1, 2, 0, 3)
    owned_qkv = owned_qkv.reshape(own, 3 * model)
    bias_sums = lax.dynamic_slice(
        by_owner, (lax.axis_index("sp"), own, 0), (1, 1, 3 * width)
    ).reshape(-1)
    grad_query_bias = bias_sums[:own]
    grad_value_bias = bias_sums[own : 2 * own]

    at = ratio * own
    owned_up = reduced[at : 2 * at].reshape(ratio, own, model).transpose(1, 0, 2).reshape(own, hidden)
    tail = reduced[2 * at + own :]
    return (
        output,
        grad_input,
        owned_qkv,
        grad_query_bias,
        grad_value_bias,
        reduced[2 * at : 2 * at + own],
        tail[0, :own],
        tail[1, :own],
        tail[2, :own],
        owned_up,
        tail[6, :at],
        reduced[:at],
        tail[3, :own],
        tail[4, :own],
        tail[5, :own],
    )


def solution(mesh):
    in_specs = (
        P(("fsdp", "sp"), None),
        P("fsdp", None),
        P(("fsdp", "sp"), None),
        P(("sp", "fsdp"), None),
        P(("sp", "fsdp")),
        P(("sp", "fsdp")),
        P(("sp", "fsdp"), None),
        P(("sp", "fsdp")),
        P(("sp", "fsdp")),
        P(("sp", "fsdp")),
        P(("sp", "fsdp"), None),
        P(("sp", "fsdp")),
        P(("sp", "fsdp"), None),
        P(("sp", "fsdp")),
        P(("sp", "fsdp")),
        P(("sp", "fsdp")),
    )
    out_specs = (
        P(("fsdp", "sp"), None),
        P(("fsdp", "sp"), None),
        P(("sp", "fsdp"), None),
        P(("sp", "fsdp")),
        P(("sp", "fsdp")),
        P(("sp", "fsdp"), None),
        P(("sp", "fsdp")),
        P(("sp", "fsdp")),
        P(("sp", "fsdp")),
        P(("sp", "fsdp"), None),
        P(("sp", "fsdp")),
        P(("sp", "fsdp"), None),
        P(("sp", "fsdp")),
        P(("sp", "fsdp")),
        P(("sp", "fsdp")),
    )
    return jax.shard_map(body, mesh=mesh, in_specs=in_specs, out_specs=out_specs, check_vma=False)
```

time: 525 us -> 413 us (0.79); the launches traced: 520 us -> 414 us
  matrix products: 104 us -> 11.7 us
  local copies, waits for them, and re-layouts: 102 us -> 36 us
  waiting for transfers between devices: 65.3 us -> 129 us
  Pallas kernels: 104 us -> 149 us
  starting transfers between devices: 63.9 us -> 38.1 us
  other arithmetic: 42.9 us -> 17.2 us
    dot_general x10 -> x0, matrix products: 87.8 us -> none  [the longest x1 30.4 us: body(): pre = jnp.dot(first_low, full_up, preferred_element_type=f32) + bias_up]
    ppermute x8, waiting for transfers between devices: 32.1 us -> 107 us  [by_sp(): return lax.ppermute(value, 'sp', [(i, i ^ flip) for i in range(groups)])]
    pallas_call x0 -> x4, Pallas kernels: none -> 68 us  [the longest x1 55.5 us: middle(): pl.pallas_call(lambda *refs: middle_kernel(groups, chunks, *refs), grid=(...]
    all_to_all x6 -> x4, starting transfers between devices: 53.4 us -> 25.3 us  [the longest x1 9.92 us: body(): lax.all_to_all(by_owner, both, split_axis=0, concat_axis=0, tiled=True)]
    convert_element_type x13 -> x4, local copies, waits for them, and re-layouts: 27.2 us -> 1.64 us  [the longest x1 1.54 us: body(): grad_qkv.astype(bf16).reshape(devices, own, 3 * width)]
    all_gather x1 -> x0, blocking collectives: 23.1 us -> none  [body(): all_f = lax.all_gather(sent, 'fsdp', axis=0, tiled=False)]
    all_to_all x0 -> x1, blocking collectives: none -> 19.2 us  [body(): lax.all_to_all(attended.reshape(groups, rows, width), 'sp', split_axis=0,...]
    pallas_call x1, Pallas kernels: 70.3 us -> 51.6 us  [attend_backward(): pl.pallas_call(lambda *refs: backward_kernel(heads, *refs), grid_spec=plt...]
  transfers between devices with their start and end apart: 16 -> 14, of which waited for: 8 -> 10; matrix products, arithmetic and copies ran while one was open for 19% -> 11% of each run, Pallas kernels for 20% -> 22%
where the time goes in v3:
time: 413 us; the launch traced here: 414 us
  Pallas kernels  149 us (36%)
  waiting for transfers between devices  129 us (31%)
  starting transfers between devices  38.1 us (9%)
  local copies, waits for them, and re-layouts  36 us (9%)
  blocking collectives  19.2 us (5%)
  other arithmetic  17.2 us (4%)
  between operations  14.4 us (3%)
  matrix products  11.7 us (3%)
    ppermute x8, waiting for transfers between devices, by_sp(): return lax.ppermute(value, 'sp', [(i, i ^ flip) for i in range(groups)])  107 us
    pallas_call x1, Pallas kernels, middle(): pl.pallas_call(lambda *refs: middle_kernel(groups, chunks, *refs), grid=(...  55.5 us
    pallas_call x1, Pallas kernels, attend_backward(): pl.pallas_call(lambda *refs: backward_kernel(heads, *refs), grid_spec=plt...  51.6 us
    pallas_call x1, Pallas kernels, attend_forward(): pl.pallas_call(lambda *refs: forward_kernel(heads, *refs), grid_spec=pltp...  29.5 us
    all_to_all x1, blocking collectives, body(): lax.all_to_all(attended.reshape(groups, rows, width), 'sp', split_axis=0,...  19.2 us
    unnamed x49, local copies, waits for them, and re-layouts  13.4 us
    ppermute x8, starting transfers between devices, by_sp(): return lax.ppermute(value, 'sp', [(i, i ^ flip) for i in range(groups)])  12.7 us
    all_to_all x1, waiting for transfers between devices, body(): lax.all_to_all(grad_mixed, 'sp', split_axis=0, concat_axis=0, tiled=True)  11.8 us
  transfers between devices with their start and end apart: 14, of which 10 were waited for; matrix products, arithmetic and copies ran while one was open for 11% of the time, Pallas kernels for 22%

profile of v3, /device:TPU:0, one launch (start us, length us, event | category | flops | bytes accessed | tf_op | source)
XLA Modules:
  0.0 414.4 jit_solution(980985167145775128)
XLA Ops:
  7.2 1.8 pack_weights.1
  9.1 2.1 spread_qkv.1
  11.2 7.3 %all-to-all-start = ((bf16[32,32,576]{2,1,0:T(8,128)(2,1)}), bf16[32,32,576]{2,1,0:T(8,128)(2,1)S(1)}, u32[]{:S(2)}, u32[]{:S(2)}) async-start(bf16[32,32,576]{2,1,0:T(8,128)(2,1)} %bitcast.55), calls=%async_computation | async-start | bytes 2621440 | tf_op jit(solution)/shard_map/all_to_all | solution.py:871
  18.5 1.8 collective-permute-start.1
  20.4 1.5 collective-permute-start
  21.8 46.2 %collective-permute-done.1.refs_3_ = bf16[768,768]{1,0:T(8,128)(2,1)S(1)} collective-permute-done((bf16[768,768]{1,0:T(8,128)(2,1)S(1)}, bf16[768,768]{1,0:T(8,128)(2,1)S(1)}, u32[]{:S(2)}, u32[]{:S(2)}) %collective-permute-start.1) | collective-permute-done | bytes 1179680 | tf_op jit(solution)/shard_map/ppermute | solution.py:768
  68.0 0.9 slice.127
  68.9 1.0 copy-done.2
  69.9 1.5 collective-permute-start.2
  71.8 0.9 slice.128
  72.6 1.0 copy-done.4
  73.7 1.5 collective-permute-start.3
  76.3 9.3 %collective-permute-done.2.refs_4_ = bf16[384,768]{1,0:T(8,128)(2,1)S(1)} collective-permute-done((bf16[384,768]{1,0:T(8,128)(2,1)}, bf16[384,768]{1,0:T(8,128)(2,1)S(1)}, u32[]{:S(2)}, u32[]{:S(2)}) %collective-permute-start.2) | collective-permute-done | bytes 589856 | tf_op jit(solution)/shard_map/ppermute | solution.py:768
  85.6 3.1 collective-permute-done.3.refs_5_
  88.6 1.3 copy-done.3
  89.9 1.3 copy-done.5
  91.2 1.3 copy-done.7
  92.5 8.6 %project.1 = (bf16[3072,256]{1,0:T(8,128)(2,1)S(1)}, bf16[3072,256]{1,0:T(8,128)(2,1)S(1)}, bf16[3072,192]{1,0:T(8,128)(2,1)S(1)}, bf16[3072,768]{1,0:T(8,128)(2,1)}) custom-call(s32[1]{0:T(128)} %bitcast.1.refs_0_, bf16[768,768]{1,0:T(8,128)(2,1)S(1)} %copy-done.7, bf16[768,768]{1,0:T(8,128)(2,1)S(1)} %copy-done.5, bf16[768,768]{1,0:T(8,128)(2,1)S(1)} %copy-done.3, ...), custom_call_target="tpu_custom_call" | custom-call | flops 2717908992 | bytes 12582912 | tf_op jit(solution)/shard_map/project/pallas_call | solution.py:396
  101.0 1.1 copy-done.10
  102.2 29.5 %attend_forward.1 = (bf16[3072,192]{1,0:T(8,128)(2,1)S(1)}, f32[8,3072]{1,0:T(8,128)S(1)}) custom-call(s32[6]{0:T(128)S(1)} %get-tuple-element.49.refs_0_, s32[6]{0:T(128)S(1)} %get-tuple-element.50.refs_1_, bf16[3072,256]{1,0:T(8,128)(2,1)S(1)} %get-tuple-element.28.refs_2_, bf16[3072,256]{1,0:T(8,128)(2,1)S(1)} %get-tuple-element.29.refs_3_, ...), custom_call_target="tpu_custom_call" | custom-call | flops 3623878656 | bytes 6291456 | tf_op jit(solution)/shard_map/attend_forward/pallas_call | solution.py:127
  132.4 1.5 copy.58
  133.9 19.2 %all_to_all.25 = bf16[4,768,192]{1,2,0:T(8,128)(2,1)} all-to-all(bf16[4,768,192]{1,2,0:T(8,128)(2,1)} %copy.58), channel_id=1, replica_groups=mesh['sp'=4,'fsdp'=8] {'sp'}, dimensions={0} | all-to-all | bytes 2359296 | tf_op jit(solution)/shard_map/all_to_all | solution.py:886
  153.1 2.5 copy.59.refs_2_
  155.6 55.5 %middle.1 = (bf16[768,768]{1,0:T(8,128)(2,1)}, f32[768,768]{1,0:T(8,128)}, bf16[4,768,192]{2,1,0:T(8,128)(2,1)}, bf16[8,4,224,768]{3,2,1,0:T(8,128)(2,1)}) custom-call(bf16[768,768]{1,0:T(8,128)(2,1)} %refs_0_.5, bf16[768,768]{1,0:T(8,128)(2,1)} %refs_1_.5, bf16[4,768,192]{2,1,0:T(8,128)(2,1)} %copy.59.refs_2_, bf16[32,224,768]{2,1,0:T(8,128)(2,1)} %bitcast.79, ...), custom_call_target="tpu_custom_call" | custom-call | flops 24461180928 | bytes 28311552 | tf_op jit(solution)/shard_map/middle/pallas_call | solution.py:714
  211.2 1.4 copy-done.16
  212.6 1.5 copy.60
  214.1 3.7 all-to-all-start.2
  218.8 11.8 %all-to-all-done.2 = bf16[4,768,192]{1,2,0:T(8,128)(2,1)S(1)} async-done(((bf16[4,768,192]{1,2,0:T(8,128)(2,1)}), bf16[4,768,192]{1,2,0:T(8,128)(2,1)S(1)}, u32[]{:S(2)}, u32[]{:S(2)}) %all-to-all-start.2) | async-done | bytes 1179680 | tf_op jit(solution)/shard_map/all_to_all | solution.py:905
  230.7 1.6 copy.61
  232.2 51.6 %attend_backward.1 = (bf16[3072,192]{1,0:T(8,128)(2,1)}, bf16[3072,192]{1,0:T(8,128)(2,1)}, bf16[3072,192]{1,0:T(8,128)(2,1)}) custom-call(s32[12]{0:T(128)} %get-tuple-element.47.refs_0_, s32[12]{0:T(128)} %get-tuple-element.48.refs_1_, bf16[3072,256]{1,0:T(8,128)(2,1)} %copy-done.8, bf16[3072,256]{1,0:T(8,128)(2,1)} %copy-done.9, ...), custom_call_target="tpu_custom_call" | custom-call | flops 9059696640 | bytes 12582912 | tf_op jit(solution)/shard_map/attend_backward/pallas_call | solution.py:240
  283.9 5.8 %fusion.12 = f32[3072,768]{1,0:T(8,128)S(1)} fusion(bf16[768,576]{1,0:T(8,128)(2,1)S(1)} %bitcast.52, bf16[3072,192]{1,0:T(8,128)(2,1)} %get-tuple-element.38, bf16[3072,192]{1,0:T(8,128)(2,1)} %get-tuple-element.37, bf16[3072,192]{1,0:T(8,128)(2,1)} %get-tuple-element.36), kind=kOutput, calls=%fused_computation.67 | convolution fusion | flops 2728525824 | bytes 13860864 | tf_op jit(solution)/shard_map/tc,dc->td/dot_general | solution.py:920
  290.0 1.1 pad_maximum_fusion.2
  291.1 1.4 collective-permute-start.4
  292.5 1.4 copy-done.21
  293.9 1.7 copy-done.19
  295.6 1.2 convolution_convert_fusion.1
  297.2 4.8 %convolution_convert_fusion = bf16[768,576]{0,1:T(8,128)(2,1)} fusion(bf16[3072,768]{1,0:T(8,128)(2,1)S(1)} %bitcast.84, bf16[3072,192]{1,0:T(8,128)(2,1)S(1)} %copy-done.21, bf16[3072,192]{1,0:T(8,128)(2,1)S(1)} %copy-done.20, bf16[3072,192]{1,0:T(8,128)(2,1)S(1)} %copy-done.19), kind=kOutput, calls=%fused_computation.4 | convolution fusion | flops 2728968192 | bytes 9142272 | tf_op jit(solution)/shard_map/td,tc->dc/dot_general | solution.py:923
  302.3 1.5 copy.62
  303.9 1.3 pad_maximum_fusion.1
  305.2 9.9 %all-to-all-start.3 = ((bf16[32,32,576]{2,1,0:T(8,128)(2,1)}), bf16[32,32,576]{2,1,0:T(8,128)(2,1)}, u32[]{:S(2)}, u32[]{:S(2)}) async-start(bf16[32,32,576]{2,1,0:T(8,128)(2,1)} %pad_maximum_fusion.1), calls=%async_computation.3 | async-start | bytes 2621440 | tf_op jit(solution)/shard_map/all_to_all | solution.py:936
  315.1 1.1 pad_maximum_fusion.3
  316.2 1.7 collective-permute-start.6
  317.9 2.0 collective-permute-done.4
  320.0 1.4 fusion.2
  321.4 1.9 collective-permute-start.5
  323.3 34.5 %collective-permute-done.6 = bf16[768,768]{1,0:T(8,128)(2,1)} collective-permute-done((bf16[768,768]{1,0:T(8,128)(2,1)}, bf16[768,768]{1,0:T(8,128)(2,1)}, u32[]{:S(2)}, u32[]{:S(2)}) %collective-permute-start.6) | collective-permute-done | bytes 1179680 | tf_op jit(solution)/shard_map/ppermute | solution.py:768
  357.8 1.4 convert_element_type.72
  359.2 10.7 %collective-permute-done.5 = bf16[384,768]{1,0:T(8,128)(2,1)} collective-permute-done((bf16[384,768]{1,0:T(8,128)(2,1)S(1)}, bf16[384,768]{1,0:T(8,128)(2,1)}, u32[]{:S(2)}, u32[]{:S(2)}) %collective-permute-start.5) | collective-permute-done | bytes 589856 | tf_op jit(solution)/shard_map/ppermute | solution.py:768
  369.9 2.9 fusion.3
  372.9 1.5 collective-permute-start.7
  374.3 4.3 %all-to-all-start.4 = ((bf16[4,224,768]{2,1,0:T(8,128)(2,1)}), bf16[4,224,768]{2,1,0:T(8,128)(2,1)}, u32[]{:S(2)}, u32[]{:S(2)}) async-start(bf16[4,224,768]{2,1,0:T(8,128)(2,1)} %bitcast.59), calls=%async_computation.5 | async-start | bytes 2752512 | tf_op jit(solution)/shard_map/all_to_all | solution.py:900
  378.7 1.7 convert_reduce_fusion.1
  380.4 0.7 copy-done.17
  381.1 0.7 slice.136
  381.8 1.9 reshape.127
  383.7 1.9 copy.64
  385.6 1.8 reshape.128
  387.4 1.3 fusion.5
  389.4 1.7 fusion.1
  391.1 1.7 maximum_add_fusion
  392.8 10.0 %all-to-all-done.4 = bf16[4,224,768]{2,1,0:T(8,128)(2,1)} async-done(((bf16[4,224,768]{2,1,0:T(8,128)(2,1)}), bf16[4,224,768]{2,1,0:T(8,128)(2,1)}, u32[]{:S(2)}, u32[]{:S(2)}) %all-to-all-start.4) | async-done | bytes 1376288 | tf_op jit(solution)/shard_map/all_to_all | solution.py:900
  402.8 1.6 convert_reduce_fusion
  406.1 0.8 fusion.15
  406.9 0.7 copy.67
  (76 shorter events, 6.8 us)
Async XLA Ops:
  7.2 148.4 %all-gather.3.cloned.1.call-start = ((), (), s32[]{:S(2)}) async-start(), calls=%async_computation.7 | async-start | bytes 11354112 | tf_op jit(solution)/shard_map/all_gather | solution.py:868
  11.2 7.4 %copy-start.6 = (bf16[768,768]{1,0:T(8,128)(2,1)S(1)}, bf16[768,768]{1,0:T(8,128)(2,1)}, u32[]{:S(2)}) copy-start(bf16[768,768]{1,0:T(8,128)(2,1)} %refs_0_.5) | copy-start | bytes 3538948
  11.2 65.0 %all-to-all-start = ((bf16[32,32,576]{2,1,0:T(8,128)(2,1)}), bf16[32,32,576]{2,1,0:T(8,128)(2,1)S(1)}, u32[]{:S(2)}, u32[]{:S(2)}) async-start(bf16[32,32,576]{2,1,0:T(8,128)(2,1)} %bitcast.55), calls=%async_computation | async-start | bytes 2621440 | tf_op jit(solution)/shard_map/all_to_all | solution.py:871
  18.5 56.7 %copy-start.18 = (s32[1,3072]{1,0:T(1,128)S(1)}, s32[1,3072]{1,0:T(1,128)}, u32[]{:S(2)}) copy-start(s32[1,3072]{1,0:T(1,128)} %param.17) | copy-start | bytes 36868
  18.5 355.9 %reduce-scatter.2.cloned.1.call-start = ((), (), s32[]{:S(2)}) async-start(), calls=%async_computation.6 | async-start | bytes 12386304 | tf_op jit(solution)/shard_map/reduce_scatter | solution.py:897
  18.5 49.5 %collective-permute-start.1 = (bf16[768,768]{1,0:T(8,128)(2,1)S(1)}, bf16[768,768]{1,0:T(8,128)(2,1)S(1)}, u32[]{:S(2)}, u32[]{:S(2)}) collective-permute-start(bf16[768,768]{1,0:T(8,128)(2,1)S(1)} %copy-done.6), channel_id=1, source_target_pairs={{0,16},{8,24},{16,0},{24,8},{1,17},{9,25},{17,1},{25,9},{2,18},{10... | collective-permute-start | bytes 3538952 | tf_op jit(solution)/shard_map/ppermute | solution.py:768
  20.4 51.4 %collective-permute-start = (bf16[768,768]{1,0:T(8,128)(2,1)S(1)}, bf16[768,768]{1,0:T(8,128)(2,1)S(1)}, u32[]{:S(2)}, u32[]{:S(2)}) collective-permute-start(bf16[768,768]{1,0:T(8,128)(2,1)S(1)} %copy-done.6), channel_id=1, source_target_pairs={{0,8},{8,0},{16,24},{24,16},{1,9},{9,1},{17,25},{25,17},{2,10},{10... | collective-permute-start | bytes 3538952 | tf_op jit(solution)/shard_map/ppermute | solution.py:768
  68.9 1.0 copy-start.2
  69.9 15.7 %collective-permute-start.2 = (bf16[384,768]{1,0:T(8,128)(2,1)}, bf16[384,768]{1,0:T(8,128)(2,1)S(1)}, u32[]{:S(2)}, u32[]{:S(2)}) collective-permute-start(bf16[384,768]{1,0:T(8,128)(2,1)} %slice.127), channel_id=1, source_target_pairs={{0,8},{8,0},{16,24},{24,16},{1,9},{9,1},{17,25},{25,17},{2,10},{10... | collective-permute-start | bytes 1769480 | tf_op jit(solution)/shard_map/ppermute | solution.py:768
  72.6 1.0 copy-start.4
  73.7 15.0 %collective-permute-start.3 = (bf16[384,768]{1,0:T(8,128)(2,1)}, bf16[384,768]{1,0:T(8,128)(2,1)}, u32[]{:S(2)}, u32[]{:S(2)}) collective-permute-start(bf16[384,768]{1,0:T(8,128)(2,1)} %slice.128), channel_id=1, source_target_pairs={{0,16},{8,24},{16,0},{24,8},{1,17},{9,25},{17,1},{25,9},{2,18},{10... | collective-permute-start | bytes 1769480 | tf_op jit(solution)/shard_map/ppermute | solution.py:768
  76.2 142.7 %copy-start = (bf16[32,32,576]{2,1,0:T(8,128)(2,1)}, bf16[32,32,576]{2,1,0:T(8,128)(2,1)S(1)}, u32[]{:S(2)}) copy-start(bf16[32,32,576]{2,1,0:T(8,128)(2,1)S(1)} %all-to-all-done.refs_7_) | copy-start | bytes 3538948
  88.6 1.3 copy-start.3
  89.9 1.3 copy-start.5
  91.2 1.3 copy-start.7
  101.0 1.1 copy-start.10
  102.2 29.5 %copy-start.8 = (bf16[3072,256]{1,0:T(8,128)(2,1)}, bf16[3072,256]{1,0:T(8,128)(2,1)S(1)}, u32[]{:S(2)}) copy-start(bf16[3072,256]{1,0:T(8,128)(2,1)S(1)} %get-tuple-element.28.refs_2_) | copy-start | bytes 4718596
  102.2 29.5 %copy-start.9 = (bf16[3072,256]{1,0:T(8,128)(2,1)}, bf16[3072,256]{1,0:T(8,128)(2,1)S(1)}, u32[]{:S(2)}) copy-start(bf16[3072,256]{1,0:T(8,128)(2,1)S(1)} %get-tuple-element.29.refs_3_) | copy-start | bytes 4718596
  131.7 0.6 copy-start.11
  132.4 20.7 %copy-start.1 = (bf16[3072,192]{1,0:T(8,128)(2,1)}, bf16[3072,192]{1,0:T(8,128)(2,1)S(1)}, u32[]{:S(2)}) copy-start(bf16[3072,192]{1,0:T(8,128)(2,1)S(1)} %get-tuple-element.31.refs_6_) | copy-start | bytes 3538948
  211.2 1.4 copy-start.16
  214.1 16.6 %all-to-all-start.2 = ((bf16[4,768,192]{1,2,0:T(8,128)(2,1)}), bf16[4,768,192]{1,2,0:T(8,128)(2,1)S(1)}, u32[]{:S(2)}, u32[]{:S(2)}) async-start(bf16[4,768,192]{1,2,0:T(8,128)(2,1)} %copy.60), calls=%async_computation.2 | async-start | bytes 2359296 | tf_op jit(solution)/shard_map/all_to_all | solution.py:905
  232.2 51.6 %slice-start = ((bf16[32,32,576]{2,1,0:T(8,128)(2,1)}), bf16[32,24,576]{2,1,0:T(8,128)(2,1)S(1)}, s32[]{:S(2)}) async-start(bf16[32,32,576]{2,1,0:T(8,128)(2,1)} %copy-done), calls=%async_computation.8 | async-start | bytes 1966080 | tf_op jit(solution)/shard_map/slice | solution.py:918
  289.6 7.1 %copy-start.14 = (f32[3072,768]{1,0:T(8,128)}, f32[3072,768]{1,0:T(8,128)S(1)}, u32[]{:S(2)}) copy-start(f32[3072,768]{1,0:T(8,128)S(1)} %fusion.12) | copy-start | bytes 28311556
  289.7 2.8 copy-start.20
  289.7 4.2 %copy-start.21 = (bf16[3072,192]{1,0:T(8,128)(2,1)S(1)}, bf16[3072,192]{1,0:T(8,128)(2,1)}, u32[]{:S(2)}) copy-start(bf16[3072,192]{1,0:T(8,128)(2,1)} %get-tuple-element.38) | copy-start | bytes 3538948
  289.9 5.6 %copy-start.19 = (bf16[3072,192]{1,0:T(8,128)(2,1)S(1)}, bf16[3072,192]{1,0:T(8,128)(2,1)}, u32[]{:S(2)}) copy-start(bf16[3072,192]{1,0:T(8,128)(2,1)} %get-tuple-element.36) | copy-start | bytes 3538948
  289.9 7.2 %slice-start.1 = ((s8[4718592]{0:T(1024)(128)(4,1)}), s8[4194304]{0:T(1024)(128)(4,1)S(1)}, s32[]{:S(2)}) async-start(s8[4718592]{0:T(1024)(128)(4,1)} %bitcast.83), calls=%async_computation.9 | async-start | bytes 8388608
  291.1 6.1 %slice-start.2 = ((s8[4718592]{0:T(1024)(128)(4,1)}), s8[524288]{0:T(1024)(128)(4,1)S(1)}, s32[]{:S(2)}) async-start(s8[4718592]{0:T(1024)(128)(4,1)} %bitcast.83), calls=%async_computation.10 | async-start | bytes 1048576
  291.1 28.8 %collective-permute-start.4 = (bf16[768,768]{1,0:T(8,128)(2,1)}, bf16[768,768]{1,0:T(8,128)(2,1)S(1)}, u32[]{:S(2)}, u32[]{:S(2)}) collective-permute-start(bf16[768,768]{1,0:T(8,128)(2,1)} %pad_maximum_fusion.2), channel_id=1, source_target_pairs={{0,8},{8,0},{16,24},{24,16},{1,9},{9,1},{17,25},{25,17},{2,10},{10... | collective-permute-start | bytes 3538952 | tf_op jit(solution)/shard_map/ppermute | solution.py:768
  305.2 69.2 %all-to-all-start.3 = ((bf16[32,32,576]{2,1,0:T(8,128)(2,1)}), bf16[32,32,576]{2,1,0:T(8,128)(2,1)}, u32[]{:S(2)}, u32[]{:S(2)}) async-start(bf16[32,32,576]{2,1,0:T(8,128)(2,1)} %pad_maximum_fusion.1), calls=%async_computation.3 | async-start | bytes 2621440 | tf_op jit(solution)/shard_map/all_to_all | solution.py:936
  316.2 41.6 %collective-permute-start.6 = (bf16[768,768]{1,0:T(8,128)(2,1)}, bf16[768,768]{1,0:T(8,128)(2,1)}, u32[]{:S(2)}, u32[]{:S(2)}) collective-permute-start(bf16[768,768]{1,0:T(8,128)(2,1)} %pad_maximum_fusion.3), channel_id=1, source_target_pairs={{0,16},{8,24},{16,0},{24,8},{1,17},{9,25},{17,1},{25,9},{2,18},{10... | collective-permute-start | bytes 3538952 | tf_op jit(solution)/shard_map/ppermute | solution.py:768
  321.4 48.5 %collective-permute-start.5 = (bf16[384,768]{1,0:T(8,128)(2,1)S(1)}, bf16[384,768]{1,0:T(8,128)(2,1)}, u32[]{:S(2)}, u32[]{:S(2)}) collective-permute-start(bf16[384,768]{1,0:T(8,128)(2,1)S(1)} %fusion.2), channel_id=1, source_target_pairs={{0,16},{8,24},{16,0},{24,8},{1,17},{9,25},{17,1},{25,9},{2,18},{10... | collective-permute-start | bytes 1769480 | tf_op jit(solution)/shard_map/ppermute | solution.py:768
  359.2 13.7 %copy-start.12 = (f32[768,768]{1,0:T(8,128)}, f32[768,768]{1,0:T(8,128)S(1)}, u32[]{:S(2)}) copy-start(f32[768,768]{1,0:T(8,128)S(1)} %convert_element_type.72) | copy-start | bytes 7077892
  372.9 16.6 %collective-permute-start.7 = (bf16[384,768]{1,0:T(8,128)(2,1)}, bf16[384,768]{1,0:T(8,128)(2,1)}, u32[]{:S(2)}, u32[]{:S(2)}) collective-permute-start(bf16[384,768]{1,0:T(8,128)(2,1)} %get-tuple-element.52), channel_id=1, source_target_pairs={{0,8},{8,0},{16,24},{24,16},{1,9},{9,1},{17,25},{25,17},{2,10},{10... | collective-permute-start | bytes 1769480 | tf_op jit(solution)/shard_map/ppermute | solution.py:768
  374.3 28.5 %all-to-all-start.4 = ((bf16[4,224,768]{2,1,0:T(8,128)(2,1)}), bf16[4,224,768]{2,1,0:T(8,128)(2,1)}, u32[]{:S(2)}, u32[]{:S(2)}) async-start(bf16[4,224,768]{2,1,0:T(8,128)(2,1)} %bitcast.59), calls=%async_computation.5 | async-start | bytes 2752512 | tf_op jit(solution)/shard_map/all_to_all | solution.py:900
  378.7 10.8 %copy-start.13 = (f32[768,768]{1,0:T(8,128)S(1)}, f32[768,768]{1,0:T(8,128)}, u32[]{:S(2)}) copy-start(f32[768,768]{1,0:T(8,128)} %copy-done.12) | copy-start | bytes 7077892
  380.4 0.7 copy-start.17
  388.7 2.4 copy-start.15
Sparse Core Ops, SparseCore 0:
  11.0 112.1 all-gather.2
  211.3 120.6 reduce-scatter.1

commit v4 on v3

v4 whole, which is shorter than its diff:
```python
import jax
import jax.numpy as jnp
from jax import lax
from jax.experimental import pallas as pl
from jax.experimental.pallas import tpu as pltpu
from jax.sharding import PartitionSpec as P

HEADS = 12
HEAD = 64
IDS = 32
far = 1e30
FQ, FK = 512, 512
BQ, BK = 512, 256
ROWS = 384
f32 = jnp.float32
bf16 = jnp.bfloat16
norm_eps = 1e-06


def padded_width(width):
    return -(-(width + IDS) // 128) * 128


def spans(seg_row, block):
    seq = seg_row.shape[0]
    count = seq // block
    first = seg_row[::block]
    last = seg_row[block - 1 :: block]
    lo = jnp.sum((seg_row[None, :] < first[:, None]).astype(jnp.int32), 1)
    hi = jnp.sum((seg_row[None, :] <= last[:, None]).astype(jnp.int32), 1)
    return lo, hi


def windows(seg_row, block, step, grain):
    lo, hi = spans(seg_row, block)
    seq = seg_row.shape[0]
    start = lo // grain * grain
    number = -(-(hi - start) // step)
    start = jnp.minimum(start, seq - number * step)
    return start.astype(jnp.int32), number.astype(jnp.int32)


def lanes_of(head, shape):
    lane = lax.broadcasted_iota(jnp.int32, shape, len(shape) - 1)
    return (lane >= head * HEAD) & (lane < (head + 1) * HEAD)


def mm(a, b):
    return jnp.dot(a, b, preferred_element_type=f32)


def mm_nt(a, b):
    return lax.dot_general(a, b, (((1,), (1,)), ((), ())), preferred_element_type=f32)


def mm_tn(a, b):
    return lax.dot_general(a, b, (((0,), (0,)), ((), ())), preferred_element_type=f32)


def forward_kernel(
    heads, start_ref, number_ref, me_ref, q_ref, k_ref, v_ref,
    o0_ref, o1_ref, o2_ref, o3_ref, lse_ref, kh, vt, scores, acc,
):
    step = pl.program_id(0)
    seq, wide = k_ref.shape
    width = heads * HEAD
    tall = HEAD + 16

    @pl.when(step == 0)
    def _():
        row = lax.broadcasted_iota(jnp.int32, (16, FK), 0)
        ones = jnp.where(row == 0, 1.0, 0.0).astype(bf16)

        def part(i, carry):
            rows = pl.ds(pl.multiple_of(i * FK, FK), FK)
            k = k_ref[rows, :]
            lane = lax.broadcasted_iota(jnp.int32, k.shape, 1)
            turned = v_ref[rows, :].T
            for h in range(heads):
                keep = lanes_of(h, k.shape) | (lane >= width)
                kept = jnp.where(keep, k, jnp.zeros_like(k))
                for c in range(FK // 128):
                    at = pl.multiple_of(i * (FK * heads) + (c * heads + h) * 128, 128)
                    kh[pl.ds(at, 128), :] = kept[c * 128 : (c + 1) * 128]
                vt[h * tall : h * tall + HEAD, rows] = turned[h * HEAD : (h + 1) * HEAD]
                vt[h * tall + HEAD : (h + 1) * tall, rows] = ones
            return carry

        lax.fori_loop(0, seq // FK, part, 0)

    q = q_ref[...]
    start = start_ref[step]
    number = number_ref[step]

    def score(j, tops):
        at = pl.multiple_of((start + j * FK) * heads, 128)
        every = mm_nt(kh[pl.ds(at, FK * heads), :], q)
        news = list(tops)
        for c in range(FK // 128):
            for h in range(heads):
                s = every[(c * heads + h) * 128 : (c * heads + h + 1) * 128]
                scores[h, pl.ds(pl.multiple_of(j * FK + c * 128, 128), 128), :] = s
                news[h] = jnp.maximum(news[h], jnp.max(s.reshape(16, 8, FQ), 0))
        return tuple(news)

    tops = lax.fori_loop(0, number, score, (jnp.full((8, FQ), -jnp.inf, f32),) * heads)
    tops = [jnp.max(top, 0, keepdims=True) for top in tops]
    acc[...] = jnp.zeros_like(acc)

    def mix(j, carry):
        rows = pl.ds(pl.multiple_of(start + j * FK, 128), FK)
        out = pl.ds(pl.multiple_of(j * FK, FK), FK)
        for h in range(heads):
            p = jnp.exp(scores[h, out, :] - tops[h]).astype(bf16)
            acc[h] += mm(vt[h * tall : (h + 1) * tall, rows], p)
        return carry

    lax.fori_loop(0, number, mix, 0)
    outs = []
    for h in range(heads):
        total = acc[h, HEAD : HEAD + 1, :]
        outs.append(acc[h, :HEAD, :] / total)
        lse_ref[h : h + 1, :] = tops[h] + jnp.log(total)
    mixed = jnp.concatenate(outs, 0).astype(bf16)
    per = o0_ref.shape[1] // 256
    for u in range(FQ // 256):
        block = step * (FQ // 256) + u
        at = pl.ds(pl.multiple_of(lax.rem(block, per) * 256, 256), 256)
        slot = lax.bitwise_xor(block // per, me_ref[0])
        for r, out_ref in enumerate((o0_ref, o1_ref, o2_ref, o3_ref)):

            @pl.when(slot == r)
            def _():
                out_ref[:, at] = mixed[:, u * 256 : (u + 1) * 256]


def attend_forward(q, k, v, starts, numbers, me, heads):
    seq, wide = q.shape
    width = heads * HEAD
    steps = seq // FQ
    cost = pl.CostEstimate(
        flops=2 * heads * seq * seq * HEAD, bytes_accessed=8 * seq * wide, transcendentals=heads * seq * seq // 3
    )
    return pl.pallas_call(
        lambda *refs: forward_kernel(heads, *refs),
        grid_spec=pltpu.PrefetchScalarGridSpec(
            num_scalar_prefetch=3,
            grid=(steps,),
            in_specs=[
                pl.BlockSpec((FQ, wide), lambda i, a, b, m: (i, 0)),
                pl.BlockSpec((seq, wide), lambda i, a, b, m: (0, 0)),
                pl.BlockSpec((seq, width), lambda i, a, b, m: (0, 0)),
            ],
            out_specs=[
                pl.BlockSpec((width, seq // 4), lambda i, a, b, m: (0, 0)),
                pl.BlockSpec((width, seq // 4), lambda i, a, b, m: (0, 0)),
                pl.BlockSpec((width, seq // 4), lambda i, a, b, m: (0, 0)),
                pl.BlockSpec((width, seq // 4), lambda i, a, b, m: (0, 0)),
                pl.BlockSpec((8, FQ), lambda i, a, b, m: (0, i)),
            ],
            scratch_shapes=[
                pltpu.VMEM((heads * seq, wide), bf16),
                pltpu.VMEM((heads * (HEAD + 16), seq), bf16),
                pltpu.VMEM((heads, seq, FQ), f32),
                pltpu.VMEM((heads, HEAD + 16, FQ), f32),
            ],
        ),
        out_shape=[
            jax.ShapeDtypeStruct((width, seq // 4), bf16),
            jax.ShapeDtypeStruct((width, seq // 4), bf16),
            jax.ShapeDtypeStruct((width, seq // 4), bf16),
            jax.ShapeDtypeStruct((width, seq // 4), bf16),
            jax.ShapeDtypeStruct((8, seq), f32),
        ],
        cost_estimate=cost,
        compiler_params=pltpu.CompilerParams(vmem_limit_bytes=48 << 20),
        name="attend_forward",
    )(starts, numbers, me, q, k, v)


def backward_kernel(
    heads, start_ref, number_ref, me_ref, q_ref, k_ref, v_ref,
    g0_ref, g1_ref, g2_ref, g3_ref, o0_ref, o1_ref, o2_ref, o3_ref, lse_ref, x_ref, w_ref, gh1_ref,
    sx_ref, sy_ref, mine_ref, low_ref, up_ref, kept_ref, sent_ref,
    qt, gt, dqt, delta, dkt, dvt, kh, vh, turned, grads, rows_ref,
):
    step = pl.program_id(0)
    seq, wide = q_ref.shape
    width = heads * HEAD
    own_rows = seq // 4
    per = own_rows // 256
    me = me_ref[0]

    @pl.when(step == 0)
    def _():
        def part(i, carry):
            rows = pl.ds(pl.multiple_of(i * 256, 256), 256)
            at = pl.ds(pl.multiple_of(lax.rem(i, per) * 256, 256), 256)
            slot = lax.bitwise_xor(i // per, me)
            qt[:, rows] = q_ref[rows, :].T[:width]
            dqt[:, rows] = jnp.zeros((width, 256), f32)
            pairs = ((g0_ref, o0_ref), (g1_ref, o1_ref), (g2_ref, o2_ref), (g3_ref, o3_ref))
            for r, (g_ref, o_ref) in enumerate(pairs):

                @pl.when(slot == r)
                def _():
                    g = g_ref[:, at]
                    gt[:, rows] = g
                    product = g.astype(f32) * o_ref[:, at].astype(f32)
                    for h in range(heads):
                        mine = slice(h * HEAD, (h + 1) * HEAD)
                        delta[h : h + 1, rows] = jnp.sum(product[mine], 0, keepdims=True)

            return carry

        lax.fori_loop(0, seq // 256, part, 0)

    start = start_ref[step]
    k = k_ref[...]
    v = v_ref[...]
    lane = lax.broadcasted_iota(jnp.int32, k.shape, 1)
    for h in range(heads):
        part = slice(h * BK, (h + 1) * BK)
        kh[part, :] = jnp.where(lanes_of(h, k.shape) | (lane >= width), k, jnp.zeros_like(k))
        vh[part, :] = jnp.where(lanes_of(h, v.shape), v, jnp.zeros_like(v))
    kt = k.T
    dkt[...] = jnp.zeros_like(dkt)
    dvt[...] = jnp.zeros_like(dvt)

    def one(i, carry):
        rows = pl.ds(pl.multiple_of(start + i * BQ, 128), BQ)
        q = q_ref[rows, :]
        ss = mm_nt(kh[...], q)
        dps = mm(vh[...], gt[:, rows])
        for h in range(heads):
            mine = slice(h * HEAD, (h + 1) * HEAD)
            part = slice(h * BK, (h + 1) * BK)
            p = jnp.exp(ss[part] - lse_ref[h : h + 1, rows])
            dp = dps[part]
            ds = (p * (dp - delta[h : h + 1, rows])).astype(bf16)
            dvt[mine, :] += mm_nt(gt[mine, rows], p.astype(bf16))
            dkt[mine, :] += mm_nt(qt[mine, rows], ds)
            dqt[mine, rows] += mm(kt[mine, :], ds)
        return carry

    lax.fori_loop(0, number_ref[step], one, 0)
    here = pl.ds(pl.multiple_of(step * BK, BK), BK)
    for c, total in ((1, dkt), (2, dvt)):
        low = total[...].astype(bf16)
        turned[c * width : (c + 1) * width, here] = low
        grads[c, here, :] = low.T

    @pl.when(step == pl.num_programs(0) - 1)
    def _():
        def part(i, carry):
            rows = pl.ds(pl.multiple_of(i * 256, 256), 256)
            low = (dqt[:, rows] * 0.125).astype(bf16)
            turned[:width, rows] = low
            grads[0, rows, :] = low.T
            return carry

        lax.fori_loop(0, seq // 256, part, 0)
        half = own_rows // 2

        def back(i, carry):
            def rows_of(lower):
                at = pl.ds(pl.multiple_of(i * own_rows + lower * half, 128), half)
                value = mm_nt(grads[0, at, :], w_ref[0])
                value = value + mm_nt(grads[1, at, :], w_ref[1])
                return value + mm_nt(grads[2, at, :], w_ref[2])

            slot = lax.bitwise_xor(i, me)
            for lower in range(2):
                value = rows_of(lower)
                here = slice(lower * half, (lower + 1) * half)

                @pl.when(slot == 0)
                def _():
                    mine_ref[here, :] = value + gh1_ref[here, :]

                @pl.when(slot == 1)
                def _():
                    if lower:
                        low_ref[...] = value
                    else:
                        sx_ref[:half] = value.astype(bf16)

                @pl.when(slot == 2)
                def _():
                    if lower:
                        sy_ref[:half] = value.astype(bf16)
                    else:
                        up_ref[...] = value

                @pl.when(slot == 3)
                def _():
                    if lower:
                        sy_ref[half:] = value.astype(bf16)
                    else:
                        sx_ref[half:] = value.astype(bf16)

            return carry

        lax.fori_loop(0, 4, back, 0)
        model = x_ref.shape[1]
        columns, _, own = kept_ref.shape[:3]
        shards = 2 * columns
        lane = lax.broadcasted_iota(jnp.int32, (128, width), 1)
        row = lax.broadcasted_iota(jnp.int32, (128, width), 0)
        tile = jnp.where(lax.rem(lane, own) == row, 1.0, 0.0).astype(bf16)
        lane = lax.broadcasted_iota(jnp.int32, (shards, width), 1)
        row = lax.broadcasted_iota(jnp.int32, (shards, width), 0)
        ones = jnp.ones((8, seq), bf16)
        rows_ref[...] = jnp.zeros_like(rows_ref)
        for j, c in enumerate((0, 2)):
            sums = mm(ones, grads[c])[:1]
            rows_ref[:, j, :] = mm_nt(jnp.where(lane // own == row, sums, 0.0).astype(bf16), tile)
        value = mm(turned[...], x_ref[...]).T.astype(bf16).reshape(4 * shards, own, 3 * width)
        for core in range(2):

            @pl.when(me_ref[3] == core)
            def _():
                for piece in range(4 * shards):
                    group, shard = piece // shards, piece % shards
                    target = kept_ref if shard % 2 == core else sent_ref
                    z = lax.bitwise_xor(me_ref[2], shard // 2)
                    r = lax.bitwise_xor(me_ref[1], group)
                    target[z, r, :, : 3 * width] = value[piece]
                    target[z, r, :, 3 * width :] = jnp.zeros((own, model - 3 * width), bf16)
                    target[z, r, :8, model - 128 :] = rows_ref[shard].astype(bf16)


def attend_backward(q, k, v, g, o, lse, starts, numbers, place, x, w, gh1, pieces, heads):
    seq, wide = q.shape
    width = heads * HEAD
    steps = seq // BK
    own_rows, model = gh1.shape
    own = model // pieces
    once = dict(pipeline_mode=pl.Buffered(1))
    whole = lambda a: pl.BlockSpec(a, lambda i, a_, b_, m_: (0,) * len(a), **once)
    cost = pl.CostEstimate(
        flops=5 * heads * seq * seq * HEAD + 12 * seq * model * width,
        bytes_accessed=16 * seq * wide,
        transcendentals=heads * seq * seq // 3,
    )
    return pl.pallas_call(
        lambda *refs: backward_kernel(heads, *refs),
        grid_spec=pltpu.PrefetchScalarGridSpec(
            num_scalar_prefetch=3,
            grid=(steps,),
            in_specs=[
                whole((seq, wide)),
                pl.BlockSpec((BK, wide), lambda i, a, b, m: (i, 0)),
                pl.BlockSpec((BK, width), lambda i, a, b, m: (i, 0)),
            ]
            + [whole((width, own_rows))] * 8
            + [whole((8, seq)), whole((seq, model)), whole((3, model, width)), whole((own_rows, model))],
            out_specs=[
                whole((own_rows, model)),
                whole((own_rows, model)),
                whole((own_rows, model)),
                whole((own_rows // 2, model)),
                whole((own_rows // 2, model)),
                whole((pieces // 8, 4, own, model)),
                whole((pieces // 8, 4, own, model)),
            ],
            scratch_shapes=[
                pltpu.VMEM((width, seq), bf16),
                pltpu.VMEM((width, seq), bf16),
                pltpu.VMEM((width, seq), f32),
                pltpu.VMEM((8, seq), f32),
                pltpu.VMEM((width, BK), f32),
                pltpu.VMEM((width, BK), f32),
                pltpu.VMEM((heads * BK, wide), bf16),
                pltpu.VMEM((heads * BK, width), bf16),
                pltpu.VMEM((3 * width, seq), bf16),
                pltpu.VMEM((3, seq, width), bf16),
                pltpu.VMEM((pieces // 4, 8, 128), f32),
            ],
        ),
        out_shape=[
            jax.ShapeDtypeStruct((own_rows, model), bf16),
            jax.ShapeDtypeStruct((own_rows, model), bf16),
            jax.ShapeDtypeStruct((own_rows, model), f32),
            jax.ShapeDtypeStruct((own_rows // 2, model), f32),
            jax.ShapeDtypeStruct((own_rows // 2, model), f32),
            jax.ShapeDtypeStruct((pieces // 8, 4, own, model), bf16),
            jax.ShapeDtypeStruct((pieces // 8, 4, own, model), bf16),
        ],
        cost_estimate=cost,
        compiler_params=pltpu.CompilerParams(vmem_limit_bytes=60 << 20),
        name="attend_backward",
    )(starts, numbers, place, q, k, v, *g, *o, lse, x, w, gh1)


def pack_kernel(ratio, groups, me_ref, down_ref, up_ref, out_ref, qkv_ref, *refs):
    vectors, (query_ref, value_ref, packed_ref, spread_ref, rows_ref) = refs[:-5], refs[-5:]
    own, model = out_ref.shape
    width = model // groups
    rows_ref[...] = jnp.zeros_like(rows_ref)
    rows_ref[0:1, :own] = query_ref[...].astype(f32)
    rows_ref[1:2, :own] = value_ref[...].astype(f32)
    biases = rows_ref[:, : 3 * width].astype(bf16)
    for g in range(groups):
        parts = [qkv_ref[:, c * model + g * width : c * model + (g + 1) * width] for c in range(3)]
        slot = lax.bitwise_xor(me_ref[0], g)
        spread_ref[slot, :own, :] = jnp.concatenate(parts, 1)
        spread_ref[slot, own:, :] = biases
    at = ratio * own
    packed_ref[:at] = down_ref[...]
    for c in range(ratio):
        packed_ref[at + c * own : at + (c + 1) * own] = up_ref[:, c * model : (c + 1) * model]
    packed_ref[2 * at : 2 * at + own] = out_ref[...]
    rows_ref[...] = jnp.zeros_like(rows_ref)
    for j, vector in enumerate(vectors):
        rows_ref[j : j + 1, : vector.shape[1]] = vector[...].astype(f32)
    packed_ref[2 * at + own :] = rows_ref[...].astype(bf16)


def pack(me, w_down, w_up, w_out, w_qkv, vectors, b_query, b_value, groups):
    own, model = w_out.shape
    ratio = w_down.shape[0] // own
    width = model // groups
    vmem = pl.BlockSpec(memory_space=pltpu.VMEM)
    return pl.pallas_call(
        lambda *refs: pack_kernel(ratio, groups, *refs),
        in_specs=[pl.BlockSpec(memory_space=pltpu.SMEM)] + [vmem] * (6 + len(vectors)),
        out_shape=[
            jax.ShapeDtypeStruct((own * (2 * ratio + 1) + 8, model), bf16),
            jax.ShapeDtypeStruct((groups, own + 8, 3 * width), bf16),
        ],
        scratch_shapes=[pltpu.VMEM((8, model), f32)],
        name="pack",
    )(me, w_down, w_up, w_out, w_qkv, *[item[None] for item in vectors], b_query[None], b_value[None])


def pack_plain(w_down, w_up, w_out, w_qkv, vectors, b_query, b_value, groups):
    own, model = w_out.shape
    ratio = w_down.shape[0] // own
    width = model // groups
    up_blocks = [w_up[:, c * model : (c + 1) * model] for c in range(ratio)]
    rows = [jnp.pad(item, (0, model - item.shape[0]))[None] for item in vectors]
    rows.append(jnp.zeros((8 - len(rows), model), bf16))
    packed = jnp.concatenate([w_down] + up_blocks + [w_out] + rows, 0)
    block = w_qkv.reshape(own, 3, groups, width).transpose(2, 0, 1, 3).reshape(groups, own, 3 * width)
    rows = jnp.pad(jnp.stack([b_query, b_value]), ((0, 6), (0, 3 * width - own)))
    return packed, jnp.concatenate([block, jnp.broadcast_to(rows, (groups, 8, 3 * width))], 1)


def project_kernel(
    heads, me_ref, x0_ref, x1u_ref, x1l_ref, x2u_ref, x2l_ref, x3u_ref, x3l_ref, seg_ref, near_ref, far_ref,
    q_ref, k_ref, v_ref, all_ref, wide_w, rows_ref, bias_ref,
):
    step = pl.program_id(0)
    rows = x0_ref.shape[0]
    half = rows // 2
    width = heads * HEAD
    wide = q_ref.shape[1]
    slot = lax.bitwise_xor(step, me_ref[0])

    own = near_ref.shape[2] - 8
    columns, groups = near_ref.shape[:2]

    @pl.when(step == 0)
    def _():
        for c, part_ref in ((0, near_ref), (1, far_ref)):
            for z in range(columns):
                shard = lax.bitwise_xor(me_ref[2], z) * 2 + lax.bitwise_xor(me_ref[3], c)
                for g in range(groups):
                    piece = lax.bitwise_xor(me_ref[1], g) * (2 * columns) + shard
                    at = pl.ds(pl.multiple_of(piece * own, 8), own)
                    for k in range(3):
                        wide_w[k, at, :] = part_ref[z, g, :own, k * width : (k + 1) * width]
                lines = part_ref[z, 0, own:, :128].astype(f32)
                for k in range(2):
                    rows_ref[k, pl.ds(shard, 1), :] = lines[k : k + 1]
        lane = lax.broadcasted_iota(jnp.int32, (128, width), 1)
        row = lax.broadcasted_iota(jnp.int32, (128, width), 0)
        tile = jnp.where(lax.rem(lane, own) == row, 1.0, 0.0).astype(bf16)
        lane = lax.broadcasted_iota(jnp.int32, (2 * columns, width), 1)
        row = lax.broadcasted_iota(jnp.int32, (2 * columns, width), 0)
        for k in range(2):
            value = jnp.where(lane // own == row, mm(rows_ref[k].astype(bf16), tile), 0.0)
            bias_ref[k : k + 1, :] = jnp.sum(value, 0, keepdims=True)

    @pl.when(slot == 0)
    def _():
        all_ref[...] = x0_ref[...]

    for k, upper, lower in ((1, x1u_ref, x1l_ref), (2, x2u_ref, x2l_ref), (3, x3u_ref, x3l_ref)):

        @pl.when(slot == k)
        def _():
            all_ref[:half] = upper[...]
            all_ref[half:] = lower[...]

    size = 256

    def part(i, carry):
        at = pl.ds(pl.multiple_of(i * size, size), size)
        x = all_ref[at, :]
        lane = lax.broadcasted_iota(jnp.int32, (size, wide - width), 1)
        same = lane == seg_ref[at, :]
        q = (mm(x, wide_w[0]) + bias_ref[0:1, :]).astype(bf16)
        q_ref[at, :width] = q * jnp.asarray(0.125, bf16)
        q_ref[at, width:] = jnp.where(same, 1.0, 0.0).astype(bf16)
        k_ref[at, :width] = mm(x, wide_w[1]).astype(bf16)
        k_ref[at, width:] = jnp.where(same, 0.0, -far).astype(bf16)
        v_ref[at, :] = (mm(x, wide_w[2]) + bias_ref[1:2, :]).astype(bf16)
        return carry

    lax.fori_loop(0, rows // size, part, 0)


def project(place, blocks, seg_row, near, away, heads):
    own_rows, model = blocks[0].shape
    width = heads * HEAD
    wide = padded_width(width)
    seq = 4 * own_rows
    once = dict(pipeline_mode=pl.Buffered(1))
    fixed = lambda a: pl.BlockSpec(a, lambda s, m: (0,) * len(a), **once)
    cost = pl.CostEstimate(
        flops=6 * seq * model * width, bytes_accessed=4 * seq * (model + wide), transcendentals=0
    )
    return pl.pallas_call(
        lambda *refs: project_kernel(heads, *refs),
        grid_spec=pltpu.PrefetchScalarGridSpec(
            num_scalar_prefetch=1,
            grid=(4,),
            in_specs=[
                fixed((own_rows, model)),
            ]
            + [fixed((own_rows // 2, model))] * 6
            + [
                pl.BlockSpec((own_rows, 1), lambda s, m: (s, 0)),
                fixed(near.shape),
                fixed(near.shape),
            ],
            out_specs=[
                pl.BlockSpec((own_rows, wide), lambda s, m: (s, 0)),
                pl.BlockSpec((own_rows, wide), lambda s, m: (s, 0)),
                pl.BlockSpec((own_rows, width), lambda s, m: (s, 0)),
                pl.BlockSpec((own_rows, model), lambda s, m: (s, 0)),
                fixed((3, model, width)),
            ],
            scratch_shapes=[
                pltpu.VMEM((2, 2 * near.shape[0], 128), f32),
                pltpu.VMEM((8, width), f32),
            ],
        ),
        out_shape=[
            jax.ShapeDtypeStruct((seq, wide), bf16),
            jax.ShapeDtypeStruct((seq, wide), bf16),
            jax.ShapeDtypeStruct((seq, width), bf16),
            jax.ShapeDtypeStruct((seq, model), bf16),
            jax.ShapeDtypeStruct((3, model, width), bf16),
        ],
        cost_estimate=cost,
        compiler_params=pltpu.CompilerParams(vmem_limit_bytes=40 << 20),
        name="project",
    )(place, *blocks, seg_row[:, None], near, away)


def normal_rows(z):
    center = jnp.mean(z, -1, keepdims=True)
    moved = z - center
    rstd = lax.rsqrt(jnp.mean(moved * moved, -1, keepdims=True) + norm_eps)
    return moved * rstd, rstd


def norm_pull(s, hat, rstd):
    inner = jnp.mean(s * hat, -1, keepdims=True)
    return rstd * (s - jnp.mean(s, -1, keepdims=True) - hat * inner)


def gelu_both(x):
    z = jnp.abs(x) * 0.7071067811865476
    t = 1.0 / (1.0 + 0.3275911 * z)
    e = jnp.exp(-(z * z))
    poly = t * (
        0.127414796 + t * (-0.142248368 + t * (0.7107068705 + t * (-0.7265760135 + t * 0.5307027145)))
    )
    tail = poly * e
    cdf = jnp.where(x >= 0.0, 1.0 - tail, tail)
    return x * cdf, cdf + x * (e * 0.3989422804014327)


def spread_vectors(chunks, small_ref, vec_ref):
    pieces, _, model = small_ref.shape

    def spread(block, size):
        count = block.shape[0]
        lane = lax.broadcasted_iota(jnp.int32, (128, model), 1)
        row = lax.broadcasted_iota(jnp.int32, (128, model), 0)
        tile = jnp.where(lax.rem(lane, size) == row, 1.0, 0.0).astype(bf16)
        wide = mm(block, tile)
        lane = lax.broadcasted_iota(jnp.int32, (count, model), 1)
        row = lax.broadcasted_iota(jnp.int32, (count, model), 0)
        keep = lane // size == row
        return jnp.sum(jnp.where(keep, wide, 0.0), 0, keepdims=True)

    vec_ref[...] = jnp.zeros_like(vec_ref)
    for j in range(6):
        vec_ref[j : j + 1, :] = spread(small_ref[:, j, :128], model // pieces)
    share = pieces // chunks
    for c in range(chunks):
        block = small_ref[c * share : (c + 1) * share, 6, :128]
        vec_ref[8 + c : 9 + c, :] = spread(block, model // share)


def gather_vectors(chunks, vec_ref, wide_ref):
    pieces, _, model = wide_ref.shape
    wide_ref[...] = jnp.zeros_like(wide_ref)

    def gather(vector, size, count):
        lane = lax.broadcasted_iota(jnp.int32, (128, model), 1)
        row = lax.broadcasted_iota(jnp.int32, (128, model), 0)
        tile = jnp.where(lax.rem(lane, size) == row, 1.0, 0.0).astype(bf16)
        lane = lax.broadcasted_iota(jnp.int32, (count, model), 1)
        row = lax.broadcasted_iota(jnp.int32, (count, model), 0)
        kept = jnp.where(lane // size == row, vector, 0.0).astype(bf16)
        return mm_nt(kept, tile)

    for j in range(6):
        wide_ref[:, j, :128] = gather(vec_ref[j : j + 1, :], model // pieces, pieces)
    share = pieces // chunks
    for c in range(chunks):
        block = gather(vec_ref[8 + c : 9 + c, :], model // share, share)
        wide_ref[c * share : (c + 1) * share, 6, :128] = block


def middle_kernel(
    groups, chunks, place_ref, x_ref, cot_ref, m0_ref, m1_ref, m2_ref, m3_ref, out_w_ref, up_ref, down_ref, small_ref,
    y_ref, gh1_ref, gm0_ref, gm1_ref, gm2_ref, gm3_ref, kept_ref, sent_ref,
    first_low, first_t, hat1, rstd1, activ_t, slope, total, gffn, gpre, vec_ref,
    gvec_ref, gdown, gup, gout, gwide, gsmall, down_sem, up_sem, out_sem, small_sem,
):
    step = pl.program_id(0)
    rows, model = x_ref.shape
    parts = rows // ROWS
    width = m0_ref.shape[0]
    mixed_refs = (m0_ref, m1_ref, m2_ref, m3_ref)
    gmix_refs = (gm0_ref, gm1_ref, gm2_ref, gm3_ref)

    def group(r):
        return lax.bitwise_xor(place_ref[1], r)

    def out_w(r):
        share = out_w_ref.shape[0] // groups
        return out_w_ref[pl.ds(group(r) * share, share)].reshape(width, model)

    def up_w():
        return up_ref[...].reshape(model, model)

    def down_w():
        return down_ref[...].reshape(model, model)

    pieces, own = out_w_ref.shape[:2]
    share = pieces // groups

    def pair(source, sem, *place):
        return [
            [
                pltpu.make_async_copy(source.at[p], target.at[place], sem.at[p])
                for target in (kept_ref, sent_ref)
            ]
            for p in range(2)
        ]

    def begin(copies):
        for p in range(2):

            @pl.when(place_ref[0] == p)
            def _():
                copies[p][0].start()
                copies[1 - p][1].start()

    def finish(copies):
        for p in range(2):
            copies[p][0].wait()

    def down_copies(slot, chunk):
        return pair(
            gdown.at[slot], down_sem.at[slot], chunk, slice(None), slice(0, chunks * own), slice(None)
        )

    def up_copies(slot, chunk):
        at = pl.ds(pl.multiple_of((chunks + chunk) * own, 8), own)
        return pair(gup.at[slot], up_sem.at[slot], slice(None), slice(None), at, slice(None))

    def out_copies():
        at = slice(2 * chunks * own, 2 * chunks * own + own)
        return pair(gout, out_sem, slice(None), slice(None), at, slice(None))

    def small_copies():
        at = slice(2 * chunks * own + own, 2 * chunks * own + own + 8)
        return pair(gsmall, small_sem, slice(None), slice(None), at, slice(None))

    def vec(i):
        return vec_ref[i : i + 1, :]

    def sums(value):
        return jnp.sum(value, 0, keepdims=True)

    @pl.when(step == 0)
    def _():
        gvec_ref[...] = jnp.zeros_like(gvec_ref)
        spread_vectors(chunks, small_ref, vec_ref)

        def part(i, carry):
            at = pl.ds(pl.multiple_of(i * ROWS, ROWS), ROWS)
            branch = vec(0)
            for r in range(groups):
                branch = branch + mm_tn(mixed_refs[r][:, at], out_w(r))
            hat, rstd = normal_rows(x_ref[at, :].astype(f32) + branch)
            value = hat * vec(1) + vec(2)
            hat1[at, :] = hat
            rstd1[at, :] = jnp.broadcast_to(rstd, (ROWS, 128))
            low = value.astype(bf16)
            first_low[at, :] = low
            first_t[:, at] = low.T
            total[at, :] = value + vec(3)
            return carry

        lax.fori_loop(0, parts, part, 0)

    @pl.when(step < chunks)
    def _():
        def part(i, carry):
            at = pl.ds(pl.multiple_of(i * ROWS, ROWS), ROWS)
            pre = mm(first_low[at, :], up_w()) + vec_ref[pl.ds(8 + step, 1), :]
            value, pull = gelu_both(pre)
            low = value.astype(bf16)
            slope[step, at, :] = pull
            activ_t[step, :, at] = low.T
            total[at, :] += mm(low, down_w())
            return carry

        lax.fori_loop(0, parts, part, 0)

    @pl.when(step == chunks - 1)
    def _():
        def part(i, carry):
            at = pl.ds(pl.multiple_of(i * ROWS, ROWS), ROWS)
            hat, rstd = normal_rows(total[at, :])
            y_ref[at, :] = (hat * vec(4) + vec(5)).astype(bf16)
            g = cot_ref[at, :].astype(f32)
            gh2 = norm_pull(g * vec(4), hat, rstd)
            total[at, :] = gh2
            low = gh2.astype(bf16)
            gffn[at, :] = low
            gvec_ref[3:4, :] += sums(low.astype(f32))
            gvec_ref[4:5, :] += sums(g * hat)
            gvec_ref[5:6, :] += sums(g)
            return carry

        lax.fori_loop(0, parts, part, 0)

    @pl.when(step >= chunks)
    def _():
        chunk = 2 * chunks - 1 - step
        slot = lax.rem(step, 2)

        @pl.when(step >= chunks + 2)
        def _():
            finish(down_copies(slot, chunk))
            finish(up_copies(slot, chunk))

        def part(i, carry):
            at = pl.ds(pl.multiple_of(i * ROWS, ROWS), ROWS)
            low = (mm_nt(gffn[at, :], down_w()) * slope[chunk, at, :]).astype(bf16)
            gpre[at, :] = low
            gvec_ref[pl.ds(8 + chunk, 1), :] += sums(low.astype(f32))
            total[at, :] += mm_nt(low, up_w())
            return carry

        lax.fori_loop(0, parts, part, 0)
        tall = 4 * chunks * own

        def weights_down(i, carry):
            at = pl.ds(pl.multiple_of(i * tall, tall), tall)
            value = mm(activ_t[chunk, at, :], gffn[...]).astype(bf16).reshape(4, chunks * own, model)
            for f in range(4):
                gdown[slot, f % 2, 2 * i + f // 2] = value[f]
            return carry

        lax.fori_loop(0, model // tall, weights_down, 0)
        begin(down_copies(slot, chunk))
        high = 16 * own

        def weights_up(i, carry):
            at = pl.ds(pl.multiple_of(i * high, high), high)
            value = mm(first_t[at, :], gpre[...]).astype(bf16).reshape(16, own, model)
            for f in range(16):
                gup[slot, f % 2, 2 * i + f // 8, (f % 8) // 2] = value[f]
            return carry

        lax.fori_loop(0, model // high, weights_up, 0)
        begin(up_copies(slot, chunk))

    @pl.when(step == 2 * chunks - 1)
    def _():
        def part(i, carry):
            at = pl.ds(pl.multiple_of(i * ROWS, ROWS), ROWS)
            g = total[at, :]
            hat = hat1[at, :]
            gh1 = norm_pull(g * vec(1), hat, rstd1[at, :1])
            gh1_ref[at, :] = gh1
            low = gh1.astype(bf16)
            gpre[at, :] = low
            gvec_ref[0:1, :] += sums(low.astype(f32))
            gvec_ref[1:2, :] += sums(g * hat)
            gvec_ref[2:3, :] += sums(g)
            for r in range(groups):
                gmix_refs[r][:, at] = mm_nt(out_w(r), low).astype(bf16)
            return carry

        lax.fori_loop(0, parts, part, 0)
        for r in range(groups):
            value = mm(mixed_refs[r][...], gpre[...]).astype(bf16).reshape(share, own, model)
            for f in range(share):
                gout[f % 2, group(r), f // 2] = value[f]
        begin(out_copies())
        gather_vectors(chunks, gvec_ref, gwide)
        for g in range(groups):
            for f in range(share):
                gsmall[f % 2, g, f // 2] = gwide[g * share + f].astype(bf16)
        begin(small_copies())
        for back in range(2):
            finish(down_copies(back, 0))
            finish(up_copies(back, 0))
        finish(out_copies())
        finish(small_copies())


def middle(place, x, cot, mixed, packed):
    rows, model = x.shape
    groups = len(mixed)
    width = mixed[0].shape[0]
    pieces = packed.shape[0]
    own = model // pieces
    chunks = (packed.shape[1] - 8 - own) // (2 * own)
    last = 2 * chunks - 1
    back = lambda s: jnp.minimum(s, last - s)
    assert chunks == groups and pieces == 8 * groups
    once = dict(pipeline_mode=pl.Buffered(1))
    fixed2 = lambda a: pl.BlockSpec(a, lambda s: (0, 0), **once)
    vectors_at = own * (2 * chunks + 1) // 8
    cost = pl.CostEstimate(
        flops=2 * rows * model * model * (3 + 6 * chunks),
        bytes_accessed=2 * model * model * (4 * chunks + 8),
        transcendentals=rows * model * chunks,
    )
    share = pieces // groups
    half = jax.ShapeDtypeStruct((groups, share // 2, packed.shape[1], model), bf16)
    return pl.pallas_call(
        lambda *refs: middle_kernel(groups, chunks, *refs),
        grid=(2 * chunks,),
        in_specs=[
            pl.BlockSpec(memory_space=pltpu.SMEM),
            fixed2((rows, model)),
            fixed2((rows, model)),
            fixed2((width, rows)),
            fixed2((width, rows)),
            fixed2((width, rows)),
            fixed2((width, rows)),
            pl.BlockSpec((pieces, own, model), lambda s: (0, 2 * chunks, 0), **once),
            pl.BlockSpec((pieces, own, model), lambda s: (0, chunks + back(s), 0)),
            pl.BlockSpec((pieces // chunks, chunks * own, model), lambda s: (back(s), 0, 0)),
            pl.BlockSpec((pieces, 8, model), lambda s: (0, vectors_at, 0), **once),
        ],
        out_specs=[
            fixed2((rows, model)),
            fixed2((rows, model)),
            fixed2((width, rows)),
            fixed2((width, rows)),
            fixed2((width, rows)),
            fixed2((width, rows)),
            pl.BlockSpec(memory_space=pl.ANY),
            pl.BlockSpec(memory_space=pl.ANY),
        ],
        out_shape=[
            jax.ShapeDtypeStruct((rows, model), bf16),
            jax.ShapeDtypeStruct((rows, model), f32),
            jax.ShapeDtypeStruct((width, rows), bf16),
            jax.ShapeDtypeStruct((width, rows), bf16),
            jax.ShapeDtypeStruct((width, rows), bf16),
            jax.ShapeDtypeStruct((width, rows), bf16),
            half,
            half,
        ],
        scratch_shapes=[
            pltpu.VMEM((rows, model), bf16),
            pltpu.VMEM((model, rows), bf16),
            pltpu.VMEM((rows, model), f32),
            pltpu.VMEM((rows, 128), f32),
            pltpu.VMEM((chunks, model, rows), bf16),
            pltpu.VMEM((chunks, rows, model), f32),
            pltpu.VMEM((rows, model), f32),
            pltpu.VMEM((rows, model), bf16),
            pltpu.VMEM((rows, model), bf16),
            pltpu.VMEM((16, model), f32),
            pltpu.VMEM((16, model), f32),
            pltpu.VMEM((2, 2, share // 2, chunks * own, model), bf16),
            pltpu.VMEM((2, 2, groups, share // 2, own, model), bf16),
            pltpu.VMEM((2, groups, share // 2, own, model), bf16),
            pltpu.VMEM((pieces, 8, model), f32),
            pltpu.VMEM((2, groups, share // 2, 8, model), bf16),
            pltpu.SemaphoreType.DMA((2, 2)),
            pltpu.SemaphoreType.DMA((2, 2)),
            pltpu.SemaphoreType.DMA((2,)),
            pltpu.SemaphoreType.DMA((2,)),
        ],
        cost_estimate=cost,
        compiler_params=pltpu.CompilerParams(vmem_limit_bytes=60 << 20),
        name="middle",
    )(place, x, cot, *mixed, packed, packed, packed, packed)


def by_sp(value, flip):
    groups = lax.axis_size("sp")
    return lax.ppermute(value, "sp", [(i, i ^ flip) for i in range(groups)])


def by_fsdp(value, flip):
    shards = lax.axis_size("fsdp")
    return lax.ppermute(value, "fsdp", [(i, i ^ flip) for i in range(shards)])


def scatter_rows(sent_x, sent_y, mine, low, up):
    half = low.shape[0]
    got_x = by_sp(sent_x, 1).astype(f32)
    got_y = by_sp(sent_y, 2).astype(f32)
    next_y = by_sp((up + got_x[half:]).astype(bf16), 2).astype(f32)
    next_x = by_sp((low + got_y[half:]).astype(bf16), 1).astype(f32)
    return mine + jnp.concatenate([got_x[:half] + next_y, got_y[:half] + next_x], 0)


def unpack(packed, ratio):
    pieces, _, model = packed.shape
    own = model // pieces
    at = ratio * own
    down = packed[:, :at].reshape(ratio * model, model)
    up = packed[:, at : 2 * at].reshape(pieces, ratio, own, model).transpose(1, 0, 2, 3)
    out = packed[:, 2 * at : 2 * at + own].reshape(model, model)
    vectors = [packed[:, 2 * at + own + j, :own].reshape(-1) for j in range(6)]
    vectors.append(packed[:, 2 * at + own + 6, :at].reshape(-1))
    return down, up.reshape(ratio, model, model), out, vectors


def repack(packed, ratio, pieces):
    if packed.shape[0] == pieces:
        return packed
    down, up, out, vectors = unpack(packed, ratio)
    model = out.shape[0]
    own = model // pieces
    up = up.reshape(ratio, pieces, own, model).transpose(1, 0, 2, 3)
    rows = [jnp.pad(v.reshape(pieces, -1), ((0, 0), (0, model - v.shape[0] // pieces))) for v in vectors]
    rows.append(jnp.zeros_like(rows[0]))
    return jnp.concatenate(
        [
            down.reshape(pieces, ratio * own, model),
            up.reshape(pieces, ratio * own, model),
            out.reshape(pieces, own, model),
            jnp.stack(rows, 1),
        ],
        1,
    )


def body(
    tokens,
    segments,
    cotangent,
    w_qkv,
    b_query,
    b_value,
    w_out,
    b_out,
    ln1_gain,
    ln1_bias,
    w_up,
    b_up,
    w_down,
    b_down,
    ln2_gain,
    ln2_bias,
):
    both = ("sp", "fsdp")
    groups = lax.axis_size("sp")
    shards = lax.axis_size("fsdp")
    devices = groups * shards
    rows, model = tokens.shape
    hidden = w_up.shape[1]
    ratio = hidden // model
    own = w_qkv.shape[0]
    pieces = devices if own % 8 == 0 else 8 * groups
    heads_local = HEADS // groups
    width = heads_local * HEAD
    seq_len = rows * groups
    seg_row = segments[0]

    me = lax.axis_index("sp").astype(jnp.int32).reshape(1)
    core = lax.rem(lax.axis_index("fsdp"), 2).astype(jnp.int32).reshape(1)
    direct = pieces == devices

    half = rows // 2
    first = by_sp(tokens[:half], 2), by_sp(tokens[half:], 1)
    second = by_sp(tokens[:half], 1), by_sp(tokens[half:], 2)
    vectors = [b_out, ln1_gain, ln1_bias, b_down, ln2_gain, ln2_bias, b_up]
    if direct:
        packed, mine = pack(me, w_down, w_up, w_out, w_qkv, vectors, b_query, b_value, groups)
        mine = jnp.stack([mine[0]] + [by_sp(mine[r], r) for r in range(1, groups)])
        near = jnp.stack([mine] + [by_fsdp(mine, 2 * z) for z in range(1, shards // 2)])
        near, first, second = lax.optimization_barrier((near, first, second))
        away = by_fsdp(near, 1)
        column = (lax.axis_index("fsdp").astype(jnp.int32) // 2).reshape(1)
        order = jnp.concatenate([me, me, column, core])
    else:
        packed, mine = pack_plain(w_down, w_up, w_out, w_qkv, vectors, b_query, b_value, groups)
        mine = jnp.broadcast_to(mine[:, None], (groups, shards) + mine.shape[1:])
        mine = mine.reshape(devices, own + 8, 3 * width)
        mine = lax.all_to_all(mine, both, split_axis=0, concat_axis=0, tiled=True)
        cut = model // pieces
        biases = lax.dynamic_slice(mine, (me[0] * shards, own, 0), (shards, 2, own))
        biases = biases.transpose(1, 0, 2).reshape(2, 8, cut).transpose(1, 0, 2)
        biases = jnp.pad(biases, ((0, 0), (0, 6), (0, 3 * width - cut)))
        mine = mine[:, :own].reshape(groups, 8, cut, 3 * width)
        mine = jnp.concatenate([mine, jnp.broadcast_to(biases[None], (groups, 8, 8, 3 * width))], 2)
        mine = mine.reshape(groups, 4, 2, cut + 8, 3 * width).transpose(2, 1, 0, 3, 4)
        near, away = mine[0], mine[1]
        order = jnp.concatenate([me, jnp.zeros((3,), jnp.int32)])
    blocks = tokens, second[0], first[1], first[0], second[1], by_sp(first[0], 1), by_sp(first[1], 2)
    packed_weights = repack(lax.all_gather(packed, both, axis=0, tiled=False), ratio, pieces)
    queries, keys, values, tokens_all, weights = project(
        order, blocks, seg_row, near, away, heads_local
    )
    forward_start, forward_number = windows(seg_row, FQ, FK, 128)
    backward_start, backward_number = windows(seg_row, BK, BQ, 128)
    *attended, logsum = attend_forward(
        queries, keys, values, forward_start, forward_number, me, heads_local
    )
    mixed = [attended[0]] + [by_sp(attended[r], r) for r in range(1, 4)]
    place = jnp.concatenate([core if direct else jnp.zeros_like(core), me])
    output, grad_h1, *grad_mixed, kept, sent = middle(place, tokens, cotangent, mixed, packed_weights)
    grad_heads = [grad_mixed[0]] + [by_sp(grad_mixed[r], r) for r in range(1, 4)]

    if not direct:
        halves = jnp.stack([kept, sent], 2).reshape(pieces, kept.shape[2], model)
        halves = repack(halves, ratio, devices).reshape(groups, shards // 2, 2, -1, model)
        kept = lax.dynamic_index_in_dim(halves, core[0], 2, keepdims=False)
        sent = lax.dynamic_index_in_dim(halves, 1 - core[0], 2, keepdims=False)
    partner = by_fsdp(sent, 1)
    total = (kept.astype(f32) + partner.astype(f32)).astype(bf16)
    total, grad_heads = lax.optimization_barrier((total, grad_heads))
    total = lax.psum_scatter(total.reshape(-1, model), "sp", scatter_dimension=0, tiled=True)
    cores = [[2 * i + c for i in range(shards // 2)] for c in range(2)]
    reduced = lax.psum_scatter(
        total, "fsdp", scatter_dimension=0, tiled=True, axis_index_groups=cores
    ).astype(f32)

    *parts, kept, sent = attend_backward(
        queries,
        keys,
        values,
        grad_heads,
        attended,
        logsum,
        backward_start,
        backward_number,
        order,
        tokens_all,
        weights,
        grad_h1,
        pieces,
        heads_local,
    )
    grad_input = scatter_rows(*parts)
    if direct:
        total = (kept.astype(f32) + by_fsdp(sent, 1).astype(f32)).astype(bf16)
        moved = [by_fsdp(total[z], 2 * z).astype(f32) for z in range(1, shards // 2)]
        total = sum(moved, total[0].astype(f32))
        by_head = jnp.stack([total[0]] + [by_sp(total[r], r) for r in range(1, groups)])
        bias_sums = total[0, :2, model - 128 : model - 128 + own]
        by_head = [lax.dynamic_index_in_dim(by_head, me[0] ^ g, keepdims=False) for g in range(groups)]
        by_head = jnp.stack([item[:, : 3 * width].reshape(own, 3, width) for item in by_head], 2)
    else:
        cut = model // pieces
        halves = jnp.stack([kept, sent], 2).transpose(1, 0, 2, 3, 4).reshape(pieces, cut, model)
        biases = halves[:8, :2, model - 128 : model - 128 + cut]
        biases = biases.transpose(1, 0, 2).reshape(2, shards, own).transpose(1, 0, 2)
        biases = jnp.pad(biases, ((0, 0), (0, 6), (0, 3 * width - own)))
        halves = halves[:, :, : 3 * width].reshape(devices, own, 3 * width)
        halves = jnp.concatenate([halves, jnp.tile(biases, (groups, 1, 1))], 1)
        halves = lax.all_to_all(halves, both, split_axis=0, concat_axis=0, tiled=True)
        halves = jnp.sum(halves.reshape(groups, shards, own + 8, 3 * width).astype(f32), 1)
        bias_sums = lax.dynamic_slice(halves, (me[0], own, 0), (1, 2, own))[0]
        by_head = halves[:, :own].reshape(groups, own, 3, width).transpose(1, 2, 0, 3)
    owned_qkv = by_head.reshape(own, 3 * model)
    grad_query_bias = bias_sums[0]
    grad_value_bias = bias_sums[1]
    at = ratio * own
    owned_up = reduced[at : 2 * at].reshape(ratio, own, model).transpose(1, 0, 2).reshape(own, hidden)
    tail = reduced[2 * at + own :]
    return (
        output,
        grad_input,
        owned_qkv,
        grad_query_bias,
        grad_value_bias,
        reduced[2 * at : 2 * at + own],
        tail[0, :own],
        tail[1, :own],
        tail[2, :own],
        owned_up,
        tail[6, :at],
        reduced[:at],
        tail[3, :own],
        tail[4, :own],
        tail[5, :own],
    )


def solution(mesh):
    in_specs = (
        P(("fsdp", "sp"), None),
        P("fsdp", None),
        P(("fsdp", "sp"), None),
        P(("sp", "fsdp"), None),
        P(("sp", "fsdp")),
        P(("sp", "fsdp")),
        P(("sp", "fsdp"), None),
        P(("sp", "fsdp")),
        P(("sp", "fsdp")),
        P(("sp", "fsdp")),
        P(("sp", "fsdp"), None),
        P(("sp", "fsdp")),
        P(("sp", "fsdp"), None),
        P(("sp", "fsdp")),
        P(("sp", "fsdp")),
        P(("sp", "fsdp")),
    )
    out_specs = (
        P(("fsdp", "sp"), None),
        P(("fsdp", "sp"), None),
        P(("sp", "fsdp"), None),
        P(("sp", "fsdp")),
        P(("sp", "fsdp")),
        P(("sp", "fsdp"), None),
        P(("sp", "fsdp")),
        P(("sp", "fsdp")),
        P(("sp", "fsdp")),
        P(("sp", "fsdp"), None),
        P(("sp", "fsdp")),
        P(("sp", "fsdp"), None),
        P(("sp", "fsdp")),
        P(("sp", "fsdp")),
        P(("sp", "fsdp")),
    )
    return jax.shard_map(body, mesh=mesh, in_specs=in_specs, out_specs=out_specs, check_vma=False)
```

time: 413 us -> 340 us (0.82); the launches traced: 414 us -> 334 us
  waiting for transfers between devices: 129 us -> 84.5 us
  local copies, waits for them, and re-layouts: 36 us -> 16.3 us
  blocking collectives: 19.2 us -> 0 us
  Pallas kernels: 149 us -> 162 us
  matrix products: 11.7 us -> 0 us
    ppermute x8 -> x22, waiting for transfers between devices: 107 us -> 37.6 us  [by_sp(): return lax.ppermute(value, 'sp', [(i, i ^ flip) for i in range(groups)])]
    ppermute x0 -> x9, waiting for transfers between devices: none -> 46.9 us  [by_fsdp(): return lax.ppermute(value, 'fsdp', [(i, i ^ flip) for i in range(shards)])]
    all_to_all x4 -> x0, starting transfers between devices: 25.3 us -> none  [the longest x1 9.92 us: body(): lax.all_to_all(by_owner, both, split_axis=0, concat_axis=0, tiled=True)]
    all_to_all x4 -> x0, waiting for transfers between devices: 21.8 us -> none  [the longest x1 11.8 us: body(): lax.all_to_all(grad_mixed, 'sp', split_axis=0, concat_axis=0, tiled=True)]
    all_to_all x1 -> x0, blocking collectives: 19.2 us -> none  [body(): lax.all_to_all(attended.reshape(groups, rows, width), 'sp', split_axis=0,...]
    pallas_call x1, Pallas kernels: 51.6 us -> 68.9 us  [attend_backward(): pl.pallas_call(lambda *refs: backward_kernel(heads, *refs), grid_spec=plt...]
    ppermute x8 -> x22, starting transfers between devices: 12.7 us -> 26 us  [by_sp(): return lax.ppermute(value, 'sp', [(i, i ^ flip) for i in range(groups)])]
    ppermute x0 -> x9, starting transfers between devices: none -> 12.3 us  [by_fsdp(): return lax.ppermute(value, 'fsdp', [(i, i ^ flip) for i in range(shards)])]
  transfers between devices with their start and end apart: 14 -> 34, of which waited for: 10 -> 16; matrix products, arithmetic and copies ran while one was open for 11% -> 7% of each run, Pallas kernels for 22% -> 32%
where the time goes in v4:
time: 340 us; the launch traced here: 334 us
  Pallas kernels  162 us (48%)
  waiting for transfers between devices  84.5 us (25%)
  starting transfers between devices  38.4 us (11%)
  other arithmetic  17.9 us (5%)
  local copies, waits for them, and re-layouts  16.3 us (5%)
  between operations  14.2 us (4%)
    pallas_call x1, Pallas kernels, attend_backward(): pl.pallas_call(lambda *refs: backward_kernel(heads, *refs), grid_spec=plt...  68.9 us
    pallas_call x1, Pallas kernels, middle(): pl.pallas_call(lambda *refs: middle_kernel(groups, chunks, *refs), grid=(...  53.2 us
    ppermute x9, waiting for transfers between devices, by_fsdp(): return lax.ppermute(value, 'fsdp', [(i, i ^ flip) for i in range(shards)])  46.9 us
    ppermute x22, waiting for transfers between devices, by_sp(): return lax.ppermute(value, 'sp', [(i, i ^ flip) for i in range(groups)])  37.6 us
    pallas_call x1, Pallas kernels, attend_forward(): pl.pallas_call(lambda *refs: forward_kernel(heads, *refs), grid_spec=pltp...  28.4 us
    ppermute x22, starting transfers between devices, by_sp(): return lax.ppermute(value, 'sp', [(i, i ^ flip) for i in range(groups)])  26 us
    ppermute x9, starting transfers between devices, by_fsdp(): return lax.ppermute(value, 'fsdp', [(i, i ^ flip) for i in range(shards)])  12.3 us
    pallas_call x1, Pallas kernels, project(): pl.pallas_call(lambda *refs: project_kernel(heads, *refs), grid_spec=pltp...  9.95 us
  transfers between devices with their start and end apart: 34, of which 16 were waited for; matrix products, arithmetic and copies ran while one was open for 7% of the time, Pallas kernels for 32%

profile of v4, /device:TPU:0, one launch (start us, length us, event | category | flops | bytes accessed | tf_op | source)
XLA Modules:
  0.0 333.7 jit_solution(1835524466841518821)
XLA Ops:
  7.2 1.9 pack.1
  9.2 0.9 fusion.14
  10.1 3.0 collective-permute-start
  13.1 1.5 collective-permute-start.1
  14.7 1.3 fusion.11
  16.0 2.0 collective-permute-start.6
  18.0 1.5 collective-permute-start.8
  20.2 2.1 collective-permute-start.3
  22.3 6.6 %collective-permute-done.3 = bf16[4,32,576]{2,1,0:T(8,128)(2,1)S(1)} collective-permute-done((bf16[4,32,576]{2,1,0:T(8,128)(2,1)S(1)}, bf16[4,32,576]{2,1,0:T(8,128)(2,1)S(1)}, u32[]{:S(2)}, u32[]{:S(2)}) %collective-permute-start.3) | collective-permute-done | bytes 147488 | tf_op jit(solution)/shard_map/ppermute | solution.py:927
  28.8 3.3 %collective-permute-start.4 = (bf16[4,32,576]{2,1,0:T(8,128)(2,1)S(1)}, bf16[4,32,576]{2,1,0:T(8,128)(2,1)S(1)}, u32[]{:S(2)}, u32[]{:S(2)}) collective-permute-start(bf16[4,32,576]{2,1,0:T(8,128)(2,1)S(1)} %get-tuple-element.121), channel_id=1, source_target_pairs={{0,4},{1,5},{2,6},{3,7},{4,0},{5,1},{6,2},{7,3},{8,12},{9,13},{10,... | collective-permute-start | bytes 442376 | tf_op jit(solution)/shard_map/ppermute | solution.py:927
  32.2 11.6 %collective-permute-done.4 = bf16[4,32,576]{2,1,0:T(8,128)(2,1)S(1)} collective-permute-done((bf16[4,32,576]{2,1,0:T(8,128)(2,1)S(1)}, bf16[4,32,576]{2,1,0:T(8,128)(2,1)S(1)}, u32[]{:S(2)}, u32[]{:S(2)}) %collective-permute-start.4) | collective-permute-done | bytes 147488 | tf_op jit(solution)/shard_map/ppermute | solution.py:927
  43.8 2.4 collective-permute-start.5
  46.2 6.2 %collective-permute-done.5 = bf16[4,32,576]{2,1,0:T(8,128)(2,1)S(1)} collective-permute-done((bf16[4,32,576]{2,1,0:T(8,128)(2,1)S(1)}, bf16[4,32,576]{2,1,0:T(8,128)(2,1)S(1)}, u32[]{:S(2)}, u32[]{:S(2)}) %collective-permute-start.5) | collective-permute-done | bytes 147488 | tf_op jit(solution)/shard_map/ppermute | solution.py:927
  52.5 0.8 copy-done.2
  53.3 0.8 copy-done.4
  54.1 1.7 collective-permute-start.10
  55.8 1.9 collective-permute-start.11
  58.8 12.2 %collective-permute-done.10.refs_6_ = bf16[384,768]{1,0:T(8,128)(2,1)} collective-permute-done((bf16[384,768]{1,0:T(8,128)(2,1)}, bf16[384,768]{1,0:T(8,128)(2,1)}, u32[]{:S(2)}, u32[]{:S(2)}) %collective-permute-start.10) | collective-permute-done | bytes 589856 | tf_op jit(solution)/shard_map/ppermute | solution.py:922
  71.0 0.8 collective-permute-done.11.refs_7_
  71.8 1.1 copy-done.3
  72.8 1.1 copy-done.5
  73.9 10.0 %project.1 = (bf16[3072,256]{1,0:T(8,128)(2,1)S(1)}, bf16[3072,256]{1,0:T(8,128)(2,1)S(1)}, bf16[3072,192]{1,0:T(8,128)(2,1)S(1)}, bf16[3072,768]{1,0:T(8,128)(2,1)}, bf16[3,768,192]{2,1,0:T(8,128)(2,1)S(1)}) custom-call(s32[4]{0:T(128)S(1)} %pad_add_fusion.1.refs_0_.refs_2_, bf16[768,768]{1,0:T(8,128)(2,1)S(1)} %copy-done, bf16[384,768]{1,0:T(8,128)(2,1)S(1)} %copy-done.3, ...), custom_call_target="tpu_custom_call" | custom-call | flops 2717908992 | bytes 12582912 | tf_op jit(solution)/shard_map/project/pallas_call | solution.py:525
  83.9 1.0 copy-done.12
  84.9 28.4 %attend_forward.1 = (bf16[192,768]{1,0:T(8,128)(2,1)S(1)}, bf16[192,768]{1,0:T(8,128)(2,1)S(1)}, bf16[192,768]{1,0:T(8,128)(2,1)S(1)}, bf16[192,768]{1,0:T(8,128)(2,1)S(1)}, f32[8,3072]{1,0:T(8,128)S(1)}) custom-call(s32[6]{0:T(128)S(1)} %get-tuple-element.95.refs_0_, s32[6]{0:T(128)S(1)} %get-tuple-element.96.refs_1_, s32[1]{0:T(128)} %bitcast.1.refs_0_.refs_2_, ...), custom_call_target="tpu_custom_call" | custom-call | flops 3623878656 | bytes 6291456 | tf_op jit(solution)/shard_map/attend_forward/pallas_call | solution.py:144
  113.3 0.7 copy-done.13
  114.1 0.6 copy-done.14
  115.0 1.7 collective-permute-start.14
  116.8 1.4 collective-permute-start.15
  118.8 5.9 %collective-permute-done.13.refs_4_ = bf16[192,768]{1,0:T(8,128)(2,1)S(1)} collective-permute-done((bf16[192,768]{1,0:T(8,128)(2,1)S(1)}, bf16[192,768]{1,0:T(8,128)(2,1)S(1)}, u32[]{:S(2)}, u32[]{:S(2)}) %collective-permute-start.13) | collective-permute-done | bytes 294944 | tf_op jit(solution)/shard_map/ppermute | solution.py:922
  124.6 4.3 %collective-permute-done.14.refs_5_ = bf16[192,768]{1,0:T(8,128)(2,1)S(1)} collective-permute-done((bf16[192,768]{1,0:T(8,128)(2,1)S(1)}, bf16[192,768]{1,0:T(8,128)(2,1)S(1)}, u32[]{:S(2)}, u32[]{:S(2)}) %collective-permute-start.14) | collective-permute-done | bytes 294944 | tf_op jit(solution)/shard_map/ppermute | solution.py:922
  129.0 1.6 collective-permute-done.15.refs_6_
  130.6 0.7 copy-done.27
  131.2 53.2 %middle.1 = (bf16[768,768]{1,0:T(8,128)(2,1)}, f32[768,768]{1,0:T(8,128)}, bf16[192,768]{1,0:T(8,128)(2,1)}, bf16[192,768]{1,0:T(8,128)(2,1)}, bf16[192,768]{1,0...) custom-call(s32[2]{0:T(128)} %pad_add_fusion.refs_0_, ...), custom_call_target="tpu_custom_call" | custom-call | flops 24461180928 | bytes 28311552 | tf_op jit(solution)/shard_map/middle/pallas_call | solution.py:856
  184.6 0.9 collective-permute-start.17
  185.5 1.5 collective-permute-start.18
  187.0 1.1 collective-permute-start.19
  188.1 5.7 %collective-permute-done.16 = bf16[4,4,224,768]{3,2,1,0:T(8,128)(2,1)S(1)} collective-permute-done((bf16[4,4,224,768]{3,2,1,0:T(8,128)(2,1)}, bf16[4,4,224,768]{3,2,1,0:T(8,128)(2,1)S(1)}, u32[]{:S(2)}, u32[]{:S(2)}) %collective-permute-start.16) | collective-permute-done | bytes 5505056 | tf_op jit(solution)/shard_map/ppermute | solution.py:927
  193.8 6.7 %add_convert_fusion = bf16[4,4,224,768]{3,2,1,0:T(8,128)(2,1)} fusion(bf16[4,4,224,768]{3,2,1,0:T(8,128)(2,1)S(1)} %collective-permute-done.16, bf16[4,4,224,768]{3,2,1,0:T(8,128)(2,1)} %get-tuple-element.67), kind=kLoop, calls=%fused_computation | loop fusion | flops 11010048 | bytes 16515072 | tf_op jit(solution)/shard_map/convert_element_type | solution.py:1054
  200.5 0.6 collective-permute-done.18.refs_8_
  201.2 0.6 copy-done.23
  202.9 68.9 %attend_backward.1 = (bf16[768,768]{1,0:T(8,128)(2,1)}, bf16[768,768]{1,0:T(8,128)(2,1)}, f32[768,768]{1,0:T(8,128)}, f32[384,768]{1,0:T(8,128)}, f32[384,768]{1...) custom-call(s32[12]{0:T(128)} %get-tuple-element.93.refs_0_, s32[12]{0:T(128)} %get-tuple-element.94.refs_1_, ...), custom_call_target="tpu_custom_call" | custom-call | flops 14495514624 | bytes 12582912 | tf_op jit(solution)/shard_map/attend_backward/pallas_call | solution.py:346
  271.8 0.8 collective-permute-start.20
  272.6 0.8 collective-permute-start.22
  274.0 1.2 add_convert_fusion.1
  275.3 1.1 collective-permute-start.25
  276.4 1.5 collective-permute-start.26
  277.9 1.8 collective-permute-start.27
  279.8 7.1 %collective-permute-done.25 = bf16[4,24,768]{2,1,0:T(8,128)(2,1)S(1)} collective-permute-done((bf16[4,24,768]{2,1,0:T(8,128)(2,1)S(1)}, bf16[4,24,768]{2,1,0:T(8,128)(2,1)S(1)}, u32[]{:S(2)}, u32[]{:S(2)}) %collective-permute-start.25) | collective-permute-done | bytes 147488 | tf_op jit(solution)/shard_map/ppermute | solution.py:927
  286.9 9.1 %collective-permute-done.26 = bf16[4,24,768]{2,1,0:T(8,128)(2,1)S(1)} collective-permute-done((bf16[4,24,768]{2,1,0:T(8,128)(2,1)S(1)}, bf16[4,24,768]{2,1,0:T(8,128)(2,1)S(1)}, u32[]{:S(2)}, u32[]{:S(2)}) %collective-permute-start.26) | collective-permute-done | bytes 147488 | tf_op jit(solution)/shard_map/ppermute | solution.py:927
  296.3 3.4 %collective-permute-start.30 = (f32[24,768]{1,0:T(8,128)S(1)}, f32[24,768]{1,0:T(8,128)S(1)}, u32[]{:S(2)}, u32[]{:S(2)}) collective-permute-start(f32[24,768]{1,0:T(8,128)S(1)} %get-tuple-element.117), channel_id=1, source_target_pairs={{0,24},{8,16},{16,8},{24,0},{1,25},{9,17},{17,9},{25,1},{2,26},{10... | collective-permute-start | bytes 221192 | tf_op jit(solution)/shard_map/ppermute | solution.py:922
  300.2 0.8 collective-permute-done.20
  301.0 1.4 convert_element_type.73
  302.4 1.0 fusion.1
  303.4 1.5 collective-permute-start.21
  305.1 1.1 fusion
  307.6 0.9 reshape.64
  308.5 9.7 %collective-permute-done.21 = bf16[384,768]{1,0:T(8,128)(2,1)} collective-permute-done((bf16[384,768]{1,0:T(8,128)(2,1)}, bf16[384,768]{1,0:T(8,128)(2,1)}, u32[]{:S(2)}, u32[]{:S(2)}) %collective-permute-start.21) | collective-permute-done | bytes 589856 | tf_op jit(solution)/shard_map/ppermute | solution.py:922
  318.2 1.2 slice_add_fusion.3
  319.4 1.7 collective-permute-done.23
  321.1 1.7 maximum_add_fusion
  322.8 1.1 convert_element_type.87
  325.0 0.8 fusion.12
  325.8 0.7 copy.36
  326.5 0.6 slice.185
  (114 shorter events, 8.3 us)
Async XLA Ops:
  7.2 123.4 %all-gather.3.cloned.1.call-start = ((), (), s32[]{:S(2)}) async-start(), calls=%async_computation.4 | async-start | bytes 11354112 | tf_op jit(solution)/shard_map/all_gather | solution.py:1034
  9.2 266.1 %reduce-scatter.3.cloned.1.call-start = ((), (), s32[]{:S(2)}) async-start(), calls=%async_computation.2 | async-start | bytes 6881280 | tf_op jit(solution)/shard_map/reduce_scatter | solution.py:1056
  10.1 9.4 %collective-permute-start = (bf16[32,576]{1,0:T(8,128)(2,1)S(1)}, bf16[32,576]{1,0:T(8,128)(2,1)S(1)}, u32[]{:S(2)}, u32[]{:S(2)}) collective-permute-start(bf16[32,576]{1,0:T(8,128)(2,1)S(1)} %get-tuple-element.125), channel_id=1, source_target_pairs={{0,8},{8,0},{16,24},{24,16},{1,9},{9,1},{17,25},{25,17},{2,10},{10... | collective-permute-start | bytes 110600 | tf_op jit(solution)/shard_map/ppermute | solution.py:922
  13.1 7.0 %collective-permute-start.1 = (bf16[32,576]{1,0:T(8,128)(2,1)S(1)}, bf16[32,576]{1,0:T(8,128)(2,1)S(1)}, u32[]{:S(2)}, u32[]{:S(2)}) collective-permute-start(bf16[32,576]{1,0:T(8,128)(2,1)S(1)} %get-tuple-element.124), channel_id=1, source_target_pairs={{0,16},{8,24},{16,0},{24,8},{1,17},{9,25},{17,1},{25,9},{2,18},{10... | collective-permute-start | bytes 110600 | tf_op jit(solution)/shard_map/ppermute | solution.py:922
  14.6 5.5 %collective-permute-start.2 = (bf16[32,576]{1,0:T(8,128)(2,1)S(1)}, bf16[32,576]{1,0:T(8,128)(2,1)S(1)}, u32[]{:S(2)}, u32[]{:S(2)}) collective-permute-start(bf16[32,576]{1,0:T(8,128)(2,1)S(1)} %get-tuple-element.123), channel_id=1, source_target_pairs={{0,24},{8,16},{16,8},{24,0},{1,25},{9,17},{17,9},{25,1},{2,26},{10... | collective-permute-start | bytes 110600 | tf_op jit(solution)/shard_map/ppermute | solution.py:922
  16.0 41.8 %copy-start.21 = (s32[1,3072]{1,0:T(1,128)S(1)}, s32[1,3072]{1,0:T(1,128)}, u32[]{:S(2)}) copy-start(s32[1,3072]{1,0:T(1,128)} %param.17) | copy-start | bytes 36868
  16.0 36.5 %collective-permute-start.6 = (bf16[384,768]{1,0:T(8,128)(2,1)S(1)}, bf16[384,768]{1,0:T(8,128)(2,1)}, u32[]{:S(2)}, u32[]{:S(2)}) collective-permute-start(bf16[384,768]{1,0:T(8,128)(2,1)S(1)} %get-tuple-element.98), channel_id=1, source_target_pairs={{0,16},{8,24},{16,0},{24,8},{1,17},{9,25},{17,1},{25,9},{2,18},{10... | collective-permute-start | bytes 1769480 | tf_op jit(solution)/shard_map/ppermute | solution.py:922
  18.0 34.4 %collective-permute-start.8 = (bf16[384,768]{1,0:T(8,128)(2,1)S(1)}, bf16[384,768]{1,0:T(8,128)(2,1)S(1)}, u32[]{:S(2)}, u32[]{:S(2)}) collective-permute-start(bf16[384,768]{1,0:T(8,128)(2,1)S(1)} %get-tuple-element.98), channel_id=1, source_target_pairs={{0,8},{8,0},{16,24},{24,16},{1,9},{9,1},{17,25},{25,17},{2,10},{10... | collective-permute-start | bytes 1769480 | tf_op jit(solution)/shard_map/ppermute | solution.py:922
  19.5 32.9 %collective-permute-start.7 = (bf16[384,768]{1,0:T(8,128)(2,1)S(1)}, bf16[384,768]{1,0:T(8,128)(2,1)}, u32[]{:S(2)}, u32[]{:S(2)}) collective-permute-start(bf16[384,768]{1,0:T(8,128)(2,1)S(1)} %get-tuple-element.97), channel_id=1, source_target_pairs={{0,8},{8,0},{16,24},{24,16},{1,9},{9,1},{17,25},{25,17},{2,10},{10... | collective-permute-start | bytes 1769480 | tf_op jit(solution)/shard_map/ppermute | solution.py:922
  20.1 33.2 %collective-permute-start.9 = (bf16[384,768]{1,0:T(8,128)(2,1)S(1)}, bf16[384,768]{1,0:T(8,128)(2,1)S(1)}, u32[]{:S(2)}, u32[]{:S(2)}) collective-permute-start(bf16[384,768]{1,0:T(8,128)(2,1)S(1)} %get-tuple-element.97), channel_id=1, source_target_pairs={{0,16},{8,24},{16,0},{24,8},{1,17},{9,25},{17,1},{25,9},{2,18},{10... | collective-permute-start | bytes 1769480 | tf_op jit(solution)/shard_map/ppermute | solution.py:922
  20.2 8.6 %collective-permute-start.3 = (bf16[4,32,576]{2,1,0:T(8,128)(2,1)S(1)}, bf16[4,32,576]{2,1,0:T(8,128)(2,1)S(1)}, u32[]{:S(2)}, u32[]{:S(2)}) collective-permute-start(bf16[4,32,576]{2,1,0:T(8,128)(2,1)S(1)} %get-tuple-element.121), channel_id=1, source_target_pairs={{0,2},{1,3},{2,0},{3,1},{4,6},{5,7},{6,4},{7,5},{8,10},{9,11},{10,... | collective-permute-start | bytes 442376 | tf_op jit(solution)/shard_map/ppermute | solution.py:927
  28.8 15.0 %collective-permute-start.4 = (bf16[4,32,576]{2,1,0:T(8,128)(2,1)S(1)}, bf16[4,32,576]{2,1,0:T(8,128)(2,1)S(1)}, u32[]{:S(2)}, u32[]{:S(2)}) collective-permute-start(bf16[4,32,576]{2,1,0:T(8,128)(2,1)S(1)} %get-tuple-element.121), channel_id=1, source_target_pairs={{0,4},{1,5},{2,6},{3,7},{4,0},{5,1},{6,2},{7,3},{8,12},{9,13},{10,... | collective-permute-start | bytes 442376 | tf_op jit(solution)/shard_map/ppermute | solution.py:927
  43.8 8.5 %collective-permute-start.5 = (bf16[4,32,576]{2,1,0:T(8,128)(2,1)S(1)}, bf16[4,32,576]{2,1,0:T(8,128)(2,1)S(1)}, u32[]{:S(2)}, u32[]{:S(2)}) collective-permute-start(bf16[4,32,576]{2,1,0:T(8,128)(2,1)S(1)} %get-tuple-element.121), channel_id=1, source_target_pairs={{0,6},{1,7},{2,4},{3,5},{4,2},{5,3},{6,0},{7,1},{8,14},{9,15},{10,... | collective-permute-start | bytes 442376 | tf_op jit(solution)/shard_map/ppermute | solution.py:927
  52.3 19.5 %copy-start = (bf16[768,768]{1,0:T(8,128)(2,1)S(1)}, bf16[768,768]{1,0:T(8,128)(2,1)}, u32[]{:S(2)}) copy-start(bf16[768,768]{1,0:T(8,128)(2,1)} %refs_1_.5) | copy-start | bytes 3538948
  52.5 0.8 copy-start.2
  53.3 0.8 copy-start.4
  54.1 4.7 %collective-permute-start.12 = (bf16[4,4,32,576]{3,2,1,0:T(8,128)(2,1)S(1)}, bf16[4,4,32,576]{3,2,1,0:T(8,128)(2,1)}, u32[]{:S(2)}, u32[]{:S(2)}) collective-permute-start(bf16[4,4,32,576]{3,2,1,0:T(8,128)(2,1)S(1)} %pad_maximum_fusion.refs_9_), channel_id=1, source_target_pairs={{0,1},{1,0},{2,3},{3,2},{4,5},{5,4},{6,7},{7,6},{8,9},{9,8},{10,11... | collective-permute-start | bytes 1769480 | tf_op jit(solution)/shard_map/ppermute | solution.py:927
  54.1 16.9 %collective-permute-start.10 = (bf16[384,768]{1,0:T(8,128)(2,1)}, bf16[384,768]{1,0:T(8,128)(2,1)}, u32[]{:S(2)}, u32[]{:S(2)}) collective-permute-start(bf16[384,768]{1,0:T(8,128)(2,1)} %collective-permute-done.6.refs_4_), channel_id=1, source_target_pairs={{0,8},{8,0},{16,24},{24,16},{1,9},{9,1},{17,25},{25,17},{2,10},{10... | collective-permute-start | bytes 1769480 | tf_op jit(solution)/shard_map/ppermute | solution.py:922
  55.8 15.9 %collective-permute-start.11 = (bf16[384,768]{1,0:T(8,128)(2,1)}, bf16[384,768]{1,0:T(8,128)(2,1)}, u32[]{:S(2)}, u32[]{:S(2)}) collective-permute-start(bf16[384,768]{1,0:T(8,128)(2,1)} %collective-permute-done.7.refs_3_), channel_id=1, source_target_pairs={{0,16},{8,24},{16,0},{24,8},{1,17},{9,25},{17,1},{25,9},{2,18},{10... | collective-permute-start | bytes 1769480 | tf_op jit(solution)/shard_map/ppermute | solution.py:922
  58.5 25.3 %copy-start.1 = (s32[4]{0:T(128)}, s32[4]{0:T(128)S(1)}, u32[]{:S(2)}) copy-start(s32[4]{0:T(128)S(1)} %pad_add_fusion.1.refs_0_.refs_2_) | copy-start | bytes 52
  71.8 1.1 copy-start.3
  72.8 1.1 copy-start.5
  83.8 1.0 copy-start.12
  84.9 28.4 %copy-start.9 = (bf16[3072,256]{1,0:T(8,128)(2,1)}, bf16[3072,256]{1,0:T(8,128)(2,1)S(1)}, u32[]{:S(2)}) copy-start(bf16[3072,256]{1,0:T(8,128)(2,1)S(1)} %get-tuple-element.58.refs_3_) | copy-start | bytes 4718596
  84.9 28.4 %copy-start.10 = (bf16[3072,256]{1,0:T(8,128)(2,1)}, bf16[3072,256]{1,0:T(8,128)(2,1)S(1)}, u32[]{:S(2)}) copy-start(bf16[3072,256]{1,0:T(8,128)(2,1)S(1)} %get-tuple-element.59.refs_4_) | copy-start | bytes 4718596
  84.9 28.5 %copy-start.11 = (bf16[3072,192]{1,0:T(8,128)(2,1)}, bf16[3072,192]{1,0:T(8,128)(2,1)S(1)}, u32[]{:S(2)}) copy-start(bf16[3072,192]{1,0:T(8,128)(2,1)S(1)} %get-tuple-element.60.refs_5_) | copy-start | bytes 3538948
  113.3 0.7 copy-start.13
  114.1 0.6 copy-start.14
  114.7 69.8 %copy-start.6 = (bf16[192,768]{1,0:T(8,128)(2,1)}, bf16[192,768]{1,0:T(8,128)(2,1)S(1)}, u32[]{:S(2)}) copy-start(bf16[192,768]{1,0:T(8,128)(2,1)S(1)} %get-tuple-element.62.refs_11_) | copy-start | bytes 884740
  114.7 69.8 %copy-start.7 = (bf16[192,768]{1,0:T(8,128)(2,1)}, bf16[192,768]{1,0:T(8,128)(2,1)S(1)}, u32[]{:S(2)}) copy-start(bf16[192,768]{1,0:T(8,128)(2,1)S(1)} %get-tuple-element.63.refs_12_) | copy-start | bytes 884740
  114.7 69.8 %copy-start.8 = (bf16[192,768]{1,0:T(8,128)(2,1)}, bf16[192,768]{1,0:T(8,128)(2,1)S(1)}, u32[]{:S(2)}) copy-start(bf16[192,768]{1,0:T(8,128)(2,1)S(1)} %get-tuple-element.64.refs_13_) | copy-start | bytes 884740
  114.7 9.9 %collective-permute-start.13 = (bf16[192,768]{1,0:T(8,128)(2,1)S(1)}, bf16[192,768]{1,0:T(8,128)(2,1)S(1)}, u32[]{:S(2)}, u32[]{:S(2)}) collective-permute-start(bf16[192,768]{1,0:T(8,128)(2,1)S(1)} %get-tuple-element.62.refs_11_), channel_id=1, source_target_pairs={{0,8},{8,0},{16,24},{24,16},{1,9},{9,1},{17,25},{25,17},{2,10},{10... | collective-permute-start | bytes 884744 | tf_op jit(solution)/shard_map/ppermute | solution.py:922
  115.0 14.0 %collective-permute-start.14 = (bf16[192,768]{1,0:T(8,128)(2,1)S(1)}, bf16[192,768]{1,0:T(8,128)(2,1)S(1)}, u32[]{:S(2)}, u32[]{:S(2)}) collective-permute-start(bf16[192,768]{1,0:T(8,128)(2,1)S(1)} %get-tuple-element.63.refs_12_), channel_id=1, source_target_pairs={{0,16},{8,24},{16,0},{24,8},{1,17},{9,25},{17,1},{25,9},{2,18},{10... | collective-permute-start | bytes 884744 | tf_op jit(solution)/shard_map/ppermute | solution.py:922
  116.8 13.8 %collective-permute-start.15 = (bf16[192,768]{1,0:T(8,128)(2,1)S(1)}, bf16[192,768]{1,0:T(8,128)(2,1)S(1)}, u32[]{:S(2)}, u32[]{:S(2)}) collective-permute-start(bf16[192,768]{1,0:T(8,128)(2,1)S(1)} %get-tuple-element.64.refs_13_), channel_id=1, source_target_pairs={{0,24},{8,16},{16,8},{24,0},{1,25},{9,17},{17,9},{25,1},{2,26},{10... | collective-permute-start | bytes 884744 | tf_op jit(solution)/shard_map/ppermute | solution.py:922
  124.6 5.9 %copy-start.25 = (bf16[192,768]{1,0:T(8,128)(2,1)}, bf16[192,768]{1,0:T(8,128)(2,1)S(1)}, u32[]{:S(2)}) copy-start(bf16[192,768]{1,0:T(8,128)(2,1)S(1)} %collective-permute-done.13.refs_4_) | copy-start | bytes 884740
  129.0 1.6 copy-start.26
  130.5 0.7 copy-start.27
  184.5 9.3 %collective-permute-start.16 = (bf16[4,4,224,768]{3,2,1,0:T(8,128)(2,1)}, bf16[4,4,224,768]{3,2,1,0:T(8,128)(2,1)S(1)}, u32[]{:S(2)}, u32[]{:S(2)}) collective-permute-start(bf16[4,4,224,768]{3,2,1,0:T(8,128)(2,1)} %get-tuple-element.68), channel_id=1, source_target_pairs={{0,1},{1,0},{2,3},{3,2},{4,5},{5,4},{6,7},{7,6},{8,9},{9,8},{10,11... | collective-permute-start | bytes 16515080 | tf_op jit(solution)/shard_map/ppermute | solution.py:927
  184.6 15.9 %collective-permute-start.17 = (bf16[192,768]{1,0:T(8,128)(2,1)}, bf16[192,768]{1,0:T(8,128)(2,1)S(1)}, u32[]{:S(2)}, u32[]{:S(2)}) collective-permute-start(bf16[192,768]{1,0:T(8,128)(2,1)} %get-tuple-element.70), channel_id=1, source_target_pairs={{0,8},{8,0},{16,24},{24,16},{1,9},{9,1},{17,25},{25,17},{2,10},{10... | collective-permute-start | bytes 884744 | tf_op jit(solution)/shard_map/ppermute | solution.py:922
  185.5 15.6 %collective-permute-start.18 = (bf16[192,768]{1,0:T(8,128)(2,1)}, bf16[192,768]{1,0:T(8,128)(2,1)S(1)}, u32[]{:S(2)}, u32[]{:S(2)}) collective-permute-start(bf16[192,768]{1,0:T(8,128)(2,1)} %get-tuple-element.71), channel_id=1, source_target_pairs={{0,16},{8,24},{16,0},{24,8},{1,17},{9,25},{17,1},{25,9},{2,18},{10... | collective-permute-start | bytes 884744 | tf_op jit(solution)/shard_map/ppermute | solution.py:922
  187.0 14.1 %collective-permute-start.19 = (bf16[192,768]{1,0:T(8,128)(2,1)}, bf16[192,768]{1,0:T(8,128)(2,1)S(1)}, u32[]{:S(2)}, u32[]{:S(2)}) collective-permute-start(bf16[192,768]{1,0:T(8,128)(2,1)} %get-tuple-element.72), channel_id=1, source_target_pairs={{0,24},{8,16},{16,8},{24,0},{1,25},{9,17},{17,9},{25,1},{2,26},{10... | collective-permute-start | bytes 884744 | tf_op jit(solution)/shard_map/ppermute | solution.py:922
  200.5 0.7 copy-start.22
  201.1 0.7 copy-start.23
  201.1 0.8 copy-start.24
  201.9 120.9 %reduce-scatter.5.cloned.1.call-start = ((), (), s32[]{:S(2)}) async-start(), calls=%async_computation.3 | async-start | bytes 1720320 | tf_op jit(solution)/shard_map/reduce_scatter | solution.py:1058
  271.8 2.2 collective-permute-start.24
  271.8 29.1 %collective-permute-start.20 = (bf16[768,768]{1,0:T(8,128)(2,1)}, bf16[768,768]{1,0:T(8,128)(2,1)}, u32[]{:S(2)}, u32[]{:S(2)}) collective-permute-start(bf16[768,768]{1,0:T(8,128)(2,1)} %get-tuple-element.82), channel_id=1, source_target_pairs={{0,8},{8,0},{16,24},{24,16},{1,9},{9,1},{17,25},{25,17},{2,10},{10... | collective-permute-start | bytes 3538952 | tf_op jit(solution)/shard_map/ppermute | solution.py:922
  272.6 32.3 %collective-permute-start.22 = (bf16[768,768]{1,0:T(8,128)(2,1)}, bf16[768,768]{1,0:T(8,128)(2,1)S(1)}, u32[]{:S(2)}, u32[]{:S(2)}) collective-permute-start(bf16[768,768]{1,0:T(8,128)(2,1)} %get-tuple-element.84), channel_id=1, source_target_pairs={{0,16},{8,24},{16,0},{24,8},{1,17},{9,25},{17,1},{25,9},{2,18},{10... | collective-permute-start | bytes 3538952 | tf_op jit(solution)/shard_map/ppermute | solution.py:922
  275.3 11.6 %collective-permute-start.25 = (bf16[4,24,768]{2,1,0:T(8,128)(2,1)S(1)}, bf16[4,24,768]{2,1,0:T(8,128)(2,1)S(1)}, u32[]{:S(2)}, u32[]{:S(2)}) collective-permute-start(bf16[4,24,768]{2,1,0:T(8,128)(2,1)S(1)} %get-tuple-element.105), channel_id=1, source_target_pairs={{0,2},{1,3},{2,0},{3,1},{4,6},{5,7},{6,4},{7,5},{8,10},{9,11},{10,... | collective-permute-start | bytes 442376 | tf_op jit(solution)/shard_map/ppermute | solution.py:927
  276.4 19.6 %collective-permute-start.26 = (bf16[4,24,768]{2,1,0:T(8,128)(2,1)S(1)}, bf16[4,24,768]{2,1,0:T(8,128)(2,1)S(1)}, u32[]{:S(2)}, u32[]{:S(2)}) collective-permute-start(bf16[4,24,768]{2,1,0:T(8,128)(2,1)S(1)} %get-tuple-element.107), channel_id=1, source_target_pairs={{0,4},{1,5},{2,6},{3,7},{4,0},{5,1},{6,2},{7,3},{8,12},{9,13},{10,... | collective-permute-start | bytes 442376 | tf_op jit(solution)/shard_map/ppermute | solution.py:927
  277.9 18.1 %collective-permute-start.27 = (bf16[4,24,768]{2,1,0:T(8,128)(2,1)S(1)}, bf16[4,24,768]{2,1,0:T(8,128)(2,1)S(1)}, u32[]{:S(2)}, u32[]{:S(2)}) collective-permute-start(bf16[4,24,768]{2,1,0:T(8,128)(2,1)S(1)} %get-tuple-element.106), channel_id=1, source_target_pairs={{0,6},{1,7},{2,4},{3,5},{4,2},{5,3},{6,0},{7,1},{8,14},{9,15},{10,... | collective-permute-start | bytes 442376 | tf_op jit(solution)/shard_map/ppermute | solution.py:927
  296.1 10.6 %collective-permute-start.28 = (f32[24,768]{1,0:T(8,128)S(1)}, f32[24,768]{1,0:T(8,128)S(1)}, u32[]{:S(2)}, u32[]{:S(2)}) collective-permute-start(f32[24,768]{1,0:T(8,128)S(1)} %get-tuple-element.119), channel_id=1, source_target_pairs={{0,8},{8,0},{16,24},{24,16},{1,9},{9,1},{17,25},{25,17},{2,10},{10... | collective-permute-start | bytes 221192 | tf_op jit(solution)/shard_map/ppermute | solution.py:922
  296.2 10.5 %collective-permute-start.29 = (f32[24,768]{1,0:T(8,128)S(1)}, f32[24,768]{1,0:T(8,128)S(1)}, u32[]{:S(2)}, u32[]{:S(2)}) collective-permute-start(f32[24,768]{1,0:T(8,128)S(1)} %get-tuple-element.118), channel_id=1, source_target_pairs={{0,16},{8,24},{16,0},{24,8},{1,17},{9,25},{17,1},{25,9},{2,18},{10... | collective-permute-start | bytes 221192 | tf_op jit(solution)/shard_map/ppermute | solution.py:922
  296.3 10.4 %collective-permute-start.30 = (f32[24,768]{1,0:T(8,128)S(1)}, f32[24,768]{1,0:T(8,128)S(1)}, u32[]{:S(2)}, u32[]{:S(2)}) collective-permute-start(f32[24,768]{1,0:T(8,128)S(1)} %get-tuple-element.117), channel_id=1, source_target_pairs={{0,24},{8,16},{16,8},{24,0},{1,25},{9,17},{17,9},{25,1},{2,26},{10... | collective-permute-start | bytes 221192 | tf_op jit(solution)/shard_map/ppermute | solution.py:922
  300.2 2.2 copy-start.20
  303.4 1.6 copy-start.19
  303.4 14.8 %collective-permute-start.21 = (bf16[384,768]{1,0:T(8,128)(2,1)}, bf16[384,768]{1,0:T(8,128)(2,1)}, u32[]{:S(2)}, u32[]{:S(2)}) collective-permute-start(bf16[384,768]{1,0:T(8,128)(2,1)} %fusion.1), channel_id=1, source_target_pairs={{0,16},{8,24},{16,0},{24,8},{1,17},{9,25},{17,1},{25,9},{2,18},{10... | collective-permute-start | bytes 1769480 | tf_op jit(solution)/shard_map/ppermute | solution.py:922
  305.1 1.6 copy-start.15
  306.7 14.4 %collective-permute-start.23 = (bf16[384,768]{1,0:T(8,128)(2,1)}, bf16[384,768]{1,0:T(8,128)(2,1)S(1)}, u32[]{:S(2)}, u32[]{:S(2)}) collective-permute-start(bf16[384,768]{1,0:T(8,128)(2,1)} %fusion), channel_id=1, source_target_pairs={{0,8},{8,0},{16,24},{24,16},{1,9},{9,1},{17,25},{25,17},{2,10},{10... | collective-permute-start | bytes 1769480 | tf_op jit(solution)/shard_map/ppermute | solution.py:922
  308.5 12.6 %copy-start.16 = (f32[768,768]{1,0:T(8,128)S(1)}, f32[768,768]{1,0:T(8,128)}, u32[]{:S(2)}) copy-start(f32[768,768]{1,0:T(8,128)} %copy-done.15) | copy-start | bytes 7077892
  319.4 1.8 copy-start.18
  322.8 2.2 copy-start.17
Sparse Core Ops, SparseCore 0:
  11.0 102.6 all-gather.2
  201.3 62.9 reduce-scatter.2
  275.4 38.6 reduce-scatter.4

commit v5 on v4

--- a/solution.py
+++ b/solution.py
@@ -180,7 +180,8 @@
 
 def backward_kernel(
     heads, start_ref, number_ref, me_ref, q_ref, k_ref, v_ref,
-    g0_ref, g1_ref, g2_ref, g3_ref, o0_ref, o1_ref, o2_ref, o3_ref, lse_ref, x_ref, w_ref, gh1_ref,
+    g0_ref, g1_ref, g2_ref, g3_ref, o0_ref, o1_ref, o2_ref, o3_ref, lse_ref,
+    x0_ref, x1_ref, x2_ref, x3u_ref, x3l_ref, w_ref, gh1_ref,
     sx_ref, sy_ref, mine_ref, low_ref, up_ref, kept_ref, sent_ref,
     qt, gt, dqt, delta, dkt, dvt, kh, vh, turned, grads, rows_ref,
 ):
@@ -302,7 +303,7 @@
             return carry
 
         lax.fori_loop(0, 4, back, 0)
-        model = x_ref.shape[1]
+        model = x0_ref.shape[1]
         columns, _, own = kept_ref.shape[:3]
         shards = 2 * columns
         lane = lax.broadcasted_iota(jnp.int32, (128, width), 1)
@@ -315,7 +316,14 @@
         for j, c in enumerate((0, 2)):
             sums = mm(ones, grads[c])[:1]
             rows_ref[:, j, :] = mm_nt(jnp.where(lane // own == row, sums, 0.0).astype(bf16), tile)
-        value = mm(turned[...], x_ref[...]).T.astype(bf16).reshape(4 * shards, own, 3 * width)
+        total = jnp.zeros((3 * width, model), f32)
+        for r, parts in enumerate(((x0_ref,), (x1_ref,), (x2_ref,), (x3u_ref, x3l_ref))):
+            first = lax.bitwise_xor(me, r) * own_rows
+            for part_ref in parts:
+                count = part_ref.shape[0]
+                total = total + mm(turned[:, pl.ds(pl.multiple_of(first, 128), count)], part_ref[...])
+                first = first + count
+        value = total.T.astype(bf16).reshape(4 * shards, own, 3 * width)
         for core in range(2):
 
             @pl.when(me_ref[3] == core)
@@ -335,6 +343,7 @@
     width = heads * HEAD
     steps = seq // BK
     own_rows, model = gh1.shape
+    half = own_rows // 2
     own = model // pieces
     once = dict(pipeline_mode=pl.Buffered(1))
     whole = lambda a: pl.BlockSpec(a, lambda i, a_, b_, m_: (0,) * len(a), **once)
@@ -354,7 +363,10 @@
                 pl.BlockSpec((BK, width), lambda i, a, b, m: (i, 0)),
             ]
             + [whole((width, own_rows))] * 8
-            + [whole((8, seq)), whole((seq, model)), whole((3, model, width)), whole((own_rows, model))],
+            + [whole((8, seq))]
+            + [whole((own_rows, model))] * 3
+            + [whole((half, model))] * 2
+            + [whole((3, model, width)), whole((own_rows, model))],
             out_specs=[
                 whole((own_rows, model)),
                 whole((own_rows, model)),
@@ -390,7 +402,7 @@
         cost_estimate=cost,
         compiler_params=pltpu.CompilerParams(vmem_limit_bytes=60 << 20),
         name="attend_backward",
-    )(starts, numbers, place, q, k, v, *g, *o, lse, x, w, gh1)
+    )(starts, numbers, place, q, k, v, *g, *o, lse, *x, w, gh1)
 
 
 def pack_kernel(ratio, groups, me_ref, down_ref, up_ref, out_ref, qkv_ref, *refs):
@@ -447,17 +459,33 @@
     return packed, jnp.concatenate([block, jnp.broadcast_to(rows, (groups, 8, 3 * width))], 1)
 
 
+def project_block(heads, x_ref, first, seg_ref, bias_ref, w_ref, q_ref, k_ref, v_ref):
+    size = 384
+    width = heads * HEAD
+    wide = q_ref.shape[1]
+
+    def part(i, carry):
+        x = x_ref[pl.ds(pl.multiple_of(i * size, size), size), :]
+        at = pl.ds(pl.multiple_of(first + i * size, size), size)
+        lane = lax.broadcasted_iota(jnp.int32, (size, wide - width), 1)
+        same = lane == seg_ref[at, :]
+        q = (mm(x, w_ref[0]) + bias_ref[0:1, :]).astype(bf16)
+        q_ref[at, :width] = q * jnp.asarray(0.125, bf16)
+        q_ref[at, width:] = jnp.where(same, 1.0, 0.0).astype(bf16)
+        k_ref[at, :width] = mm(x, w_ref[1]).astype(bf16)
+        k_ref[at, width:] = jnp.where(same, 0.0, -far).astype(bf16)
+        v_ref[at, :] = (mm(x, w_ref[2]) + bias_ref[1:2, :]).astype(bf16)
+        return carry
+
+    lax.fori_loop(0, x_ref.shape[0] // size, part, 0)
+
+
 def project_kernel(
-    heads, me_ref, x0_ref, x1u_ref, x1l_ref, x2u_ref, x2l_ref, x3u_ref, x3l_ref, seg_ref, near_ref, far_ref,
-    q_ref, k_ref, v_ref, all_ref, wide_w, rows_ref, bias_ref,
+    heads, me_ref, x0_ref, x1_ref, x2_ref, seg_ref, near_ref, far_ref,
+    q_ref, k_ref, v_ref, wide_w, bias_ref, rows_ref,
 ):
     step = pl.program_id(0)
-    rows = x0_ref.shape[0]
-    half = rows // 2
     width = heads * HEAD
-    wide = q_ref.shape[1]
-    slot = lax.bitwise_xor(step, me_ref[0])
-
     own = near_ref.shape[2] - 8
     columns, groups = near_ref.shape[:2]
 
@@ -479,37 +507,21 @@
         tile = jnp.where(lax.rem(lane, own) == row, 1.0, 0.0).astype(bf16)
         lane = lax.broadcasted_iota(jnp.int32, (2 * columns, width), 1)
         row = lax.broadcasted_iota(jnp.int32, (2 * columns, width), 0)
+        bias_ref[...] = jnp.zeros_like(bias_ref)
         for k in range(2):
             value = jnp.where(lane // own == row, mm(rows_ref[k].astype(bf16), tile), 0.0)
             bias_ref[k : k + 1, :] = jnp.sum(value, 0, keepdims=True)
 
-    @pl.when(slot == 0)
-    def _():
-        all_ref[...] = x0_ref[...]
-
-    for k, upper, lower in ((1, x1u_ref, x1l_ref), (2, x2u_ref, x2l_ref), (3, x3u_ref, x3l_ref)):
-
-        @pl.when(slot == k)
+    for k, part_ref in ((0, x0_ref), (1, x1_ref), (2, x2_ref)):
+
+        @pl.when(step == k)
         def _():
-            all_ref[:half] = upper[...]
-            all_ref[half:] = lower[...]
-
-    size = 256
-
-    def part(i, carry):
-        at = pl.ds(pl.multiple_of(i * size, size), size)
-        x = all_ref[at, :]
-        lane = lax.broadcasted_iota(jnp.int32, (size, wide - width), 1)
-        same = lane == seg_ref[at, :]
-        q = (mm(x, wide_w[0]) + bias_ref[0:1, :]).astype(bf16)
-        q_ref[at, :width] = q * jnp.asarray(0.125, bf16)
-        q_ref[at, width:] = jnp.where(same, 1.0, 0.0).astype(bf16)
-        k_ref[at, :width] = mm(x, wide_w[1]).astype(bf16)
-        k_ref[at, width:] = jnp.where(same, 0.0, -far).astype(bf16)
-        v_ref[at, :] = (mm(x, wide_w[2]) + bias_ref[1:2, :]).astype(bf16)
-        return carry
-
-    lax.fori_loop(0, rows // size, part, 0)
+            project_block(heads, part_ref, 0, seg_ref, bias_ref, wide_w, q_ref, k_ref, v_ref)
+
+
+def project_last_kernel(heads, me_ref, upper_ref, lower_ref, seg_ref, w_ref, bias_ref, *refs):
+    project_block(heads, upper_ref, 0, seg_ref, bias_ref, w_ref, *refs[-3:])
+    project_block(heads, lower_ref, upper_ref.shape[0], seg_ref, bias_ref, w_ref, *refs[-3:])
 
 
 def project(place, blocks, seg_row, near, away, heads):
@@ -519,46 +531,98 @@
     seq = 4 * own_rows
     once = dict(pipeline_mode=pl.Buffered(1))
     fixed = lambda a: pl.BlockSpec(a, lambda s, m: (0,) * len(a), **once)
-    cost = pl.CostEstimate(
-        flops=6 * seq * model * width, bytes_accessed=4 * seq * (model + wide), transcendentals=0
-    )
-    return pl.pallas_call(
+
+    def rows_of(slot):
+        at = lambda s, m: (lax.bitwise_xor(s + slot, m[0]), 0)
+        return [pl.BlockSpec((own_rows, n), at) for n in (1, wide, wide, width)]
+
+    def cost(part):
+        return pl.CostEstimate(
+            flops=6 * part * own_rows * model * width,
+            bytes_accessed=4 * part * own_rows * (model + wide),
+            transcendentals=0,
+        )
+
+    params = pltpu.CompilerParams(vmem_limit_bytes=40 << 20)
+    arrays = [
+        jax.ShapeDtypeStruct((seq, wide), bf16),
+        jax.ShapeDtypeStruct((seq, wide), bf16),
+        jax.ShapeDtypeStruct((seq, width), bf16),
+    ]
+    segments = seg_row[:, None]
+    *made, weights, biases = pl.pallas_call(
         lambda *refs: project_kernel(heads, *refs),
         grid_spec=pltpu.PrefetchScalarGridSpec(
             num_scalar_prefetch=1,
-            grid=(4,),
-            in_specs=[
-                fixed((own_rows, model)),
-            ]
-            + [fixed((own_rows // 2, model))] * 6
-            + [
-                pl.BlockSpec((own_rows, 1), lambda s, m: (s, 0)),
-                fixed(near.shape),
-                fixed(near.shape),
-            ],
-            out_specs=[
-                pl.BlockSpec((own_rows, wide), lambda s, m: (s, 0)),
-                pl.BlockSpec((own_rows, wide), lambda s, m: (s, 0)),
-                pl.BlockSpec((own_rows, width), lambda s, m: (s, 0)),
-                pl.BlockSpec((own_rows, model), lambda s, m: (s, 0)),
-                fixed((3, model, width)),
-            ],
-            scratch_shapes=[
-                pltpu.VMEM((2, 2 * near.shape[0], 128), f32),
-                pltpu.VMEM((8, width), f32),
-            ],
+            grid=(3,),
+            in_specs=[fixed((own_rows, model))] * 3 + rows_of(0)[:1] + [fixed(near.shape)] * 2,
+            out_specs=rows_of(0)[1:] + [fixed((3, model, width)), fixed((8, width))],
+            scratch_shapes=[pltpu.VMEM((2, 2 * near.shape[0], 128), f32)],
         ),
-        out_shape=[
-            jax.ShapeDtypeStruct((seq, wide), bf16),
-            jax.ShapeDtypeStruct((seq, wide), bf16),
-            jax.ShapeDtypeStruct((seq, width), bf16),
-            jax.ShapeDtypeStruct((seq, model), bf16),
-            jax.ShapeDtypeStruct((3, model, width), bf16),
-        ],
-        cost_estimate=cost,
-        compiler_params=pltpu.CompilerParams(vmem_limit_bytes=40 << 20),
+        out_shape=arrays
+        + [jax.ShapeDtypeStruct((3, model, width), bf16), jax.ShapeDtypeStruct((8, width), f32)],
+        cost_estimate=cost(3),
+        compiler_params=params,
         name="project",
-    )(place, *blocks, seg_row[:, None], near, away)
+    )(place, *blocks[:3], segments, near, away)
+    made = pl.pallas_call(
+        lambda *refs: project_last_kernel(heads, *refs),
+        grid_spec=pltpu.PrefetchScalarGridSpec(
+            num_scalar_prefetch=1,
+            grid=(1,),
+            in_specs=[fixed((own_rows // 2, model))] * 2
+            + rows_of(3)[:1]
+            + [fixed((3, model, width)), fixed((8, width))]
+            + [pl.BlockSpec(memory_space=pl.ANY)] * 3,
+            out_specs=rows_of(3)[1:],
+        ),
+        out_shape=arrays,
+        input_output_aliases={6: 0, 7: 1, 8: 2},
+        cost_estimate=cost(1),
+        compiler_params=params,
+        name="project_last",
+    )(place, *blocks[3:], segments, weights, biases, *made)
+    return *made, weights
+
+
+def finish_kernel(ratio, place_ref, *refs):
+    head_refs, reduced_ref = refs[:4], refs[4]
+    qkv_ref, down_ref, up_ref, out_ref = refs[5:9]
+    vector_refs, query_ref, value_ref = refs[9:16], refs[16], refs[17]
+    own, model = out_ref.shape
+    width = model // 4
+    at = ratio * own
+    for m in range(4):
+
+        @pl.when(place_ref[1] == m)
+        def _():
+            for r in range(4):
+                for c in range(3):
+                    spot = c * model + (m ^ r) * width
+                    qkv_ref[:, spot : spot + width] = head_refs[r][:, c * width : (c + 1) * width]
+
+    down_ref[...] = reduced_ref[:at].astype(f32)
+    for c in range(ratio):
+        up_ref[:, c * model : (c + 1) * model] = reduced_ref[at + c * own : at + (c + 1) * own].astype(f32)
+    out_ref[...] = reduced_ref[2 * at : 2 * at + own].astype(f32)
+    lines = reduced_ref[2 * at + own :].astype(f32)
+    for j, ref in enumerate(vector_refs):
+        ref[...] = lines[j : j + 1, : ref.shape[1]]
+    for j, ref in enumerate((query_ref, value_ref)):
+        ref[...] = head_refs[0][j : j + 1, model - 128 : model - 128 + own]
+
+
+def finish(place, by_head, reduced, ratio):
+    own, model = by_head[0].shape
+    vmem = pl.BlockSpec(memory_space=pltpu.VMEM)
+    shapes = [(own, 3 * model), (ratio * own, model), (own, ratio * model), (own, model)]
+    shapes += [(1, own)] * 6 + [(1, ratio * own)] + [(1, own)] * 2
+    return pl.pallas_call(
+        lambda *refs: finish_kernel(ratio, *refs),
+        in_specs=[pl.BlockSpec(memory_space=pltpu.SMEM)] + [vmem] * 5,
+        out_shape=[jax.ShapeDtypeStruct(shape, f32) for shape in shapes],
+        name="finish",
+    )(place, *by_head, reduced)
 
 
 def normal_rows(z):
@@ -1005,15 +1069,15 @@
     direct = pieces == devices
 
     half = rows // 2
-    first = by_sp(tokens[:half], 2), by_sp(tokens[half:], 1)
-    second = by_sp(tokens[:half], 1), by_sp(tokens[half:], 2)
     vectors = [b_out, ln1_gain, ln1_bias, b_down, ln2_gain, ln2_bias, b_up]
     if direct:
         packed, mine = pack(me, w_down, w_up, w_out, w_qkv, vectors, b_query, b_value, groups)
         mine = jnp.stack([mine[0]] + [by_sp(mine[r], r) for r in range(1, groups)])
+        mine, moved = lax.optimization_barrier((mine, tokens))
+        along_x, along_y = by_sp(moved, 1), by_sp(moved, 2)
         near = jnp.stack([mine] + [by_fsdp(mine, 2 * z) for z in range(1, shards // 2)])
-        near, first, second = lax.optimization_barrier((near, first, second))
-        away = by_fsdp(near, 1)
+        sent, along_x, along_y = lax.optimization_barrier((near, along_x, along_y))
+        away = by_fsdp(sent, 1)
         column = (lax.axis_index("fsdp").astype(jnp.int32) // 2).reshape(1)
         order = jnp.concatenate([me, me, column, core])
     else:
@@ -1030,9 +1094,10 @@
         mine = mine.reshape(groups, 4, 2, cut + 8, 3 * width).transpose(2, 1, 0, 3, 4)
         near, away = mine[0], mine[1]
         order = jnp.concatenate([me, jnp.zeros((3,), jnp.int32)])
-    blocks = tokens, second[0], first[1], first[0], second[1], by_sp(first[0], 1), by_sp(first[1], 2)
+        along_x, along_y = by_sp(tokens, 1), by_sp(tokens, 2)
+    blocks = tokens, along_x, along_y, by_sp(along_y[:half], 1), by_sp(along_x[half:], 2)
     packed_weights = repack(lax.all_gather(packed, both, axis=0, tiled=False), ratio, pieces)
-    queries, keys, values, tokens_all, weights = project(
+    queries, keys, values, weights = project(
         order, blocks, seg_row, near, away, heads_local
     )
     forward_start, forward_number = windows(seg_row, FQ, FK, 128)
@@ -1057,7 +1122,7 @@
     cores = [[2 * i + c for i in range(shards // 2)] for c in range(2)]
     reduced = lax.psum_scatter(
         total, "fsdp", scatter_dimension=0, tiled=True, axis_index_groups=cores
-    ).astype(f32)
+    )
 
     *parts, kept, sent = attend_backward(
         queries,
@@ -1069,7 +1134,7 @@
         backward_start,
         backward_number,
         order,
-        tokens_all,
+        blocks,
         weights,
         grad_h1,
         pieces,
@@ -1080,10 +1145,10 @@
         total = (kept.astype(f32) + by_fsdp(sent, 1).astype(f32)).astype(bf16)
         moved = [by_fsdp(total[z], 2 * z).astype(f32) for z in range(1, shards // 2)]
         total = sum(moved, total[0].astype(f32))
-        by_head = jnp.stack([total[0]] + [by_sp(total[r], r) for r in range(1, groups)])
-        bias_sums = total[0, :2, model - 128 : model - 128 + own]
-        by_head = [lax.dynamic_index_in_dim(by_head, me[0] ^ g, keepdims=False) for g in range(groups)]
-        by_head = jnp.stack([item[:, : 3 * width].reshape(own, 3, width) for item in by_head], 2)
+        by_head = [total[0]] + [by_sp(total[r], r) for r in range(1, groups)]
+        weights = finish(order, by_head, reduced, ratio)
+        vectors = [item.reshape(-1) for item in weights[4:]]
+        owned_qkv, owned_down, owned_up, owned_out = weights[:4]
     else:
         cut = model // pieces
         halves = jnp.stack([kept, sent], 2).transpose(1, 0, 2, 3, 4).reshape(pieces, cut, model)
@@ -1096,28 +1161,26 @@
         halves = jnp.sum(halves.reshape(groups, shards, own + 8, 3 * width).astype(f32), 1)
         bias_sums = lax.dynamic_slice(halves, (me[0], own, 0), (1, 2, own))[0]
         by_head = halves[:, :own].reshape(groups, own, 3, width).transpose(1, 2, 0, 3)
-    owned_qkv = by_head.reshape(own, 3 * model)
-    grad_query_bias = bias_sums[0]
-    grad_value_bias = bias_sums[1]
-    at = ratio * own
-    owned_up = reduced[at : 2 * at].reshape(ratio, own, model).transpose(1, 0, 2).reshape(own, hidden)
-    tail = reduced[2 * at + own :]
+        owned_qkv = by_head.reshape(own, 3 * model)
+        at = ratio * own
+        reduced = reduced.astype(f32)
+        owned_up = reduced[at : 2 * at].reshape(ratio, own, model).transpose(1, 0, 2)
+        owned_up = owned_up.reshape(own, hidden)
+        owned_down, owned_out = reduced[:at], reduced[2 * at : 2 * at + own]
+        tail = reduced[2 * at + own :]
+        vectors = [tail[i, :own] for i in range(6)] + [tail[6, :at], bias_sums[0], bias_sums[1]]
     return (
         output,
         grad_input,
         owned_qkv,
-        grad_query_bias,
-        grad_value_bias,
-        reduced[2 * at : 2 * at + own],
-        tail[0, :own],
-        tail[1, :own],
-        tail[2, :own],
+        vectors[7],
+        vectors[8],
+        owned_out,
+        *vectors[:3],
         owned_up,
-        tail[6, :at],
-        reduced[:at],
-        tail[3, :own],
-        tail[4, :own],
-        tail[5, :own],
+        vectors[6],
+        owned_down,
+        *vectors[3:6],
     )
 
 

time: 340 us -> 321 us (0.944); the launches traced: 334 us -> 320 us
  local copies, waits for them, and re-layouts: 16.3 us -> 9.57 us
  other arithmetic: 17.9 us -> 11.3 us
  waiting for transfers between devices: 84.5 us -> 88.7 us
  starting transfers between devices: 38.4 us -> 34.5 us
    ppermute x22 -> x20, waiting for transfers between devices: 37.6 us -> 64.8 us  [by_sp(): return lax.ppermute(value, 'sp', [(i, i ^ flip) for i in range(groups)])]
    ppermute x9, waiting for transfers between devices: 46.9 us -> 23.9 us  [by_fsdp(): return lax.ppermute(value, 'fsdp', [(i, i ^ flip) for i in range(shards)])]
    ppermute x22 -> x20, starting transfers between devices: 26 us -> 21.9 us  [by_sp(): return lax.ppermute(value, 'sp', [(i, i ^ flip) for i in range(groups)])]
    pallas_call x0 -> x2, Pallas kernels: none -> 3.85 us  [the longest x1 2.2 us: finish(): pl.pallas_call(lambda *refs: finish_kernel(ratio, *refs), in_specs=[pl.Bl...]
    pallas_call x1, Pallas kernels: 9.95 us -> 6.13 us  [project(): pl.pallas_call(lambda *refs: project_kernel(heads, *refs), grid_spec=pltp...]
    unnamed x56 -> x62, local copies, waits for them, and re-layouts: 8.2 us -> 5.92 us
  transfers between devices with their start and end apart: 34 -> 32, of which waited for: 16 -> 17; matrix products, arithmetic and copies ran while one was open for 7% -> 5% of each run, Pallas kernels for 32% -> 33%
where the time goes in v5:
time: 321 us; the launch traced here: 320 us
  Pallas kernels  161 us (50%)
  waiting for transfers between devices  88.7 us (28%)
  starting transfers between devices  34.5 us (11%)
  between operations  14.2 us (4%)
  other arithmetic  11.3 us (4%)
  local copies, waits for them, and re-layouts  9.57 us (3%)
    pallas_call x1, Pallas kernels, attend_backward(): pl.pallas_call(lambda *refs: backward_kernel(heads, *refs), grid_spec=plt...  69 us
    ppermute x20, waiting for transfers between devices, by_sp(): return lax.ppermute(value, 'sp', [(i, i ^ flip) for i in range(groups)])  64.8 us
    pallas_call x1, Pallas kernels, middle(): pl.pallas_call(lambda *refs: middle_kernel(groups, chunks, *refs), grid=(...  53.2 us
    pallas_call x1, Pallas kernels, attend_forward(): pl.pallas_call(lambda *refs: forward_kernel(heads, *refs), grid_spec=pltp...  27.2 us
    ppermute x9, waiting for transfers between devices, by_fsdp(): return lax.ppermute(value, 'fsdp', [(i, i ^ flip) for i in range(shards)])  23.9 us
    ppermute x20, starting transfers between devices, by_sp(): return lax.ppermute(value, 'sp', [(i, i ^ flip) for i in range(groups)])  21.9 us
    ppermute x9, starting transfers between devices, by_fsdp(): return lax.ppermute(value, 'fsdp', [(i, i ^ flip) for i in range(shards)])  12.5 us
    convert_element_type x1, other arithmetic, body(): total = (kept.astype(f32) + partner.astype(f32)).astype(bf16)  6.65 us
  transfers between devices with their start and end apart: 32, of which 17 were waited for; matrix products, arithmetic and copies ran while one was open for 5% of the time, Pallas kernels for 33%

profile of v5, /device:TPU:0, one launch (start us, length us, event | category | flops | bytes accessed | tf_op | source)
XLA Modules:
  0.0 319.6 jit_solution(8465681728792478828)
XLA Ops:
  7.2 1.9 pack.1
  9.3 0.9 fusion.10
  10.1 3.0 collective-permute-start
  13.1 1.5 collective-permute-start.1
  14.7 0.4 collective-permute-done
  15.1 2.0 collective-permute-done.1
  17.1 2.4 collective-permute-done.2
  19.6 0.6 collective-permute-start.6
  20.2 2.0 collective-permute-start.3
  22.3 2.6 collective-permute-start.4
  24.9 5.5 %collective-permute-done.3 = bf16[4,32,576]{2,1,0:T(8,128)(2,1)S(1)} collective-permute-done((bf16[4,32,576]{2,1,0:T(8,128)(2,1)S(1)}, bf16[4,32,576]{2,1,0:T(8,128)(2,1)S(1)}, u32[]{:S(2)}, u32[]{:S(2)}) %collective-permute-start.3) | collective-permute-done | bytes 147488 | tf_op jit(solution)/shard_map/ppermute | solution.py:991
  30.4 12.0 %collective-permute-done.4 = bf16[4,32,576]{2,1,0:T(8,128)(2,1)S(1)} collective-permute-done((bf16[4,32,576]{2,1,0:T(8,128)(2,1)S(1)}, bf16[4,32,576]{2,1,0:T(8,128)(2,1)S(1)}, u32[]{:S(2)}, u32[]{:S(2)}) %collective-permute-start.4) | collective-permute-done | bytes 147488 | tf_op jit(solution)/shard_map/ppermute | solution.py:991
  42.5 5.8 %collective-permute-done.6.refs_2_.refs_16_ = bf16[768,768]{1,0:T(8,128)(2,1)S(1)} collective-permute-done((bf16[768,768]{1,0:T(8,128)(2,1)}, bf16[768,768]{1,0:T(8,128)(2,1)S(1)}, u32[]{:S(2)}, u32[]{:S(2)}) %collective-permute-start.6) | collective-permute-done | bytes 1179680 | tf_op jit(solution)/shard_map/ppermute | solution.py:986
  48.3 0.5 collective-permute-done.7.refs_3_.refs_17_
  49.0 0.5 copy.37.refs_4_.refs_3_
  49.5 1.2 slice.72
  50.7 1.4 collective-permute-start.8
  52.2 0.7 collective-permute-start.9
  53.3 1.1 copy-done.5
  54.3 1.3 copy-done.9
  55.6 6.1 %project.1 = (bf16[3072,256]{1,0:T(8,128)(2,1)S(1)}, bf16[3072,256]{1,0:T(8,128)(2,1)S(1)}, bf16[3072,192]{1,0:T(8,128)(2,1)S(1)}, bf16[3,768,192]{2,1,0:T(8,128)(2,1)S(1)}, f32[8,192]{1,0:T(8,128)S(1)}) custom-call(s32[4]{0:T(128)S(1)} %pad_add_fusion.1.refs_0_.refs_2_, bf16[768,768]{1,0:T(8,128)(2,1)S(1)} %copy-done.11, bf16[768,768]{1,0:T(8,128)(2,1)S(1)} %copy-done.9, ...), custom_call_target="tpu_custom_call" | custom-call | flops 2038431744 | bytes 9437184 | tf_op jit(solution)/shard_map/project/pallas_call | solution.py:553
  61.8 11.4 %collective-permute-done.8.refs_1_.refs_18_ = bf16[384,768]{1,0:T(8,128)(2,1)S(1)} collective-permute-done((bf16[384,768]{1,0:T(8,128)(2,1)S(1)}, bf16[384,768]{1,0:T(8,128)(2,1)S(1)}, u32[]{:S(2)}, u32[]{:S(2)}) %collective-permute-start.8) | collective-permute-done | bytes 589856 | tf_op jit(solution)/shard_map/ppermute | solution.py:986
  73.1 1.6 project_last.1
  74.9 27.2 %attend_forward.1 = (bf16[192,768]{1,0:T(8,128)(2,1)S(1)}, bf16[192,768]{1,0:T(8,128)(2,1)S(1)}, bf16[192,768]{1,0:T(8,128)(2,1)S(1)}, bf16[192,768]{1,0:T(8,128)(2,1)S(1)}, f32[8,3072]{1,0:T(8,128)S(1)}) custom-call(s32[6]{0:T(128)S(1)} %get-tuple-element.127.refs_0_, s32[6]{0:T(128)S(1)} %get-tuple-element.128.refs_1_, s32[1]{0:T(128)} %bitcast.1.refs_0_.refs_2_, ...), custom_call_target="tpu_custom_call" | custom-call | flops 3623878656 | bytes 6291456 | tf_op jit(solution)/shard_map/attend_forward/pallas_call | solution.py:144
  102.1 0.7 copy-done.15
  102.8 0.6 copy-done.16
  103.5 0.3 collective-permute-start.11
  103.8 1.7 collective-permute-start.12
  105.5 1.5 collective-permute-start.13
  107.0 0.6 pad_add_fusion.refs_0_
  107.6 5.8 %collective-permute-done.11.refs_4_ = bf16[192,768]{1,0:T(8,128)(2,1)S(1)} collective-permute-done((bf16[192,768]{1,0:T(8,128)(2,1)S(1)}, bf16[192,768]{1,0:T(8,128)(2,1)S(1)}, u32[]{:S(2)}, u32[]{:S(2)}) %collective-permute-start.11) | collective-permute-done | bytes 294944 | tf_op jit(solution)/shard_map/ppermute | solution.py:986
  113.3 6.4 %collective-permute-done.13.refs_6_ = bf16[192,768]{1,0:T(8,128)(2,1)S(1)} collective-permute-done((bf16[192,768]{1,0:T(8,128)(2,1)S(1)}, bf16[192,768]{1,0:T(8,128)(2,1)S(1)}, u32[]{:S(2)}, u32[]{:S(2)}) %collective-permute-start.13) | collective-permute-done | bytes 294944 | tf_op jit(solution)/shard_map/ppermute | solution.py:986
  119.7 0.7 copy-done.30
  120.5 53.2 %middle.1 = (bf16[768,768]{1,0:T(8,128)(2,1)}, f32[768,768]{1,0:T(8,128)}, bf16[192,768]{1,0:T(8,128)(2,1)}, bf16[192,768]{1,0:T(8,128)(2,1)}, bf16[192,768]{1,0...) custom-call(s32[2]{0:T(128)} %pad_add_fusion.refs_0_, ...), custom_call_target="tpu_custom_call" | custom-call | flops 24461180928 | bytes 28311552 | tf_op jit(solution)/shard_map/middle/pallas_call | solution.py:920
  173.8 1.1 collective-permute-start.15
  174.9 1.5 collective-permute-start.16
  176.4 0.9 collective-permute-start.17
  177.3 5.7 %collective-permute-done.14 = bf16[4,4,224,768]{3,2,1,0:T(8,128)(2,1)S(1)} collective-permute-done((bf16[4,4,224,768]{3,2,1,0:T(8,128)(2,1)}, bf16[4,4,224,768]{3,2,1,0:T(8,128)(2,1)S(1)}, u32[]{:S(2)}, u32[]{:S(2)}) %collective-permute-start.14) | collective-permute-done | bytes 5505056 | tf_op jit(solution)/shard_map/ppermute | solution.py:991
  183.0 6.7 %add_convert_fusion = bf16[4,4,224,768]{3,2,1,0:T(8,128)(2,1)} fusion(bf16[4,4,224,768]{3,2,1,0:T(8,128)(2,1)S(1)} %collective-permute-done.14, bf16[4,4,224,768]{3,2,1,0:T(8,128)(2,1)} %get-tuple-element.88), kind=kLoop, calls=%fused_computation | loop fusion | flops 11010048 | bytes 16515072 | tf_op jit(solution)/shard_map/convert_element_type | solution.py:1119
  189.7 0.9 collective-permute-done.16.refs_8_
  190.6 0.7 copy-done.26
  191.5 0.2 convert_reduce_fusion
  191.8 0.5 subtract_minimum_fusion
  192.3 69.0 %attend_backward.1 = (bf16[768,768]{1,0:T(8,128)(2,1)}, bf16[768,768]{1,0:T(8,128)(2,1)}, f32[768,768]{1,0:T(8,128)}, f32[384,768]{1,0:T(8,128)}, f32[384,768]{1...) custom-call(s32[12]{0:T(128)} %get-tuple-element.125.refs_0_, ...), custom_call_target="tpu_custom_call" | custom-call | flops 14495514624 | bytes 12582912 | tf_op jit(solution)/shard_map/attend_backward/pallas_call | solution.py:355
  261.4 0.7 collective-permute-start.18
  262.1 0.8 collective-permute-start.22
  262.9 1.2 collective-permute-start.20
  264.1 0.6 collective-permute-done.22
  264.9 1.6 collective-permute-start.23
  266.5 4.0 %collective-permute-start.24 = (bf16[4,24,768]{2,1,0:T(8,128)(2,1)S(1)}, bf16[4,24,768]{2,1,0:T(8,128)(2,1)S(1)}, u32[]{:S(2)}, u32[]{:S(2)}) collective-permute-start(bf16[4,24,768]{2,1,0:T(8,128)(2,1)S(1)} %get-tuple-element.131), channel_id=1, source_target_pairs={{0,4},{1,5},{2,6},{3,7},{4,0},{5,1},{6,2},{7,3},{8,12},{9,13},{10,... | collective-permute-start | bytes 442376 | tf_op jit(solution)/shard_map/ppermute | solution.py:991
  270.5 1.4 collective-permute-start.25
  271.9 18.0 %collective-permute-done.18 = bf16[768,768]{1,0:T(8,128)(2,1)S(1)} collective-permute-done((bf16[768,768]{1,0:T(8,128)(2,1)}, bf16[768,768]{1,0:T(8,128)(2,1)S(1)}, u32[]{:S(2)}, u32[]{:S(2)}) %collective-permute-start.18) | collective-permute-done | bytes 1179680 | tf_op jit(solution)/shard_map/ppermute | solution.py:986
  290.2 1.1 collective-permute-start.19
  291.7 1.1 collective-permute-start.21
  292.9 0.6 slice_bitcast_fusion.4
  293.5 1.0 collective-permute-start.26
  294.5 1.0 collective-permute-start.27
  295.5 1.5 collective-permute-start.28
  297.0 8.9 %collective-permute-done.19 = bf16[384,768]{1,0:T(8,128)(2,1)S(1)} collective-permute-done((bf16[384,768]{1,0:T(8,128)(2,1)S(1)}, bf16[384,768]{1,0:T(8,128)(2,1)S(1)}, u32[]{:S(2)}, u32[]{:S(2)}) %collective-permute-start.19) | collective-permute-done | bytes 589856 | tf_op jit(solution)/shard_map/ppermute | solution.py:986
  306.1 1.9 collective-permute-done.21
  308.1 1.7 maximum_add_fusion
  309.8 0.4 collective-permute-done.28.refs_4_
  310.4 0.4 copy-done.24
  310.8 2.2 finish.1
  (100 shorter events, 2.7 us)
Async XLA Ops:
  7.2 41.6 %copy-start.21 = (s32[1,3072]{1,0:T(1,128)S(1)}, s32[1,3072]{1,0:T(1,128)}, u32[]{:S(2)}) copy-start(s32[1,3072]{1,0:T(1,128)} %param.17) | copy-start | bytes 36868
  7.2 112.5 %all-gather.3.cloned.1.call-start = ((), (), s32[]{:S(2)}) async-start(), calls=%async_computation.4 | async-start | bytes 11354112 | tf_op jit(solution)/shard_map/all_gather | solution.py:1099
  9.2 254.8 %reduce-scatter.3.cloned.1.call-start = ((), (), s32[]{:S(2)}) async-start(), calls=%async_computation.2 | async-start | bytes 6881280 | tf_op jit(solution)/shard_map/reduce_scatter | solution.py:1121
  10.1 5.0 %collective-permute-start = (bf16[32,576]{1,0:T(8,128)(2,1)S(1)}, bf16[32,576]{1,0:T(8,128)(2,1)S(1)}, u32[]{:S(2)}, u32[]{:S(2)}) collective-permute-start(bf16[32,576]{1,0:T(8,128)(2,1)S(1)} %get-tuple-element.139), channel_id=1, source_target_pairs={{0,8},{8,0},{16,24},{24,16},{1,9},{9,1},{17,25},{25,17},{2,10},{10... | collective-permute-start | bytes 110600 | tf_op jit(solution)/shard_map/ppermute | solution.py:986
  13.1 4.0 %collective-permute-start.1 = (bf16[32,576]{1,0:T(8,128)(2,1)S(1)}, bf16[32,576]{1,0:T(8,128)(2,1)S(1)}, u32[]{:S(2)}, u32[]{:S(2)}) collective-permute-start(bf16[32,576]{1,0:T(8,128)(2,1)S(1)} %get-tuple-element.138), channel_id=1, source_target_pairs={{0,16},{8,24},{16,0},{24,8},{1,17},{9,25},{17,1},{25,9},{2,18},{10... | collective-permute-start | bytes 110600 | tf_op jit(solution)/shard_map/ppermute | solution.py:986
  14.6 4.9 %collective-permute-start.2 = (bf16[32,576]{1,0:T(8,128)(2,1)S(1)}, bf16[32,576]{1,0:T(8,128)(2,1)S(1)}, u32[]{:S(2)}, u32[]{:S(2)}) collective-permute-start(bf16[32,576]{1,0:T(8,128)(2,1)S(1)} %get-tuple-element.137), channel_id=1, source_target_pairs={{0,24},{8,16},{16,8},{24,0},{1,25},{9,17},{17,9},{25,1},{2,26},{10... | collective-permute-start | bytes 110600 | tf_op jit(solution)/shard_map/ppermute | solution.py:986
  19.6 28.7 %collective-permute-start.6 = (bf16[768,768]{1,0:T(8,128)(2,1)}, bf16[768,768]{1,0:T(8,128)(2,1)S(1)}, u32[]{:S(2)}, u32[]{:S(2)}) collective-permute-start(bf16[768,768]{1,0:T(8,128)(2,1)} %refs_15_.1), channel_id=1, source_target_pairs={{0,8},{8,0},{16,24},{24,16},{1,9},{9,1},{17,25},{25,17},{2,10},{10... | collective-permute-start | bytes 3538952 | tf_op jit(solution)/shard_map/ppermute | solution.py:986
  20.2 28.6 %collective-permute-start.7 = (bf16[768,768]{1,0:T(8,128)(2,1)}, bf16[768,768]{1,0:T(8,128)(2,1)}, u32[]{:S(2)}, u32[]{:S(2)}) collective-permute-start(bf16[768,768]{1,0:T(8,128)(2,1)} %refs_15_.1), channel_id=1, source_target_pairs={{0,16},{8,24},{16,0},{24,8},{1,17},{9,25},{17,1},{25,9},{2,18},{10... | collective-permute-start | bytes 3538952 | tf_op jit(solution)/shard_map/ppermute | solution.py:986
  20.2 10.1 %collective-permute-start.3 = (bf16[4,32,576]{2,1,0:T(8,128)(2,1)S(1)}, bf16[4,32,576]{2,1,0:T(8,128)(2,1)S(1)}, u32[]{:S(2)}, u32[]{:S(2)}) collective-permute-start(bf16[4,32,576]{2,1,0:T(8,128)(2,1)S(1)} %pad_maximum_fusion.1), channel_id=1, source_target_pairs={{0,2},{1,3},{2,0},{3,1},{4,6},{5,7},{6,4},{7,5},{8,10},{9,11},{10,... | collective-permute-start | bytes 442376 | tf_op jit(solution)/shard_map/ppermute | solution.py:991
  22.3 20.1 %collective-permute-start.4 = (bf16[4,32,576]{2,1,0:T(8,128)(2,1)S(1)}, bf16[4,32,576]{2,1,0:T(8,128)(2,1)S(1)}, u32[]{:S(2)}, u32[]{:S(2)}) collective-permute-start(bf16[4,32,576]{2,1,0:T(8,128)(2,1)S(1)} %pad_maximum_fusion.1), channel_id=1, source_target_pairs={{0,4},{1,5},{2,6},{3,7},{4,0},{5,1},{6,2},{7,3},{8,12},{9,13},{10,... | collective-permute-start | bytes 442376 | tf_op jit(solution)/shard_map/ppermute | solution.py:991
  24.9 17.5 %collective-permute-start.5 = (bf16[4,32,576]{2,1,0:T(8,128)(2,1)S(1)}, bf16[4,32,576]{2,1,0:T(8,128)(2,1)S(1)}, u32[]{:S(2)}, u32[]{:S(2)}) collective-permute-start(bf16[4,32,576]{2,1,0:T(8,128)(2,1)S(1)} %pad_maximum_fusion.1), channel_id=1, source_target_pairs={{0,6},{1,7},{2,4},{3,5},{4,2},{5,3},{6,0},{7,1},{8,14},{9,15},{10,... | collective-permute-start | bytes 442376 | tf_op jit(solution)/shard_map/ppermute | solution.py:991
  42.5 9.7 %copy-start.4 = (bf16[4,4,32,576]{3,2,1,0:T(8,128)(2,1)}, bf16[4,4,32,576]{3,2,1,0:T(8,128)(2,1)S(1)}, u32[]{:S(2)}) copy-start(bf16[4,4,32,576]{3,2,1,0:T(8,128)(2,1)S(1)} %pad_maximum_fusion.refs_5_) | copy-start | bytes 1769476
  48.3 3.9 %copy-start.8 = (bf16[768,768]{1,0:T(8,128)(2,1)}, bf16[768,768]{1,0:T(8,128)(2,1)S(1)}, u32[]{:S(2)}) copy-start(bf16[768,768]{1,0:T(8,128)(2,1)S(1)} %collective-permute-done.6.refs_2_.refs_16_) | copy-start | bytes 3538948
  48.8 4.4 %collective-permute-start.10 = (bf16[4,4,32,576]{3,2,1,0:T(8,128)(2,1)S(1)}, bf16[4,4,32,576]{3,2,1,0:T(8,128)(2,1)}, u32[]{:S(2)}, u32[]{:S(2)}) collective-permute-start(bf16[4,4,32,576]{3,2,1,0:T(8,128)(2,1)S(1)} %pad_maximum_fusion.refs_5_), channel_id=1, source_target_pairs={{0,1},{1,0},{2,3},{3,2},{4,5},{5,4},{6,7},{7,6},{8,9},{9,8},{10,11... | collective-permute-start | bytes 1769480 | tf_op jit(solution)/shard_map/ppermute | solution.py:991
  49.5 3.7 %copy-start.11 = (bf16[768,768]{1,0:T(8,128)(2,1)S(1)}, bf16[768,768]{1,0:T(8,128)(2,1)}, u32[]{:S(2)}) copy-start(bf16[768,768]{1,0:T(8,128)(2,1)} %refs_15_.1) | copy-start | bytes 3538948
  50.7 22.4 %collective-permute-start.8 = (bf16[384,768]{1,0:T(8,128)(2,1)S(1)}, bf16[384,768]{1,0:T(8,128)(2,1)S(1)}, u32[]{:S(2)}, u32[]{:S(2)}) collective-permute-start(bf16[384,768]{1,0:T(8,128)(2,1)S(1)} %slice.72), channel_id=1, source_target_pairs={{0,8},{8,0},{16,24},{24,16},{1,9},{9,1},{17,25},{25,17},{2,10},{10... | collective-permute-start | bytes 1769480 | tf_op jit(solution)/shard_map/ppermute | solution.py:986
  52.2 20.9 %collective-permute-start.9 = (bf16[384,768]{1,0:T(8,128)(2,1)S(1)}, bf16[384,768]{1,0:T(8,128)(2,1)S(1)}, u32[]{:S(2)}, u32[]{:S(2)}) collective-permute-start(bf16[384,768]{1,0:T(8,128)(2,1)S(1)} %slice.73), channel_id=1, source_target_pairs={{0,16},{8,24},{16,0},{24,8},{1,17},{9,25},{17,1},{25,9},{2,18},{10... | collective-permute-start | bytes 1769480 | tf_op jit(solution)/shard_map/ppermute | solution.py:986
  53.0 20.2 %copy-start.10 = (s32[4]{0:T(128)}, s32[4]{0:T(128)S(1)}, u32[]{:S(2)}) copy-start(s32[4]{0:T(128)S(1)} %pad_add_fusion.1.refs_0_.refs_2_) | copy-start | bytes 52
  53.2 1.1 copy-start.5
  54.3 1.3 copy-start.9
  61.8 13.0 %copy-start.3 = (bf16[3,768,192]{2,1,0:T(8,128)(2,1)}, bf16[3,768,192]{2,1,0:T(8,128)(2,1)S(1)}, u32[]{:S(2)}) copy-start(bf16[3,768,192]{2,1,0:T(8,128)(2,1)S(1)} %get-tuple-element.74.refs_4_.refs_20_) | copy-start | bytes 2654212
  73.1 1.7 copy-start.6
  73.1 1.7 copy-start.7
  74.8 27.3 %copy-start = (bf16[3072,256]{1,0:T(8,128)(2,1)}, bf16[3072,256]{1,0:T(8,128)(2,1)S(1)}, u32[]{:S(2)}) copy-start(bf16[3072,256]{1,0:T(8,128)(2,1)S(1)} %get-tuple-element.79.refs_3_) | copy-start | bytes 4718596
  74.8 27.3 %copy-start.1 = (bf16[3072,256]{1,0:T(8,128)(2,1)}, bf16[3072,256]{1,0:T(8,128)(2,1)S(1)}, u32[]{:S(2)}) copy-start(bf16[3072,256]{1,0:T(8,128)(2,1)S(1)} %get-tuple-element.80.refs_4_) | copy-start | bytes 4718596
  74.8 27.3 %copy-start.2 = (bf16[3072,192]{1,0:T(8,128)(2,1)}, bf16[3072,192]{1,0:T(8,128)(2,1)S(1)}, u32[]{:S(2)}) copy-start(bf16[3072,192]{1,0:T(8,128)(2,1)S(1)} %get-tuple-element.81.refs_5_) | copy-start | bytes 3538948
  102.1 0.7 copy-start.15
  102.8 0.6 copy-start.16
  103.5 70.2 %copy-start.12 = (bf16[192,768]{1,0:T(8,128)(2,1)}, bf16[192,768]{1,0:T(8,128)(2,1)S(1)}, u32[]{:S(2)}) copy-start(bf16[192,768]{1,0:T(8,128)(2,1)S(1)} %get-tuple-element.83.refs_11_) | copy-start | bytes 884740
  103.5 70.2 %copy-start.13 = (bf16[192,768]{1,0:T(8,128)(2,1)}, bf16[192,768]{1,0:T(8,128)(2,1)S(1)}, u32[]{:S(2)}) copy-start(bf16[192,768]{1,0:T(8,128)(2,1)S(1)} %get-tuple-element.84.refs_12_) | copy-start | bytes 884740
  103.5 70.2 %copy-start.14 = (bf16[192,768]{1,0:T(8,128)(2,1)}, bf16[192,768]{1,0:T(8,128)(2,1)S(1)}, u32[]{:S(2)}) copy-start(bf16[192,768]{1,0:T(8,128)(2,1)S(1)} %get-tuple-element.85.refs_13_) | copy-start | bytes 884740
  103.5 9.9 %collective-permute-start.11 = (bf16[192,768]{1,0:T(8,128)(2,1)S(1)}, bf16[192,768]{1,0:T(8,128)(2,1)S(1)}, u32[]{:S(2)}, u32[]{:S(2)}) collective-permute-start(bf16[192,768]{1,0:T(8,128)(2,1)S(1)} %get-tuple-element.83.refs_11_), channel_id=1, source_target_pairs={{0,8},{8,0},{16,24},{24,16},{1,9},{9,1},{17,25},{25,17},{2,10},{10... | collective-permute-start | bytes 884744 | tf_op jit(solution)/shard_map/ppermute | solution.py:986
  103.8 9.5 %collective-permute-start.12 = (bf16[192,768]{1,0:T(8,128)(2,1)S(1)}, bf16[192,768]{1,0:T(8,128)(2,1)S(1)}, u32[]{:S(2)}, u32[]{:S(2)}) collective-permute-start(bf16[192,768]{1,0:T(8,128)(2,1)S(1)} %get-tuple-element.84.refs_12_), channel_id=1, source_target_pairs={{0,16},{8,24},{16,0},{24,8},{1,17},{9,25},{17,1},{25,9},{2,18},{10... | collective-permute-start | bytes 884744 | tf_op jit(solution)/shard_map/ppermute | solution.py:986
  105.5 14.2 %collective-permute-start.13 = (bf16[192,768]{1,0:T(8,128)(2,1)S(1)}, bf16[192,768]{1,0:T(8,128)(2,1)S(1)}, u32[]{:S(2)}, u32[]{:S(2)}) collective-permute-start(bf16[192,768]{1,0:T(8,128)(2,1)S(1)} %get-tuple-element.85.refs_13_), channel_id=1, source_target_pairs={{0,24},{8,16},{16,8},{24,0},{1,25},{9,17},{17,9},{25,1},{2,26},{10... | collective-permute-start | bytes 884744 | tf_op jit(solution)/shard_map/ppermute | solution.py:986
  113.3 6.4 %copy-start.28 = (bf16[192,768]{1,0:T(8,128)(2,1)}, bf16[192,768]{1,0:T(8,128)(2,1)S(1)}, u32[]{:S(2)}) copy-start(bf16[192,768]{1,0:T(8,128)(2,1)S(1)} %collective-permute-done.11.refs_4_) | copy-start | bytes 884740
  113.3 6.4 %copy-start.29 = (bf16[192,768]{1,0:T(8,128)(2,1)}, bf16[192,768]{1,0:T(8,128)(2,1)S(1)}, u32[]{:S(2)}) copy-start(bf16[192,768]{1,0:T(8,128)(2,1)S(1)} %collective-permute-done.12.refs_5_) | copy-start | bytes 884740
  119.7 0.7 copy-start.30
  173.7 9.3 %collective-permute-start.14 = (bf16[4,4,224,768]{3,2,1,0:T(8,128)(2,1)}, bf16[4,4,224,768]{3,2,1,0:T(8,128)(2,1)S(1)}, u32[]{:S(2)}, u32[]{:S(2)}) collective-permute-start(bf16[4,4,224,768]{3,2,1,0:T(8,128)(2,1)} %get-tuple-element.89), channel_id=1, source_target_pairs={{0,1},{1,0},{2,3},{3,2},{4,5},{5,4},{6,7},{7,6},{8,9},{9,8},{10,11... | collective-permute-start | bytes 16515080 | tf_op jit(solution)/shard_map/ppermute | solution.py:991
  173.8 15.9 %collective-permute-start.15 = (bf16[192,768]{1,0:T(8,128)(2,1)}, bf16[192,768]{1,0:T(8,128)(2,1)S(1)}, u32[]{:S(2)}, u32[]{:S(2)}) collective-permute-start(bf16[192,768]{1,0:T(8,128)(2,1)} %get-tuple-element.91), channel_id=1, source_target_pairs={{0,8},{8,0},{16,24},{24,16},{1,9},{9,1},{17,25},{25,17},{2,10},{10... | collective-permute-start | bytes 884744 | tf_op jit(solution)/shard_map/ppermute | solution.py:986
  174.9 15.6 %collective-permute-start.16 = (bf16[192,768]{1,0:T(8,128)(2,1)}, bf16[192,768]{1,0:T(8,128)(2,1)S(1)}, u32[]{:S(2)}, u32[]{:S(2)}) collective-permute-start(bf16[192,768]{1,0:T(8,128)(2,1)} %get-tuple-element.92), channel_id=1, source_target_pairs={{0,16},{8,24},{16,0},{24,8},{1,17},{9,25},{17,1},{25,9},{2,18},{10... | collective-permute-start | bytes 884744 | tf_op jit(solution)/shard_map/ppermute | solution.py:986
  176.4 14.1 %collective-permute-start.17 = (bf16[192,768]{1,0:T(8,128)(2,1)}, bf16[192,768]{1,0:T(8,128)(2,1)S(1)}, u32[]{:S(2)}, u32[]{:S(2)}) collective-permute-start(bf16[192,768]{1,0:T(8,128)(2,1)} %get-tuple-element.93), channel_id=1, source_target_pairs={{0,24},{8,16},{16,8},{24,0},{1,25},{9,17},{17,9},{25,1},{2,26},{10... | collective-permute-start | bytes 884744 | tf_op jit(solution)/shard_map/ppermute | solution.py:986
  189.7 0.9 copy-start.25
  190.5 0.7 copy-start.26
  190.5 0.8 copy-start.27
  191.4 118.9 %reduce-scatter.5.cloned.1.call-start = ((), (), s32[]{:S(2)}) async-start(), calls=%async_computation.3 | async-start | bytes 1720320 | tf_op jit(solution)/shard_map/reduce_scatter | solution.py:1123
  261.4 3.4 %copy-start.20 = (bf16[4,4,24,768]{3,2,1,0:T(8,128)(2,1)S(1)}, bf16[4,4,24,768]{3,2,1,0:T(8,128)(2,1)}, u32[]{:S(2)}) copy-start(bf16[4,4,24,768]{3,2,1,0:T(8,128)(2,1)} %get-tuple-element.105) | copy-start | bytes 1769476
  261.4 28.5 %collective-permute-start.18 = (bf16[768,768]{1,0:T(8,128)(2,1)}, bf16[768,768]{1,0:T(8,128)(2,1)S(1)}, u32[]{:S(2)}, u32[]{:S(2)}) collective-permute-start(bf16[768,768]{1,0:T(8,128)(2,1)} %get-tuple-element.101), channel_id=1, source_target_pairs={{0,8},{8,0},{16,24},{24,16},{1,9},{9,1},{17,25},{25,17},{2,10},{10... | collective-permute-start | bytes 3538952 | tf_op jit(solution)/shard_map/ppermute | solution.py:986
  262.1 2.7 collective-permute-start.22
  262.9 28.5 %collective-permute-start.20 = (bf16[768,768]{1,0:T(8,128)(2,1)}, bf16[768,768]{1,0:T(8,128)(2,1)S(1)}, u32[]{:S(2)}, u32[]{:S(2)}) collective-permute-start(bf16[768,768]{1,0:T(8,128)(2,1)} %get-tuple-element.103), channel_id=1, source_target_pairs={{0,16},{8,24},{16,0},{24,8},{1,17},{9,25},{17,1},{25,9},{2,18},{10... | collective-permute-start | bytes 3538952 | tf_op jit(solution)/shard_map/ppermute | solution.py:986
  264.9 27.9 %collective-permute-start.23 = (bf16[4,24,768]{2,1,0:T(8,128)(2,1)S(1)}, bf16[4,24,768]{2,1,0:T(8,128)(2,1)S(1)}, u32[]{:S(2)}, u32[]{:S(2)}) collective-permute-start(bf16[4,24,768]{2,1,0:T(8,128)(2,1)S(1)} %get-tuple-element.129), channel_id=1, source_target_pairs={{0,2},{1,3},{2,0},{3,1},{4,6},{5,7},{6,4},{7,5},{8,10},{9,11},{10,... | collective-permute-start | bytes 442376 | tf_op jit(solution)/shard_map/ppermute | solution.py:991
  266.5 26.3 %collective-permute-start.24 = (bf16[4,24,768]{2,1,0:T(8,128)(2,1)S(1)}, bf16[4,24,768]{2,1,0:T(8,128)(2,1)S(1)}, u32[]{:S(2)}, u32[]{:S(2)}) collective-permute-start(bf16[4,24,768]{2,1,0:T(8,128)(2,1)S(1)} %get-tuple-element.131), channel_id=1, source_target_pairs={{0,4},{1,5},{2,6},{3,7},{4,0},{5,1},{6,2},{7,3},{8,12},{9,13},{10,... | collective-permute-start | bytes 442376 | tf_op jit(solution)/shard_map/ppermute | solution.py:991
  270.5 19.5 %copy-start.19 = (f32[384,768]{1,0:T(8,128)S(1)}, f32[384,768]{1,0:T(8,128)}, u32[]{:S(2)}) copy-start(f32[384,768]{1,0:T(8,128)} %get-tuple-element.102) | copy-start | bytes 3538948
  270.5 22.3 %collective-permute-start.25 = (bf16[4,24,768]{2,1,0:T(8,128)(2,1)S(1)}, bf16[4,24,768]{2,1,0:T(8,128)(2,1)S(1)}, u32[]{:S(2)}, u32[]{:S(2)}) collective-permute-start(bf16[4,24,768]{2,1,0:T(8,128)(2,1)S(1)} %get-tuple-element.130), channel_id=1, source_target_pairs={{0,6},{1,7},{2,4},{3,5},{4,2},{5,3},{6,0},{7,1},{8,14},{9,15},{10,... | collective-permute-start | bytes 442376 | tf_op jit(solution)/shard_map/ppermute | solution.py:991
  290.2 1.3 copy-start.18
  290.2 15.7 %collective-permute-start.19 = (bf16[384,768]{1,0:T(8,128)(2,1)S(1)}, bf16[384,768]{1,0:T(8,128)(2,1)S(1)}, u32[]{:S(2)}, u32[]{:S(2)}) collective-permute-start(bf16[384,768]{1,0:T(8,128)(2,1)S(1)} %fusion.1), channel_id=1, source_target_pairs={{0,16},{8,24},{16,0},{24,8},{1,17},{9,25},{17,1},{25,9},{2,18},{10... | collective-permute-start | bytes 1769480 | tf_op jit(solution)/shard_map/ppermute | solution.py:986
  291.7 16.3 %collective-permute-start.21 = (bf16[384,768]{1,0:T(8,128)(2,1)S(1)}, bf16[384,768]{1,0:T(8,128)(2,1)S(1)}, u32[]{:S(2)}, u32[]{:S(2)}) collective-permute-start(bf16[384,768]{1,0:T(8,128)(2,1)S(1)} %fusion), channel_id=1, source_target_pairs={{0,8},{8,0},{16,24},{24,16},{1,9},{9,1},{17,25},{25,17},{2,10},{10... | collective-permute-start | bytes 1769480 | tf_op jit(solution)/shard_map/ppermute | solution.py:986
  293.5 16.3 %collective-permute-start.26 = (f32[24,768]{1,0:T(8,128)S(1)}, f32[24,768]{1,0:T(8,128)S(1)}, u32[]{:S(2)}, u32[]{:S(2)}) collective-permute-start(f32[24,768]{1,0:T(8,128)S(1)} %get-tuple-element.134), channel_id=1, source_target_pairs={{0,8},{8,0},{16,24},{24,16},{1,9},{9,1},{17,25},{25,17},{2,10},{10... | collective-permute-start | bytes 221192 | tf_op jit(solution)/shard_map/ppermute | solution.py:986
  294.5 15.3 %collective-permute-start.27 = (f32[24,768]{1,0:T(8,128)S(1)}, f32[24,768]{1,0:T(8,128)S(1)}, u32[]{:S(2)}, u32[]{:S(2)}) collective-permute-start(f32[24,768]{1,0:T(8,128)S(1)} %get-tuple-element.133), channel_id=1, source_target_pairs={{0,16},{8,24},{16,0},{24,8},{1,17},{9,25},{17,1},{25,9},{2,18},{10... | collective-permute-start | bytes 221192 | tf_op jit(solution)/shard_map/ppermute | solution.py:986
  295.5 14.7 %collective-permute-start.28 = (f32[24,768]{1,0:T(8,128)S(1)}, f32[24,768]{1,0:T(8,128)S(1)}, u32[]{:S(2)}, u32[]{:S(2)}) collective-permute-start(f32[24,768]{1,0:T(8,128)S(1)} %get-tuple-element.132), channel_id=1, source_target_pairs={{0,24},{8,16},{16,8},{24,0},{1,25},{9,17},{17,9},{25,1},{2,26},{10... | collective-permute-start | bytes 221192 | tf_op jit(solution)/shard_map/ppermute | solution.py:986
  306.1 2.0 copy-start.17
  309.8 0.6 copy-start.22
  309.8 0.6 copy-start.23
  310.2 0.6 copy-start.24
Sparse Core Ops, SparseCore 0:
  11.6 105.5 all-gather.2
  190.7 63.8 reduce-scatter.2
  264.2 42.3 reduce-scatter.4

commit v6 on v5

--- a/solution.py
+++ b/solution.py
@@ -180,10 +180,9 @@
 
 def backward_kernel(
     heads, start_ref, number_ref, me_ref, q_ref, k_ref, v_ref,
-    g0_ref, g1_ref, g2_ref, g3_ref, o0_ref, o1_ref, o2_ref, o3_ref, lse_ref,
-    x0_ref, x1_ref, x2_ref, x3u_ref, x3l_ref, w_ref, gh1_ref,
-    sx_ref, sy_ref, mine_ref, low_ref, up_ref, kept_ref, sent_ref,
-    qt, gt, dqt, delta, dkt, dvt, kh, vh, turned, grads, rows_ref,
+    g0_ref, g1_ref, g2_ref, g3_ref, o0_ref, o1_ref, o2_ref, o3_ref, lse_ref, w_ref, gh1_ref,
+    sx_ref, sy_ref, mine_ref, low_ref, up_ref, turned,
+    qt, gt, dqt, delta, dkt, dvt, kh, vh, grads,
 ):
     step = pl.program_id(0)
     seq, wide = q_ref.shape
@@ -303,52 +302,18 @@
             return carry
 
         lax.fori_loop(0, 4, back, 0)
-        model = x0_ref.shape[1]
-        columns, _, own = kept_ref.shape[:3]
-        shards = 2 * columns
-        lane = lax.broadcasted_iota(jnp.int32, (128, width), 1)
-        row = lax.broadcasted_iota(jnp.int32, (128, width), 0)
-        tile = jnp.where(lax.rem(lane, own) == row, 1.0, 0.0).astype(bf16)
-        lane = lax.broadcasted_iota(jnp.int32, (shards, width), 1)
-        row = lax.broadcasted_iota(jnp.int32, (shards, width), 0)
-        ones = jnp.ones((8, seq), bf16)
-        rows_ref[...] = jnp.zeros_like(rows_ref)
-        for j, c in enumerate((0, 2)):
-            sums = mm(ones, grads[c])[:1]
-            rows_ref[:, j, :] = mm_nt(jnp.where(lane // own == row, sums, 0.0).astype(bf16), tile)
-        total = jnp.zeros((3 * width, model), f32)
-        for r, parts in enumerate(((x0_ref,), (x1_ref,), (x2_ref,), (x3u_ref, x3l_ref))):
-            first = lax.bitwise_xor(me, r) * own_rows
-            for part_ref in parts:
-                count = part_ref.shape[0]
-                total = total + mm(turned[:, pl.ds(pl.multiple_of(first, 128), count)], part_ref[...])
-                first = first + count
-        value = total.T.astype(bf16).reshape(4 * shards, own, 3 * width)
-        for core in range(2):
-
-            @pl.when(me_ref[3] == core)
-            def _():
-                for piece in range(4 * shards):
-                    group, shard = piece // shards, piece % shards
-                    target = kept_ref if shard % 2 == core else sent_ref
-                    z = lax.bitwise_xor(me_ref[2], shard // 2)
-                    r = lax.bitwise_xor(me_ref[1], group)
-                    target[z, r, :, : 3 * width] = value[piece]
-                    target[z, r, :, 3 * width :] = jnp.zeros((own, model - 3 * width), bf16)
-                    target[z, r, :8, model - 128 :] = rows_ref[shard].astype(bf16)
-
-
-def attend_backward(q, k, v, g, o, lse, starts, numbers, place, x, w, gh1, pieces, heads):
+
+
+def attend_backward(q, k, v, g, o, lse, starts, numbers, place, w, gh1, heads):
     seq, wide = q.shape
     width = heads * HEAD
     steps = seq // BK
     own_rows, model = gh1.shape
     half = own_rows // 2
-    own = model // pieces
     once = dict(pipeline_mode=pl.Buffered(1))
     whole = lambda a: pl.BlockSpec(a, lambda i, a_, b_, m_: (0,) * len(a), **once)
     cost = pl.CostEstimate(
-        flops=5 * heads * seq * seq * HEAD + 12 * seq * model * width,
+        flops=5 * heads * seq * seq * HEAD + 6 * seq * model * width,
         bytes_accessed=16 * seq * wide,
         transcendentals=heads * seq * seq // 3,
     )
@@ -364,8 +329,6 @@
             ]
             + [whole((width, own_rows))] * 8
             + [whole((8, seq))]
-            + [whole((own_rows, model))] * 3
-            + [whole((half, model))] * 2
             + [whole((3, model, width)), whole((own_rows, model))],
             out_specs=[
                 whole((own_rows, model)),
@@ -373,8 +336,7 @@
                 whole((own_rows, model)),
                 whole((own_rows // 2, model)),
                 whole((own_rows // 2, model)),
-                whole((pieces // 8, 4, own, model)),
-                whole((pieces // 8, 4, own, model)),
+                whole((3 * width, seq)),
             ],
             scratch_shapes=[
                 pltpu.VMEM((width, seq), bf16),
@@ -385,9 +347,7 @@
                 pltpu.VMEM((width, BK), f32),
                 pltpu.VMEM((heads * BK, wide), bf16),
                 pltpu.VMEM((heads * BK, width), bf16),
-                pltpu.VMEM((3 * width, seq), bf16),
                 pltpu.VMEM((3, seq, width), bf16),
-                pltpu.VMEM((pieces // 4, 8, 128), f32),
             ],
         ),
         out_shape=[
@@ -396,13 +356,69 @@
             jax.ShapeDtypeStruct((own_rows, model), f32),
             jax.ShapeDtypeStruct((own_rows // 2, model), f32),
             jax.ShapeDtypeStruct((own_rows // 2, model), f32),
-            jax.ShapeDtypeStruct((pieces // 8, 4, own, model), bf16),
-            jax.ShapeDtypeStruct((pieces // 8, 4, own, model), bf16),
+            jax.ShapeDtypeStruct((3 * width, seq), bf16),
         ],
         cost_estimate=cost,
         compiler_params=pltpu.CompilerParams(vmem_limit_bytes=60 << 20),
         name="attend_backward",
-    )(starts, numbers, place, q, k, v, *g, *o, lse, *x, w, gh1)
+    )(starts, numbers, place, q, k, v, *g, *o, lse, w, gh1)
+
+
+def weight_kernel(me_ref, turned, x0_ref, x1_ref, x2_ref, x3u_ref, x3l_ref, kept_ref, sent_ref, rows_ref):
+    seq = turned.shape[1]
+    width = turned.shape[0] // 3
+    model = x0_ref.shape[1]
+    columns, _, own = kept_ref.shape[:3]
+    shards = 2 * columns
+    lane = lax.broadcasted_iota(jnp.int32, (128, width), 1)
+    row = lax.broadcasted_iota(jnp.int32, (128, width), 0)
+    tile = jnp.where(lax.rem(lane, own) == row, 1.0, 0.0).astype(bf16)
+    lane = lax.broadcasted_iota(jnp.int32, (shards, width), 1)
+    row = lax.broadcasted_iota(jnp.int32, (shards, width), 0)
+    ones = jnp.ones((8, seq), bf16)
+    rows_ref[...] = jnp.zeros_like(rows_ref)
+    for j, c in enumerate((0, 2)):
+        sums = mm_nt(ones, turned[c * width : (c + 1) * width, :])[:1]
+        rows_ref[:, j, :] = mm_nt(jnp.where(lane // own == row, sums, 0.0).astype(bf16), tile)
+    me = me_ref[0]
+    own_rows = x0_ref.shape[0]
+    total = jnp.zeros((3 * width, model), f32)
+    for r, parts in enumerate(((x0_ref,), (x1_ref,), (x2_ref,), (x3u_ref, x3l_ref))):
+        first = lax.bitwise_xor(me, r) * own_rows
+        for part_ref in parts:
+            count = part_ref.shape[0]
+            total = total + mm(turned[:, pl.ds(pl.multiple_of(first, 128), count)], part_ref[...])
+            first = first + count
+    value = total.T.astype(bf16).reshape(4 * shards, own, 3 * width)
+    for core in range(2):
+
+        @pl.when(me_ref[3] == core)
+        def _():
+            for piece in range(4 * shards):
+                group, shard = piece // shards, piece % shards
+                target = kept_ref if shard % 2 == core else sent_ref
+                z = lax.bitwise_xor(me_ref[2], shard // 2)
+                r = lax.bitwise_xor(me_ref[1], group)
+                target[z, r, :, : 3 * width] = value[piece]
+                target[z, r, :, 3 * width :] = jnp.zeros((own, model - 3 * width), bf16)
+                target[z, r, :8, model - 128 :] = rows_ref[shard].astype(bf16)
+
+
+def weight_gradient(place, turned, x, pieces):
+    model = x[0].shape[1]
+    own = model // pieces
+    vmem = pl.BlockSpec(memory_space=pltpu.VMEM)
+    return pl.pallas_call(
+        weight_kernel,
+        in_specs=[pl.BlockSpec(memory_space=pltpu.SMEM)] + [vmem] * 6,
+        out_shape=[jax.ShapeDtypeStruct((pieces // 8, 4, own, model), bf16)] * 2,
+        scratch_shapes=[pltpu.VMEM((pieces // 4, 8, 128), f32)],
+        cost_estimate=pl.CostEstimate(
+            flops=16 * turned.size * model, bytes_accessed=2 * turned.size * 3, transcendentals=0
+        ),
+        compiler_params=pltpu.CompilerParams(vmem_limit_bytes=40 << 20),
+        name="weight_gradient",
+    )(place, turned, *x)
 
 
 def pack_kernel(ratio, groups, me_ref, down_ref, up_ref, out_ref, qkv_ref, *refs):
@@ -993,11 +1009,12 @@
 
 def scatter_rows(sent_x, sent_y, mine, low, up):
     half = low.shape[0]
-    got_x = by_sp(sent_x, 1).astype(f32)
-    got_y = by_sp(sent_y, 2).astype(f32)
-    next_y = by_sp((up + got_x[half:]).astype(bf16), 2).astype(f32)
-    next_x = by_sp((low + got_y[half:]).astype(bf16), 1).astype(f32)
-    return mine + jnp.concatenate([got_x[:half] + next_y, got_y[:half] + next_x], 0)
+    got_x, got_y = lax.optimization_barrier((by_sp(sent_x, 1), by_sp(sent_y, 2)))
+    next_y = by_sp((up + got_x[half:].astype(f32)).astype(bf16), 2)
+    next_x = by_sp((low + got_y[half:].astype(f32)).astype(bf16), 1)
+    upper = got_x[:half].astype(f32) + next_y.astype(f32)
+    lower = got_y[:half].astype(f32) + next_x.astype(f32)
+    return mine + jnp.concatenate([upper, lower], 0)
 
 
 def unpack(packed, ratio):
@@ -1119,12 +1136,7 @@
     total = (kept.astype(f32) + partner.astype(f32)).astype(bf16)
     total, grad_heads = lax.optimization_barrier((total, grad_heads))
     total = lax.psum_scatter(total.reshape(-1, model), "sp", scatter_dimension=0, tiled=True)
-    cores = [[2 * i + c for i in range(shards // 2)] for c in range(2)]
-    reduced = lax.psum_scatter(
-        total, "fsdp", scatter_dimension=0, tiled=True, axis_index_groups=cores
-    )
-
-    *parts, kept, sent = attend_backward(
+    *parts, turned = attend_backward(
         queries,
         keys,
         values,
@@ -1133,12 +1145,15 @@
         logsum,
         backward_start,
         backward_number,
-        order,
-        blocks,
+        me,
         weights,
         grad_h1,
-        pieces,
         heads_local,
+    )
+    kept, sent = weight_gradient(order, turned, blocks, pieces)
+    cores = [[2 * i + c for i in range(shards // 2)] for c in range(2)]
+    reduced = lax.psum_scatter(
+        total, "fsdp", scatter_dimension=0, tiled=True, axis_index_groups=cores
     )
     grad_input = scatter_rows(*parts)
     if direct:

time: 321 us -> 322 us (level)
  waiting for transfers between devices: 88.7 us -> 83.6 us
  other arithmetic: 11.3 us -> 15.2 us
  starting transfers between devices: 34.5 us -> 31.1 us
    ppermute x20, waiting for transfers between devices: 64.8 us -> 46 us  [by_sp(): return lax.ppermute(value, 'sp', [(i, i ^ flip) for i in range(groups)])]
    ppermute x9, waiting for transfers between devices: 23.9 us -> 31.5 us  [by_fsdp(): return lax.ppermute(value, 'fsdp', [(i, i ^ flip) for i in range(shards)])]
    pallas_call x0 -> x1, Pallas kernels: none -> 6.08 us  [weight_gradient(): pl.pallas_call(weight_kernel, in_specs=[pl.BlockSpec(memory_space=pltpu.S...]
    reduce_scatter x1, waiting for transfers between devices: 0.01 us -> 6.08 us  [body(): lax.psum_scatter(total, 'fsdp', scatter_dimension=0, tiled=True, axis_ind...]
    pallas_call x1, Pallas kernels: 69 us -> 64.2 us  [attend_backward(): pl.pallas_call(lambda *refs: backward_kernel(heads, *refs), grid_spec=plt...]
    unnamed x62 -> x72, local copies, waits for them, and re-layouts: 5.92 us -> 7.48 us
  transfers between devices with their start and end apart: 32 -> 32, of which waited for: 17 -> 20; matrix products, arithmetic and copies ran while one was open for 5% -> 6% of each run, Pallas kernels for 33% -> 33%
where the time goes in v6:
time: 322 us; the launch traced here: 319 us
  Pallas kernels  164 us (51%)
  waiting for transfers between devices  83.6 us (26%)
  starting transfers between devices  31.1 us (10%)
  other arithmetic  15.2 us (5%)
  between operations  14.2 us (4%)
  local copies, waits for them, and re-layouts  11.1 us (3%)
    pallas_call x1, Pallas kernels, attend_backward(): pl.pallas_call(lambda *refs: backward_kernel(heads, *refs), grid_spec=plt...  64.2 us
    pallas_call x1, Pallas kernels, middle(): pl.pallas_call(lambda *refs: middle_kernel(groups, chunks, *refs), grid=(...  53.2 us
    ppermute x20, waiting for transfers between devices, by_sp(): return lax.ppermute(value, 'sp', [(i, i ^ flip) for i in range(groups)])  46 us
    ppermute x9, waiting for transfers between devices, by_fsdp(): return lax.ppermute(value, 'fsdp', [(i, i ^ flip) for i in range(shards)])  31.5 us
    pallas_call x1, Pallas kernels, attend_forward(): pl.pallas_call(lambda *refs: forward_kernel(heads, *refs), grid_spec=pltp...  28.5 us
    ppermute x20, starting transfers between devices, by_sp(): return lax.ppermute(value, 'sp', [(i, i ^ flip) for i in range(groups)])  21.4 us
    ppermute x9, starting transfers between devices, by_fsdp(): return lax.ppermute(value, 'fsdp', [(i, i ^ flip) for i in range(shards)])  9.56 us
    unnamed x72, local copies, waits for them, and re-layouts  7.48 us
  transfers between devices with their start and end apart: 32, of which 20 were waited for; matrix products, arithmetic and copies ran while one was open for 6% of the time, Pallas kernels for 33%

profile of v6, /device:TPU:0, one launch (start us, length us, event | category | flops | bytes accessed | tf_op | source)
XLA Modules:
  0.0 319.2 jit_solution(3266575054176423771)
XLA Ops:
  7.2 2.0 pack.1
  9.3 0.9 fusion.8
  10.2 3.0 collective-permute-start
  13.2 1.5 collective-permute-start.1
  15.2 2.0 collective-permute-done.1
  17.2 2.4 collective-permute-done.2
  19.7 0.6 collective-permute-start.6
  20.3 2.0 collective-permute-start.3
  22.4 2.6 collective-permute-start.4
  25.0 5.4 %collective-permute-done.3 = bf16[4,32,576]{2,1,0:T(8,128)(2,1)S(1)} collective-permute-done((bf16[4,32,576]{2,1,0:T(8,128)(2,1)S(1)}, bf16[4,32,576]{2,1,0:T(8,128)(2,1)S(1)}, u32[]{:S(2)}, u32[]{:S(2)}) %collective-permute-start.3) | collective-permute-done | bytes 147488 | tf_op jit(solution)/shard_map/ppermute | solution.py:1007
  30.4 12.1 %collective-permute-done.4 = bf16[4,32,576]{2,1,0:T(8,128)(2,1)S(1)} collective-permute-done((bf16[4,32,576]{2,1,0:T(8,128)(2,1)S(1)}, bf16[4,32,576]{2,1,0:T(8,128)(2,1)S(1)}, u32[]{:S(2)}, u32[]{:S(2)}) %collective-permute-start.4) | collective-permute-done | bytes 147488 | tf_op jit(solution)/shard_map/ppermute | solution.py:1007
  42.6 5.6 %collective-permute-done.6.refs_2_.x1_ref = bf16[768,768]{1,0:T(8,128)(2,1)S(1)} collective-permute-done((bf16[768,768]{1,0:T(8,128)(2,1)S(1)}, bf16[768,768]{1,0:T(8,128)(2,1)S(1)}, u32[]{:S(2)}, u32[]{:S(2)}) %collective-permute-start.6) | collective-permute-done | bytes 1179680 | tf_op jit(solution)/shard_map/ppermute | solution.py:1002
  49.4 1.2 slice.72
  50.6 1.4 collective-permute-start.8
  52.1 0.8 collective-permute-start.9
  53.3 1.3 copy-done.11
  54.5 6.1 %project.1 = (bf16[3072,256]{1,0:T(8,128)(2,1)S(1)}, bf16[3072,256]{1,0:T(8,128)(2,1)S(1)}, bf16[3072,192]{1,0:T(8,128)(2,1)S(1)}, bf16[3,768,192]{2,1,0:T(8,128)(2,1)S(1)}, f32[8,192]{1,0:T(8,128)S(1)}) custom-call(s32[4]{0:T(128)S(1)} %pad_add_fusion.1.refs_0_.me_ref, bf16[768,768]{1,0:T(8,128)(2,1)S(1)} %copy-done.15, bf16[768,768]{1,0:T(8,128)(2,1)S(1)} %copy-done.11, ...), custom_call_target="tpu_custom_call" | custom-call | flops 2038431744 | bytes 9437184 | tf_op jit(solution)/shard_map/project/pallas_call | solution.py:569
  60.7 12.5 %collective-permute-done.8.refs_1_.x3u_ref = bf16[384,768]{1,0:T(8,128)(2,1)S(1)} collective-permute-done((bf16[384,768]{1,0:T(8,128)(2,1)S(1)}, bf16[384,768]{1,0:T(8,128)(2,1)S(1)}, u32[]{:S(2)}, u32[]{:S(2)}) %collective-permute-start.8) | collective-permute-done | bytes 589856 | tf_op jit(solution)/shard_map/ppermute | solution.py:1002
  73.2 1.6 project_last.1
  74.9 28.5 %attend_forward.1 = (bf16[192,768]{1,0:T(8,128)(2,1)S(1)}, bf16[192,768]{1,0:T(8,128)(2,1)S(1)}, bf16[192,768]{1,0:T(8,128)(2,1)S(1)}, bf16[192,768]{1,0:T(8,128)(2,1)S(1)}, f32[8,3072]{1,0:T(8,128)S(1)}) custom-call(s32[6]{0:T(128)S(1)} %get-tuple-element.133.refs_0_, s32[6]{0:T(128)S(1)} %get-tuple-element.134.refs_1_, s32[1]{0:T(128)} %bitcast.1.refs_0_.refs_2_, ...), custom_call_target="tpu_custom_call" | custom-call | flops 3623878656 | bytes 6291456 | tf_op jit(solution)/shard_map/attend_forward/pallas_call | solution.py:144
  103.5 0.7 copy-done.21
  104.2 0.6 copy-done.22
  105.1 1.8 collective-permute-start.12
  106.9 1.4 collective-permute-start.13
  108.3 0.6 pad_add_fusion.refs_0_
  108.9 5.9 %collective-permute-done.11.refs_4_ = bf16[192,768]{1,0:T(8,128)(2,1)S(1)} collective-permute-done((bf16[192,768]{1,0:T(8,128)(2,1)S(1)}, bf16[192,768]{1,0:T(8,128)(2,1)S(1)}, u32[]{:S(2)}, u32[]{:S(2)}) %collective-permute-start.11) | collective-permute-done | bytes 294944 | tf_op jit(solution)/shard_map/ppermute | solution.py:1002
  114.8 3.4 %collective-permute-done.12.refs_5_ = bf16[192,768]{1,0:T(8,128)(2,1)S(1)} collective-permute-done((bf16[192,768]{1,0:T(8,128)(2,1)S(1)}, bf16[192,768]{1,0:T(8,128)(2,1)S(1)}, u32[]{:S(2)}, u32[]{:S(2)}) %collective-permute-start.12) | collective-permute-done | bytes 294944 | tf_op jit(solution)/shard_map/ppermute | solution.py:1002
  118.2 1.6 collective-permute-done.13.refs_6_
  119.8 0.7 copy-done.35
  120.5 53.2 %middle.1 = (bf16[768,768]{1,0:T(8,128)(2,1)}, f32[768,768]{1,0:T(8,128)}, bf16[192,768]{1,0:T(8,128)(2,1)}, bf16[192,768]{1,0:T(8,128)(2,1)}, bf16[192,768]{1,0...) custom-call(s32[2]{0:T(128)} %pad_add_fusion.refs_0_, ...), custom_call_target="tpu_custom_call" | custom-call | flops 24461180928 | bytes 28311552 | tf_op jit(solution)/shard_map/middle/pallas_call | solution.py:936
  173.8 1.2 collective-permute-start.15
  174.9 1.5 collective-permute-start.16
  176.4 0.9 collective-permute-start.17
  177.3 5.7 %collective-permute-done.14 = bf16[4,4,224,768]{3,2,1,0:T(8,128)(2,1)S(1)} collective-permute-done((bf16[4,4,224,768]{3,2,1,0:T(8,128)(2,1)}, bf16[4,4,224,768]{3,2,1,0:T(8,128)(2,1)S(1)}, u32[]{:S(2)}, u32[]{:S(2)}) %collective-permute-start.14) | collective-permute-done | bytes 5505056 | tf_op jit(solution)/shard_map/ppermute | solution.py:1007
  183.0 6.6 %add_convert_fusion = bf16[4,4,224,768]{3,2,1,0:T(8,128)(2,1)} fusion(bf16[4,4,224,768]{3,2,1,0:T(8,128)(2,1)S(1)} %collective-permute-done.14, bf16[4,4,224,768]{3,2,1,0:T(8,128)(2,1)} %get-tuple-element.91), kind=kLoop, calls=%fused_computation | loop fusion | flops 11010048 | bytes 16515072 | tf_op jit(solution)/shard_map/convert_element_type | solution.py:1136
  189.6 0.9 collective-permute-done.16.refs_8_
  190.6 0.7 copy-done.31
  192.4 64.2 %attend_backward.1 = (bf16[768,768]{1,0:T(8,128)(2,1)}, bf16[768,768]{1,0:T(8,128)(2,1)}, f32[768,768]{1,0:T(8,128)}, f32[384,768]{1,0:T(8,128)}, f32[384,768]{1,0:T(8,128)}, /*index=5*/bf16[576,3072]{1,0:T(8,128)(2,1)}) custom-call(s32[12]{0:T(128)} %get-tuple-element.131.refs_0_, s32[12]{0:T(128)} %get-tuple-element.132.refs_1_, s32[1]{0:T(128)} %bitcast.1.refs_0_.refs_2_, ...), custom_call_target="tpu_custom_call" | custom-call | flops 11777605632 | bytes 12582912 | tf_op jit(solution)/shard_map/attend_backward/pallas_call | solution.py:320
  256.6 0.7 collective-permute-start.18
  257.3 0.9 collective-permute-start.19
  258.3 1.3 copy-done.16
  259.5 2.0 copy-done.20
  261.5 6.1 %weight_gradient.1 = (bf16[4,4,24,768]{3,2,1,0:T(8,128)(2,1)S(1)}, bf16[4,4,24,768]{3,2,1,0:T(8,128)(2,1)S(1)}) custom-call(s32[4]{0:T(128)S(1)} %pad_add_fusion.1.refs_0_.me_ref, bf16[576,3072]{1,0:T(8,128)(2,1)S(1)} %copy-done.20, bf16[768,768]{1,0:T(8,128)(2,1)S(1)} %copy-done.16, bf16[768,768]{1,0:T(8,128)(2,1)S(1)} %copy-done.12, ...), custom_call_target="tpu_custom_call" | custom-call | flops 21743271936 | bytes 10616832 | tf_op jit(solution)/shard_map/weight_gradient/pallas_call | solution.py:411
  267.8 1.9 collective-permute-done.22
  269.9 2.4 collective-permute-start.23
  272.5 2.2 collective-permute-start.25
  274.7 7.9 %collective-permute-done.18 = bf16[768,768]{1,0:T(8,128)(2,1)} collective-permute-done((bf16[768,768]{1,0:T(8,128)(2,1)}, bf16[768,768]{1,0:T(8,128)(2,1)}, u32[]{:S(2)}, u32[]{:S(2)}) %collective-permute-start.18) | collective-permute-done | bytes 1179680 | tf_op jit(solution)/shard_map/ppermute | solution.py:1002
  282.6 1.1 collective-permute-done.19
  283.7 1.3 add_convert_fusion.3
  285.0 1.2 collective-permute-start.20
  286.2 1.2 add_convert_fusion.2
  287.4 0.6 collective-permute-start.21
  288.0 6.3 %collective-permute-done.24 = bf16[4,24,768]{2,1,0:T(8,128)(2,1)S(1)} collective-permute-done((bf16[4,24,768]{2,1,0:T(8,128)(2,1)S(1)}, bf16[4,24,768]{2,1,0:T(8,128)(2,1)S(1)}, u32[]{:S(2)}, u32[]{:S(2)}) %collective-permute-start.24) | collective-permute-done | bytes 147488 | tf_op jit(solution)/shard_map/ppermute | solution.py:1007
  294.4 0.6 slice_bitcast_fusion.4
  295.0 0.6 collective-permute-start.26
  295.6 1.7 collective-permute-start.27
  297.3 1.2 collective-permute-start.28
  298.5 0.6 collective-permute-done.20
  299.1 1.2 convert_add_fusion.1
  300.3 1.2 collective-permute-done.21
  301.5 1.2 convert_add_fusion
  302.7 1.7 maximum_add_fusion
  304.4 6.1 %reduce-scatter.5.cloned.1.call-done.refs_5_ = bf16[224,768]{1,0:T(8,128)(2,1)} async-done(((bf16[896,768]{1,0:T(8,128)(2,1)}), bf16[224,768]{1,0:T(8,128)(2,1)}) %reduce-scatter.5.cloned.1.call-update) | async-done | bytes 344080 | tf_op jit(solution)/shard_map/reduce_scatter | solution.py:1155
  310.5 2.2 finish.1
  (109 shorter events, 4.6 us)
Async XLA Ops:
  7.2 12.5 %copy-start.14 = (bf16[768,768]{1,0:T(8,128)(2,1)S(1)}, bf16[768,768]{1,0:T(8,128)(2,1)}, u32[]{:S(2)}) copy-start(bf16[768,768]{1,0:T(8,128)(2,1)} %x0_ref.1) | copy-start | bytes 3538948
  7.2 112.6 %all-gather.3.cloned.1.call-start = ((), (), s32[]{:S(2)}) async-start(), calls=%async_computation.4 | async-start | bytes 11354112 | tf_op jit(solution)/shard_map/all_gather | solution.py:1116
  9.3 39.4 %copy-start.26 = (s32[1,3072]{1,0:T(1,128)S(1)}, s32[1,3072]{1,0:T(1,128)}, u32[]{:S(2)}) copy-start(s32[1,3072]{1,0:T(1,128)} %param.17) | copy-start | bytes 36868
  9.3 258.4 %reduce-scatter.3.cloned.1.call-start = ((), (), s32[]{:S(2)}) async-start(), calls=%async_computation.2 | async-start | bytes 6881280 | tf_op jit(solution)/shard_map/reduce_scatter | solution.py:1138
  10.2 5.0 %collective-permute-start = (bf16[32,576]{1,0:T(8,128)(2,1)S(1)}, bf16[32,576]{1,0:T(8,128)(2,1)S(1)}, u32[]{:S(2)}, u32[]{:S(2)}) collective-permute-start(bf16[32,576]{1,0:T(8,128)(2,1)S(1)} %get-tuple-element.145), channel_id=1, source_target_pairs={{0,8},{8,0},{16,24},{24,16},{1,9},{9,1},{17,25},{25,17},{2,10},{10... | collective-permute-start | bytes 110600 | tf_op jit(solution)/shard_map/ppermute | solution.py:1002
  13.2 4.0 %collective-permute-start.1 = (bf16[32,576]{1,0:T(8,128)(2,1)S(1)}, bf16[32,576]{1,0:T(8,128)(2,1)S(1)}, u32[]{:S(2)}, u32[]{:S(2)}) collective-permute-start(bf16[32,576]{1,0:T(8,128)(2,1)S(1)} %get-tuple-element.144), channel_id=1, source_target_pairs={{0,16},{8,24},{16,0},{24,8},{1,17},{9,25},{17,1},{25,9},{2,18},{10... | collective-permute-start | bytes 110600 | tf_op jit(solution)/shard_map/ppermute | solution.py:1002
  14.7 4.9 %collective-permute-start.2 = (bf16[32,576]{1,0:T(8,128)(2,1)S(1)}, bf16[32,576]{1,0:T(8,128)(2,1)S(1)}, u32[]{:S(2)}, u32[]{:S(2)}) collective-permute-start(bf16[32,576]{1,0:T(8,128)(2,1)S(1)} %get-tuple-element.143), channel_id=1, source_target_pairs={{0,24},{8,16},{16,8},{24,0},{1,25},{9,17},{17,9},{25,1},{2,26},{10... | collective-permute-start | bytes 110600 | tf_op jit(solution)/shard_map/ppermute | solution.py:1002
  19.7 28.5 %collective-permute-start.6 = (bf16[768,768]{1,0:T(8,128)(2,1)S(1)}, bf16[768,768]{1,0:T(8,128)(2,1)S(1)}, u32[]{:S(2)}, u32[]{:S(2)}) collective-permute-start(bf16[768,768]{1,0:T(8,128)(2,1)S(1)} %copy-done.14), channel_id=1, source_target_pairs={{0,8},{8,0},{16,24},{24,16},{1,9},{9,1},{17,25},{25,17},{2,10},{10... | collective-permute-start | bytes 3538952 | tf_op jit(solution)/shard_map/ppermute | solution.py:1002
  20.3 28.4 %collective-permute-start.7 = (bf16[768,768]{1,0:T(8,128)(2,1)S(1)}, bf16[768,768]{1,0:T(8,128)(2,1)}, u32[]{:S(2)}, u32[]{:S(2)}) collective-permute-start(bf16[768,768]{1,0:T(8,128)(2,1)S(1)} %copy-done.14), channel_id=1, source_target_pairs={{0,16},{8,24},{16,0},{24,8},{1,17},{9,25},{17,1},{25,9},{2,18},{10... | collective-permute-start | bytes 3538952 | tf_op jit(solution)/shard_map/ppermute | solution.py:1002
  20.3 10.0 %collective-permute-start.3 = (bf16[4,32,576]{2,1,0:T(8,128)(2,1)S(1)}, bf16[4,32,576]{2,1,0:T(8,128)(2,1)S(1)}, u32[]{:S(2)}, u32[]{:S(2)}) collective-permute-start(bf16[4,32,576]{2,1,0:T(8,128)(2,1)S(1)} %pad_maximum_fusion.1), channel_id=1, source_target_pairs={{0,2},{1,3},{2,0},{3,1},{4,6},{5,7},{6,4},{7,5},{8,10},{9,11},{10,... | collective-permute-start | bytes 442376 | tf_op jit(solution)/shard_map/ppermute | solution.py:1007
  22.4 20.1 %collective-permute-start.4 = (bf16[4,32,576]{2,1,0:T(8,128)(2,1)S(1)}, bf16[4,32,576]{2,1,0:T(8,128)(2,1)S(1)}, u32[]{:S(2)}, u32[]{:S(2)}) collective-permute-start(bf16[4,32,576]{2,1,0:T(8,128)(2,1)S(1)} %pad_maximum_fusion.1), channel_id=1, source_target_pairs={{0,4},{1,5},{2,6},{3,7},{4,0},{5,1},{6,2},{7,3},{8,12},{9,13},{10,... | collective-permute-start | bytes 442376 | tf_op jit(solution)/shard_map/ppermute | solution.py:1007
  24.9 17.5 %collective-permute-start.5 = (bf16[4,32,576]{2,1,0:T(8,128)(2,1)S(1)}, bf16[4,32,576]{2,1,0:T(8,128)(2,1)S(1)}, u32[]{:S(2)}, u32[]{:S(2)}) collective-permute-start(bf16[4,32,576]{2,1,0:T(8,128)(2,1)S(1)} %pad_maximum_fusion.1), channel_id=1, source_target_pairs={{0,6},{1,7},{2,4},{3,5},{4,2},{5,3},{6,0},{7,1},{8,14},{9,15},{10,... | collective-permute-start | bytes 442376 | tf_op jit(solution)/shard_map/ppermute | solution.py:1007
  42.6 8.0 %copy-start.4 = (bf16[4,4,32,576]{3,2,1,0:T(8,128)(2,1)}, bf16[4,4,32,576]{3,2,1,0:T(8,128)(2,1)S(1)}, u32[]{:S(2)}) copy-start(bf16[4,4,32,576]{3,2,1,0:T(8,128)(2,1)S(1)} %pad_maximum_fusion.refs_5_) | copy-start | bytes 1769476
  48.2 3.9 %copy-start.10 = (bf16[768,768]{1,0:T(8,128)(2,1)}, bf16[768,768]{1,0:T(8,128)(2,1)S(1)}, u32[]{:S(2)}) copy-start(bf16[768,768]{1,0:T(8,128)(2,1)S(1)} %collective-permute-done.6.refs_2_.x1_ref) | copy-start | bytes 3538948
  48.7 4.5 %collective-permute-start.10 = (bf16[4,4,32,576]{3,2,1,0:T(8,128)(2,1)S(1)}, bf16[4,4,32,576]{3,2,1,0:T(8,128)(2,1)}, u32[]{:S(2)}, u32[]{:S(2)}) collective-permute-start(bf16[4,4,32,576]{3,2,1,0:T(8,128)(2,1)S(1)} %pad_maximum_fusion.refs_5_), channel_id=1, source_target_pairs={{0,1},{1,0},{2,3},{3,2},{4,5},{5,4},{6,7},{7,6},{8,9},{9,8},{10,11... | collective-permute-start | bytes 1769480 | tf_op jit(solution)/shard_map/ppermute | solution.py:1007
  49.4 3.8 %copy-start.15 = (bf16[768,768]{1,0:T(8,128)(2,1)S(1)}, bf16[768,768]{1,0:T(8,128)(2,1)}, u32[]{:S(2)}) copy-start(bf16[768,768]{1,0:T(8,128)(2,1)} %x0_ref.1) | copy-start | bytes 3538948
  50.6 22.5 %collective-permute-start.8 = (bf16[384,768]{1,0:T(8,128)(2,1)S(1)}, bf16[384,768]{1,0:T(8,128)(2,1)S(1)}, u32[]{:S(2)}, u32[]{:S(2)}) collective-permute-start(bf16[384,768]{1,0:T(8,128)(2,1)S(1)} %slice.72), channel_id=1, source_target_pairs={{0,8},{8,0},{16,24},{24,16},{1,9},{9,1},{17,25},{25,17},{2,10},{10... | collective-permute-start | bytes 1769480 | tf_op jit(solution)/shard_map/ppermute | solution.py:1002
  52.1 1.2 copy-start.5
  52.1 21.1 %collective-permute-start.9 = (bf16[384,768]{1,0:T(8,128)(2,1)S(1)}, bf16[384,768]{1,0:T(8,128)(2,1)S(1)}, u32[]{:S(2)}, u32[]{:S(2)}) collective-permute-start(bf16[384,768]{1,0:T(8,128)(2,1)S(1)} %slice.73), channel_id=1, source_target_pairs={{0,16},{8,24},{16,0},{24,8},{1,17},{9,25},{17,1},{25,9},{2,18},{10... | collective-permute-start | bytes 1769480 | tf_op jit(solution)/shard_map/ppermute | solution.py:1002
  52.9 205.3 %copy-start.13 = (s32[4]{0:T(128)}, s32[4]{0:T(128)S(1)}, u32[]{:S(2)}) copy-start(s32[4]{0:T(128)S(1)} %pad_add_fusion.1.refs_0_.me_ref) | copy-start | bytes 52
  53.2 1.3 copy-start.11
  60.7 14.2 %copy-start.3 = (bf16[3,768,192]{2,1,0:T(8,128)(2,1)}, bf16[3,768,192]{2,1,0:T(8,128)(2,1)S(1)}, u32[]{:S(2)}) copy-start(bf16[3,768,192]{2,1,0:T(8,128)(2,1)S(1)} %get-tuple-element.77.refs_4_.refs_15_) | copy-start | bytes 2654212
  73.2 1.7 copy-start.6
  73.2 1.7 copy-start.8
  74.9 28.6 %copy-start = (bf16[3072,256]{1,0:T(8,128)(2,1)}, bf16[3072,256]{1,0:T(8,128)(2,1)S(1)}, u32[]{:S(2)}) copy-start(bf16[3072,256]{1,0:T(8,128)(2,1)S(1)} %get-tuple-element.82.refs_3_) | copy-start | bytes 4718596
  74.9 28.6 %copy-start.1 = (bf16[3072,256]{1,0:T(8,128)(2,1)}, bf16[3072,256]{1,0:T(8,128)(2,1)S(1)}, u32[]{:S(2)}) copy-start(bf16[3072,256]{1,0:T(8,128)(2,1)S(1)} %get-tuple-element.83.refs_4_) | copy-start | bytes 4718596
  74.9 28.6 %copy-start.2 = (bf16[3072,192]{1,0:T(8,128)(2,1)}, bf16[3072,192]{1,0:T(8,128)(2,1)S(1)}, u32[]{:S(2)}) copy-start(bf16[3072,192]{1,0:T(8,128)(2,1)S(1)} %get-tuple-element.84.refs_5_) | copy-start | bytes 3538948
  104.8 68.8 %copy-start.17 = (bf16[192,768]{1,0:T(8,128)(2,1)}, bf16[192,768]{1,0:T(8,128)(2,1)S(1)}, u32[]{:S(2)}) copy-start(bf16[192,768]{1,0:T(8,128)(2,1)S(1)} %get-tuple-element.86.refs_11_) | copy-start | bytes 884740
  104.8 68.8 %copy-start.18 = (bf16[192,768]{1,0:T(8,128)(2,1)}, bf16[192,768]{1,0:T(8,128)(2,1)S(1)}, u32[]{:S(2)}) copy-start(bf16[192,768]{1,0:T(8,128)(2,1)S(1)} %get-tuple-element.87.refs_12_) | copy-start | bytes 884740
  104.8 68.9 %copy-start.19 = (bf16[192,768]{1,0:T(8,128)(2,1)}, bf16[192,768]{1,0:T(8,128)(2,1)S(1)}, u32[]{:S(2)}) copy-start(bf16[192,768]{1,0:T(8,128)(2,1)S(1)} %get-tuple-element.88.refs_13_) | copy-start | bytes 884740
  104.8 9.9 %collective-permute-start.11 = (bf16[192,768]{1,0:T(8,128)(2,1)S(1)}, bf16[192,768]{1,0:T(8,128)(2,1)S(1)}, u32[]{:S(2)}, u32[]{:S(2)}) collective-permute-start(bf16[192,768]{1,0:T(8,128)(2,1)S(1)} %get-tuple-element.86.refs_11_), channel_id=1, source_target_pairs={{0,8},{8,0},{16,24},{24,16},{1,9},{9,1},{17,25},{25,17},{2,10},{10... | collective-permute-start | bytes 884744 | tf_op jit(solution)/shard_map/ppermute | solution.py:1002
  105.1 13.0 %collective-permute-start.12 = (bf16[192,768]{1,0:T(8,128)(2,1)S(1)}, bf16[192,768]{1,0:T(8,128)(2,1)S(1)}, u32[]{:S(2)}, u32[]{:S(2)}) collective-permute-start(bf16[192,768]{1,0:T(8,128)(2,1)S(1)} %get-tuple-element.87.refs_12_), channel_id=1, source_target_pairs={{0,16},{8,24},{16,0},{24,8},{1,17},{9,25},{17,1},{25,9},{2,18},{10... | collective-permute-start | bytes 884744 | tf_op jit(solution)/shard_map/ppermute | solution.py:1002
  106.9 12.9 %collective-permute-start.13 = (bf16[192,768]{1,0:T(8,128)(2,1)S(1)}, bf16[192,768]{1,0:T(8,128)(2,1)S(1)}, u32[]{:S(2)}, u32[]{:S(2)}) collective-permute-start(bf16[192,768]{1,0:T(8,128)(2,1)S(1)} %get-tuple-element.88.refs_13_), channel_id=1, source_target_pairs={{0,24},{8,16},{16,8},{24,0},{1,25},{9,17},{17,9},{25,1},{2,26},{10... | collective-permute-start | bytes 884744 | tf_op jit(solution)/shard_map/ppermute | solution.py:1002
  114.8 5.0 %copy-start.33 = (bf16[192,768]{1,0:T(8,128)(2,1)}, bf16[192,768]{1,0:T(8,128)(2,1)S(1)}, u32[]{:S(2)}) copy-start(bf16[192,768]{1,0:T(8,128)(2,1)S(1)} %collective-permute-done.11.refs_4_) | copy-start | bytes 884740
  118.2 1.6 copy-start.34
  173.7 9.3 %collective-permute-start.14 = (bf16[4,4,224,768]{3,2,1,0:T(8,128)(2,1)}, bf16[4,4,224,768]{3,2,1,0:T(8,128)(2,1)S(1)}, u32[]{:S(2)}, u32[]{:S(2)}) collective-permute-start(bf16[4,4,224,768]{3,2,1,0:T(8,128)(2,1)} %get-tuple-element.92), channel_id=1, source_target_pairs={{0,1},{1,0},{2,3},{3,2},{4,5},{5,4},{6,7},{7,6},{8,9},{9,8},{10,11... | collective-permute-start | bytes 16515080 | tf_op jit(solution)/shard_map/ppermute | solution.py:1007
  173.8 15.9 %collective-permute-start.15 = (bf16[192,768]{1,0:T(8,128)(2,1)}, bf16[192,768]{1,0:T(8,128)(2,1)S(1)}, u32[]{:S(2)}, u32[]{:S(2)}) collective-permute-start(bf16[192,768]{1,0:T(8,128)(2,1)} %get-tuple-element.94), channel_id=1, source_target_pairs={{0,8},{8,0},{16,24},{24,16},{1,9},{9,1},{17,25},{25,17},{2,10},{10... | collective-permute-start | bytes 884744 | tf_op jit(solution)/shard_map/ppermute | solution.py:1002
  174.9 15.6 %collective-permute-start.16 = (bf16[192,768]{1,0:T(8,128)(2,1)}, bf16[192,768]{1,0:T(8,128)(2,1)S(1)}, u32[]{:S(2)}, u32[]{:S(2)}) collective-permute-start(bf16[192,768]{1,0:T(8,128)(2,1)} %get-tuple-element.95), channel_id=1, source_target_pairs={{0,16},{8,24},{16,0},{24,8},{1,17},{9,25},{17,1},{25,9},{2,18},{10... | collective-permute-start | bytes 884744 | tf_op jit(solution)/shard_map/ppermute | solution.py:1002
  176.4 14.1 %collective-permute-start.17 = (bf16[192,768]{1,0:T(8,128)(2,1)}, bf16[192,768]{1,0:T(8,128)(2,1)S(1)}, u32[]{:S(2)}, u32[]{:S(2)}) collective-permute-start(bf16[192,768]{1,0:T(8,128)(2,1)} %get-tuple-element.96), channel_id=1, source_target_pairs={{0,24},{8,16},{16,8},{24,0},{1,25},{9,17},{17,9},{25,1},{2,26},{10... | collective-permute-start | bytes 884744 | tf_op jit(solution)/shard_map/ppermute | solution.py:1002
  189.6 1.0 copy-start.30
  190.6 0.8 copy-start.32
  191.4 119.1 %reduce-scatter.5.cloned.1.call-start = ((), (), s32[]{:S(2)}) async-start(), calls=%async_computation.3 | async-start | bytes 1720320 | tf_op jit(solution)/shard_map/reduce_scatter | solution.py:1155
  192.3 65.9 %copy-start.7 = (bf16[384,768]{1,0:T(8,128)(2,1)S(1)}, bf16[384,768]{1,0:T(8,128)(2,1)}, u32[]{:S(2)}) copy-start(bf16[384,768]{1,0:T(8,128)(2,1)} %copy-done.6) | copy-start | bytes 1769476
  192.3 65.9 %copy-start.9 = (bf16[384,768]{1,0:T(8,128)(2,1)S(1)}, bf16[384,768]{1,0:T(8,128)(2,1)}, u32[]{:S(2)}) copy-start(bf16[384,768]{1,0:T(8,128)(2,1)} %copy-done.8) | copy-start | bytes 1769476
  192.4 65.9 %copy-start.12 = (bf16[768,768]{1,0:T(8,128)(2,1)S(1)}, bf16[768,768]{1,0:T(8,128)(2,1)}, u32[]{:S(2)}) copy-start(bf16[768,768]{1,0:T(8,128)(2,1)} %copy-done.10) | copy-start | bytes 3538948
  256.6 26.0 %collective-permute-start.18 = (bf16[768,768]{1,0:T(8,128)(2,1)}, bf16[768,768]{1,0:T(8,128)(2,1)}, u32[]{:S(2)}, u32[]{:S(2)}) collective-permute-start(bf16[768,768]{1,0:T(8,128)(2,1)} %get-tuple-element.104), channel_id=1, source_target_pairs={{0,8},{8,0},{16,24},{24,16},{1,9},{9,1},{17,25},{25,17},{2,10},{10... | collective-permute-start | bytes 3538952 | tf_op jit(solution)/shard_map/ppermute | solution.py:1002
  257.3 26.4 %collective-permute-start.19 = (bf16[768,768]{1,0:T(8,128)(2,1)}, bf16[768,768]{1,0:T(8,128)(2,1)}, u32[]{:S(2)}, u32[]{:S(2)}) collective-permute-start(bf16[768,768]{1,0:T(8,128)(2,1)} %get-tuple-element.105), channel_id=1, source_target_pairs={{0,16},{8,24},{16,0},{24,8},{1,17},{9,25},{17,1},{25,9},{2,18},{10... | collective-permute-start | bytes 3538952 | tf_op jit(solution)/shard_map/ppermute | solution.py:1002
  258.3 1.3 copy-start.16
  259.5 2.0 copy-start.20
  267.6 2.1 collective-permute-start.22
  269.7 14.0 %copy-start.25 = (f32[384,768]{1,0:T(8,128)S(1)}, f32[384,768]{1,0:T(8,128)}, u32[]{:S(2)}) copy-start(f32[384,768]{1,0:T(8,128)} %get-tuple-element.107) | copy-start | bytes 3538948
  269.9 18.1 %collective-permute-start.23 = (bf16[4,24,768]{2,1,0:T(8,128)(2,1)S(1)}, bf16[4,24,768]{2,1,0:T(8,128)(2,1)S(1)}, u32[]{:S(2)}, u32[]{:S(2)}) collective-permute-start(bf16[4,24,768]{2,1,0:T(8,128)(2,1)S(1)} %get-tuple-element.135), channel_id=1, source_target_pairs={{0,2},{1,3},{2,0},{3,1},{4,6},{5,7},{6,4},{7,5},{8,10},{9,11},{10,... | collective-permute-start | bytes 442376 | tf_op jit(solution)/shard_map/ppermute | solution.py:1007
  272.2 22.1 %collective-permute-start.24 = (bf16[4,24,768]{2,1,0:T(8,128)(2,1)S(1)}, bf16[4,24,768]{2,1,0:T(8,128)(2,1)S(1)}, u32[]{:S(2)}, u32[]{:S(2)}) collective-permute-start(bf16[4,24,768]{2,1,0:T(8,128)(2,1)S(1)} %get-tuple-element.137), channel_id=1, source_target_pairs={{0,4},{1,5},{2,6},{3,7},{4,0},{5,1},{6,2},{7,3},{8,12},{9,13},{10,... | collective-permute-start | bytes 442376 | tf_op jit(solution)/shard_map/ppermute | solution.py:1007
  272.5 21.8 %collective-permute-start.25 = (bf16[4,24,768]{2,1,0:T(8,128)(2,1)S(1)}, bf16[4,24,768]{2,1,0:T(8,128)(2,1)S(1)}, u32[]{:S(2)}, u32[]{:S(2)}) collective-permute-start(bf16[4,24,768]{2,1,0:T(8,128)(2,1)S(1)} %get-tuple-element.136), channel_id=1, source_target_pairs={{0,6},{1,7},{2,4},{3,5},{4,2},{5,3},{6,0},{7,1},{8,14},{9,15},{10,... | collective-permute-start | bytes 442376 | tf_op jit(solution)/shard_map/ppermute | solution.py:1007
  283.7 2.5 copy-start.24
  285.0 14.1 %collective-permute-start.20 = (bf16[384,768]{1,0:T(8,128)(2,1)S(1)}, bf16[384,768]{1,0:T(8,128)(2,1)S(1)}, u32[]{:S(2)}, u32[]{:S(2)}) collective-permute-start(bf16[384,768]{1,0:T(8,128)(2,1)S(1)} %add_convert_fusion.3), channel_id=1, source_target_pairs={{0,16},{8,24},{16,0},{24,8},{1,17},{9,25},{17,1},{25,9},{2,18},{10... | collective-permute-start | bytes 1769480 | tf_op jit(solution)/shard_map/ppermute | solution.py:1002
  287.4 14.1 %collective-permute-start.21 = (bf16[384,768]{1,0:T(8,128)(2,1)S(1)}, bf16[384,768]{1,0:T(8,128)(2,1)S(1)}, u32[]{:S(2)}, u32[]{:S(2)}) collective-permute-start(bf16[384,768]{1,0:T(8,128)(2,1)S(1)} %add_convert_fusion.2), channel_id=1, source_target_pairs={{0,8},{8,0},{16,24},{24,16},{1,9},{9,1},{17,25},{25,17},{2,10},{10... | collective-permute-start | bytes 1769480 | tf_op jit(solution)/shard_map/ppermute | solution.py:1002
  295.0 9.3 %collective-permute-start.26 = (f32[24,768]{1,0:T(8,128)S(1)}, f32[24,768]{1,0:T(8,128)S(1)}, u32[]{:S(2)}, u32[]{:S(2)}) collective-permute-start(f32[24,768]{1,0:T(8,128)S(1)} %get-tuple-element.140), channel_id=1, source_target_pairs={{0,8},{8,0},{16,24},{24,16},{1,9},{9,1},{17,25},{25,17},{2,10},{10... | collective-permute-start | bytes 221192 | tf_op jit(solution)/shard_map/ppermute | solution.py:1002
  295.6 8.8 %collective-permute-start.27 = (f32[24,768]{1,0:T(8,128)S(1)}, f32[24,768]{1,0:T(8,128)S(1)}, u32[]{:S(2)}, u32[]{:S(2)}) collective-permute-start(f32[24,768]{1,0:T(8,128)S(1)} %get-tuple-element.139), channel_id=1, source_target_pairs={{0,16},{8,24},{16,0},{24,8},{1,17},{9,25},{17,1},{25,9},{2,18},{10... | collective-permute-start | bytes 221192 | tf_op jit(solution)/shard_map/ppermute | solution.py:1002
  297.3 7.1 %collective-permute-start.28 = (f32[24,768]{1,0:T(8,128)S(1)}, f32[24,768]{1,0:T(8,128)S(1)}, u32[]{:S(2)}, u32[]{:S(2)}) collective-permute-start(f32[24,768]{1,0:T(8,128)S(1)} %get-tuple-element.138), channel_id=1, source_target_pairs={{0,24},{8,16},{16,8},{24,0},{1,25},{9,17},{17,9},{25,1},{2,26},{10... | collective-permute-start | bytes 221192 | tf_op jit(solution)/shard_map/ppermute | solution.py:1002
  300.3 2.4 copy-start.23
  304.4 6.1 %copy-start.27 = (f32[24,768]{1,0:T(8,128)}, f32[24,768]{1,0:T(8,128)S(1)}, u32[]{:S(2)}) copy-start(f32[24,768]{1,0:T(8,128)S(1)} %collective-permute-done.26.refs_2_) | copy-start | bytes 221188
  304.4 6.1 %copy-start.28 = (f32[24,768]{1,0:T(8,128)}, f32[24,768]{1,0:T(8,128)S(1)}, u32[]{:S(2)}) copy-start(f32[24,768]{1,0:T(8,128)S(1)} %collective-permute-done.27.refs_3_) | copy-start | bytes 221188
  304.4 6.1 %copy-start.29 = (f32[24,768]{1,0:T(8,128)}, f32[24,768]{1,0:T(8,128)S(1)}, u32[]{:S(2)}) copy-start(f32[24,768]{1,0:T(8,128)S(1)} %collective-permute-done.28.refs_4_) | copy-start | bytes 221188
  (4 other events, 2.8 us)
Sparse Core Ops, SparseCore 0:
  11.6 105.8 all-gather.2
  190.7 62.7 reduce-scatter.2
  267.9 42.5 reduce-scatter.4

commit v7 on v6

--- a/solution.py
+++ b/solution.py
@@ -11,7 +11,7 @@
 far = 1e30
 FQ, FK = 512, 512
 BQ, BK = 512, 256
-ROWS = 384
+ROWS = 768
 f32 = jnp.float32
 bf16 = jnp.bfloat16
 norm_eps = 1e-06

time: 322 us -> 319 us (level)
  Pallas kernels: 164 us -> 159 us
    ppermute x20, waiting for transfers between devices: 46 us -> 53.1 us  [by_sp(): return lax.ppermute(value, 'sp', [(i, i ^ flip) for i in range(groups)])]
    ppermute x9, waiting for transfers between devices: 31.5 us -> 28 us  [by_fsdp(): return lax.ppermute(value, 'fsdp', [(i, i ^ flip) for i in range(shards)])]
where the time goes in v7:
time: 319 us; the launch traced here: 316 us
  Pallas kernels  159 us (50%)
  waiting for transfers between devices  85 us (27%)
  starting transfers between devices  32.1 us (10%)
  other arithmetic  15.2 us (5%)
  between operations  14.2 us (4%)
  local copies, waits for them, and re-layouts  11.1 us (3%)
    pallas_call x1, Pallas kernels, attend_backward(): pl.pallas_call(lambda *refs: backward_kernel(heads, *refs), grid_spec=plt...  63.4 us
    ppermute x20, waiting for transfers between devices, by_sp(): return lax.ppermute(value, 'sp', [(i, i ^ flip) for i in range(groups)])  53.1 us
    pallas_call x1, Pallas kernels, middle(): pl.pallas_call(lambda *refs: middle_kernel(groups, chunks, *refs), grid=(...  50 us
    ppermute x9, waiting for transfers between devices, by_fsdp(): return lax.ppermute(value, 'fsdp', [(i, i ^ flip) for i in range(shards)])  28 us
    pallas_call x1, Pallas kernels, attend_forward(): pl.pallas_call(lambda *refs: forward_kernel(heads, *refs), grid_spec=pltp...  27.2 us
    ppermute x20, starting transfers between devices, by_sp(): return lax.ppermute(value, 'sp', [(i, i ^ flip) for i in range(groups)])  21.8 us
    ppermute x9, starting transfers between devices, by_fsdp(): return lax.ppermute(value, 'fsdp', [(i, i ^ flip) for i in range(shards)])  10.2 us
    unnamed x72, local copies, waits for them, and re-layouts  7.48 us
  transfers between devices with their start and end apart: 32, of which 20 were waited for; matrix products, arithmetic and copies ran while one was open for 6% of the time, Pallas kernels for 33%

profile of v7, /device:TPU:0, one launch (start us, length us, event | category | flops | bytes accessed | tf_op | source)
XLA Modules:
  0.0 316.3 jit_solution(1716757558981122507)
XLA Ops:
  7.2 2.0 pack.1
  9.3 0.9 fusion.8
  10.2 3.0 collective-permute-start
  13.2 1.5 collective-permute-start.1
  15.2 2.0 collective-permute-done.1
  17.2 2.4 collective-permute-done.2
  19.7 0.6 collective-permute-start.6
  20.3 2.0 collective-permute-start.3
  22.4 2.6 collective-permute-start.4
  25.0 5.4 %collective-permute-done.3 = bf16[4,32,576]{2,1,0:T(8,128)(2,1)S(1)} collective-permute-done((bf16[4,32,576]{2,1,0:T(8,128)(2,1)S(1)}, bf16[4,32,576]{2,1,0:T(8,128)(2,1)S(1)}, u32[]{:S(2)}, u32[]{:S(2)}) %collective-permute-start.3) | collective-permute-done | bytes 147488 | tf_op jit(solution)/shard_map/ppermute | solution.py:1007
  30.4 12.1 %collective-permute-done.4 = bf16[4,32,576]{2,1,0:T(8,128)(2,1)S(1)} collective-permute-done((bf16[4,32,576]{2,1,0:T(8,128)(2,1)S(1)}, bf16[4,32,576]{2,1,0:T(8,128)(2,1)S(1)}, u32[]{:S(2)}, u32[]{:S(2)}) %collective-permute-start.4) | collective-permute-done | bytes 147488 | tf_op jit(solution)/shard_map/ppermute | solution.py:1007
  42.6 5.6 %collective-permute-done.6.refs_2_.x1_ref = bf16[768,768]{1,0:T(8,128)(2,1)S(1)} collective-permute-done((bf16[768,768]{1,0:T(8,128)(2,1)S(1)}, bf16[768,768]{1,0:T(8,128)(2,1)S(1)}, u32[]{:S(2)}, u32[]{:S(2)}) %collective-permute-start.6) | collective-permute-done | bytes 1179680 | tf_op jit(solution)/shard_map/ppermute | solution.py:1002
  49.4 1.2 slice.72
  50.6 1.4 collective-permute-start.8
  52.1 0.8 collective-permute-start.9
  53.3 1.3 copy-done.11
  54.5 6.1 %project.1 = (bf16[3072,256]{1,0:T(8,128)(2,1)S(1)}, bf16[3072,256]{1,0:T(8,128)(2,1)S(1)}, bf16[3072,192]{1,0:T(8,128)(2,1)S(1)}, bf16[3,768,192]{2,1,0:T(8,128)(2,1)S(1)}, f32[8,192]{1,0:T(8,128)S(1)}) custom-call(s32[4]{0:T(128)S(1)} %pad_add_fusion.1.refs_0_.me_ref, bf16[768,768]{1,0:T(8,128)(2,1)S(1)} %copy-done.15, bf16[768,768]{1,0:T(8,128)(2,1)S(1)} %copy-done.11, ...), custom_call_target="tpu_custom_call" | custom-call | flops 2038431744 | bytes 9437184 | tf_op jit(solution)/shard_map/project/pallas_call | solution.py:569
  60.7 12.5 %collective-permute-done.8.refs_1_.x3u_ref = bf16[384,768]{1,0:T(8,128)(2,1)S(1)} collective-permute-done((bf16[384,768]{1,0:T(8,128)(2,1)S(1)}, bf16[384,768]{1,0:T(8,128)(2,1)S(1)}, u32[]{:S(2)}, u32[]{:S(2)}) %collective-permute-start.8) | collective-permute-done | bytes 589856 | tf_op jit(solution)/shard_map/ppermute | solution.py:1002
  73.2 1.6 project_last.1
  74.9 27.2 %attend_forward.1 = (bf16[192,768]{1,0:T(8,128)(2,1)S(1)}, bf16[192,768]{1,0:T(8,128)(2,1)S(1)}, bf16[192,768]{1,0:T(8,128)(2,1)S(1)}, bf16[192,768]{1,0:T(8,128)(2,1)S(1)}, f32[8,3072]{1,0:T(8,128)S(1)}) custom-call(s32[6]{0:T(128)S(1)} %get-tuple-element.133.refs_0_, s32[6]{0:T(128)S(1)} %get-tuple-element.134.refs_1_, s32[1]{0:T(128)} %bitcast.1.refs_0_.refs_2_, ...), custom_call_target="tpu_custom_call" | custom-call | flops 3623878656 | bytes 6291456 | tf_op jit(solution)/shard_map/attend_forward/pallas_call | solution.py:144
  102.2 0.7 copy-done.21
  102.9 0.6 copy-done.22
  103.8 1.8 collective-permute-start.12
  105.6 1.4 collective-permute-start.13
  107.0 0.6 pad_add_fusion.refs_0_
  107.6 5.8 %collective-permute-done.11.refs_4_ = bf16[192,768]{1,0:T(8,128)(2,1)S(1)} collective-permute-done((bf16[192,768]{1,0:T(8,128)(2,1)S(1)}, bf16[192,768]{1,0:T(8,128)(2,1)S(1)}, u32[]{:S(2)}, u32[]{:S(2)}) %collective-permute-start.11) | collective-permute-done | bytes 294944 | tf_op jit(solution)/shard_map/ppermute | solution.py:1002
  113.4 4.8 %collective-permute-done.12.refs_5_ = bf16[192,768]{1,0:T(8,128)(2,1)S(1)} collective-permute-done((bf16[192,768]{1,0:T(8,128)(2,1)S(1)}, bf16[192,768]{1,0:T(8,128)(2,1)S(1)}, u32[]{:S(2)}, u32[]{:S(2)}) %collective-permute-start.12) | collective-permute-done | bytes 294944 | tf_op jit(solution)/shard_map/ppermute | solution.py:1002
  118.2 1.6 collective-permute-done.13.refs_6_
  119.8 0.7 copy-done.35
  120.5 50.0 %middle.1 = (bf16[768,768]{1,0:T(8,128)(2,1)}, f32[768,768]{1,0:T(8,128)}, bf16[192,768]{1,0:T(8,128)(2,1)}, bf16[192,768]{1,0:T(8,128)(2,1)}, bf16[192,768]{1,0...) custom-call(s32[2]{0:T(128)} %pad_add_fusion.refs_0_, ...), custom_call_target="tpu_custom_call" | custom-call | flops 24461180928 | bytes 28311552 | tf_op jit(solution)/shard_map/middle/pallas_call | solution.py:936
  170.6 1.2 collective-permute-start.15
  171.8 1.5 collective-permute-start.16
  173.3 0.9 collective-permute-start.17
  174.2 5.7 %collective-permute-done.14 = bf16[4,4,224,768]{3,2,1,0:T(8,128)(2,1)S(1)} collective-permute-done((bf16[4,4,224,768]{3,2,1,0:T(8,128)(2,1)}, bf16[4,4,224,768]{3,2,1,0:T(8,128)(2,1)S(1)}, u32[]{:S(2)}, u32[]{:S(2)}) %collective-permute-start.14) | collective-permute-done | bytes 5505056 | tf_op jit(solution)/shard_map/ppermute | solution.py:1007
  179.9 6.6 %add_convert_fusion = bf16[4,4,224,768]{3,2,1,0:T(8,128)(2,1)} fusion(bf16[4,4,224,768]{3,2,1,0:T(8,128)(2,1)S(1)} %collective-permute-done.14, bf16[4,4,224,768]{3,2,1,0:T(8,128)(2,1)} %get-tuple-element.91), kind=kLoop, calls=%fused_computation | loop fusion | flops 11010048 | bytes 16515072 | tf_op jit(solution)/shard_map/convert_element_type | solution.py:1136
  186.5 0.9 collective-permute-done.16.refs_8_
  187.5 0.7 copy-done.31
  188.7 0.5 subtract_minimum_fusion
  189.2 63.4 %attend_backward.1 = (bf16[768,768]{1,0:T(8,128)(2,1)}, bf16[768,768]{1,0:T(8,128)(2,1)}, f32[768,768]{1,0:T(8,128)}, f32[384,768]{1,0:T(8,128)}, f32[384,768]{1,0:T(8,128)}, /*index=5*/bf16[576,3072]{1,0:T(8,128)(2,1)}) custom-call(s32[12]{0:T(128)} %get-tuple-element.131.refs_0_, s32[12]{0:T(128)} %get-tuple-element.132.refs_1_, s32[1]{0:T(128)} %bitcast.1.refs_0_.refs_2_, ...), custom_call_target="tpu_custom_call" | custom-call | flops 11777605632 | bytes 12582912 | tf_op jit(solution)/shard_map/attend_backward/pallas_call | solution.py:320
  252.6 1.1 collective-permute-start.18
  253.7 0.9 collective-permute-start.19
  254.6 1.3 copy-done.16
  255.9 2.0 copy-done.20
  257.9 6.1 %weight_gradient.1 = (bf16[4,4,24,768]{3,2,1,0:T(8,128)(2,1)S(1)}, bf16[4,4,24,768]{3,2,1,0:T(8,128)(2,1)S(1)}) custom-call(s32[4]{0:T(128)S(1)} %pad_add_fusion.1.refs_0_.me_ref, bf16[576,3072]{1,0:T(8,128)(2,1)S(1)} %copy-done.20, bf16[768,768]{1,0:T(8,128)(2,1)S(1)} %copy-done.16, bf16[768,768]{1,0:T(8,128)(2,1)S(1)} %copy-done.12, ...), custom_call_target="tpu_custom_call" | custom-call | flops 21743271936 | bytes 10616832 | tf_op jit(solution)/shard_map/weight_gradient/pallas_call | solution.py:411
  264.1 1.9 collective-permute-done.22
  266.2 2.9 collective-permute-start.23
  269.1 2.6 collective-permute-start.24
  271.7 8.7 %collective-permute-done.18 = bf16[768,768]{1,0:T(8,128)(2,1)} collective-permute-done((bf16[768,768]{1,0:T(8,128)(2,1)}, bf16[768,768]{1,0:T(8,128)(2,1)}, u32[]{:S(2)}, u32[]{:S(2)}) %collective-permute-start.18) | collective-permute-done | bytes 1179680 | tf_op jit(solution)/shard_map/ppermute | solution.py:1002
  280.4 1.1 collective-permute-done.19
  281.5 1.3 add_convert_fusion.3
  282.8 1.3 collective-permute-start.20
  284.1 1.2 add_convert_fusion.2
  285.2 0.6 collective-permute-start.21
  285.8 2.9 collective-permute-done.24
  288.8 0.6 slice_bitcast_fusion.4
  289.4 0.8 collective-permute-start.26
  290.2 2.7 collective-permute-start.28
  292.9 4.7 %collective-permute-done.20 = bf16[384,768]{1,0:T(8,128)(2,1)S(1)} collective-permute-done((bf16[384,768]{1,0:T(8,128)(2,1)S(1)}, bf16[384,768]{1,0:T(8,128)(2,1)S(1)}, u32[]{:S(2)}, u32[]{:S(2)}) %collective-permute-start.20) | collective-permute-done | bytes 589856 | tf_op jit(solution)/shard_map/ppermute | solution.py:1002
  297.6 1.2 convert_add_fusion.1
  298.8 2.1 collective-permute-done.21
  300.9 1.2 convert_add_fusion
  302.1 1.7 maximum_add_fusion
  303.8 3.8 %reduce-scatter.5.cloned.1.call-done.refs_5_ = bf16[224,768]{1,0:T(8,128)(2,1)} async-done(((bf16[896,768]{1,0:T(8,128)(2,1)}), bf16[224,768]{1,0:T(8,128)(2,1)}) %reduce-scatter.5.cloned.1.call-update) | async-done | bytes 344080 | tf_op jit(solution)/shard_map/reduce_scatter | solution.py:1155
  307.6 2.2 finish.1
  (109 shorter events, 3.8 us)
Async XLA Ops:
  7.2 12.5 %copy-start.14 = (bf16[768,768]{1,0:T(8,128)(2,1)S(1)}, bf16[768,768]{1,0:T(8,128)(2,1)}, u32[]{:S(2)}) copy-start(bf16[768,768]{1,0:T(8,128)(2,1)} %x0_ref.1) | copy-start | bytes 3538948
  7.2 112.6 %all-gather.3.cloned.1.call-start = ((), (), s32[]{:S(2)}) async-start(), calls=%async_computation.4 | async-start | bytes 11354112 | tf_op jit(solution)/shard_map/all_gather | solution.py:1116
  9.3 39.4 %copy-start.26 = (s32[1,3072]{1,0:T(1,128)S(1)}, s32[1,3072]{1,0:T(1,128)}, u32[]{:S(2)}) copy-start(s32[1,3072]{1,0:T(1,128)} %param.17) | copy-start | bytes 36868
  9.3 254.8 %reduce-scatter.3.cloned.1.call-start = ((), (), s32[]{:S(2)}) async-start(), calls=%async_computation.2 | async-start | bytes 6881280 | tf_op jit(solution)/shard_map/reduce_scatter | solution.py:1138
  10.2 5.0 %collective-permute-start = (bf16[32,576]{1,0:T(8,128)(2,1)S(1)}, bf16[32,576]{1,0:T(8,128)(2,1)S(1)}, u32[]{:S(2)}, u32[]{:S(2)}) collective-permute-start(bf16[32,576]{1,0:T(8,128)(2,1)S(1)} %get-tuple-element.145), channel_id=1, source_target_pairs={{0,8},{8,0},{16,24},{24,16},{1,9},{9,1},{17,25},{25,17},{2,10},{10... | collective-permute-start | bytes 110600 | tf_op jit(solution)/shard_map/ppermute | solution.py:1002
  13.2 4.0 %collective-permute-start.1 = (bf16[32,576]{1,0:T(8,128)(2,1)S(1)}, bf16[32,576]{1,0:T(8,128)(2,1)S(1)}, u32[]{:S(2)}, u32[]{:S(2)}) collective-permute-start(bf16[32,576]{1,0:T(8,128)(2,1)S(1)} %get-tuple-element.144), channel_id=1, source_target_pairs={{0,16},{8,24},{16,0},{24,8},{1,17},{9,25},{17,1},{25,9},{2,18},{10... | collective-permute-start | bytes 110600 | tf_op jit(solution)/shard_map/ppermute | solution.py:1002
  14.7 4.9 %collective-permute-start.2 = (bf16[32,576]{1,0:T(8,128)(2,1)S(1)}, bf16[32,576]{1,0:T(8,128)(2,1)S(1)}, u32[]{:S(2)}, u32[]{:S(2)}) collective-permute-start(bf16[32,576]{1,0:T(8,128)(2,1)S(1)} %get-tuple-element.143), channel_id=1, source_target_pairs={{0,24},{8,16},{16,8},{24,0},{1,25},{9,17},{17,9},{25,1},{2,26},{10... | collective-permute-start | bytes 110600 | tf_op jit(solution)/shard_map/ppermute | solution.py:1002
  19.7 28.5 %collective-permute-start.6 = (bf16[768,768]{1,0:T(8,128)(2,1)S(1)}, bf16[768,768]{1,0:T(8,128)(2,1)S(1)}, u32[]{:S(2)}, u32[]{:S(2)}) collective-permute-start(bf16[768,768]{1,0:T(8,128)(2,1)S(1)} %copy-done.14), channel_id=1, source_target_pairs={{0,8},{8,0},{16,24},{24,16},{1,9},{9,1},{17,25},{25,17},{2,10},{10... | collective-permute-start | bytes 3538952 | tf_op jit(solution)/shard_map/ppermute | solution.py:1002
  20.3 28.4 %collective-permute-start.7 = (bf16[768,768]{1,0:T(8,128)(2,1)S(1)}, bf16[768,768]{1,0:T(8,128)(2,1)}, u32[]{:S(2)}, u32[]{:S(2)}) collective-permute-start(bf16[768,768]{1,0:T(8,128)(2,1)S(1)} %copy-done.14), channel_id=1, source_target_pairs={{0,16},{8,24},{16,0},{24,8},{1,17},{9,25},{17,1},{25,9},{2,18},{10... | collective-permute-start | bytes 3538952 | tf_op jit(solution)/shard_map/ppermute | solution.py:1002
  20.3 10.0 %collective-permute-start.3 = (bf16[4,32,576]{2,1,0:T(8,128)(2,1)S(1)}, bf16[4,32,576]{2,1,0:T(8,128)(2,1)S(1)}, u32[]{:S(2)}, u32[]{:S(2)}) collective-permute-start(bf16[4,32,576]{2,1,0:T(8,128)(2,1)S(1)} %pad_maximum_fusion.1), channel_id=1, source_target_pairs={{0,2},{1,3},{2,0},{3,1},{4,6},{5,7},{6,4},{7,5},{8,10},{9,11},{10,... | collective-permute-start | bytes 442376 | tf_op jit(solution)/shard_map/ppermute | solution.py:1007
  22.4 20.1 %collective-permute-start.4 = (bf16[4,32,576]{2,1,0:T(8,128)(2,1)S(1)}, bf16[4,32,576]{2,1,0:T(8,128)(2,1)S(1)}, u32[]{:S(2)}, u32[]{:S(2)}) collective-permute-start(bf16[4,32,576]{2,1,0:T(8,128)(2,1)S(1)} %pad_maximum_fusion.1), channel_id=1, source_target_pairs={{0,4},{1,5},{2,6},{3,7},{4,0},{5,1},{6,2},{7,3},{8,12},{9,13},{10,... | collective-permute-start | bytes 442376 | tf_op jit(solution)/shard_map/ppermute | solution.py:1007
  24.9 17.5 %collective-permute-start.5 = (bf16[4,32,576]{2,1,0:T(8,128)(2,1)S(1)}, bf16[4,32,576]{2,1,0:T(8,128)(2,1)S(1)}, u32[]{:S(2)}, u32[]{:S(2)}) collective-permute-start(bf16[4,32,576]{2,1,0:T(8,128)(2,1)S(1)} %pad_maximum_fusion.1), channel_id=1, source_target_pairs={{0,6},{1,7},{2,4},{3,5},{4,2},{5,3},{6,0},{7,1},{8,14},{9,15},{10,... | collective-permute-start | bytes 442376 | tf_op jit(solution)/shard_map/ppermute | solution.py:1007
  42.6 8.0 %copy-start.4 = (bf16[4,4,32,576]{3,2,1,0:T(8,128)(2,1)}, bf16[4,4,32,576]{3,2,1,0:T(8,128)(2,1)S(1)}, u32[]{:S(2)}) copy-start(bf16[4,4,32,576]{3,2,1,0:T(8,128)(2,1)S(1)} %pad_maximum_fusion.refs_5_) | copy-start | bytes 1769476
  48.2 3.9 %copy-start.10 = (bf16[768,768]{1,0:T(8,128)(2,1)}, bf16[768,768]{1,0:T(8,128)(2,1)S(1)}, u32[]{:S(2)}) copy-start(bf16[768,768]{1,0:T(8,128)(2,1)S(1)} %collective-permute-done.6.refs_2_.x1_ref) | copy-start | bytes 3538948
  48.7 4.5 %collective-permute-start.10 = (bf16[4,4,32,576]{3,2,1,0:T(8,128)(2,1)S(1)}, bf16[4,4,32,576]{3,2,1,0:T(8,128)(2,1)}, u32[]{:S(2)}, u32[]{:S(2)}) collective-permute-start(bf16[4,4,32,576]{3,2,1,0:T(8,128)(2,1)S(1)} %pad_maximum_fusion.refs_5_), channel_id=1, source_target_pairs={{0,1},{1,0},{2,3},{3,2},{4,5},{5,4},{6,7},{7,6},{8,9},{9,8},{10,11... | collective-permute-start | bytes 1769480 | tf_op jit(solution)/shard_map/ppermute | solution.py:1007
  49.4 3.8 %copy-start.15 = (bf16[768,768]{1,0:T(8,128)(2,1)S(1)}, bf16[768,768]{1,0:T(8,128)(2,1)}, u32[]{:S(2)}) copy-start(bf16[768,768]{1,0:T(8,128)(2,1)} %x0_ref.1) | copy-start | bytes 3538948
  50.6 22.5 %collective-permute-start.8 = (bf16[384,768]{1,0:T(8,128)(2,1)S(1)}, bf16[384,768]{1,0:T(8,128)(2,1)S(1)}, u32[]{:S(2)}, u32[]{:S(2)}) collective-permute-start(bf16[384,768]{1,0:T(8,128)(2,1)S(1)} %slice.72), channel_id=1, source_target_pairs={{0,8},{8,0},{16,24},{24,16},{1,9},{9,1},{17,25},{25,17},{2,10},{10... | collective-permute-start | bytes 1769480 | tf_op jit(solution)/shard_map/ppermute | solution.py:1002
  52.1 1.2 copy-start.5
  52.1 21.1 %collective-permute-start.9 = (bf16[384,768]{1,0:T(8,128)(2,1)S(1)}, bf16[384,768]{1,0:T(8,128)(2,1)S(1)}, u32[]{:S(2)}, u32[]{:S(2)}) collective-permute-start(bf16[384,768]{1,0:T(8,128)(2,1)S(1)} %slice.73), channel_id=1, source_target_pairs={{0,16},{8,24},{16,0},{24,8},{1,17},{9,25},{17,1},{25,9},{2,18},{10... | collective-permute-start | bytes 1769480 | tf_op jit(solution)/shard_map/ppermute | solution.py:1002
  52.9 201.7 %copy-start.13 = (s32[4]{0:T(128)}, s32[4]{0:T(128)S(1)}, u32[]{:S(2)}) copy-start(s32[4]{0:T(128)S(1)} %pad_add_fusion.1.refs_0_.me_ref) | copy-start | bytes 52
  53.2 1.3 copy-start.11
  60.7 14.2 %copy-start.3 = (bf16[3,768,192]{2,1,0:T(8,128)(2,1)}, bf16[3,768,192]{2,1,0:T(8,128)(2,1)S(1)}, u32[]{:S(2)}) copy-start(bf16[3,768,192]{2,1,0:T(8,128)(2,1)S(1)} %get-tuple-element.77.refs_4_.refs_15_) | copy-start | bytes 2654212
  73.2 1.7 copy-start.6
  73.2 1.7 copy-start.8
  74.9 27.3 %copy-start = (bf16[3072,256]{1,0:T(8,128)(2,1)}, bf16[3072,256]{1,0:T(8,128)(2,1)S(1)}, u32[]{:S(2)}) copy-start(bf16[3072,256]{1,0:T(8,128)(2,1)S(1)} %get-tuple-element.82.refs_3_) | copy-start | bytes 4718596
  74.9 27.3 %copy-start.1 = (bf16[3072,256]{1,0:T(8,128)(2,1)}, bf16[3072,256]{1,0:T(8,128)(2,1)S(1)}, u32[]{:S(2)}) copy-start(bf16[3072,256]{1,0:T(8,128)(2,1)S(1)} %get-tuple-element.83.refs_4_) | copy-start | bytes 4718596
  74.9 27.3 %copy-start.2 = (bf16[3072,192]{1,0:T(8,128)(2,1)}, bf16[3072,192]{1,0:T(8,128)(2,1)S(1)}, u32[]{:S(2)}) copy-start(bf16[3072,192]{1,0:T(8,128)(2,1)S(1)} %get-tuple-element.84.refs_5_) | copy-start | bytes 3538948
  103.5 67.0 %copy-start.17 = (bf16[192,768]{1,0:T(8,128)(2,1)}, bf16[192,768]{1,0:T(8,128)(2,1)S(1)}, u32[]{:S(2)}) copy-start(bf16[192,768]{1,0:T(8,128)(2,1)S(1)} %get-tuple-element.86.refs_11_) | copy-start | bytes 884740
  103.5 67.0 %copy-start.18 = (bf16[192,768]{1,0:T(8,128)(2,1)}, bf16[192,768]{1,0:T(8,128)(2,1)S(1)}, u32[]{:S(2)}) copy-start(bf16[192,768]{1,0:T(8,128)(2,1)S(1)} %get-tuple-element.87.refs_12_) | copy-start | bytes 884740
  103.5 67.0 %copy-start.19 = (bf16[192,768]{1,0:T(8,128)(2,1)}, bf16[192,768]{1,0:T(8,128)(2,1)S(1)}, u32[]{:S(2)}) copy-start(bf16[192,768]{1,0:T(8,128)(2,1)S(1)} %get-tuple-element.88.refs_13_) | copy-start | bytes 884740
  103.5 9.9 %collective-permute-start.11 = (bf16[192,768]{1,0:T(8,128)(2,1)S(1)}, bf16[192,768]{1,0:T(8,128)(2,1)S(1)}, u32[]{:S(2)}, u32[]{:S(2)}) collective-permute-start(bf16[192,768]{1,0:T(8,128)(2,1)S(1)} %get-tuple-element.86.refs_11_), channel_id=1, source_target_pairs={{0,8},{8,0},{16,24},{24,16},{1,9},{9,1},{17,25},{25,17},{2,10},{10... | collective-permute-start | bytes 884744 | tf_op jit(solution)/shard_map/ppermute | solution.py:1002
  103.8 14.3 %collective-permute-start.12 = (bf16[192,768]{1,0:T(8,128)(2,1)S(1)}, bf16[192,768]{1,0:T(8,128)(2,1)S(1)}, u32[]{:S(2)}, u32[]{:S(2)}) collective-permute-start(bf16[192,768]{1,0:T(8,128)(2,1)S(1)} %get-tuple-element.87.refs_12_), channel_id=1, source_target_pairs={{0,16},{8,24},{16,0},{24,8},{1,17},{9,25},{17,1},{25,9},{2,18},{10... | collective-permute-start | bytes 884744 | tf_op jit(solution)/shard_map/ppermute | solution.py:1002
  105.6 14.2 %collective-permute-start.13 = (bf16[192,768]{1,0:T(8,128)(2,1)S(1)}, bf16[192,768]{1,0:T(8,128)(2,1)S(1)}, u32[]{:S(2)}, u32[]{:S(2)}) collective-permute-start(bf16[192,768]{1,0:T(8,128)(2,1)S(1)} %get-tuple-element.88.refs_13_), channel_id=1, source_target_pairs={{0,24},{8,16},{16,8},{24,0},{1,25},{9,17},{17,9},{25,1},{2,26},{10... | collective-permute-start | bytes 884744 | tf_op jit(solution)/shard_map/ppermute | solution.py:1002
  113.4 6.4 %copy-start.33 = (bf16[192,768]{1,0:T(8,128)(2,1)}, bf16[192,768]{1,0:T(8,128)(2,1)S(1)}, u32[]{:S(2)}) copy-start(bf16[192,768]{1,0:T(8,128)(2,1)S(1)} %collective-permute-done.11.refs_4_) | copy-start | bytes 884740
  118.2 1.6 copy-start.34
  170.6 9.3 %collective-permute-start.14 = (bf16[4,4,224,768]{3,2,1,0:T(8,128)(2,1)}, bf16[4,4,224,768]{3,2,1,0:T(8,128)(2,1)S(1)}, u32[]{:S(2)}, u32[]{:S(2)}) collective-permute-start(bf16[4,4,224,768]{3,2,1,0:T(8,128)(2,1)} %get-tuple-element.92), channel_id=1, source_target_pairs={{0,1},{1,0},{2,3},{3,2},{4,5},{5,4},{6,7},{7,6},{8,9},{9,8},{10,11... | collective-permute-start | bytes 16515080 | tf_op jit(solution)/shard_map/ppermute | solution.py:1007
  170.6 15.9 %collective-permute-start.15 = (bf16[192,768]{1,0:T(8,128)(2,1)}, bf16[192,768]{1,0:T(8,128)(2,1)S(1)}, u32[]{:S(2)}, u32[]{:S(2)}) collective-permute-start(bf16[192,768]{1,0:T(8,128)(2,1)} %get-tuple-element.94), channel_id=1, source_target_pairs={{0,8},{8,0},{16,24},{24,16},{1,9},{9,1},{17,25},{25,17},{2,10},{10... | collective-permute-start | bytes 884744 | tf_op jit(solution)/shard_map/ppermute | solution.py:1002
  171.8 15.6 %collective-permute-start.16 = (bf16[192,768]{1,0:T(8,128)(2,1)}, bf16[192,768]{1,0:T(8,128)(2,1)S(1)}, u32[]{:S(2)}, u32[]{:S(2)}) collective-permute-start(bf16[192,768]{1,0:T(8,128)(2,1)} %get-tuple-element.95), channel_id=1, source_target_pairs={{0,16},{8,24},{16,0},{24,8},{1,17},{9,25},{17,1},{25,9},{2,18},{10... | collective-permute-start | bytes 884744 | tf_op jit(solution)/shard_map/ppermute | solution.py:1002
  173.3 14.2 %collective-permute-start.17 = (bf16[192,768]{1,0:T(8,128)(2,1)}, bf16[192,768]{1,0:T(8,128)(2,1)S(1)}, u32[]{:S(2)}, u32[]{:S(2)}) collective-permute-start(bf16[192,768]{1,0:T(8,128)(2,1)} %get-tuple-element.96), channel_id=1, source_target_pairs={{0,24},{8,16},{16,8},{24,0},{1,25},{9,17},{17,9},{25,1},{2,26},{10... | collective-permute-start | bytes 884744 | tf_op jit(solution)/shard_map/ppermute | solution.py:1002
  186.5 1.0 copy-start.30
  187.4 0.8 copy-start.32
  188.3 119.3 %reduce-scatter.5.cloned.1.call-start = ((), (), s32[]{:S(2)}) async-start(), calls=%async_computation.3 | async-start | bytes 1720320 | tf_op jit(solution)/shard_map/reduce_scatter | solution.py:1155
  189.2 65.4 %copy-start.7 = (bf16[384,768]{1,0:T(8,128)(2,1)S(1)}, bf16[384,768]{1,0:T(8,128)(2,1)}, u32[]{:S(2)}) copy-start(bf16[384,768]{1,0:T(8,128)(2,1)} %copy-done.6) | copy-start | bytes 1769476
  189.2 65.4 %copy-start.9 = (bf16[384,768]{1,0:T(8,128)(2,1)S(1)}, bf16[384,768]{1,0:T(8,128)(2,1)}, u32[]{:S(2)}) copy-start(bf16[384,768]{1,0:T(8,128)(2,1)} %copy-done.8) | copy-start | bytes 1769476
  189.2 65.4 %copy-start.12 = (bf16[768,768]{1,0:T(8,128)(2,1)S(1)}, bf16[768,768]{1,0:T(8,128)(2,1)}, u32[]{:S(2)}) copy-start(bf16[768,768]{1,0:T(8,128)(2,1)} %copy-done.10) | copy-start | bytes 3538948
  252.6 27.8 %collective-permute-start.18 = (bf16[768,768]{1,0:T(8,128)(2,1)}, bf16[768,768]{1,0:T(8,128)(2,1)}, u32[]{:S(2)}, u32[]{:S(2)}) collective-permute-start(bf16[768,768]{1,0:T(8,128)(2,1)} %get-tuple-element.104), channel_id=1, source_target_pairs={{0,8},{8,0},{16,24},{24,16},{1,9},{9,1},{17,25},{25,17},{2,10},{10... | collective-permute-start | bytes 3538952 | tf_op jit(solution)/shard_map/ppermute | solution.py:1002
  253.7 27.8 %collective-permute-start.19 = (bf16[768,768]{1,0:T(8,128)(2,1)}, bf16[768,768]{1,0:T(8,128)(2,1)}, u32[]{:S(2)}, u32[]{:S(2)}) collective-permute-start(bf16[768,768]{1,0:T(8,128)(2,1)} %get-tuple-element.105), channel_id=1, source_target_pairs={{0,16},{8,24},{16,0},{24,8},{1,17},{9,25},{17,1},{25,9},{2,18},{10... | collective-permute-start | bytes 3538952 | tf_op jit(solution)/shard_map/ppermute | solution.py:1002
  254.6 1.3 copy-start.16
  255.9 2.0 copy-start.20
  264.0 2.1 collective-permute-start.22
  266.1 15.5 %copy-start.25 = (f32[384,768]{1,0:T(8,128)S(1)}, f32[384,768]{1,0:T(8,128)}, u32[]{:S(2)}) copy-start(f32[384,768]{1,0:T(8,128)} %get-tuple-element.107) | copy-start | bytes 3538948
  266.2 19.6 %collective-permute-start.23 = (bf16[4,24,768]{2,1,0:T(8,128)(2,1)S(1)}, bf16[4,24,768]{2,1,0:T(8,128)(2,1)S(1)}, u32[]{:S(2)}, u32[]{:S(2)}) collective-permute-start(bf16[4,24,768]{2,1,0:T(8,128)(2,1)S(1)} %get-tuple-element.135), channel_id=1, source_target_pairs={{0,2},{1,3},{2,0},{3,1},{4,6},{5,7},{6,4},{7,5},{8,10},{9,11},{10,... | collective-permute-start | bytes 442376 | tf_op jit(solution)/shard_map/ppermute | solution.py:1007
  269.1 19.6 %collective-permute-start.24 = (bf16[4,24,768]{2,1,0:T(8,128)(2,1)S(1)}, bf16[4,24,768]{2,1,0:T(8,128)(2,1)S(1)}, u32[]{:S(2)}, u32[]{:S(2)}) collective-permute-start(bf16[4,24,768]{2,1,0:T(8,128)(2,1)S(1)} %get-tuple-element.137), channel_id=1, source_target_pairs={{0,4},{1,5},{2,6},{3,7},{4,0},{5,1},{6,2},{7,3},{8,12},{9,13},{10,... | collective-permute-start | bytes 442376 | tf_op jit(solution)/shard_map/ppermute | solution.py:1007
  271.7 17.0 %collective-permute-start.25 = (bf16[4,24,768]{2,1,0:T(8,128)(2,1)S(1)}, bf16[4,24,768]{2,1,0:T(8,128)(2,1)S(1)}, u32[]{:S(2)}, u32[]{:S(2)}) collective-permute-start(bf16[4,24,768]{2,1,0:T(8,128)(2,1)S(1)} %get-tuple-element.136), channel_id=1, source_target_pairs={{0,6},{1,7},{2,4},{3,5},{4,2},{5,3},{6,0},{7,1},{8,14},{9,15},{10,... | collective-permute-start | bytes 442376 | tf_op jit(solution)/shard_map/ppermute | solution.py:1007
  281.5 2.5 copy-start.24
  282.8 14.8 %collective-permute-start.20 = (bf16[384,768]{1,0:T(8,128)(2,1)S(1)}, bf16[384,768]{1,0:T(8,128)(2,1)S(1)}, u32[]{:S(2)}, u32[]{:S(2)}) collective-permute-start(bf16[384,768]{1,0:T(8,128)(2,1)S(1)} %add_convert_fusion.3), channel_id=1, source_target_pairs={{0,16},{8,24},{16,0},{24,8},{1,17},{9,25},{17,1},{25,9},{2,18},{10... | collective-permute-start | bytes 1769480 | tf_op jit(solution)/shard_map/ppermute | solution.py:1002
  285.2 15.6 %collective-permute-start.21 = (bf16[384,768]{1,0:T(8,128)(2,1)S(1)}, bf16[384,768]{1,0:T(8,128)(2,1)S(1)}, u32[]{:S(2)}, u32[]{:S(2)}) collective-permute-start(bf16[384,768]{1,0:T(8,128)(2,1)S(1)} %add_convert_fusion.2), channel_id=1, source_target_pairs={{0,8},{8,0},{16,24},{24,16},{1,9},{9,1},{17,25},{25,17},{2,10},{10... | collective-permute-start | bytes 1769480 | tf_op jit(solution)/shard_map/ppermute | solution.py:1002
  289.4 14.3 %collective-permute-start.26 = (f32[24,768]{1,0:T(8,128)S(1)}, f32[24,768]{1,0:T(8,128)S(1)}, u32[]{:S(2)}, u32[]{:S(2)}) collective-permute-start(f32[24,768]{1,0:T(8,128)S(1)} %get-tuple-element.140), channel_id=1, source_target_pairs={{0,8},{8,0},{16,24},{24,16},{1,9},{9,1},{17,25},{25,17},{2,10},{10... | collective-permute-start | bytes 221192 | tf_op jit(solution)/shard_map/ppermute | solution.py:1002
  290.2 13.6 %collective-permute-start.27 = (f32[24,768]{1,0:T(8,128)S(1)}, f32[24,768]{1,0:T(8,128)S(1)}, u32[]{:S(2)}, u32[]{:S(2)}) collective-permute-start(f32[24,768]{1,0:T(8,128)S(1)} %get-tuple-element.139), channel_id=1, source_target_pairs={{0,16},{8,24},{16,0},{24,8},{1,17},{9,25},{17,1},{25,9},{2,18},{10... | collective-permute-start | bytes 221192 | tf_op jit(solution)/shard_map/ppermute | solution.py:1002
  290.2 13.6 %collective-permute-start.28 = (f32[24,768]{1,0:T(8,128)S(1)}, f32[24,768]{1,0:T(8,128)S(1)}, u32[]{:S(2)}, u32[]{:S(2)}) collective-permute-start(f32[24,768]{1,0:T(8,128)S(1)} %get-tuple-element.138), channel_id=1, source_target_pairs={{0,24},{8,16},{16,8},{24,0},{1,25},{9,17},{17,9},{25,1},{2,26},{10... | collective-permute-start | bytes 221192 | tf_op jit(solution)/shard_map/ppermute | solution.py:1002
  298.8 3.3 %copy-start.23 = (f32[768,768]{1,0:T(8,128)S(1)}, f32[768,768]{1,0:T(8,128)}, u32[]{:S(2)}) copy-start(f32[768,768]{1,0:T(8,128)} %get-tuple-element.103) | copy-start | bytes 7077892
  303.8 3.8 %copy-start.27 = (f32[24,768]{1,0:T(8,128)}, f32[24,768]{1,0:T(8,128)S(1)}, u32[]{:S(2)}) copy-start(f32[24,768]{1,0:T(8,128)S(1)} %collective-permute-done.26.refs_2_) | copy-start | bytes 221188
  303.8 3.8 %copy-start.28 = (f32[24,768]{1,0:T(8,128)}, f32[24,768]{1,0:T(8,128)S(1)}, u32[]{:S(2)}) copy-start(f32[24,768]{1,0:T(8,128)S(1)} %collective-permute-done.27.refs_3_) | copy-start | bytes 221188
  303.8 3.8 %copy-start.29 = (f32[24,768]{1,0:T(8,128)}, f32[24,768]{1,0:T(8,128)S(1)}, u32[]{:S(2)}) copy-start(f32[24,768]{1,0:T(8,128)S(1)} %collective-permute-done.28.refs_4_) | copy-start | bytes 221188
  (4 other events, 2.8 us)
Sparse Core Ops, SparseCore 0:
  11.6 105.8 all-gather.2
  187.6 64.8 reduce-scatter.2
  264.2 43.2 reduce-scatter.4
